TPU v7x, 256 devices: a whole 4x4x8 slice. The times are simulated.
256 devices in a mesh: grp: 8 (over x, core), seq: 32 (over z, y).
Axes of the slice: x: 4, y: 4, z: 8, core: 2. Of those that a mesh axis runs over, the one named last changes fastest.
Arguments:
- spikes: bfloat16 [8, 4096, 256], P('grp', 'seq'), may hold values from -6 to 6
- session_of_bin: int32 [8, 4096], P('grp', 'seq'), may hold values from 0 to 15, as said below
- session_slot: int32 [16], replicated, may hold values from 0 to 15, as said below
- readin_weight: bfloat16 [16, 256, 4096], P('grp'), may hold values from -0.375 to 0.375
- short_kernel: float32 [3, 2048], replicated, may hold values from -3.5 to 3.5
- long_filter: float32 [2048, 4096], P('seq')
- skip_gain: float32 [2048], P('seq'), may hold values from 0.5 to 1.5
- readout_weight: bfloat16 [16, 2048, 256], P('grp'), may hold values from -0.125 to 0.125
- out_grad: bfloat16 [8, 4096, 2048], P('grp', 'seq'), may hold values from -0.03125 to 0.03125
Outputs:
- denoised: bfloat16 [8, 4096, 256], P('grp', 'seq')
- filter_grad: float32 [2048, 4096], P('seq')
Inputs may be any that keep to these rules, and one draw needn't show every extreme that they name: `session_slot`: each slot holds exactly one session. `session_of_bin`: each sequence is made of aligned runs of 16 bins of one session (trials); among the 128 bins of one device at most 32 belong to sessions whose slots lie in one aligned range of 2 slots, and in every such block some range takes exactly 32.
All inputs are finite; a program needn't handle non-finite values.
Results may differ from a plain program's by a relative error of at most 0.017.
Values may be sent and summed in bfloat16 or wider, within the bound.
No kernel may reach another device: no remote copies, remote signals or barrier semaphores. Data moves between devices by JAX's collectives and lax.ppermute only.
A program may use at most 128 MiB of HBM per device.

v0:
```python
import functools

import jax
import jax.numpy as jnp
import numpy as np
from jax import lax
from jax.experimental import pallas as pl
from jax.experimental.pallas import tpu as pltpu
from jax.sharding import PartitionSpec as P

BLOCK = 128
TRIAL = 16
Z = 8
Y = 4
BLOCKS = Z * Y
CHANS = 64
LANE8 = 8
GROUPS = CHANS // LANE8
LENGTH = BLOCKS * BLOCK
PAD_ROWS = 16
Y_STEPS = (0, -1, 1, 2)
f32 = jnp.float32
bf16 = jnp.bfloat16


def transform_tables():
    slow = np.arange(BLOCKS)
    fast = np.arange(BLOCK)
    first = np.exp(-2j * np.pi * (np.outer(slow, slow) / BLOCKS + slow[None, :] / (4.0 * BLOCKS)))
    twist = np.exp(-2j * np.pi * (slow[:, None] + 0.25) * fast[None, :] / LENGTH)
    second = np.exp(-2j * np.pi * np.outer(fast, fast) / BLOCK)
    eye = np.eye(LANE8)
    spread_first = np.concatenate([np.kron(first.real, eye), np.kron(first.imag, eye)], 0)
    forward_second = np.block([[second.real, second.imag], [-second.imag, second.real]])
    back = second.conj()
    back_second = np.block([[back.real, back.imag], [-back.imag, back.real]])
    back_first = first.conj().T / LENGTH
    spread_back = np.concatenate([np.kron(back_first.real, eye), np.kron(-back_first.imag, eye)], 1)
    as_bf16 = lambda table: jnp.asarray(table.astype(np.float32), bf16)
    twists = np.stack([twist.real, twist.imag]).astype(np.float32)
    return (
        as_bf16(spread_first),
        as_bf16(forward_second),
        as_bf16(back_second),
        as_bf16(spread_back),
        jnp.asarray(twists),
    )


def twists_of(twist_ref):
    shape = (BLOCKS, LANE8, BLOCK)
    cosine = jnp.broadcast_to(twist_ref[0][:, None, :], shape).reshape(BLOCKS * LANE8, BLOCK)
    sine = jnp.broadcast_to(twist_ref[1][:, None, :], shape).reshape(BLOCKS * LANE8, BLOCK)
    return cosine, sine


def forward(signal, first_ref, second_ref, cosine, sine):
    rows = BLOCKS * LANE8
    part = jnp.dot(first_ref[...], signal.astype(bf16), preferred_element_type=f32)
    real, imag = part[:rows], part[rows:]
    turned = jnp.concatenate([real * cosine - imag * sine, real * sine + imag * cosine], 1)
    return jnp.dot(turned.astype(bf16), second_ref[...], preferred_element_type=f32)


def backward(real, imag, back_second_ref, back_first_ref, cosine, sine):
    both = jnp.concatenate([real, imag], 1).astype(bf16)
    part = jnp.dot(both, back_second_ref[...], preferred_element_type=f32)
    real, imag = part[:, :BLOCK], part[:, BLOCK:]
    turned = jnp.concatenate([real * cosine + imag * sine, imag * cosine - real * sine], 0)
    return jnp.dot(back_first_ref[...], turned.astype(bf16), preferred_element_type=f32)


def filter_kernel(filter_ref, first_ref, second_ref, twist_ref, spectrum_ref):
    cosine, sine = twists_of(twist_ref)

    def step(group, carry):
        rows = filter_ref[pl.ds(pl.multiple_of(group * LANE8, LANE8), LANE8), :]
        signal = jnp.concatenate([rows[:, i * BLOCK : (i + 1) * BLOCK] for i in range(BLOCKS)], 0)
        spectrum_ref[group] = forward(signal, first_ref, second_ref, cosine, sine)
        return carry

    lax.fori_loop(0, GROUPS, step, 0)


def read_in_kernel(chunk_ref, weight_ref, out_ref):
    blocks = chunk_ref.shape[0]
    slots = weight_ref.shape[0]
    width = weight_ref.shape[2]
    trials = BLOCK // TRIAL
    for index in range(blocks):
        rows = chunk_ref[index, :BLOCK, :]
        marks = chunk_ref[index, BLOCK:, :].astype(f32)[:trials, :width]
        marks = jnp.broadcast_to(marks[:, None, :], (trials, TRIAL, width)).reshape(BLOCK, width)
        chosen = jnp.zeros((BLOCK, width), f32)
        for slot in range(slots):
            product = jnp.dot(rows, weight_ref[slot], preferred_element_type=f32)
            chosen = jnp.where(marks == slot, product, chosen)
        out_ref[index] = chosen.T.astype(bf16)


def read_in(chunk, weights, ordinal):
    blocks = chunk.shape[0]
    width = weights.shape[2]
    flops = 2 * blocks * BLOCK * weights.shape[0] * weights.shape[1] * width
    return pl.pallas_call(
        read_in_kernel,
        out_shape=jax.ShapeDtypeStruct((blocks, width, BLOCK), bf16),
        in_specs=[pl.BlockSpec(memory_space=pltpu.VMEM)] * 2,
        out_specs=pl.BlockSpec(memory_space=pltpu.VMEM),
        compiler_params=pltpu.CompilerParams(vmem_limit_bytes=16 << 20),
        cost_estimate=pl.CostEstimate(flops=flops, bytes_accessed=chunk.size * 2 + weights.size * 2, transcendentals=0),
        name="read_in",
    )(chunk, weights)


def main_kernel(place_ref, taps_ref, gain_ref, filter_ref, first_ref, second_ref, back_second_ref, back_first_ref, twist_ref, *rest):
    chunk_refs = rest[:-5]
    gated_ref, gate_ref, spectrum_ref, value_all, gate_all = rest[-5:]
    z = place_ref[0]
    y = place_ref[1]
    steps = (0, -1, 1, -2, 2, -3, 3, 4)
    for chunk_ref, z_step in zip(chunk_refs, steps):
        for index, y_step in enumerate(Y_STEPS):
            block = lax.rem(z + (z_step + Z), Z) * Y + lax.rem(y + (y_step + Y), Y)
            both = chunk_ref[index].astype(f32)
            value_all[block] = both[:CHANS]
            gate_all[block] = both[CHANS:]
    cosine, sine = twists_of(twist_ref)
    lane = lax.broadcasted_iota(jnp.int32, (BLOCKS, LANE8, BLOCK), 2)
    rows = BLOCKS * LANE8

    def one_group(group):
        here = pl.ds(pl.multiple_of(group * LANE8, LANE8), LANE8)
        value = value_all[:, here, :]
        taps = taps_ref[:, here, :]
        total = taps[0][None] * value
        for shift in (1, 2):
            rolled = pltpu.roll(value.reshape(rows, BLOCK), shift, 1).reshape(BLOCKS, LANE8, BLOCK)
            before = jnp.concatenate([jnp.zeros((1, LANE8, BLOCK), f32), rolled[:-1]], 0)
            total = total + taps[shift][None] * jnp.where(lane < shift, before, rolled)
        signal = total.astype(bf16).astype(f32).reshape(rows, BLOCK)
        spectrum = forward(signal, first_ref, second_ref, cosine, sine)
        spectrum_ref[group] = spectrum
        weight = filter_ref[group]
        real = spectrum[:, :BLOCK] * weight[:, :BLOCK] - spectrum[:, BLOCK:] * weight[:, BLOCK:]
        imag = spectrum[:, :BLOCK] * weight[:, BLOCK:] + spectrum[:, BLOCK:] * weight[:, :BLOCK]
        long_part = backward(real, imag, back_second_ref, back_first_ref, cosine, sine)
        mixed = long_part.reshape(BLOCKS, LANE8, BLOCK) + gain_ref[here, :][None] * signal.reshape(BLOCKS, LANE8, BLOCK)
        gate = gate_all[:, here, :]
        return gate * mixed.astype(bf16).astype(f32), gate

    def step(pair, carry):
        gated_low, gate_low = one_group(pair * 2)
        gated_high, gate_high = one_group(pair * 2 + 1)
        here = pl.ds(pl.multiple_of(pair * 2 * LANE8, 2 * LANE8), 2 * LANE8)
        gated_ref[:, here, :] = jnp.concatenate([gated_low, gated_high], 1).astype(bf16)
        gate_ref[:, here, :] = jnp.concatenate([gate_low, gate_high], 1).astype(bf16)
        return carry

    lax.fori_loop(0, GROUPS // 2, step, 0)


def gradient_kernel(grad_ref, gate_ref, spectrum_ref, first_ref, second_ref, back_second_ref, back_first_ref, twist_ref, out_ref):
    cosine, sine = twists_of(twist_ref)
    rows = BLOCKS * LANE8

    def one_group(product, group):
        grad_spectrum = forward(product.reshape(rows, BLOCK), first_ref, second_ref, cosine, sine)
        spectrum = spectrum_ref[group]
        real = spectrum[:, :BLOCK] * grad_spectrum[:, :BLOCK] + spectrum[:, BLOCK:] * grad_spectrum[:, BLOCK:]
        imag = spectrum[:, :BLOCK] * grad_spectrum[:, BLOCK:] - spectrum[:, BLOCK:] * grad_spectrum[:, :BLOCK]
        result = backward(real, imag, back_second_ref, back_first_ref, cosine, sine)
        return jnp.concatenate([result[i * LANE8 : (i + 1) * LANE8] for i in range(BLOCKS)], 1)

    def step(pair, carry):
        here = pl.ds(pl.multiple_of(pair * 2 * LANE8, 2 * LANE8), 2 * LANE8)
        product = grad_ref[:, here, :].astype(f32) * gate_ref[:, here, :].astype(f32)
        product = product.astype(bf16).astype(f32)
        low = one_group(product[:, :LANE8], pair * 2)
        high = one_group(product[:, LANE8:], pair * 2 + 1)
        out_ref[here, :] = jnp.concatenate([low, high], 0).astype(bf16)
        return carry

    lax.fori_loop(0, GROUPS // 2, step, 0)


def read_out_kernel(place_ref, rows_ref, chunk_ref, weight_ref, out_ref):
    y = place_ref[1]
    trials = BLOCK // TRIAL
    slots = weight_ref.shape[0]
    inner = weight_ref.shape[1]
    width = weight_ref.shape[2]
    pieces = []
    marks = []
    for index, y_step in enumerate(Y_STEPS):
        block = lax.rem(y + (y_step + Y), Y)
        pieces.append(rows_ref[:, block, :, :].reshape(inner, BLOCK).T)
        mark = chunk_ref[index, BLOCK:, :].astype(f32)[:trials, :width]
        marks.append(jnp.broadcast_to(mark[:, None, :], (trials, TRIAL, width)).reshape(BLOCK, width))
    rows = jnp.concatenate(pieces, 0)
    marks = jnp.concatenate(marks, 0)
    chosen = jnp.zeros((Y * BLOCK, width), f32)
    for slot in range(slots):
        product = jnp.dot(rows, weight_ref[slot], preferred_element_type=f32)
        chosen = jnp.where(marks == slot, product, chosen)
    for index, y_step in enumerate(Y_STEPS):
        block = lax.rem(y + (y_step + Y), Y)
        out_ref[block] = chosen[index * BLOCK : (index + 1) * BLOCK].astype(bf16)


def along_y(value, step):
    return lax.ppermute(value, "seq", [(z * Y + y, z * Y + (y + step) % Y) for z in range(Z) for y in range(Y)])


def along_z(value, step):
    return lax.ppermute(value, "seq", [(z * Y + y, (z + step) % Z * Y + y) for z in range(Z) for y in range(Y)])


def whole(count):
    return [pl.BlockSpec(memory_space=pltpu.VMEM)] * count


def local(spikes, session_of_bin, session_slot, readin_weight, short_kernel, long_filter, skip_gain, readout_weight, out_grad):
    experts_here = readin_weight.shape[0]
    in_chans = spikes.shape[2]
    model_width = short_kernel.shape[1]
    place = lax.axis_index("seq")
    scalar = pl.BlockSpec(memory_space=pltpu.SMEM)
    z_groups = [[z * Y + y for z in range(Z)] for y in range(Y)]
    y_groups = [[z * Y + y for y in range(Y)] for z in range(Z)]
    coords = jnp.stack([place // Y, place % Y]).astype(jnp.int32)
    first, second, back_second, back_first, twists = transform_tables()

    split = readin_weight.reshape(experts_here, in_chans, 2, BLOCKS, CHANS)
    own = lax.dynamic_index_in_dim(split, place, 3, keepdims=False).reshape(experts_here, in_chans, 2 * CHANS)
    in_weights = lax.all_gather(own, "grp", axis=0, tiled=True)
    split = readout_weight.reshape(experts_here, Z, Y, CHANS, in_chans)
    own = lax.dynamic_index_in_dim(split, place % Y, 2, keepdims=False).reshape(experts_here, Z * CHANS, in_chans)
    out_weights = lax.all_gather(own, "grp", axis=0, tiled=True)

    sessions = session_of_bin[0, ::TRIAL]
    matches = sessions[:, None] == jnp.arange(session_slot.shape[0], dtype=jnp.int32)[None, :]
    slots = jnp.sum(jnp.where(matches, session_slot[None, :], 0), axis=1)
    marks = jnp.broadcast_to(slots.astype(bf16)[:, None], (slots.shape[0], in_chans))
    padding = jnp.zeros((PAD_ROWS - slots.shape[0], in_chans), bf16)
    block = jnp.concatenate([spikes[0], marks, padding], 0)
    chunk = jnp.stack([block, along_y(block, 1), along_y(block, -1), along_y(block, 2)])
    chunks = [chunk]
    right = left = chunk
    for _ in range(3):
        right, left = along_z(right, 1), along_z(left, -1)
        chunks += [right, left]
    last = [along_z(right[: Y // 2], 1), along_z(left[Y // 2 :], -1)]
    parts = [read_in(piece, in_weights, 0) for piece in chunks]
    parts.append(jnp.concatenate([read_in(piece, in_weights, 0) for piece in last], 0))

    spectrum_shape = jax.ShapeDtypeStruct((GROUPS, BLOCKS * LANE8, 2 * BLOCK), f32)
    plane = (BLOCKS, CHANS, BLOCK)
    params = pltpu.CompilerParams(vmem_limit_bytes=32 << 20)
    work = 2 * GROUPS * (512 * 256 * 128 + 256 * 256 * 256)
    filter_spectrum = pl.pallas_call(
        filter_kernel,
        out_shape=spectrum_shape,
        in_specs=whole(4),
        out_specs=whole(1)[0],
        compiler_params=params,
        cost_estimate=pl.CostEstimate(flops=work, bytes_accessed=4 << 20, transcendentals=0),
        name="filter_transform",
    )(long_filter, first, second, twists)

    taps = lax.dynamic_slice_in_dim(short_kernel, place * CHANS, CHANS, 1)
    taps = jnp.broadcast_to(taps[:, :, None], (short_kernel.shape[0], CHANS, BLOCK))
    gains = jnp.broadcast_to(skip_gain[:, None], (CHANS, BLOCK))
    gated, gates, spectrum = pl.pallas_call(
        main_kernel,
        out_shape=(jax.ShapeDtypeStruct(plane, bf16), jax.ShapeDtypeStruct(plane, bf16), spectrum_shape),
        in_specs=[scalar] + whole(8 + len(parts)),
        out_specs=tuple(whole(3)),
        scratch_shapes=[pltpu.VMEM(plane, f32), pltpu.VMEM(plane, f32)],
        compiler_params=params,
        cost_estimate=pl.CostEstimate(flops=2 * work, bytes_accessed=8 << 20, transcendentals=0),
        name="long_convolution",
    )(coords, taps, gains, filter_spectrum, first, second, back_second, back_first, twists, *parts)

    arrived = lax.all_to_all(gated.reshape(Z, Y, CHANS, BLOCK), "seq", split_axis=0, concat_axis=0, tiled=True, axis_index_groups=z_groups)
    partial = pl.pallas_call(
        read_out_kernel,
        out_shape=jax.ShapeDtypeStruct((Y, BLOCK, in_chans), bf16),
        in_specs=[scalar] + whole(3),
        out_specs=whole(1)[0],
        compiler_params=params,
        cost_estimate=pl.CostEstimate(flops=2 * 512 * 512 * 4096, bytes_accessed=6 << 20, transcendentals=0),
        name="read_out",
    )(coords, arrived, chunk, out_weights)
    pieces = lax.all_to_all(partial, "seq", split_axis=0, concat_axis=0, tiled=True, axis_index_groups=y_groups)
    denoised = jnp.sum(pieces.astype(f32), 0).astype(bf16)

    turned = out_grad[0].T.reshape(BLOCKS, CHANS, BLOCK)
    grads = lax.all_to_all(turned, "seq", split_axis=0, concat_axis=0, tiled=True)
    own_grad = pl.pallas_call(
        gradient_kernel,
        out_shape=jax.ShapeDtypeStruct((CHANS, LENGTH), bf16),
        in_specs=whole(8),
        out_specs=whole(1)[0],
        compiler_params=params,
        cost_estimate=pl.CostEstimate(flops=2 * work, bytes_accessed=5 << 20, transcendentals=0),
        name="filter_gradient",
    )(grads, gates, spectrum, first, second, back_second, back_first, twists)
    all_grads = lax.all_gather(own_grad, "grp", axis=0, tiled=False)
    filter_grad = jnp.sum(all_grads.astype(f32), 0)
    return denoised[None], filter_grad


def solution(mesh):
    placed = (
        P("grp", "seq", None),
        P("grp", "seq"),
        P(),
        P("grp", None, None),
        P(),
        P("seq", None),
        P("seq"),
        P("grp", None, None),
        P("grp", "seq", None),
    )
    return jax.shard_map(
        local,
        mesh=mesh,
        in_specs=placed,
        out_specs=(P("grp", "seq", None), P("seq", None)),
        check_vma=False,
    )
```

profile of v0, /device:TPU:8, one launch (start us, length us, event | category | flops | bytes accessed | tf_op | source)
XLA Modules:
  0.0 153.3 jit_solution(10641145373060985982)
XLA Ops:
  7.3 6.5 %copy.27 = bf16[2,256,4096]{1,2,0:T(8,128)(2,1)} copy(bf16[2,256,4096]{2,1,0:T(8,128)(2,1)} %param.17) | data formatting | bytes 8388608 | tf_op args[3]
  17.0 1.7 %collective-permute-start = (bf16[144,256]{1,0:T(8,128)(2,1)S(1)}, bf16[144,256]{1,0:T(8,128)(2,1)S(1)}, u32[]{:S(2)}, u32[]{:S(2)}) collective-permute-start(bf16[144,256]{1,0:T(8,128)(2,1)S(1)} %maximum_maximum_fusion), channel_id=1, source_target_pairs={{0,1},{1,2},{2,3},{3,0},{4,5},{5,6},{6,7},{7,4},{8,9},{9,10},{10,1... | collective-permute-start | bytes 221192 | tf_op jit(solution)/shard_map/ppermute | solution.py:212
  19.3 2.0 %collective-permute-start.2 = (bf16[144,256]{1,0:T(8,128)(2,1)S(1)}, bf16[144,256]{1,0:T(8,128)(2,1)S(1)}, u32[]{:S(2)}, u32[]{:S(2)}) collective-permute-start(bf16[144,256]{1,0:T(8,128)(2,1)S(1)} %maximum_maximum_fusion), channel_id=1, source_target_pairs={{0,2},{1,3},{2,0},{3,1},{4,6},{5,7},{6,4},{7,5},{8,10},{9,11},{10,... | collective-permute-start | bytes 221192 | tf_op jit(solution)/shard_map/ppermute | solution.py:212
  21.6 2.2 %collective-permute-done.1 = bf16[144,256]{1,0:T(8,128)(2,1)S(1)} collective-permute-done((bf16[144,256]{1,0:T(8,128)(2,1)S(1)}, bf16[144,256]{1,0:T(8,128)(2,1)S(1)}, u32[]{:S(2)}, u32[]{:S(2)}) %collective-permute-start.1) | collective-permute-done | bytes 73760 | tf_op jit(solution)/shard_map/ppermute | solution.py:212
  23.8 1.4 collective-permute-done.2
  25.2 1.7 %collective-permute-start.3 = (bf16[4,144,256]{2,1,0:T(8,128)(2,1)S(1)}, bf16[4,144,256]{2,1,0:T(8,128)(2,1)S(1)}, u32[]{:S(2)}, u32[]{:S(2)}) collective-permute-start(bf16[4,144,256]{2,1,0:T(8,128)(2,1)S(1)} %pad_maximum_fusion.chunk_ref), channel_id=1, source_target_pairs={{0,4},{1,5},{2,6},{3,7},{4,8},{5,9},{6,10},{7,11},{8,12},{9,13},{1... | collective-permute-start | bytes 884744 | tf_op jit(solution)/shard_map/ppermute | solution.py:216
  27.0 4.0 %collective-permute-start.4 = (bf16[4,144,256]{2,1,0:T(8,128)(2,1)S(1)}, bf16[4,144,256]{2,1,0:T(8,128)(2,1)S(1)}, u32[]{:S(2)}, u32[]{:S(2)}) collective-permute-start(bf16[4,144,256]{2,1,0:T(8,128)(2,1)S(1)} %pad_maximum_fusion.chunk_ref), channel_id=1, source_target_pairs={{0,28},{1,29},{2,30},{3,31},{4,0},{5,1},{6,2},{7,3},{8,4},{9,5},{1... | collective-permute-start | bytes 884744 | tf_op jit(solution)/shard_map/ppermute | solution.py:216
  31.7 4.9 %collective-permute-done.3.chunk_ref = bf16[4,144,256]{2,1,0:T(8,128)(2,1)S(1)} collective-permute-done((bf16[4,144,256]{2,1,0:T(8,128)(2,1)S(1)}, bf16[4,144,256]{2,1,0:T(8,128)(2,1)S(1)}, u32[]{:S(2)}, u32[]{:S(2)}) %collective-permute-start.3) | collective-permute-done | bytes 294944 | tf_op jit(solution)/shard_map/ppermute | solution.py:216
  37.3 3.2 %collective-permute-start.6 = (bf16[4,144,256]{2,1,0:T(8,128)(2,1)S(1)}, bf16[4,144,256]{2,1,0:T(8,128)(2,1)}, u32[]{:S(2)}, u32[]{:S(2)}) collective-permute-start(bf16[4,144,256]{2,1,0:T(8,128)(2,1)S(1)} %collective-permute-done.4.chunk_ref), channel_id=1, source_target_pairs={{0,28},{1,29},{2,30},{3,31},{4,0},{5,1},{6,2},{7,3},{8,4},{9,5},{1... | collective-permute-start | bytes 884744 | tf_op jit(solution)/shard_map/ppermute | solution.py:216
  41.3 3.5 %collective-permute-done.5.chunk_ref = bf16[4,144,256]{2,1,0:T(8,128)(2,1)} collective-permute-done((bf16[4,144,256]{2,1,0:T(8,128)(2,1)S(1)}, bf16[4,144,256]{2,1,0:T(8,128)(2,1)}, u32[]{:S(2)}, u32[]{:S(2)}) %collective-permute-start.5) | collective-permute-done | bytes 294944 | tf_op jit(solution)/shard_map/ppermute | solution.py:216
  44.8 3.8 %collective-permute-start.8 = (bf16[4,144,256]{2,1,0:T(8,128)(2,1)}, bf16[4,144,256]{2,1,0:T(8,128)(2,1)}, u32[]{:S(2)}, u32[]{:S(2)}) collective-permute-start(bf16[4,144,256]{2,1,0:T(8,128)(2,1)} %collective-permute-done.6.chunk_ref), channel_id=1, source_target_pairs={{0,28},{1,29},{2,30},{3,31},{4,0},{5,1},{6,2},{7,3},{8,4},{9,5},{1... | collective-permute-start | bytes 884744 | tf_op jit(solution)/shard_map/ppermute | solution.py:216
  49.6 8.4 %all-to-all-start.2 = ((bf16[32,64,128]{2,1,0:T(8,128)(2,1)}), bf16[32,64,128]{2,1,0:T(8,128)(2,1)S(1)}, u32[]{:S(2)}, u32[]{:S(2)}) async-start(bf16[32,64,128]{2,1,0:T(8,128)(2,1)} %bitcast.28), calls=%async_computation.2 | async-start | bytes 1048576 | tf_op jit(solution)/shard_map/all_to_all | solution.py:299
  59.7 1.5 collective-permute-start.9
  62.1 2.0 %collective-permute-start.10 = (bf16[2,144,256]{2,1,0:T(8,128)(2,1)S(1)}, bf16[2,144,256]{2,1,0:T(8,128)(2,1)S(1)}, u32[]{:S(2)}, u32[]{:S(2)}) collective-permute-start(bf16[2,144,256]{2,1,0:T(8,128)(2,1)S(1)} %slice.13), channel_id=1, source_target_pairs={{0,28},{1,29},{2,30},{3,31},{4,0},{5,1},{6,2},{7,3},{8,4},{9,5},{1... | collective-permute-start | bytes 442376 | tf_op jit(solution)/shard_map/ppermute | solution.py:216
  65.4 3.4 %filter_transform.1.filter_ref = f32[8,256,256]{2,1,0:T(8,128)S(1)} custom-call(f32[64,4096]{1,0:T(8,128)S(1)} %copy-done.9, bf16[512,256]{1,0:T(8,128)(2,1)S(1)} %copy-done.5, bf16[256,256]{1,0:T(8,128)(2,1)S(1)} %copy-done.8, f32[2,32,128]{2,1,0:T(8,128)S(1)} %copy-done.15), custom_call_target="tpu_custom_call" | custom-call | flops 536870912 | bytes 4194304 | tf_op jit(solution)/shard_map/filter_transform/pallas_call | solution.py:261
  68.8 1.4 copy-done.1
  75.2 1.3 read_in.14.rest_5_
  76.6 2.3 %read_in.15.rest_6_ = bf16[4,128,128]{2,1,0:T(8,128)(2,1)S(1)} custom-call(bf16[4,144,256]{2,1,0:T(8,128)(2,1)} %collective-permute-done.8.chunk_ref, bf16[16,256,128]{2,1,0:T(8,128)(2,1)S(1)} %copy-done.3), custom_call_target="tpu_custom_call" | custom-call | flops 536870912 | bytes 1343488 | tf_op jit(solution)/shard_map/read_in/pallas_call | solution.py:105
  78.9 2.4 %read_in.12.rest_3_ = bf16[4,128,128]{2,1,0:T(8,128)(2,1)S(1)} custom-call(bf16[4,144,256]{2,1,0:T(8,128)(2,1)} %collective-permute-done.5.chunk_ref, bf16[16,256,128]{2,1,0:T(8,128)(2,1)S(1)} %copy-done.3), custom_call_target="tpu_custom_call" | custom-call | flops 536870912 | bytes 1343488 | tf_op jit(solution)/shard_map/read_in/pallas_call | solution.py:105
  81.3 2.4 %read_in.13.rest_4_ = bf16[4,128,128]{2,1,0:T(8,128)(2,1)S(1)} custom-call(bf16[4,144,256]{2,1,0:T(8,128)(2,1)} %collective-permute-done.6.chunk_ref, bf16[16,256,128]{2,1,0:T(8,128)(2,1)S(1)} %copy-done.3), custom_call_target="tpu_custom_call" | custom-call | flops 536870912 | bytes 1343488 | tf_op jit(solution)/shard_map/read_in/pallas_call | solution.py:105
  83.8 1.3 read_in.10.rest_1_
  85.1 1.3 read_in.11.rest_2_
  86.4 1.3 read_in.9.rest_0_
  87.9 6.5 %long_convolution.1 = (bf16[32,64,128]{2,1,0:T(8,128)(2,1)S(1)}, bf16[32,64,128]{2,1,0:T(8,128)(2,1)S(1)}, f32[8,256,256]{2,1,0:T(8,128)S(1)}) custom-call(s32[2]{0:T(128)S(1)} %pad_add_fusion.place_ref, f32[3,64,128]{2,1,0:T(8,128)S(1)} %broadcast_in_dim.22.taps_ref, f32[64,128]{1,0:T(8,128)S(1)} %broadcast_in_dim.23.gain_ref, ...), custom_call_target="tpu_custom_call" | custom-call | flops 1073741824 | bytes 8388608 | tf_op jit(solution)/shard_map/long_convolution/pallas_call | solution.py:274
  94.4 1.4 copy-done.6
  97.4 1.6 %copy-done.7 = f32[8,256,256]{2,1,0:T(8,128)S(1)} copy-done((f32[8,256,256]{2,1,0:T(8,128)S(1)}, f32[8,256,256]{2,1,0:T(8,128)}, u32[]{:S(2)}) %copy-start.7) | copy-done | bytes 2097176
  100.0 6.4 %filter_gradient.1 = bf16[64,4096]{1,0:T(8,128)(2,1)} custom-call(bf16[32,64,128]{2,1,0:T(8,128)(2,1)S(1)} %all-to-all-done.2.grad_ref, bf16[32,64,128]{2,1,0:T(8,128)(2,1)S(1)} %copy-done.12, f32[8,256,256]{2,1,0:T(8,128)S(1)} %copy-done.7, bf16[512,256]{1,0:T(8,128)(2,1)S(1)} %copy-done.5, bf16[256,256]{1,0:T(8,128)(2,1)S(1)} %copy-done.8, ...), custom_call_target="tpu_custom_call" | custom-call | flops 1073741824 | bytes 5242880 | tf_op jit(solution)/shard_map/filter_gradient/pallas_call | solution.py:300
  106.4 19.4 %all_to_all.15.rows_ref = bf16[8,4,64,128]{3,2,1,0:T(8,128)(2,1)S(1)} all-to-all(bf16[8,4,64,128]{3,2,1,0:T(8,128)(2,1)} %bitcast.24), channel_id=1, replica_groups={{0,4,8,12,16,20,24,28},{1,5,9,13,17,21,25,29},{2,6,10,14,18,22,26,30},{..., dimensions={0} | all-to-all | bytes 1048576 | tf_op jit(solution)/shard_map/all_to_all | solution.py:285
  126.8 2.3 %copy-done.21 = bf16[16,512,256]{2,1,0:T(8,128)(2,1)S(1)} copy-done((bf16[16,512,256]{2,1,0:T(8,128)(2,1)S(1)}, bf16[16,512,256]{2,1,0:T(8,128)(2,1)}, u32[]{:S(2)}) %copy-start.21) | copy-done | bytes 4194328
  129.1 2.9 %read_out.1 = bf16[4,128,256]{2,1,0:T(8,128)(2,1)S(1)} custom-call(s32[2]{0:T(128)S(1)} %pad_add_fusion.place_ref, bf16[8,4,64,128]{3,2,1,0:T(8,128)(2,1)S(1)} %all_to_all.15.rows_ref, bf16[4,144,256]{2,1,0:T(8,128)(2,1)S(1)} %copy-done.18, bf16[16,512,256]{2,1,0:T(8,128)(2,1)S(1)} %copy-done.21), custom_call_target="tpu_custom_call" | custom-call | flops 2147483648 | bytes 6291456 | tf_op jit(solution)/shard_map/read_out/pallas_call | solution.py:286
  132.0 10.1 %all_to_all.16 = bf16[4,128,256]{2,1,0:T(8,128)(2,1)S(1)} all-to-all(bf16[4,128,256]{2,1,0:T(8,128)(2,1)S(1)} %read_out.1), channel_id=1, replica_groups={{0,1,2,3},{4,5,6,7},{8,9,10,11},{12,13,14,15},{16,17,18,19},{20,21,22,2..., dimensions={0} | all-to-all | bytes 524288 | tf_op jit(solution)/shard_map/all_to_all | solution.py:295
  142.8 4.0 %convert_reduce_fusion = f32[64,4096]{1,0:T(8,128)} fusion(bf16[8,64,4096]{2,1,0:T(8,128)(2,1)} %bitcast.26), kind=kLoop, calls=%fused_computation | loop fusion | flops 3932160 | bytes 5242880 | tf_op jit(solution)/shard_map/reduce_sum | solution.py:310
  (101 shorter events, 20.7 us)
Async XLA Ops:
  7.2 8.4 %copy-start = (bf16[2,2048,256]{2,1,0:T(8,128)(2,1)S(1)}, bf16[2,2048,256]{2,1,0:T(8,128)(2,1)}, u32[]{:S(2)}) copy-start(bf16[2,2048,256]{2,1,0:T(8,128)(2,1)} %param.21) | copy-start | bytes 6291460
  7.2 64.2 %all-gather.5.cloned.1.call-start = ((), (), s32[]{:S(2)}) async-start(), calls=%async_computation.3 | async-start | bytes 1179648 | tf_op jit(solution)/shard_map/all_gather | solution.py:236
  7.2 9.2 %copy-start.29 = (s32[1,128]{1,0:T(1,128)S(1)}, s32[1,128]{1,0:T(1,128)}, u32[]{:S(2)}) copy-start(s32[1,128]{1,0:T(1,128)} %param.15) | copy-start | bytes 1540
  7.2 9.3 %copy-start.30 = (s32[16]{0:T(128)S(1)}, s32[16]{0:T(128)}, u32[]{:S(2)}) copy-start(s32[16]{0:T(128)} %param.16) | copy-start | bytes 196
  7.3 9.6 %copy-start.27 = (bf16[1,128,256]{2,1,0:T(8,128)(2,1)S(1)}, bf16[1,128,256]{2,1,0:T(8,128)(2,1)}, u32[]{:S(2)}) copy-start(bf16[1,128,256]{2,1,0:T(8,128)(2,1)} %param.14) | copy-start | bytes 196612
  7.3 41.4 %copy-start.26 = (bf16[1,128,2048]{2,1,0:T(8,128)(2,1)S(1)}, bf16[1,128,2048]{2,1,0:T(8,128)(2,1)}, u32[]{:S(2)}) copy-start(bf16[1,128,2048]{2,1,0:T(8,128)(2,1)} %param.22) | copy-start | bytes 1572868
  13.8 50.3 %copy-start.5 = (bf16[512,256]{1,0:T(8,128)(2,1)S(1)}, bf16[512,256]{1,0:T(8,128)(2,1)}, u32[]{:S(2)}) copy-start(bf16[512,256]{1,0:T(8,128)(2,1)} %constant.61.clone.first_ref) | copy-start | bytes 786436
  13.8 50.3 %copy-start.8 = (bf16[256,256]{1,0:T(8,128)(2,1)S(1)}, bf16[256,256]{1,0:T(8,128)(2,1)}, u32[]{:S(2)}) copy-start(bf16[256,256]{1,0:T(8,128)(2,1)} %constant.62.clone.second_ref) | copy-start | bytes 393220
  13.8 50.3 %copy-start.15 = (f32[2,32,128]{2,1,0:T(8,128)S(1)}, f32[2,32,128]{2,1,0:T(8,128)}, u32[]{:S(2)}) copy-start(f32[2,32,128]{2,1,0:T(8,128)} %constant.65.clone.twist_ref) | copy-start | bytes 98308
  15.5 110.3 %all-gather.7.cloned.1.call-start = ((), (), s32[]{:S(2)}) async-start(), calls=%async_computation.4 | async-start | bytes 4718592 | tf_op jit(solution)/shard_map/all_gather | solution.py:239
  17.0 4.6 %collective-permute-start = (bf16[144,256]{1,0:T(8,128)(2,1)S(1)}, bf16[144,256]{1,0:T(8,128)(2,1)S(1)}, u32[]{:S(2)}, u32[]{:S(2)}) collective-permute-start(bf16[144,256]{1,0:T(8,128)(2,1)S(1)} %maximum_maximum_fusion), channel_id=1, source_target_pairs={{0,1},{1,2},{2,3},{3,0},{4,5},{5,6},{6,7},{7,4},{8,9},{9,10},{10,1... | collective-permute-start | bytes 221192 | tf_op jit(solution)/shard_map/ppermute | solution.py:212
  18.6 5.1 %collective-permute-start.1 = (bf16[144,256]{1,0:T(8,128)(2,1)S(1)}, bf16[144,256]{1,0:T(8,128)(2,1)S(1)}, u32[]{:S(2)}, u32[]{:S(2)}) collective-permute-start(bf16[144,256]{1,0:T(8,128)(2,1)S(1)} %maximum_maximum_fusion), channel_id=1, source_target_pairs={{0,3},{1,0},{2,1},{3,2},{4,7},{5,4},{6,5},{7,6},{8,11},{9,8},{10,9... | collective-permute-start | bytes 221192 | tf_op jit(solution)/shard_map/ppermute | solution.py:212
  19.3 5.9 %collective-permute-start.2 = (bf16[144,256]{1,0:T(8,128)(2,1)S(1)}, bf16[144,256]{1,0:T(8,128)(2,1)S(1)}, u32[]{:S(2)}, u32[]{:S(2)}) collective-permute-start(bf16[144,256]{1,0:T(8,128)(2,1)S(1)} %maximum_maximum_fusion), channel_id=1, source_target_pairs={{0,2},{1,3},{2,0},{3,1},{4,6},{5,7},{6,4},{7,5},{8,10},{9,11},{10,... | collective-permute-start | bytes 221192 | tf_op jit(solution)/shard_map/ppermute | solution.py:212
  25.2 11.4 %collective-permute-start.3 = (bf16[4,144,256]{2,1,0:T(8,128)(2,1)S(1)}, bf16[4,144,256]{2,1,0:T(8,128)(2,1)S(1)}, u32[]{:S(2)}, u32[]{:S(2)}) collective-permute-start(bf16[4,144,256]{2,1,0:T(8,128)(2,1)S(1)} %pad_maximum_fusion.chunk_ref), channel_id=1, source_target_pairs={{0,4},{1,5},{2,6},{3,7},{4,8},{5,9},{6,10},{7,11},{8,12},{9,13},{1... | collective-permute-start | bytes 884744 | tf_op jit(solution)/shard_map/ppermute | solution.py:216
  27.0 10.4 %collective-permute-start.4 = (bf16[4,144,256]{2,1,0:T(8,128)(2,1)S(1)}, bf16[4,144,256]{2,1,0:T(8,128)(2,1)S(1)}, u32[]{:S(2)}, u32[]{:S(2)}) collective-permute-start(bf16[4,144,256]{2,1,0:T(8,128)(2,1)S(1)} %pad_maximum_fusion.chunk_ref), channel_id=1, source_target_pairs={{0,28},{1,29},{2,30},{3,31},{4,0},{5,1},{6,2},{7,3},{8,4},{9,5},{1... | collective-permute-start | bytes 884744 | tf_op jit(solution)/shard_map/ppermute | solution.py:216
  36.6 8.1 %collective-permute-start.5 = (bf16[4,144,256]{2,1,0:T(8,128)(2,1)S(1)}, bf16[4,144,256]{2,1,0:T(8,128)(2,1)}, u32[]{:S(2)}, u32[]{:S(2)}) collective-permute-start(bf16[4,144,256]{2,1,0:T(8,128)(2,1)S(1)} %collective-permute-done.3.chunk_ref), channel_id=1, source_target_pairs={{0,4},{1,5},{2,6},{3,7},{4,8},{5,9},{6,10},{7,11},{8,12},{9,13},{1... | collective-permute-start | bytes 884744 | tf_op jit(solution)/shard_map/ppermute | solution.py:216
  37.3 7.5 %collective-permute-start.6 = (bf16[4,144,256]{2,1,0:T(8,128)(2,1)S(1)}, bf16[4,144,256]{2,1,0:T(8,128)(2,1)}, u32[]{:S(2)}, u32[]{:S(2)}) collective-permute-start(bf16[4,144,256]{2,1,0:T(8,128)(2,1)S(1)} %collective-permute-done.4.chunk_ref), channel_id=1, source_target_pairs={{0,28},{1,29},{2,30},{3,31},{4,0},{5,1},{6,2},{7,3},{8,4},{9,5},{1... | collective-permute-start | bytes 884744 | tf_op jit(solution)/shard_map/ppermute | solution.py:216
  44.7 13.5 %collective-permute-start.7 = (bf16[4,144,256]{2,1,0:T(8,128)(2,1)}, bf16[4,144,256]{2,1,0:T(8,128)(2,1)S(1)}, u32[]{:S(2)}, u32[]{:S(2)}) collective-permute-start(bf16[4,144,256]{2,1,0:T(8,128)(2,1)} %collective-permute-done.5.chunk_ref), channel_id=1, source_target_pairs={{0,4},{1,5},{2,6},{3,7},{4,8},{5,9},{6,10},{7,11},{8,12},{9,13},{1... | collective-permute-start | bytes 884744 | tf_op jit(solution)/shard_map/ppermute | solution.py:216
  44.8 16.3 %collective-permute-start.8 = (bf16[4,144,256]{2,1,0:T(8,128)(2,1)}, bf16[4,144,256]{2,1,0:T(8,128)(2,1)}, u32[]{:S(2)}, u32[]{:S(2)}) collective-permute-start(bf16[4,144,256]{2,1,0:T(8,128)(2,1)} %collective-permute-done.6.chunk_ref), channel_id=1, source_target_pairs={{0,28},{1,29},{2,30},{3,31},{4,0},{5,1},{6,2},{7,3},{8,4},{9,5},{1... | collective-permute-start | bytes 884744 | tf_op jit(solution)/shard_map/ppermute | solution.py:216
  49.6 47.7 %all-to-all-start.2 = ((bf16[32,64,128]{2,1,0:T(8,128)(2,1)}), bf16[32,64,128]{2,1,0:T(8,128)(2,1)S(1)}, u32[]{:S(2)}, u32[]{:S(2)}) async-start(bf16[32,64,128]{2,1,0:T(8,128)(2,1)} %bitcast.28), calls=%async_computation.2 | async-start | bytes 1048576 | tf_op jit(solution)/shard_map/all_to_all | solution.py:299
  58.1 84.7 %all-gather.9.cloned.1.call-start = ((), (), s32[]{:S(2)}) async-start(), calls=%async_computation.5 | async-start | bytes 4718592 | tf_op jit(solution)/shard_map/all_gather | solution.py:309
  59.7 11.7 %collective-permute-start.9 = (bf16[2,144,256]{2,1,0:T(8,128)(2,1)}, bf16[2,144,256]{2,1,0:T(8,128)(2,1)S(1)}, u32[]{:S(2)}, u32[]{:S(2)}) collective-permute-start(bf16[2,144,256]{2,1,0:T(8,128)(2,1)} %slice.12), channel_id=1, source_target_pairs={{0,4},{1,5},{2,6},{3,7},{4,8},{5,9},{6,10},{7,11},{8,12},{9,13},{1... | collective-permute-start | bytes 442376 | tf_op jit(solution)/shard_map/ppermute | solution.py:216
  62.1 11.4 %collective-permute-start.10 = (bf16[2,144,256]{2,1,0:T(8,128)(2,1)S(1)}, bf16[2,144,256]{2,1,0:T(8,128)(2,1)S(1)}, u32[]{:S(2)}, u32[]{:S(2)}) collective-permute-start(bf16[2,144,256]{2,1,0:T(8,128)(2,1)S(1)} %slice.13), channel_id=1, source_target_pairs={{0,28},{1,29},{2,30},{3,31},{4,0},{5,1},{6,2},{7,3},{8,4},{9,5},{1... | collective-permute-start | bytes 442376 | tf_op jit(solution)/shard_map/ppermute | solution.py:216
  75.2 8.5 %copy-start.23 = (bf16[4,144,256]{2,1,0:T(8,128)(2,1)S(1)}, bf16[4,144,256]{2,1,0:T(8,128)(2,1)}, u32[]{:S(2)}) copy-start(bf16[4,144,256]{2,1,0:T(8,128)(2,1)} %copy-done.22) | copy-start | bytes 884740
  76.5 8.5 %copy-start.25 = (bf16[4,144,256]{2,1,0:T(8,128)(2,1)S(1)}, bf16[4,144,256]{2,1,0:T(8,128)(2,1)}, u32[]{:S(2)}) copy-start(bf16[4,144,256]{2,1,0:T(8,128)(2,1)} %copy-done.24) | copy-start | bytes 884740
  78.9 7.5 %copy-start.4 = (bf16[16,256,128]{2,1,0:T(8,128)(2,1)S(1)}, bf16[16,256,128]{2,1,0:T(8,128)(2,1)}, u32[]{:S(2)}) copy-start(bf16[16,256,128]{2,1,0:T(8,128)(2,1)} %all-gather.5.cloned.1.call-done.weight_ref) | copy-start | bytes 3145732
  78.9 7.5 %copy-start.17 = (bf16[4,144,256]{2,1,0:T(8,128)(2,1)S(1)}, bf16[4,144,256]{2,1,0:T(8,128)(2,1)}, u32[]{:S(2)}) copy-start(bf16[4,144,256]{2,1,0:T(8,128)(2,1)} %copy-done.16) | copy-start | bytes 884740
  81.3 6.6 %copy-start.28 = (f32[64]{0:T(128)S(1)}, f32[64]{0:T(128)}, u32[]{:S(2)}) copy-start(f32[64]{0:T(128)} %param.20) | copy-start | bytes 772
  81.3 6.6 %copy-start.2 = (f32[8,256,256]{2,1,0:T(8,128)S(1)}, f32[8,256,256]{2,1,0:T(8,128)}, u32[]{:S(2)}) copy-start(f32[8,256,256]{2,1,0:T(8,128)} %copy-done.1) | copy-start | bytes 6291460
  81.3 6.6 %copy-start.10 = (bf16[256,512]{1,0:T(8,128)(2,1)S(1)}, bf16[256,512]{1,0:T(8,128)(2,1)}, u32[]{:S(2)}) copy-start(bf16[256,512]{1,0:T(8,128)(2,1)} %constant.64.clone.back_first_ref) | copy-start | bytes 786436
  81.3 6.6 %copy-start.13 = (bf16[256,256]{1,0:T(8,128)(2,1)S(1)}, bf16[256,256]{1,0:T(8,128)(2,1)}, u32[]{:S(2)}) copy-start(bf16[256,256]{1,0:T(8,128)(2,1)} %constant.63.clone.back_second_ref) | copy-start | bytes 393220
  126.8 2.3 %copy-start.21 = (bf16[16,512,256]{2,1,0:T(8,128)(2,1)S(1)}, bf16[16,512,256]{2,1,0:T(8,128)(2,1)}, u32[]{:S(2)}) copy-start(bf16[16,512,256]{2,1,0:T(8,128)(2,1)} %all-gather.7.cloned.1.call-done.weight_ref) | copy-start | bytes 12582916
  (14 other events, 14.4 us)
Sparse Core Ops, SparseCore 0:
  15.6 28.7 all-gather.4
  46.3 34.5 all-gather.6
  106.5 35.0 all-gather.8
where the time goes:
time: 155 us; the launch traced here: 153 us
  Pallas kernels  33 us (21%)
  blocking collectives  29.6 us (19%)
  local copies, waits for them, and re-layouts  29.5 us (19%)
  starting transfers between devices  29.3 us (19%)
  between operations  14.1 us (9%)
  waiting for transfers between devices  12.7 us (8%)
  other arithmetic  5.17 us (3%)
    unnamed x63, local copies, waits for them, and re-layouts  23.2 us
    all_to_all x1, blocking collectives, local(): lax.all_to_all(gated.reshape(Z, Y, CHANS, BLOCK), 'seq', split_axis=0, co...  19.4 us
    ppermute x8, starting transfers between devices, along_z(): lax.ppermute(value, 'seq', [(z * Y + y, (z + step) % Z * Y + y) for z in...  16.3 us
    pallas_call x9, Pallas kernels, read_in(): pl.pallas_call(read_in_kernel, out_shape=jax.ShapeDtypeStruct((blocks, wi...  13.9 us
    all_to_all x1, blocking collectives, local(): lax.all_to_all(partial, 'seq', split_axis=0, concat_axis=0, tiled=True, a...  10.1 us
    ppermute x8, waiting for transfers between devices, along_z(): lax.ppermute(value, 'seq', [(z * Y + y, (z + step) % Z * Y + y) for z in...  8.9 us
    all_to_all x1, starting transfers between devices, local(): lax.all_to_all(turned, 'seq', split_axis=0, concat_axis=0, tiled=True)  8.45 us
    pallas_call x1, Pallas kernels, local(): pl.pallas_call(main_kernel, out_shape=(jax.ShapeDtypeStruct(plane, bf16),...  6.46 us
  transfers between devices with their start and end apart: 15, of which 7 were waited for; matrix products, arithmetic and copies ran while one was open for 4% of the time, Pallas kernels for 22%

commit v1 on v0

v1 whole, which is shorter than its diff:
```python
import jax
import jax.numpy as jnp
import numpy as np
from jax import lax
from jax.experimental import pallas as pl
from jax.experimental.pallas import tpu as pltpu
from jax.sharding import PartitionSpec as P

BLOCK = 128
TRIAL = 16
Z = 8
Y = 4
BLOCKS = Z * Y
CHANS = 64
LANE8 = 8
GROUPS = CHANS // LANE8
LENGTH = BLOCKS * BLOCK
Y_STEPS = (0, -1, 1, 2)
Z_STEPS = (0, -1, 1, -2, 2, -3, 3, 4)
f32 = jnp.float32
bf16 = jnp.bfloat16


def transform_tables():
    slow = np.arange(BLOCKS)
    fast = np.arange(BLOCK)
    first = np.exp(-2j * np.pi * (np.outer(slow, slow) / BLOCKS + slow[None, :] / (4.0 * BLOCKS)))
    twist = np.exp(-2j * np.pi * (slow[:, None] + 0.25) * fast[None, :] / LENGTH)
    second = np.exp(-2j * np.pi * np.outer(fast, fast) / BLOCK)
    eye = np.eye(LANE8)
    spread_first = np.concatenate([np.kron(first.real, eye), np.kron(first.imag, eye)], 0)
    forward_second = np.block([[second.real, second.imag], [-second.imag, second.real]])
    back = second.conj()
    back_second = np.block([[back.real, back.imag], [-back.imag, back.real]])
    back_first = first.conj().T / LENGTH
    spread_back = np.concatenate([np.kron(back_first.real, eye), np.kron(-back_first.imag, eye)], 1)
    as_bf16 = lambda table: jnp.asarray(table.astype(np.float32), bf16)
    twists = np.stack([twist.real, twist.imag]).astype(np.float32)
    return (
        as_bf16(spread_first),
        as_bf16(forward_second),
        as_bf16(back_second),
        as_bf16(spread_back),
        jnp.asarray(twists),
    )


def twists_of(twist_ref):
    shape = (BLOCKS, LANE8, BLOCK)
    cosine = jnp.broadcast_to(twist_ref[0][:, None, :], shape).reshape(BLOCKS * LANE8, BLOCK)
    sine = jnp.broadcast_to(twist_ref[1][:, None, :], shape).reshape(BLOCKS * LANE8, BLOCK)
    return cosine, sine


def forward(signal, first_ref, second_ref, cosine, sine):
    rows = BLOCKS * LANE8
    part = jnp.dot(first_ref[...], signal.astype(bf16), preferred_element_type=f32)
    real, imag = part[:rows], part[rows:]
    turned = jnp.concatenate([real * cosine - imag * sine, real * sine + imag * cosine], 1)
    return jnp.dot(turned.astype(bf16), second_ref[...], preferred_element_type=f32)


def backward(real, imag, back_second_ref, back_first_ref, cosine, sine):
    both = jnp.concatenate([real, imag], 1).astype(bf16)
    part = jnp.dot(both, back_second_ref[...], preferred_element_type=f32)
    real, imag = part[:, :BLOCK], part[:, BLOCK:]
    turned = jnp.concatenate([real * cosine + imag * sine, imag * cosine - real * sine], 0)
    return jnp.dot(back_first_ref[...], turned.astype(bf16), preferred_element_type=f32)


def filter_kernel(filter_ref, first_ref, second_ref, twist_ref, spectrum_ref):
    cosine, sine = twists_of(twist_ref)

    def step(group, carry):
        rows = filter_ref[pl.ds(pl.multiple_of(group * LANE8, LANE8), LANE8), :]
        signal = jnp.concatenate([rows[:, i * BLOCK : (i + 1) * BLOCK] for i in range(BLOCKS)], 0)
        spectrum_ref[group] = forward(signal, first_ref, second_ref, cosine, sine)
        return carry

    lax.fori_loop(0, GROUPS, step, 0)


def start_all(copies):
    for copy in copies:
        copy.start()


def wait_all(copies):
    for copy in copies:
        copy.wait()


def weight_copies(weight_hbm, weight, sems):
    copies = []
    for slot in range(weight_hbm.shape[0]):
        lanes = pl.ds(slot % 2 * 2 * CHANS, 2 * CHANS)
        copies.append(pltpu.make_async_copy(weight_hbm.at[slot], weight.at[slot // 2, :, lanes], sems.at[slot]))
    return copies


def project(rows_ref, start, weight):
    width = 2 * CHANS
    rows = rows_ref[pl.ds(start, 2), :BLOCK, :].reshape(2 * BLOCK, rows_ref.shape[2])
    marks = rows_ref[pl.ds(start, 2), BLOCK:, :].astype(f32)[:, :, :width].reshape(2 * BLOCK // TRIAL, width)
    marks = jnp.broadcast_to(marks[:, None, :], (2 * BLOCK // TRIAL, TRIAL, width)).reshape(2 * BLOCK, width)
    chosen = jnp.zeros((2 * BLOCK, width), f32)
    for pair in range(weight.shape[0]):
        product = jnp.dot(rows, weight[pair], preferred_element_type=f32)
        chosen = jnp.where(marks == 2 * pair, product[:, :width], chosen)
        chosen = jnp.where(marks == 2 * pair + 1, product[:, width:], chosen)
    return chosen[:BLOCK].T.astype(bf16), chosen[BLOCK:].T.astype(bf16)


def read_in_kernel(weight_hbm, *rest):
    chunk_refs = rest[:-5]
    out_ref, rows, weight, weight_sems, sems = rest[-5:]
    loads = weight_copies(weight_hbm, weight, weight_sems)
    for index, chunk in enumerate(chunk_refs):
        loads.append(pltpu.make_async_copy(chunk, rows.at[pl.ds(index * Y, Y)], sems.at[index]))
    start_all(loads)
    wait_all(loads)

    def step(pair, carry):
        low, high = project(rows, pair * 2, weight)
        out_ref[pair * 2] = low
        out_ref[pair * 2 + 1] = high
        return carry

    lax.fori_loop(0, rows.shape[0] // 2, step, 0)


def read_in(chunks, weights):
    blocks = len(chunks) * Y
    in_chans = weights.shape[1]
    width = weights.shape[2]
    flops = 2 * blocks * BLOCK * weights.shape[0] * in_chans * width
    return pl.pallas_call(
        read_in_kernel,
        out_shape=jax.ShapeDtypeStruct((blocks, width, BLOCK), bf16),
        in_specs=[pl.BlockSpec(memory_space=pltpu.HBM)] * (1 + len(chunks)),
        out_specs=whole(1)[0],
        scratch_shapes=[
            pltpu.VMEM((blocks,) + chunks[0].shape[1:], bf16),
            pltpu.VMEM((weights.shape[0] // 2, in_chans, 2 * width), bf16),
            pltpu.SemaphoreType.DMA((weights.shape[0],)),
            pltpu.SemaphoreType.DMA((len(chunks),)),
        ],
        compiler_params=pltpu.CompilerParams(vmem_limit_bytes=60 << 20),
        cost_estimate=pl.CostEstimate(flops=flops, bytes_accessed=4 << 20, transcendentals=0),
        name="read_in",
    )(weights, *chunks)


def block_of(place_ref, index):
    z = lax.rem(place_ref[0] + (Z_STEPS[index // Y] + Z), Z)
    y = lax.rem(place_ref[1] + (Y_STEPS[index % Y] + Y), Y)
    return z * Y + y


def main_kernel(place_ref, taps_ref, gain_ref, twist_ref, early_hbm, right_hbm, left_hbm, last_right_hbm, last_left_hbm, weight_hbm, filter_hbm, grad_hbm, *rest):
    table_hbms = rest[:4]
    gated_ref, out_ref, both, rows, weight, spectra, grad_all, *rest = rest[4:]
    tables = rest[:4]
    weight_sems, row_sems, early_sems, sems = rest[4:]
    half = Y // 2
    late = [
        pltpu.make_async_copy(right_hbm, rows.at[pl.ds(0, Y)], row_sems.at[0]),
        pltpu.make_async_copy(left_hbm, rows.at[pl.ds(Y, Y)], row_sems.at[1]),
        pltpu.make_async_copy(last_right_hbm, rows.at[pl.ds(2 * Y, half)], row_sems.at[2]),
        pltpu.make_async_copy(last_left_hbm, rows.at[pl.ds(2 * Y + half, half)], row_sems.at[3]),
    ] + weight_copies(weight_hbm, weight, weight_sems)
    early = early_hbm.shape[0]
    others = [
        pltpu.make_async_copy(early_hbm.at[index], both.at[block_of(place_ref, index)], early_sems.at[index])
        for index in range(early)
    ]
    pairs = [(filter_hbm, spectra), (grad_hbm, grad_all)] + list(zip(table_hbms, tables))
    others += [pltpu.make_async_copy(source, target, sems.at[index]) for index, (source, target) in enumerate(pairs)]
    start_all(late)
    start_all(others)
    wait_all(late)
    for index in range(0, rows.shape[0], 2):
        low, high = project(rows, index, weight)
        both[block_of(place_ref, early + index)] = low
        both[block_of(place_ref, early + index + 1)] = high
    cosine, sine = twists_of(twist_ref)
    lane = lax.broadcasted_iota(jnp.int32, (BLOCKS, LANE8, BLOCK), 2)
    count = BLOCKS * LANE8
    cube = (BLOCKS, LANE8, BLOCK)
    wait_all(others)
    first_ref, second_ref, back_second_ref, back_first_ref = tables

    def one_group(group, value, gate, grads):
        here = pl.ds(pl.multiple_of(group * LANE8, LANE8), LANE8)
        taps = taps_ref[:, here, :]
        total = taps[0][None] * value
        for shift in (1, 2):
            rolled = pltpu.roll(value.reshape(count, BLOCK), shift, 1).reshape(cube)
            before = jnp.concatenate([jnp.zeros((1, LANE8, BLOCK), f32), rolled[:-1]], 0)
            total = total + taps[shift][None] * jnp.where(lane < shift, before, rolled)
        signal = total.astype(bf16).astype(f32).reshape(count, BLOCK)
        spectrum = forward(signal, first_ref, second_ref, cosine, sine)
        own_re, own_im = spectrum[:, :BLOCK], spectrum[:, BLOCK:]
        weight = spectra[group]
        real = own_re * weight[:, :BLOCK] - own_im * weight[:, BLOCK:]
        imag = own_re * weight[:, BLOCK:] + own_im * weight[:, :BLOCK]
        long_part = backward(real, imag, back_second_ref, back_first_ref, cosine, sine)
        mixed = long_part.reshape(cube) + gain_ref[here, :][None] * signal.reshape(cube)
        gated = gate * mixed.astype(bf16).astype(f32)
        mixed_grad = (grads * gate).reshape(count, BLOCK)
        turned = forward(mixed_grad, first_ref, second_ref, cosine, sine)
        real = own_re * turned[:, :BLOCK] + own_im * turned[:, BLOCK:]
        imag = own_re * turned[:, BLOCK:] - own_im * turned[:, :BLOCK]
        result = backward(real, imag, back_second_ref, back_first_ref, cosine, sine)
        return gated, jnp.concatenate([result[i * LANE8 : (i + 1) * LANE8] for i in range(BLOCKS)], 1)

    def step(pair, carry):
        here = pl.ds(pl.multiple_of(pair * 2 * LANE8, 2 * LANE8), 2 * LANE8)
        there = pl.ds(pl.multiple_of(CHANS + pair * 2 * LANE8, 2 * LANE8), 2 * LANE8)
        value = both[:, here, :].astype(f32)
        gate = both[:, there, :].astype(f32)
        grads = grad_all[:, here, :].astype(f32)
        gated_low, low = one_group(pair * 2, value[:, :LANE8], gate[:, :LANE8], grads[:, :LANE8])
        gated_high, high = one_group(pair * 2 + 1, value[:, LANE8:], gate[:, LANE8:], grads[:, LANE8:])
        gated_ref[:, here, :] = jnp.concatenate([gated_low, gated_high], 1).astype(bf16)
        out_ref[here, :] = jnp.concatenate([low, high], 0).astype(bf16)
        return carry

    lax.fori_loop(0, GROUPS // 2, step, 0)


def read_out_kernel(place_ref, rows_ref, mark_ref, weight_hbm, out_ref, weight, sems):
    y = place_ref[1]
    trials = BLOCK // TRIAL
    slots, inner, width = weight.shape
    loads = [pltpu.make_async_copy(weight_hbm.at[slot], weight.at[slot], sems.at[slot]) for slot in range(slots)]
    start_all(loads)
    pieces = []
    marks = []
    for index, y_step in enumerate(Y_STEPS):
        block = lax.rem(y + (y_step + Y), Y)
        pieces.append(rows_ref[:, block, :, :].reshape(inner, BLOCK).T)
        mark = mark_ref[index].astype(f32)
        marks.append(jnp.broadcast_to(mark[:, None, :], (trials, TRIAL, width)).reshape(BLOCK, width))
    rows = jnp.concatenate(pieces, 0)
    marks = jnp.concatenate(marks, 0)
    chosen = jnp.zeros((Y * BLOCK, width), f32)
    for slot in range(slots):
        loads[slot].wait()
        product = jnp.dot(rows, weight[slot], preferred_element_type=f32)
        chosen = jnp.where(marks == slot, product, chosen)
    for index, y_step in enumerate(Y_STEPS):
        block = lax.rem(y + (y_step + Y), Y)
        out_ref[block] = chosen[index * BLOCK : (index + 1) * BLOCK].astype(bf16)


def sum_kernel(parts_ref, out_ref):
    total = parts_ref[0].astype(f32)
    for index in range(1, parts_ref.shape[0]):
        total = total + parts_ref[index].astype(f32)
    out_ref[...] = total


def along_y(value, step):
    return lax.ppermute(value, "seq", [(z * Y + y, z * Y + (y + step) % Y) for z in range(Z) for y in range(Y)])


def along_z(value, step):
    return lax.ppermute(value, "seq", [(z * Y + y, (z + step) % Z * Y + y) for z in range(Z) for y in range(Y)])


def whole(count):
    return [pl.BlockSpec(memory_space=pltpu.VMEM)] * count


def local(spikes, session_of_bin, session_slot, readin_weight, short_kernel, long_filter, skip_gain, readout_weight, out_grad):
    experts_here = readin_weight.shape[0]
    in_chans = spikes.shape[2]
    model_width = short_kernel.shape[1]
    place = lax.axis_index("seq")
    scalar = pl.BlockSpec(memory_space=pltpu.SMEM)
    z_groups = [[z * Y + y for z in range(Z)] for y in range(Y)]
    y_groups = [[z * Y + y for y in range(Y)] for z in range(Z)]
    coords = jnp.stack([place // Y, place % Y]).astype(jnp.int32)
    first, second, back_second, back_first, twists = transform_tables()

    own = jnp.concatenate(
        [lax.dynamic_slice_in_dim(readin_weight, start + place * CHANS, CHANS, 2) for start in (0, model_width)], 2
    )
    in_weights = lax.all_gather(own, "grp", axis=0, tiled=True)
    split = readout_weight.reshape(experts_here, Z, Y, CHANS, in_chans)
    own = lax.dynamic_index_in_dim(split, place % Y, 2, keepdims=False).reshape(experts_here, Z * CHANS, in_chans)
    out_weights = lax.all_gather(own, "grp", axis=0, tiled=True)

    sessions = session_of_bin[0, ::TRIAL]
    matches = sessions[:, None] == jnp.arange(session_slot.shape[0], dtype=jnp.int32)[None, :]
    slots = jnp.sum(jnp.where(matches, session_slot[None, :], 0), axis=1)
    marks = jnp.broadcast_to(slots.astype(bf16)[:, None], (slots.shape[0], in_chans))
    block = jnp.concatenate([spikes[0], marks], 0)
    chunk = jnp.stack([block, along_y(block, 1), along_y(block, -1), along_y(block, 2)])
    chunks = [chunk]
    right = left = chunk
    turned = out_grad[0].T.reshape(BLOCKS, CHANS, BLOCK)
    for _ in range(3):
        right, left = along_z(right, 1), along_z(left, -1)
        chunks += [right, left]
    early = read_in(chunks[:5], in_weights)
    right, left, turned, early = lax.optimization_barrier((right, left, turned, early))
    last_right, last_left = along_z(right[: Y // 2], 1), along_z(left[Y // 2 :], -1)
    grads = lax.all_to_all(turned, "seq", split_axis=0, concat_axis=0, tiled=True)

    spectrum_shape = jax.ShapeDtypeStruct((GROUPS, BLOCKS * LANE8, 2 * BLOCK), f32)
    plane = (BLOCKS, CHANS, BLOCK)
    params = pltpu.CompilerParams(vmem_limit_bytes=60 << 20)
    work = 2 * GROUPS * (512 * 256 * 128 + 256 * 256 * 256)
    filter_spectrum = pl.pallas_call(
        filter_kernel,
        out_shape=spectrum_shape,
        in_specs=whole(4),
        out_specs=whole(1)[0],
        compiler_params=params,
        cost_estimate=pl.CostEstimate(flops=work, bytes_accessed=4 << 20, transcendentals=0),
        name="filter_transform",
    )(long_filter, first, second, twists)

    taps = lax.dynamic_slice_in_dim(short_kernel, place * CHANS, CHANS, 1)
    taps = jnp.broadcast_to(taps[:, :, None], (short_kernel.shape[0], CHANS, BLOCK))
    gains = jnp.broadcast_to(skip_gain[:, None], (CHANS, BLOCK))
    tables = (first, second, back_second, back_first)
    late_rows = 2 * Y + Y
    gated, own_grad = pl.pallas_call(
        main_kernel,
        out_shape=(jax.ShapeDtypeStruct(plane, bf16), jax.ShapeDtypeStruct((CHANS, LENGTH), bf16)),
        in_specs=[scalar] + whole(3) + [pl.BlockSpec(memory_space=pltpu.HBM)] * 12,
        out_specs=tuple(whole(2)),
        scratch_shapes=[
            pltpu.VMEM((BLOCKS, 2 * CHANS, BLOCK), bf16),
            pltpu.VMEM((late_rows,) + chunk.shape[1:], bf16),
            pltpu.VMEM((in_weights.shape[0] // 2, in_chans, 4 * CHANS), bf16),
            pltpu.VMEM(spectrum_shape.shape, f32),
            pltpu.VMEM(plane, bf16),
        ]
        + [pltpu.VMEM(table.shape, bf16) for table in tables]
        + [pltpu.SemaphoreType.DMA((count,)) for count in (in_weights.shape[0], 4, early.shape[0], 6)],
        compiler_params=pltpu.CompilerParams(vmem_limit_bytes=60 << 20),
        cost_estimate=pl.CostEstimate(flops=4 * work, bytes_accessed=8 << 20, transcendentals=0),
        name="long_convolution",
    )(coords, taps, gains, twists, early, right, left, last_right, last_left, in_weights, filter_spectrum, grads, *tables)
    all_grads = lax.all_gather(own_grad, "grp", axis=0, tiled=False)

    arrived = lax.all_to_all(gated.reshape(Z, Y, CHANS, BLOCK), "seq", split_axis=0, concat_axis=0, tiled=True, axis_index_groups=z_groups)
    partial = pl.pallas_call(
        read_out_kernel,
        out_shape=jax.ShapeDtypeStruct((Y, BLOCK, in_chans), bf16),
        in_specs=[scalar] + whole(2) + [pl.BlockSpec(memory_space=pltpu.HBM)],
        out_specs=whole(1)[0],
        scratch_shapes=[pltpu.VMEM(out_weights.shape, bf16), pltpu.SemaphoreType.DMA((out_weights.shape[0],))],
        compiler_params=pltpu.CompilerParams(vmem_limit_bytes=60 << 20),
        cost_estimate=pl.CostEstimate(flops=2 * 512 * 512 * 4096, bytes_accessed=6 << 20, transcendentals=0),
        name="read_out",
    )(coords, arrived, chunk[:, BLOCK:, :], out_weights)
    pieces = lax.all_to_all(partial, "seq", split_axis=0, concat_axis=0, tiled=True, axis_index_groups=y_groups)
    denoised = jnp.sum(pieces.astype(f32), 0).astype(bf16)

    step = 2 * LANE8
    filter_grad = pl.pallas_call(
        sum_kernel,
        out_shape=jax.ShapeDtypeStruct((CHANS, LENGTH), f32),
        grid=(CHANS // step,),
        in_specs=[pl.BlockSpec((all_grads.shape[0], step, LENGTH), lambda i: (0, i, 0))],
        out_specs=pl.BlockSpec((step, LENGTH), lambda i: (i, 0)),
        compiler_params=params,
        cost_estimate=pl.CostEstimate(flops=all_grads.size, bytes_accessed=5 << 20, transcendentals=0),
        name="sum_gradients",
    )(all_grads)
    return denoised[None], filter_grad


def solution(mesh):
    placed = (
        P("grp", "seq", None),
        P("grp", "seq"),
        P(),
        P("grp", None, None),
        P(),
        P("seq", None),
        P("seq"),
        P("grp", None, None),
        P("grp", "seq", None),
    )
    return jax.shard_map(
        local,
        mesh=mesh,
        in_specs=placed,
        out_specs=(P("grp", "seq", None), P("seq", None)),
        check_vma=False,
    )
```

time: 155 us -> 146 us (0.942)
  local copies, waits for them, and re-layouts: 29.5 us -> 9.49 us
  blocking collectives: 29.6 us -> 10.3 us
  waiting for transfers between devices: 12.7 us -> 31 us
  Pallas kernels: 33 us -> 44.9 us
  starting transfers between devices: 29.3 us -> 31.8 us
    unnamed x63 -> x22, local copies, waits for them, and re-layouts: 23.2 us -> 0.84 us
    all_to_all x1 -> x0, blocking collectives: 19.4 us -> none  [local(): lax.all_to_all(gated.reshape(Z, Y, CHANS, BLOCK), 'seq', split_axis=0, co...]
    all_to_all x0 -> x1, waiting for transfers between devices: none -> 13.5 us  [local(): lax.all_to_all(gated.reshape(Z, Y, CHANS, BLOCK), 'seq', split_axis=0, co...]
    pallas_call x1, Pallas kernels: 6.46 us -> 17.1 us  [local(): pl.pallas_call(main_kernel, out_shape=(jax.ShapeDtypeStruct(plane, bf16),...]
    pallas_call x1, Pallas kernels: 2.92 us -> 9.63 us  [local(): pl.pallas_call(read_out_kernel, out_shape=jax.ShapeDtypeStruct((Y, BLOCK,...]
    pallas_call x9 -> x1, Pallas kernels: 13.9 us -> 7.88 us  [read_in(): pl.pallas_call(read_in_kernel, out_shape=jax.ShapeDtypeStruct((blocks, wi...]
    reduce_sum x1 -> x0, other arithmetic: 3.97 us -> none  [local(): filter_grad = jnp.sum(all_grads.astype(f32), 0)]
    all_to_all x0 -> x1, starting transfers between devices: none -> 3.5 us  [local(): lax.all_to_all(gated.reshape(Z, Y, CHANS, BLOCK), 'seq', split_axis=0, co...]
  transfers between devices with their start and end apart: 15 -> 16, of which waited for: 7 -> 9; matrix products, arithmetic and copies ran while one was open for 4% -> 7% of each run, Pallas kernels for 22% -> 28%
where the time goes in v1:
time: 146 us; the launch traced here: 145 us
  Pallas kernels  44.9 us (31%)
  starting transfers between devices  31.8 us (22%)
  waiting for transfers between devices  31 us (21%)
  between operations  14 us (10%)
  blocking collectives  10.3 us (7%)
  local copies, waits for them, and re-layouts  9.49 us (6%)
  other arithmetic  3.83 us (3%)
    pallas_call x1, Pallas kernels, local(): pl.pallas_call(main_kernel, out_shape=(jax.ShapeDtypeStruct(plane, bf16),...  17.1 us
    ppermute x8, starting transfers between devices, along_z(): lax.ppermute(value, 'seq', [(z * Y + y, (z + step) % Z * Y + y) for z in...  15.3 us
    all_to_all x1, waiting for transfers between devices, local(): lax.all_to_all(gated.reshape(Z, Y, CHANS, BLOCK), 'seq', split_axis=0, co...  13.5 us
    ppermute x8, waiting for transfers between devices, along_z(): lax.ppermute(value, 'seq', [(z * Y + y, (z + step) % Z * Y + y) for z in...  12.4 us
    all_to_all x1, blocking collectives, local(): lax.all_to_all(partial, 'seq', split_axis=0, concat_axis=0, tiled=True, a...  10.3 us
    pallas_call x1, Pallas kernels, local(): pl.pallas_call(read_out_kernel, out_shape=jax.ShapeDtypeStruct((Y, BLOCK,...  9.63 us
    all_to_all x1, starting transfers between devices, local(): lax.all_to_all(turned, 'seq', split_axis=0, concat_axis=0, tiled=True)  8.47 us
    pallas_call x1, Pallas kernels, read_in(): pl.pallas_call(read_in_kernel, out_shape=jax.ShapeDtypeStruct((blocks, wi...  7.88 us
  transfers between devices with their start and end apart: 16, of which 9 were waited for; matrix products, arithmetic and copies ran while one was open for 7% of the time, Pallas kernels for 28%

profile of v1, /device:TPU:8, one launch (start us, length us, event | category | flops | bytes accessed | tf_op | source)
XLA Modules:
  0.0 145.4 jit_solution(12234006681104880002)
XLA Ops:
  7.2 1.2 constant_dynamic-slice_fusion.2
  8.5 0.8 pad_maximum_fusion.1
  9.4 0.9 constant_dynamic-slice_fusion
  11.0 0.8 select_reduce_fusion
  11.9 0.9 fusion
  12.8 1.7 %collective-permute-start = (bf16[136,256]{1,0:T(8,128)(2,1)S(1)}, bf16[136,256]{1,0:T(8,128)(2,1)S(1)}, u32[]{:S(2)}, u32[]{:S(2)}) collective-permute-start(bf16[136,256]{1,0:T(8,128)(2,1)S(1)} %get-tuple-element.17), channel_id=1, source_target_pairs={{0,1},{1,2},{2,3},{3,0},{4,5},{5,6},{6,7},{7,4},{8,9},{9,10},{10,1... | collective-permute-start | bytes 208904 | tf_op jit(solution)/shard_map/ppermute | solution.py:265
  15.2 2.0 %collective-permute-start.2 = (bf16[136,256]{1,0:T(8,128)(2,1)S(1)}, bf16[136,256]{1,0:T(8,128)(2,1)S(1)}, u32[]{:S(2)}, u32[]{:S(2)}) collective-permute-start(bf16[136,256]{1,0:T(8,128)(2,1)S(1)} %get-tuple-element.17), channel_id=1, source_target_pairs={{0,2},{1,3},{2,0},{3,1},{4,6},{5,7},{6,4},{7,5},{8,10},{9,11},{10,... | collective-permute-start | bytes 208904 | tf_op jit(solution)/shard_map/ppermute | solution.py:265
  17.4 2.2 %collective-permute-done.1 = bf16[136,256]{1,0:T(8,128)(2,1)S(1)} collective-permute-done((bf16[136,256]{1,0:T(8,128)(2,1)S(1)}, bf16[136,256]{1,0:T(8,128)(2,1)S(1)}, u32[]{:S(2)}, u32[]{:S(2)}) %collective-permute-start.1) | collective-permute-done | bytes 69664 | tf_op jit(solution)/shard_map/ppermute | solution.py:265
  19.5 1.5 %collective-permute-done.2 = bf16[136,256]{1,0:T(8,128)(2,1)S(1)} collective-permute-done((bf16[136,256]{1,0:T(8,128)(2,1)S(1)}, bf16[136,256]{1,0:T(8,128)(2,1)S(1)}, u32[]{:S(2)}, u32[]{:S(2)}) %collective-permute-start.2) | collective-permute-done | bytes 69664 | tf_op jit(solution)/shard_map/ppermute | solution.py:265
  21.1 1.7 %collective-permute-start.3 = (bf16[4,136,256]{2,1,0:T(8,128)(2,1)S(1)}, bf16[4,136,256]{2,1,0:T(8,128)(2,1)S(1)}, u32[]{:S(2)}, u32[]{:S(2)}) collective-permute-start(bf16[4,136,256]{2,1,0:T(8,128)(2,1)S(1)} %pad_maximum_fusion.rest_0_), channel_id=1, source_target_pairs={{0,4},{1,5},{2,6},{3,7},{4,8},{5,9},{6,10},{7,11},{8,12},{9,13},{1... | collective-permute-start | bytes 835592 | tf_op jit(solution)/shard_map/ppermute | solution.py:269
  22.8 4.0 %collective-permute-start.6 = (bf16[4,136,256]{2,1,0:T(8,128)(2,1)S(1)}, bf16[4,136,256]{2,1,0:T(8,128)(2,1)S(1)}, u32[]{:S(2)}, u32[]{:S(2)}) collective-permute-start(bf16[4,136,256]{2,1,0:T(8,128)(2,1)S(1)} %pad_maximum_fusion.rest_0_), channel_id=1, source_target_pairs={{0,28},{1,29},{2,30},{3,31},{4,0},{5,1},{6,2},{7,3},{8,4},{9,5},{1... | collective-permute-start | bytes 835592 | tf_op jit(solution)/shard_map/ppermute | solution.py:269
  26.8 5.2 %collective-permute-done.3.rest_1_ = bf16[4,136,256]{2,1,0:T(8,128)(2,1)S(1)} collective-permute-done((bf16[4,136,256]{2,1,0:T(8,128)(2,1)S(1)}, bf16[4,136,256]{2,1,0:T(8,128)(2,1)S(1)}, u32[]{:S(2)}, u32[]{:S(2)}) %collective-permute-start.3) | collective-permute-done | bytes 278560 | tf_op jit(solution)/shard_map/ppermute | solution.py:269
  32.1 3.2 %collective-permute-start.7 = (bf16[4,136,256]{2,1,0:T(8,128)(2,1)S(1)}, bf16[4,136,256]{2,1,0:T(8,128)(2,1)}, u32[]{:S(2)}, u32[]{:S(2)}) collective-permute-start(bf16[4,136,256]{2,1,0:T(8,128)(2,1)S(1)} %collective-permute-done.6.rest_2_), channel_id=1, source_target_pairs={{0,28},{1,29},{2,30},{3,31},{4,0},{5,1},{6,2},{7,3},{8,4},{9,5},{1... | collective-permute-start | bytes 835592 | tf_op jit(solution)/shard_map/ppermute | solution.py:269
  35.3 4.6 %collective-permute-done.4.rest_3_ = bf16[4,136,256]{2,1,0:T(8,128)(2,1)} collective-permute-done((bf16[4,136,256]{2,1,0:T(8,128)(2,1)S(1)}, bf16[4,136,256]{2,1,0:T(8,128)(2,1)}, u32[]{:S(2)}, u32[]{:S(2)}) %collective-permute-start.4) | collective-permute-done | bytes 278560 | tf_op jit(solution)/shard_map/ppermute | solution.py:269
  39.9 3.2 %collective-permute-start.8 = (bf16[4,136,256]{2,1,0:T(8,128)(2,1)}, bf16[4,136,256]{2,1,0:T(8,128)(2,1)S(1)}, u32[]{:S(2)}, u32[]{:S(2)}) collective-permute-start(bf16[4,136,256]{2,1,0:T(8,128)(2,1)} %collective-permute-done.7.rest_4_), channel_id=1, source_target_pairs={{0,28},{1,29},{2,30},{3,31},{4,0},{5,1},{6,2},{7,3},{8,4},{9,5},{1... | collective-permute-start | bytes 835592 | tf_op jit(solution)/shard_map/ppermute | solution.py:269
  43.2 2.1 %copy.20 = bf16[2048,128]{1,0:T(8,128)(2,1)} copy(bf16[2048,128]{0,1:T(8,128)(2,1)} %bitcast.23) | data formatting | bytes 1048576 | tf_op jit(solution)/shard_map/transpose | solution.py:303
  45.2 7.9 %read_in.1.early_hbm = bf16[20,128,128]{2,1,0:T(8,128)(2,1)} custom-call(bf16[16,256,128]{2,1,0:T(8,128)(2,1)} %all-gather.5.cloned.1.call-done.weight_hbm, bf16[4,136,256]{2,1,0:T(8,128)(2,1)} %copy-done.3, bf16[4,136,256]{2,1,0:T(8,128)(2,1)} %copy-done.7, bf16[4,136,256]{2,1,0:T(8,128)(2,1)} %copy-done.8, ...), custom_call_target="tpu_custom_call" | custom-call | flops 2684354560 | bytes 4194304 | tf_op jit(solution)/shard_map/read_in/pallas_call | solution.py:137
  53.2 8.5 %all-to-all-start = ((bf16[32,64,128]{2,1,0:T(8,128)(2,1)}), bf16[32,64,128]{2,1,0:T(8,128)(2,1)S(1)}, u32[]{:S(2)}, u32[]{:S(2)}) async-start(bf16[32,64,128]{2,1,0:T(8,128)(2,1)} %bitcast.10), calls=%async_computation | async-start | bytes 1048576 | tf_op jit(solution)/shard_map/all_to_all | solution.py:310
  62.3 2.8 %collective-permute-start.10 = (bf16[2,136,256]{2,1,0:T(8,128)(2,1)S(1)}, bf16[2,136,256]{2,1,0:T(8,128)(2,1)S(1)}, u32[]{:S(2)}, u32[]{:S(2)}) collective-permute-start(bf16[2,136,256]{2,1,0:T(8,128)(2,1)S(1)} %slice.14), channel_id=1, source_target_pairs={{0,28},{1,29},{2,30},{3,31},{4,0},{5,1},{6,2},{7,3},{8,4},{9,5},{1... | collective-permute-start | bytes 417800 | tf_op jit(solution)/shard_map/ppermute | solution.py:269
  65.4 6.1 %filter_transform.1.filter_hbm = f32[8,256,256]{2,1,0:T(8,128)} custom-call(f32[64,4096]{1,0:T(8,128)} %filter_ref.1, bf16[512,256]{1,0:T(8,128)(2,1)} %constant.58.clone.first_ref.rest_0_, bf16[256,256]{1,0:T(8,128)(2,1)} %constant.59.clone.second_ref.rest_1_, f32[2,32,128]{2,1,0:T(8,128)} %constant.62.clone.twist_ref), custom_call_target="tpu_custom_call" | custom-call | flops 536870912 | bytes 4194304 | tf_op jit(solution)/shard_map/filter_transform/pallas_call | solution.py:316
  72.3 1.4 collective-permute-done.10.last_left_hbm
  73.7 1.1 collective-permute-done.9.last_right_hbm
  74.8 1.3 all-to-all-done.grad_hbm
  76.2 0.9 broadcast_in_dim.20.taps_ref
  77.7 17.1 %long_convolution.1 = (bf16[32,64,128]{2,1,0:T(8,128)(2,1)}, bf16[64,4096]{1,0:T(8,128)(2,1)}) custom-call(s32[2]{0:T(128)} %pad_add_fusion.place_ref, f32[3,64,128]{2,1,0:T(8,128)} %broadcast_in_dim.20.taps_ref, f32[64,128]{1,0:T(8,128)} %broadcast_in_dim.21.gain_ref, f32[2,32,128]{2,1,0:T(8,128)} %constant.62.clone.twist_ref, ...), custom_call_target="tpu_custom_call" | custom-call | flops 2147483648 | bytes 8388608 | tf_op jit(solution)/shard_map/long_convolution/pallas_call | solution.py:331
  94.9 3.5 %all-to-all-start.1 = ((bf16[8,4,64,128]{3,2,1,0:T(8,128)(2,1)}), bf16[8,4,64,128]{3,2,1,0:T(8,128)(2,1)S(1)}, u32[]{:S(2)}, u32[]{:S(2)}) async-start(bf16[8,4,64,128]{3,2,1,0:T(8,128)(2,1)} %bitcast.24), calls=%async_computation.1 | async-start | bytes 1048576 | tf_op jit(solution)/shard_map/all_to_all | solution.py:351
  98.4 1.3 slice.16.mark_ref
  99.8 13.5 %all-to-all-done.1.rows_ref = bf16[8,4,64,128]{3,2,1,0:T(8,128)(2,1)S(1)} async-done(((bf16[8,4,64,128]{3,2,1,0:T(8,128)(2,1)}), bf16[8,4,64,128]{3,2,1,0:T(8,128)(2,1)S(1)}, u32[]{:S(2)}, u32[]{:S(2)}) %all-to-all-start.1) | async-done | bytes 524320 | tf_op jit(solution)/shard_map/all_to_all | solution.py:351
  113.2 0.8 copy-done.2
  114.0 9.6 %read_out.1 = bf16[4,128,256]{2,1,0:T(8,128)(2,1)} custom-call(s32[2]{0:T(128)} %pad_add_fusion.place_ref, bf16[8,4,64,128]{3,2,1,0:T(8,128)(2,1)} %copy-done.2, bf16[4,8,256]{2,1,0:T(8,128)(2,1)} %slice.16.mark_ref, bf16[16,512,256]{2,1,0:T(8,128)(2,1)} %all-gather.7.cloned.1.call-done.weight_hbm), custom_call_target="tpu_custom_call" | custom-call | flops 2147483648 | bytes 6291456 | tf_op jit(solution)/shard_map/read_out/pallas_call | solution.py:352
  123.7 10.3 %all_to_all.15 = bf16[4,128,256]{2,1,0:T(8,128)(2,1)S(1)} all-to-all(bf16[4,128,256]{2,1,0:T(8,128)(2,1)} %read_out.1), channel_id=1, replica_groups={{0,1,2,3},{4,5,6,7},{8,9,10,11},{12,13,14,15},{16,17,18,19},{20,21,22,2..., dimensions={0} | all-to-all | bytes 524288 | tf_op jit(solution)/shard_map/all_to_all | solution.py:362
  134.7 4.2 %sum_gradients.1 = f32[64,4096]{1,0:T(8,128)} custom-call(bf16[8,64,4096]{2,1,0:T(8,128)(2,1)} %bitcast.21), custom_call_target="tpu_custom_call" | custom-call | flops 2097152 | bytes 5242880 | tf_op jit(solution)/shard_map/sum_gradients/pallas_call | solution.py:366
  (49 shorter events, 4.9 us)
Async XLA Ops:
  7.2 2.2 %copy-start = (bf16[2,2048,256]{2,1,0:T(8,128)(2,1)S(1)}, bf16[2,2048,256]{2,1,0:T(8,128)(2,1)}, u32[]{:S(2)}) copy-start(bf16[2,2048,256]{2,1,0:T(8,128)(2,1)} %param.21) | copy-start | bytes 6291460
  7.2 38.1 %all-gather.5.cloned.1.call-start = ((), (), s32[]{:S(2)}) async-start(), calls=%async_computation.3 | async-start | bytes 1179648 | tf_op jit(solution)/shard_map/all_gather | solution.py:290
  9.3 104.0 %all-gather.7.cloned.1.call-start = ((), (), s32[]{:S(2)}) async-start(), calls=%async_computation.4 | async-start | bytes 4718592 | tf_op jit(solution)/shard_map/all_gather | solution.py:293
  12.8 4.6 %collective-permute-start = (bf16[136,256]{1,0:T(8,128)(2,1)S(1)}, bf16[136,256]{1,0:T(8,128)(2,1)S(1)}, u32[]{:S(2)}, u32[]{:S(2)}) collective-permute-start(bf16[136,256]{1,0:T(8,128)(2,1)S(1)} %get-tuple-element.17), channel_id=1, source_target_pairs={{0,1},{1,2},{2,3},{3,0},{4,5},{5,6},{6,7},{7,4},{8,9},{9,10},{10,1... | collective-permute-start | bytes 208904 | tf_op jit(solution)/shard_map/ppermute | solution.py:265
  14.5 5.1 %collective-permute-start.1 = (bf16[136,256]{1,0:T(8,128)(2,1)S(1)}, bf16[136,256]{1,0:T(8,128)(2,1)S(1)}, u32[]{:S(2)}, u32[]{:S(2)}) collective-permute-start(bf16[136,256]{1,0:T(8,128)(2,1)S(1)} %get-tuple-element.17), channel_id=1, source_target_pairs={{0,3},{1,0},{2,1},{3,2},{4,7},{5,4},{6,5},{7,6},{8,11},{9,8},{10,9... | collective-permute-start | bytes 208904 | tf_op jit(solution)/shard_map/ppermute | solution.py:265
  15.2 5.8 %collective-permute-start.2 = (bf16[136,256]{1,0:T(8,128)(2,1)S(1)}, bf16[136,256]{1,0:T(8,128)(2,1)S(1)}, u32[]{:S(2)}, u32[]{:S(2)}) collective-permute-start(bf16[136,256]{1,0:T(8,128)(2,1)S(1)} %get-tuple-element.17), channel_id=1, source_target_pairs={{0,2},{1,3},{2,0},{3,1},{4,6},{5,7},{6,4},{7,5},{8,10},{9,11},{10,... | collective-permute-start | bytes 208904 | tf_op jit(solution)/shard_map/ppermute | solution.py:265
  21.0 24.2 %copy-start.3 = (bf16[4,136,256]{2,1,0:T(8,128)(2,1)}, bf16[4,136,256]{2,1,0:T(8,128)(2,1)S(1)}, u32[]{:S(2)}) copy-start(bf16[4,136,256]{2,1,0:T(8,128)(2,1)S(1)} %pad_maximum_fusion.rest_0_) | copy-start | bytes 835588
  21.1 11.0 %collective-permute-start.3 = (bf16[4,136,256]{2,1,0:T(8,128)(2,1)S(1)}, bf16[4,136,256]{2,1,0:T(8,128)(2,1)S(1)}, u32[]{:S(2)}, u32[]{:S(2)}) collective-permute-start(bf16[4,136,256]{2,1,0:T(8,128)(2,1)S(1)} %pad_maximum_fusion.rest_0_), channel_id=1, source_target_pairs={{0,4},{1,5},{2,6},{3,7},{4,8},{5,9},{6,10},{7,11},{8,12},{9,13},{1... | collective-permute-start | bytes 835592 | tf_op jit(solution)/shard_map/ppermute | solution.py:269
  22.8 9.3 %collective-permute-start.6 = (bf16[4,136,256]{2,1,0:T(8,128)(2,1)S(1)}, bf16[4,136,256]{2,1,0:T(8,128)(2,1)S(1)}, u32[]{:S(2)}, u32[]{:S(2)}) collective-permute-start(bf16[4,136,256]{2,1,0:T(8,128)(2,1)S(1)} %pad_maximum_fusion.rest_0_), channel_id=1, source_target_pairs={{0,28},{1,29},{2,30},{3,31},{4,0},{5,1},{6,2},{7,3},{8,4},{9,5},{1... | collective-permute-start | bytes 835592 | tf_op jit(solution)/shard_map/ppermute | solution.py:269
  32.1 13.2 %copy-start.7 = (bf16[4,136,256]{2,1,0:T(8,128)(2,1)}, bf16[4,136,256]{2,1,0:T(8,128)(2,1)S(1)}, u32[]{:S(2)}) copy-start(bf16[4,136,256]{2,1,0:T(8,128)(2,1)S(1)} %collective-permute-done.3.rest_1_) | copy-start | bytes 835588
  32.1 7.9 %collective-permute-start.4 = (bf16[4,136,256]{2,1,0:T(8,128)(2,1)S(1)}, bf16[4,136,256]{2,1,0:T(8,128)(2,1)}, u32[]{:S(2)}, u32[]{:S(2)}) collective-permute-start(bf16[4,136,256]{2,1,0:T(8,128)(2,1)S(1)} %collective-permute-done.3.rest_1_), channel_id=1, source_target_pairs={{0,4},{1,5},{2,6},{3,7},{4,8},{5,9},{6,10},{7,11},{8,12},{9,13},{1... | collective-permute-start | bytes 835592 | tf_op jit(solution)/shard_map/ppermute | solution.py:269
  32.1 13.2 %copy-start.8 = (bf16[4,136,256]{2,1,0:T(8,128)(2,1)}, bf16[4,136,256]{2,1,0:T(8,128)(2,1)S(1)}, u32[]{:S(2)}) copy-start(bf16[4,136,256]{2,1,0:T(8,128)(2,1)S(1)} %collective-permute-done.6.rest_2_) | copy-start | bytes 835588
  32.1 7.9 %collective-permute-start.7 = (bf16[4,136,256]{2,1,0:T(8,128)(2,1)S(1)}, bf16[4,136,256]{2,1,0:T(8,128)(2,1)}, u32[]{:S(2)}, u32[]{:S(2)}) collective-permute-start(bf16[4,136,256]{2,1,0:T(8,128)(2,1)S(1)} %collective-permute-done.6.rest_2_), channel_id=1, source_target_pairs={{0,28},{1,29},{2,30},{3,31},{4,0},{5,1},{6,2},{7,3},{8,4},{9,5},{1... | collective-permute-start | bytes 835592 | tf_op jit(solution)/shard_map/ppermute | solution.py:269
  39.9 13.2 %collective-permute-start.5 = (bf16[4,136,256]{2,1,0:T(8,128)(2,1)}, bf16[4,136,256]{2,1,0:T(8,128)(2,1)S(1)}, u32[]{:S(2)}, u32[]{:S(2)}) collective-permute-start(bf16[4,136,256]{2,1,0:T(8,128)(2,1)} %collective-permute-done.4.rest_3_), channel_id=1, source_target_pairs={{0,4},{1,5},{2,6},{3,7},{4,8},{5,9},{6,10},{7,11},{8,12},{9,13},{1... | collective-permute-start | bytes 835592 | tf_op jit(solution)/shard_map/ppermute | solution.py:269
  39.9 13.2 %collective-permute-start.8 = (bf16[4,136,256]{2,1,0:T(8,128)(2,1)}, bf16[4,136,256]{2,1,0:T(8,128)(2,1)S(1)}, u32[]{:S(2)}, u32[]{:S(2)}) collective-permute-start(bf16[4,136,256]{2,1,0:T(8,128)(2,1)} %collective-permute-done.7.rest_4_), channel_id=1, source_target_pairs={{0,28},{1,29},{2,30},{3,31},{4,0},{5,1},{6,2},{7,3},{8,4},{9,5},{1... | collective-permute-start | bytes 835592 | tf_op jit(solution)/shard_map/ppermute | solution.py:269
  53.1 23.9 %copy-start.6 = (f32[64]{0:T(128)S(1)}, f32[64]{0:T(128)}, u32[]{:S(2)}) copy-start(f32[64]{0:T(128)} %param.20) | copy-start | bytes 772
  53.2 24.6 %copy-start.4 = (bf16[4,136,256]{2,1,0:T(8,128)(2,1)}, bf16[4,136,256]{2,1,0:T(8,128)(2,1)S(1)}, u32[]{:S(2)}) copy-start(bf16[4,136,256]{2,1,0:T(8,128)(2,1)S(1)} %collective-permute-done.5.right_hbm) | copy-start | bytes 835588
  53.2 24.6 %copy-start.5 = (bf16[4,136,256]{2,1,0:T(8,128)(2,1)}, bf16[4,136,256]{2,1,0:T(8,128)(2,1)S(1)}, u32[]{:S(2)}) copy-start(bf16[4,136,256]{2,1,0:T(8,128)(2,1)S(1)} %collective-permute-done.8.left_hbm) | copy-start | bytes 835588
  53.2 23.0 %all-to-all-start = ((bf16[32,64,128]{2,1,0:T(8,128)(2,1)}), bf16[32,64,128]{2,1,0:T(8,128)(2,1)S(1)}, u32[]{:S(2)}, u32[]{:S(2)}) async-start(bf16[32,64,128]{2,1,0:T(8,128)(2,1)} %bitcast.10), calls=%async_computation | async-start | bytes 1048576 | tf_op jit(solution)/shard_map/all_to_all | solution.py:310
  61.7 73.0 %all-gather.9.cloned.1.call-start = ((), (), s32[]{:S(2)}) async-start(), calls=%async_computation.5 | async-start | bytes 4718592 | tf_op jit(solution)/shard_map/all_gather | solution.py:349
  62.3 11.4 %collective-permute-start.10 = (bf16[2,136,256]{2,1,0:T(8,128)(2,1)S(1)}, bf16[2,136,256]{2,1,0:T(8,128)(2,1)S(1)}, u32[]{:S(2)}, u32[]{:S(2)}) collective-permute-start(bf16[2,136,256]{2,1,0:T(8,128)(2,1)S(1)} %slice.14), channel_id=1, source_target_pairs={{0,28},{1,29},{2,30},{3,31},{4,0},{5,1},{6,2},{7,3},{8,4},{9,5},{1... | collective-permute-start | bytes 417800 | tf_op jit(solution)/shard_map/ppermute | solution.py:269
  65.2 9.7 %collective-permute-start.9 = (bf16[2,136,256]{2,1,0:T(8,128)(2,1)S(1)}, bf16[2,136,256]{2,1,0:T(8,128)(2,1)S(1)}, u32[]{:S(2)}, u32[]{:S(2)}) collective-permute-start(bf16[2,136,256]{2,1,0:T(8,128)(2,1)S(1)} %slice.13), channel_id=1, source_target_pairs={{0,4},{1,5},{2,6},{3,7},{4,8},{5,9},{6,10},{7,11},{8,12},{9,13},{1... | collective-permute-start | bytes 417800 | tf_op jit(solution)/shard_map/ppermute | solution.py:269
  73.7 4.0 %copy-start.9 = (bf16[2,136,256]{2,1,0:T(8,128)(2,1)}, bf16[2,136,256]{2,1,0:T(8,128)(2,1)S(1)}, u32[]{:S(2)}) copy-start(bf16[2,136,256]{2,1,0:T(8,128)(2,1)S(1)} %collective-permute-done.10.last_left_hbm) | copy-start | bytes 417796
  74.8 2.9 %copy-start.10 = (bf16[2,136,256]{2,1,0:T(8,128)(2,1)}, bf16[2,136,256]{2,1,0:T(8,128)(2,1)S(1)}, u32[]{:S(2)}) copy-start(bf16[2,136,256]{2,1,0:T(8,128)(2,1)S(1)} %collective-permute-done.9.last_right_hbm) | copy-start | bytes 417796
  76.2 1.6 %copy-start.1 = (bf16[32,64,128]{2,1,0:T(8,128)(2,1)}, bf16[32,64,128]{2,1,0:T(8,128)(2,1)S(1)}, u32[]{:S(2)}) copy-start(bf16[32,64,128]{2,1,0:T(8,128)(2,1)S(1)} %all-to-all-done.grad_hbm) | copy-start | bytes 1572868
  94.9 18.3 %all-to-all-start.1 = ((bf16[8,4,64,128]{3,2,1,0:T(8,128)(2,1)}), bf16[8,4,64,128]{3,2,1,0:T(8,128)(2,1)S(1)}, u32[]{:S(2)}, u32[]{:S(2)}) async-start(bf16[8,4,64,128]{3,2,1,0:T(8,128)(2,1)} %bitcast.24), calls=%async_computation.1 | async-start | bytes 1048576 | tf_op jit(solution)/shard_map/all_to_all | solution.py:351
  113.2 0.8 copy-start.2
Sparse Core Ops, SparseCore 0:
  10.4 28.7 all-gather.4
  41.1 34.6 all-gather.6
  95.0 31.9 all-gather.8

commit v2 on v1

--- a/solution.py
+++ b/solution.py
@@ -52,32 +52,37 @@
     return cosine, sine
 
 
-def forward(signal, first_ref, second_ref, cosine, sine):
+def forward(low, high, first_ref, second_ref, cosine, sine):
     rows = BLOCKS * LANE8
-    part = jnp.dot(first_ref[...], signal.astype(bf16), preferred_element_type=f32)
-    real, imag = part[:rows], part[rows:]
-    turned = jnp.concatenate([real * cosine - imag * sine, real * sine + imag * cosine], 1)
-    return jnp.dot(turned.astype(bf16), second_ref[...], preferred_element_type=f32)
-
-
-def backward(real, imag, back_second_ref, back_first_ref, cosine, sine):
-    both = jnp.concatenate([real, imag], 1).astype(bf16)
-    part = jnp.dot(both, back_second_ref[...], preferred_element_type=f32)
-    real, imag = part[:, :BLOCK], part[:, BLOCK:]
-    turned = jnp.concatenate([real * cosine + imag * sine, imag * cosine - real * sine], 0)
-    return jnp.dot(back_first_ref[...], turned.astype(bf16), preferred_element_type=f32)
+    signals = jnp.concatenate([low, high], 1).astype(bf16)
+    part = jnp.dot(first_ref[...], signals, preferred_element_type=f32)
+    turned = []
+    for lanes in (slice(0, BLOCK), slice(BLOCK, 2 * BLOCK)):
+        real, imag = part[:rows, lanes], part[rows:, lanes]
+        turned.append(jnp.concatenate([real * cosine - imag * sine, real * sine + imag * cosine], 1))
+    return jnp.dot(jnp.concatenate(turned, 0).astype(bf16), second_ref[...], preferred_element_type=f32)
+
+
+def backward(spectra, back_second_ref, back_first_ref, cosine, sine):
+    rows = BLOCKS * LANE8
+    part = jnp.dot(spectra.astype(bf16), back_second_ref[...], preferred_element_type=f32)
+    turned = []
+    for start in (0, rows):
+        real, imag = part[start : start + rows, :BLOCK], part[start : start + rows, BLOCK:]
+        turned.append(jnp.concatenate([real * cosine + imag * sine, imag * cosine - real * sine], 0))
+    return jnp.dot(back_first_ref[...], jnp.concatenate(turned, 1).astype(bf16), preferred_element_type=f32)
 
 
 def filter_kernel(filter_ref, first_ref, second_ref, twist_ref, spectrum_ref):
     cosine, sine = twists_of(twist_ref)
-
-    def step(group, carry):
-        rows = filter_ref[pl.ds(pl.multiple_of(group * LANE8, LANE8), LANE8), :]
-        signal = jnp.concatenate([rows[:, i * BLOCK : (i + 1) * BLOCK] for i in range(BLOCKS)], 0)
-        spectrum_ref[group] = forward(signal, first_ref, second_ref, cosine, sine)
-        return carry
-
-    lax.fori_loop(0, GROUPS, step, 0)
+    rows = BLOCKS * LANE8
+    signals = []
+    for start in (0, LANE8):
+        pieces = [filter_ref[start : start + LANE8, i * BLOCK : (i + 1) * BLOCK] for i in range(BLOCKS)]
+        signals.append(jnp.concatenate(pieces, 0))
+    spectra = forward(*signals, first_ref, second_ref, cosine, sine)
+    spectrum_ref[0] = spectra[:rows]
+    spectrum_ref[1] = spectra[rows:]
 
 
 def start_all(copies):
@@ -98,16 +103,40 @@
     return copies
 
 
+def masks_of(marks, width):
+    trials = marks.shape[0]
+    marks = marks[:, :width].astype(jnp.int32)
+    marks = jnp.broadcast_to(marks[:, None, :], (trials, TRIAL, width)).reshape(trials * TRIAL, width)
+    return marks
+
+
+def pick(leaf, marks, count):
+    level = 0
+    stack = []
+    for index in range(count):
+        node = leaf(index)
+        level = 0
+        while stack and stack[-1][0] == level:
+            node = jnp.where((marks & (1 << level)) != 0, node, stack.pop()[1])
+            level += 1
+        stack.append((level, node))
+    return stack[0][1]
+
+
 def project(rows_ref, start, weight):
     width = 2 * CHANS
     rows = rows_ref[pl.ds(start, 2), :BLOCK, :].reshape(2 * BLOCK, rows_ref.shape[2])
-    marks = rows_ref[pl.ds(start, 2), BLOCK:, :].astype(f32)[:, :, :width].reshape(2 * BLOCK // TRIAL, width)
-    marks = jnp.broadcast_to(marks[:, None, :], (2 * BLOCK // TRIAL, TRIAL, width)).reshape(2 * BLOCK, width)
-    chosen = jnp.zeros((2 * BLOCK, width), f32)
-    for pair in range(weight.shape[0]):
-        product = jnp.dot(rows, weight[pair], preferred_element_type=f32)
-        chosen = jnp.where(marks == 2 * pair, product[:, :width], chosen)
-        chosen = jnp.where(marks == 2 * pair + 1, product[:, width:], chosen)
+    marks = rows_ref[pl.ds(start, 2), BLOCK:, :].astype(f32).reshape(2 * BLOCK // TRIAL, rows_ref.shape[2])
+    marks = masks_of(marks, width)
+    products = {}
+
+    def leaf(slot):
+        if slot % 2 == 0:
+            products[0] = jnp.dot(rows, weight[slot // 2], preferred_element_type=f32)
+            return products[0][:, :width]
+        return products[0][:, width:]
+
+    chosen = pick(leaf, marks, 2 * weight.shape[0])
     return chosen[:BLOCK].T.astype(bf16), chosen[BLOCK:].T.astype(bf16)
 
 
@@ -199,20 +228,19 @@
             before = jnp.concatenate([jnp.zeros((1, LANE8, BLOCK), f32), rolled[:-1]], 0)
             total = total + taps[shift][None] * jnp.where(lane < shift, before, rolled)
         signal = total.astype(bf16).astype(f32).reshape(count, BLOCK)
-        spectrum = forward(signal, first_ref, second_ref, cosine, sine)
-        own_re, own_im = spectrum[:, :BLOCK], spectrum[:, BLOCK:]
+        mixed_grad = (grads * gate).reshape(count, BLOCK)
+        spectra_two = forward(signal, mixed_grad, first_ref, second_ref, cosine, sine)
+        own_re, own_im = spectra_two[:count, :BLOCK], spectra_two[:count, BLOCK:]
+        grad_re, grad_im = spectra_two[count:, :BLOCK], spectra_two[count:, BLOCK:]
         weight = spectra[group]
-        real = own_re * weight[:, :BLOCK] - own_im * weight[:, BLOCK:]
-        imag = own_re * weight[:, BLOCK:] + own_im * weight[:, :BLOCK]
-        long_part = backward(real, imag, back_second_ref, back_first_ref, cosine, sine)
-        mixed = long_part.reshape(cube) + gain_ref[here, :][None] * signal.reshape(cube)
+        filter_re, filter_im = weight[:, :BLOCK], weight[:, BLOCK:]
+        mix = jnp.concatenate([own_re * filter_re - own_im * filter_im, own_re * filter_im + own_im * filter_re], 1)
+        lag = jnp.concatenate([own_re * grad_re + own_im * grad_im, own_re * grad_im - own_im * grad_re], 1)
+        result = backward(jnp.concatenate([mix, lag], 0), back_second_ref, back_first_ref, cosine, sine)
+        mixed = result[:, :BLOCK].reshape(cube) + gain_ref[here, :][None] * signal.reshape(cube)
         gated = gate * mixed.astype(bf16).astype(f32)
-        mixed_grad = (grads * gate).reshape(count, BLOCK)
-        turned = forward(mixed_grad, first_ref, second_ref, cosine, sine)
-        real = own_re * turned[:, :BLOCK] + own_im * turned[:, BLOCK:]
-        imag = own_re * turned[:, BLOCK:] - own_im * turned[:, :BLOCK]
-        result = backward(real, imag, back_second_ref, back_first_ref, cosine, sine)
-        return gated, jnp.concatenate([result[i * LANE8 : (i + 1) * LANE8] for i in range(BLOCKS)], 1)
+        pieces = [result[i * LANE8 : (i + 1) * LANE8, BLOCK:] for i in range(BLOCKS)]
+        return gated, jnp.concatenate(pieces, 1)
 
     def step(pair, carry):
         here = pl.ds(pl.multiple_of(pair * 2 * LANE8, 2 * LANE8), 2 * LANE8)
@@ -222,43 +250,39 @@
         grads = grad_all[:, here, :].astype(f32)
         gated_low, low = one_group(pair * 2, value[:, :LANE8], gate[:, :LANE8], grads[:, :LANE8])
         gated_high, high = one_group(pair * 2 + 1, value[:, LANE8:], gate[:, LANE8:], grads[:, LANE8:])
-        gated_ref[:, here, :] = jnp.concatenate([gated_low, gated_high], 1).astype(bf16)
+        gated = jnp.concatenate([gated_low, gated_high], 1).astype(bf16).reshape(Z, Y, 2 * LANE8, BLOCK)
+        for y in range(Y):
+            gated_ref[y, :, here, :] = gated[:, y]
         out_ref[here, :] = jnp.concatenate([low, high], 0).astype(bf16)
         return carry
 
     lax.fori_loop(0, GROUPS // 2, step, 0)
 
 
-def read_out_kernel(place_ref, rows_ref, mark_ref, weight_hbm, out_ref, weight, sems):
-    y = place_ref[1]
-    trials = BLOCK // TRIAL
-    slots, inner, width = weight.shape
-    loads = [pltpu.make_async_copy(weight_hbm.at[slot], weight.at[slot], sems.at[slot]) for slot in range(slots)]
-    start_all(loads)
-    pieces = []
-    marks = []
-    for index, y_step in enumerate(Y_STEPS):
-        block = lax.rem(y + (y_step + Y), Y)
-        pieces.append(rows_ref[:, block, :, :].reshape(inner, BLOCK).T)
-        mark = mark_ref[index].astype(f32)
-        marks.append(jnp.broadcast_to(mark[:, None, :], (trials, TRIAL, width)).reshape(BLOCK, width))
-    rows = jnp.concatenate(pieces, 0)
-    marks = jnp.concatenate(marks, 0)
-    chosen = jnp.zeros((Y * BLOCK, width), f32)
-    for slot in range(slots):
-        loads[slot].wait()
-        product = jnp.dot(rows, weight[slot], preferred_element_type=f32)
-        chosen = jnp.where(marks == slot, product, chosen)
-    for index, y_step in enumerate(Y_STEPS):
-        block = lax.rem(y + (y_step + Y), Y)
-        out_ref[block] = chosen[index * BLOCK : (index + 1) * BLOCK].astype(bf16)
-
-
-def sum_kernel(parts_ref, out_ref):
-    total = parts_ref[0].astype(f32)
-    for index in range(1, parts_ref.shape[0]):
-        total = total + parts_ref[index].astype(f32)
-    out_ref[...] = total
+def read_out_kernel(place_ref, rows_ref, mark_ref, weight_ref, out_ref):
+    slots, inner, width = weight_ref.shape
+
+    def block_at(index):
+        up = (index + 1) // 2
+        step = jnp.where(index % 2 == 1, Z - up, index // 2)
+        return lax.rem(place_ref[0] + step, Z)
+
+    def step(pair, carry):
+        pieces = []
+        marks = []
+        for index in range(2):
+            block = block_at(pair * 2 + index)
+            pieces.append(rows_ref[:, block, :, :].reshape(inner, BLOCK).T)
+            marks.append(mark_ref[pair * 2 + index].astype(f32))
+        rows = jnp.concatenate(pieces, 0)
+        marks = masks_of(jnp.concatenate(marks, 0), width)
+        leaf = lambda slot: jnp.dot(rows, weight_ref[slot], preferred_element_type=f32)
+        chosen = pick(leaf, marks, slots)
+        for index in range(2):
+            out_ref[block_at(pair * 2 + index)] = chosen[index * BLOCK : (index + 1) * BLOCK].astype(bf16)
+        return carry
+
+    lax.fori_loop(0, Z // 2, step, 0)
 
 
 def along_y(value, step):
@@ -269,12 +293,19 @@
     return lax.ppermute(value, "seq", [(z * Y + y, (z + step) % Z * Y + y) for z in range(Z) for y in range(Y)])
 
 
+def gather_weights(own):
+    groups = lax.axis_size("grp")
+    copies = jnp.broadcast_to(own[None], (groups,) + own.shape)
+    gathered = lax.all_to_all(copies, "grp", split_axis=0, concat_axis=0, tiled=True)
+    return gathered.reshape((groups * own.shape[0],) + own.shape[1:])
+
+
 def whole(count):
     return [pl.BlockSpec(memory_space=pltpu.VMEM)] * count
 
 
 def local(spikes, session_of_bin, session_slot, readin_weight, short_kernel, long_filter, skip_gain, readout_weight, out_grad):
-    experts_here = readin_weight.shape[0]
+    groups = lax.axis_size("grp")
     in_chans = spikes.shape[2]
     model_width = short_kernel.shape[1]
     place = lax.axis_index("seq")
@@ -287,10 +318,9 @@
     own = jnp.concatenate(
         [lax.dynamic_slice_in_dim(readin_weight, start + place * CHANS, CHANS, 2) for start in (0, model_width)], 2
     )
-    in_weights = lax.all_gather(own, "grp", axis=0, tiled=True)
-    split = readout_weight.reshape(experts_here, Z, Y, CHANS, in_chans)
-    own = lax.dynamic_index_in_dim(split, place % Y, 2, keepdims=False).reshape(experts_here, Z * CHANS, in_chans)
-    out_weights = lax.all_gather(own, "grp", axis=0, tiled=True)
+    in_weights = gather_weights(own)
+    own = lax.dynamic_slice_in_dim(readout_weight, place // Y * (Y * CHANS), Y * CHANS, 1)
+    out_weights = gather_weights(own)
 
     sessions = session_of_bin[0, ::TRIAL]
     matches = sessions[:, None] == jnp.arange(session_slot.shape[0], dtype=jnp.int32)[None, :]
@@ -301,23 +331,29 @@
     chunks = [chunk]
     right = left = chunk
     turned = out_grad[0].T.reshape(BLOCKS, CHANS, BLOCK)
-    for _ in range(3):
+    for _ in range(2):
         right, left = along_z(right, 1), along_z(left, -1)
         chunks += [right, left]
-    early = read_in(chunks[:5], in_weights)
+    right, left, in_weights = lax.optimization_barrier((right, left, in_weights))
+    right, left = along_z(right, 1), along_z(left, -1)
+    early = read_in(chunks, in_weights)
     right, left, turned, early = lax.optimization_barrier((right, left, turned, early))
     last_right, last_left = along_z(right[: Y // 2], 1), along_z(left[Y // 2 :], -1)
     grads = lax.all_to_all(turned, "seq", split_axis=0, concat_axis=0, tiled=True)
+    chunks += [right, left]
 
     spectrum_shape = jax.ShapeDtypeStruct((GROUPS, BLOCKS * LANE8, 2 * BLOCK), f32)
     plane = (BLOCKS, CHANS, BLOCK)
     params = pltpu.CompilerParams(vmem_limit_bytes=60 << 20)
     work = 2 * GROUPS * (512 * 256 * 128 + 256 * 256 * 256)
+    pair = 2 * LANE8
     filter_spectrum = pl.pallas_call(
         filter_kernel,
         out_shape=spectrum_shape,
-        in_specs=whole(4),
-        out_specs=whole(1)[0],
+        grid=(GROUPS // 2,),
+        in_specs=[pl.BlockSpec((pair, LENGTH), lambda i: (i, 0))]
+        + [pl.BlockSpec(table.shape, lambda i, rank=table.ndim: (0,) * rank) for table in (first, second, twists)],
+        out_specs=pl.BlockSpec((2,) + spectrum_shape.shape[1:], lambda i: (i, 0, 0)),
         compiler_params=params,
         cost_estimate=pl.CostEstimate(flops=work, bytes_accessed=4 << 20, transcendentals=0),
         name="filter_transform",
@@ -330,7 +366,10 @@
     late_rows = 2 * Y + Y
     gated, own_grad = pl.pallas_call(
         main_kernel,
-        out_shape=(jax.ShapeDtypeStruct(plane, bf16), jax.ShapeDtypeStruct((CHANS, LENGTH), bf16)),
+        out_shape=(
+            jax.ShapeDtypeStruct((Y, Z, CHANS, BLOCK), bf16),
+            jax.ShapeDtypeStruct((CHANS, LENGTH), bf16),
+        ),
         in_specs=[scalar] + whole(3) + [pl.BlockSpec(memory_space=pltpu.HBM)] * 12,
         out_specs=tuple(whole(2)),
         scratch_shapes=[
@@ -346,33 +385,22 @@
         cost_estimate=pl.CostEstimate(flops=4 * work, bytes_accessed=8 << 20, transcendentals=0),
         name="long_convolution",
     )(coords, taps, gains, twists, early, right, left, last_right, last_left, in_weights, filter_spectrum, grads, *tables)
-    all_grads = lax.all_gather(own_grad, "grp", axis=0, tiled=False)
-
-    arrived = lax.all_to_all(gated.reshape(Z, Y, CHANS, BLOCK), "seq", split_axis=0, concat_axis=0, tiled=True, axis_index_groups=z_groups)
+    arrived = lax.all_to_all(gated, "seq", split_axis=0, concat_axis=0, tiled=True, axis_index_groups=y_groups)
+    shares = lax.all_to_all(own_grad.reshape(groups, CHANS // groups, LENGTH), "grp", split_axis=0, concat_axis=0, tiled=True)
+    share = jnp.sum(shares.astype(f32), 0).astype(bf16)
+    filter_grad = lax.all_gather(share, "grp", axis=0, tiled=True).astype(f32)
+    marks = jnp.stack([piece[0, BLOCK:, :] for piece in chunks + [last_right]])
     partial = pl.pallas_call(
         read_out_kernel,
-        out_shape=jax.ShapeDtypeStruct((Y, BLOCK, in_chans), bf16),
-        in_specs=[scalar] + whole(2) + [pl.BlockSpec(memory_space=pltpu.HBM)],
+        out_shape=jax.ShapeDtypeStruct((Z, BLOCK, in_chans), bf16),
+        in_specs=[scalar] + whole(3),
         out_specs=whole(1)[0],
-        scratch_shapes=[pltpu.VMEM(out_weights.shape, bf16), pltpu.SemaphoreType.DMA((out_weights.shape[0],))],
-        compiler_params=pltpu.CompilerParams(vmem_limit_bytes=60 << 20),
+        compiler_params=params,
         cost_estimate=pl.CostEstimate(flops=2 * 512 * 512 * 4096, bytes_accessed=6 << 20, transcendentals=0),
         name="read_out",
-    )(coords, arrived, chunk[:, BLOCK:, :], out_weights)
-    pieces = lax.all_to_all(partial, "seq", split_axis=0, concat_axis=0, tiled=True, axis_index_groups=y_groups)
+    )(coords, arrived, marks, out_weights)
+    pieces = lax.all_to_all(partial, "seq", split_axis=0, concat_axis=0, tiled=True, axis_index_groups=z_groups)
     denoised = jnp.sum(pieces.astype(f32), 0).astype(bf16)
-
-    step = 2 * LANE8
-    filter_grad = pl.pallas_call(
-        sum_kernel,
-        out_shape=jax.ShapeDtypeStruct((CHANS, LENGTH), f32),
-        grid=(CHANS // step,),
-        in_specs=[pl.BlockSpec((all_grads.shape[0], step, LENGTH), lambda i: (0, i, 0))],
-        out_specs=pl.BlockSpec((step, LENGTH), lambda i: (i, 0)),
-        compiler_params=params,
-        cost_estimate=pl.CostEstimate(flops=all_grads.size, bytes_accessed=5 << 20, transcendentals=0),
-        name="sum_gradients",
-    )(all_grads)
     return denoised[None], filter_grad
 
 

time: 146 us -> 161 us (1.10); the launches traced: 145 us -> 159 us
  starting transfers between devices: 31.8 us -> 50 us
  Pallas kernels: 44.9 us -> 31.2 us
  waiting for transfers between devices: 31 us -> 44.5 us
  between operations: 14 us -> 0.9 us
  local copies, waits for them, and re-layouts: 9.49 us -> 16.3 us
  blocking collectives: 10.3 us -> 13.1 us
    all_to_all x1 -> x5, starting transfers between devices: 3.5 us -> 22.6 us  [the longest x2 8.64 us: gather_weights(): lax.all_to_all(copies, 'grp', split_axis=0, concat_axis=0, tiled=True)]
    pallas_call x4 -> x3, Pallas kernels: 37.1 us -> 23.2 us  [the longest x1 12.9 us: local(): pl.pallas_call(main_kernel, out_shape=(jax.ShapeDtypeStruct((Y, Z, CHANS,...]
    all_gather x0 -> x1, blocking collectives: none -> 13.1 us  [local(): filter_grad = lax.all_gather(share, 'grp', axis=0, tiled=True).astype(f32)]
    all_to_all x1, waiting for transfers between devices: 1.34 us -> 14.1 us  [local(): lax.all_to_all(turned, 'seq', split_axis=0, concat_axis=0, tiled=True)]
    all_to_all x1 -> x0, blocking collectives: 10.3 us -> none  [local(): lax.all_to_all(partial, 'seq', split_axis=0, concat_axis=0, tiled=True, a...]
    unnamed x22 -> x37, local copies, waits for them, and re-layouts: 0.84 us -> 5.48 us
    broadcast_in_dim x0 -> x2, local copies, waits for them, and re-layouts: none -> 2.7 us  [gather_weights(): copies = jnp.broadcast_to(own[None], (groups,) + own.shape)]
    ppermute x8, waiting for transfers between devices: 12.4 us -> 14.4 us  [along_z(): lax.ppermute(value, 'seq', [(z * Y + y, (z + step) % Z * Y + y) for z in...]
  transfers between devices with their start and end apart: 16 -> 17, of which waited for: 9 -> 11; matrix products, arithmetic and copies ran while one was open for 7% -> 8% of each run, Pallas kernels for 28% -> 20%
where the time goes in v2:
time: 161 us; the launch traced here: 159 us
  starting transfers between devices  50 us (31%)
  waiting for transfers between devices  44.5 us (28%)
  Pallas kernels  31.2 us (19%)
  local copies, waits for them, and re-layouts  16.3 us (10%)
  blocking collectives  13.1 us (8%)
  other arithmetic  2.82 us (2%)
    ppermute x8, starting transfers between devices, along_z(): lax.ppermute(value, 'seq', [(z * Y + y, (z + step) % Z * Y + y) for z in...  16.1 us
    ppermute x8, waiting for transfers between devices, along_z(): lax.ppermute(value, 'seq', [(z * Y + y, (z + step) % Z * Y + y) for z in...  14.4 us
    all_to_all x1, waiting for transfers between devices, local(): lax.all_to_all(turned, 'seq', split_axis=0, concat_axis=0, tiled=True)  14.1 us
    all_gather x1, blocking collectives, local(): filter_grad = lax.all_gather(share, 'grp', axis=0, tiled=True).astype(f32)  13.1 us
    pallas_call x1, Pallas kernels, local(): pl.pallas_call(main_kernel, out_shape=(jax.ShapeDtypeStruct((Y, Z, CHANS,...  12.9 us
    all_to_all x2, starting transfers between devices, gather_weights(): lax.all_to_all(copies, 'grp', split_axis=0, concat_axis=0, tiled=True)  8.64 us
    pallas_call x1, Pallas kernels, read_in(): pl.pallas_call(read_in_kernel, out_shape=jax.ShapeDtypeStruct((blocks, wi...  7.95 us
    all_to_all x1, starting transfers between devices, local(): lax.all_to_all(turned, 'seq', split_axis=0, concat_axis=0, tiled=True)  6.87 us
  transfers between devices with their start and end apart: 17, of which 11 were waited for; matrix products, arithmetic and copies ran while one was open for 8% of the time, Pallas kernels for 20%

profile of v2, /device:TPU:8, one launch (start us, length us, event | category | flops | bytes accessed | tf_op | source)
XLA Modules:
  0.0 158.8 jit_solution(15337537027183191147)
XLA Ops:
  0.7 1.3 constant_dynamic-slice_fusion.2
  2.1 1.2 broadcast_in_dim.29
  3.2 4.3 %all-to-all-start = ((bf16[8,2,256,128]{3,2,1,0:T(8,128)(2,1)}), bf16[8,2,256,128]{3,2,1,0:T(8,128)(2,1)S(1)}, u32[]{:S(2)}, u32[]{:S(2)}) async-start(bf16[8,2,256,128]{3,2,1,0:T(8,128)(2,1)} %broadcast_in_dim.29), calls=%async_computation | async-start | bytes 2097152 | tf_op jit(solution)/shard_map/all_to_all | solution.py:299
  7.9 1.7 %collective-permute-start = (bf16[136,256]{1,0:T(8,128)(2,1)S(1)}, bf16[136,256]{1,0:T(8,128)(2,1)S(1)}, u32[]{:S(2)}, u32[]{:S(2)}) collective-permute-start(bf16[136,256]{1,0:T(8,128)(2,1)S(1)} %get-tuple-element.23), channel_id=1, source_target_pairs={{0,1},{1,2},{2,3},{3,0},{4,5},{5,6},{6,7},{7,4},{8,9},{9,10},{10,1... | collective-permute-start | bytes 208904 | tf_op jit(solution)/shard_map/ppermute | solution.py:289
  10.1 2.3 %collective-permute-start.2 = (bf16[136,256]{1,0:T(8,128)(2,1)S(1)}, bf16[136,256]{1,0:T(8,128)(2,1)S(1)}, u32[]{:S(2)}, u32[]{:S(2)}) collective-permute-start(bf16[136,256]{1,0:T(8,128)(2,1)S(1)} %get-tuple-element.23), channel_id=1, source_target_pairs={{0,2},{1,3},{2,0},{3,1},{4,6},{5,7},{6,4},{7,5},{8,10},{9,11},{10,... | collective-permute-start | bytes 208904 | tf_op jit(solution)/shard_map/ppermute | solution.py:289
  12.6 1.3 collective-permute-done.1
  13.9 2.2 %collective-permute-done.2 = bf16[136,256]{1,0:T(8,128)(2,1)S(1)} collective-permute-done((bf16[136,256]{1,0:T(8,128)(2,1)S(1)}, bf16[136,256]{1,0:T(8,128)(2,1)S(1)}, u32[]{:S(2)}, u32[]{:S(2)}) %collective-permute-start.2) | collective-permute-done | bytes 69664 | tf_op jit(solution)/shard_map/ppermute | solution.py:289
  16.2 2.0 %collective-permute-start.3 = (bf16[4,136,256]{2,1,0:T(8,128)(2,1)S(1)}, bf16[4,136,256]{2,1,0:T(8,128)(2,1)S(1)}, u32[]{:S(2)}, u32[]{:S(2)}) collective-permute-start(bf16[4,136,256]{2,1,0:T(8,128)(2,1)S(1)} %pad_maximum_fusion.rest_0_), channel_id=1, source_target_pairs={{0,4},{1,5},{2,6},{3,7},{4,8},{5,9},{6,10},{7,11},{8,12},{9,13},{1... | collective-permute-start | bytes 835592 | tf_op jit(solution)/shard_map/ppermute | solution.py:293
  18.2 4.0 %collective-permute-start.5 = (bf16[4,136,256]{2,1,0:T(8,128)(2,1)S(1)}, bf16[4,136,256]{2,1,0:T(8,128)(2,1)S(1)}, u32[]{:S(2)}, u32[]{:S(2)}) collective-permute-start(bf16[4,136,256]{2,1,0:T(8,128)(2,1)S(1)} %pad_maximum_fusion.rest_0_), channel_id=1, source_target_pairs={{0,28},{1,29},{2,30},{3,31},{4,0},{5,1},{6,2},{7,3},{8,4},{9,5},{1... | collective-permute-start | bytes 835592 | tf_op jit(solution)/shard_map/ppermute | solution.py:293
  22.2 6.3 %collective-permute-done.3.rest_1_ = bf16[4,136,256]{2,1,0:T(8,128)(2,1)S(1)} collective-permute-done((bf16[4,136,256]{2,1,0:T(8,128)(2,1)S(1)}, bf16[4,136,256]{2,1,0:T(8,128)(2,1)S(1)}, u32[]{:S(2)}, u32[]{:S(2)}) %collective-permute-start.3) | collective-permute-done | bytes 278560 | tf_op jit(solution)/shard_map/ppermute | solution.py:293
  28.5 3.2 %collective-permute-start.6 = (bf16[4,136,256]{2,1,0:T(8,128)(2,1)S(1)}, bf16[4,136,256]{2,1,0:T(8,128)(2,1)}, u32[]{:S(2)}, u32[]{:S(2)}) collective-permute-start(bf16[4,136,256]{2,1,0:T(8,128)(2,1)S(1)} %collective-permute-done.5.rest_2_), channel_id=1, source_target_pairs={{0,28},{1,29},{2,30},{3,31},{4,0},{5,1},{6,2},{7,3},{8,4},{9,5},{1... | collective-permute-start | bytes 835592 | tf_op jit(solution)/shard_map/ppermute | solution.py:293
  31.7 5.5 %collective-permute-done.4.rest_3_ = bf16[4,136,256]{2,1,0:T(8,128)(2,1)S(1)} collective-permute-done((bf16[4,136,256]{2,1,0:T(8,128)(2,1)S(1)}, bf16[4,136,256]{2,1,0:T(8,128)(2,1)S(1)}, u32[]{:S(2)}, u32[]{:S(2)}) %collective-permute-start.4) | collective-permute-done | bytes 278560 | tf_op jit(solution)/shard_map/ppermute | solution.py:293
  38.1 3.2 %collective-permute-start.8 = (bf16[4,136,256]{2,1,0:T(8,128)(2,1)}, bf16[4,136,256]{2,1,0:T(8,128)(2,1)}, u32[]{:S(2)}, u32[]{:S(2)}) collective-permute-start(bf16[4,136,256]{2,1,0:T(8,128)(2,1)} %collective-permute-done.6.rest_4_), channel_id=1, source_target_pairs={{0,28},{1,29},{2,30},{3,31},{4,0},{5,1},{6,2},{7,3},{8,4},{9,5},{1... | collective-permute-start | bytes 835592 | tf_op jit(solution)/shard_map/ppermute | solution.py:293
  41.3 2.1 %copy.17 = bf16[2048,128]{1,0:T(8,128)(2,1)} copy(bf16[2048,128]{0,1:T(8,128)(2,1)} %bitcast.19) | data formatting | bytes 1048576 | tf_op jit(solution)/shard_map/transpose | solution.py:333
  43.4 7.9 %read_in.1.early_hbm = bf16[20,128,128]{2,1,0:T(8,128)(2,1)} custom-call(bf16[16,256,128]{2,1,0:T(8,128)(2,1)} %bitcast.17, bf16[4,136,256]{2,1,0:T(8,128)(2,1)} %copy-done.4, bf16[4,136,256]{2,1,0:T(8,128)(2,1)} %copy-done.10, bf16[4,136,256]{2,1,0:T(8,128)(2,1)} %copy-done.11, bf16[4,136,256]{2,1,0:T(8,128)(2,1)} %copy-done.9, ...), custom_call_target="tpu_custom_call" | custom-call | flops 2684354560 | bytes 4194304 | tf_op jit(solution)/shard_map/read_in/pallas_call | solution.py:166
  51.4 6.9 %all-to-all-start.1 = ((bf16[32,64,128]{2,1,0:T(8,128)(2,1)}), bf16[32,64,128]{2,1,0:T(8,128)(2,1)S(1)}, u32[]{:S(2)}, u32[]{:S(2)}) async-start(bf16[32,64,128]{2,1,0:T(8,128)(2,1)} %bitcast.11), calls=%async_computation.1 | async-start | bytes 1048576 | tf_op jit(solution)/shard_map/all_to_all | solution.py:342
  58.3 14.1 %all-to-all-done.1.grad_hbm = bf16[32,64,128]{2,1,0:T(8,128)(2,1)S(1)} async-done(((bf16[32,64,128]{2,1,0:T(8,128)(2,1)}), bf16[32,64,128]{2,1,0:T(8,128)(2,1)S(1)}, u32[]{:S(2)}, u32[]{:S(2)}) %all-to-all-start.1) | async-done | bytes 524320 | tf_op jit(solution)/shard_map/all_to_all | solution.py:342
  72.4 1.5 broadcast_in_dim.30
  74.0 4.3 %all-to-all-start.3 = ((bf16[8,2,256,256]{3,2,1,0:T(8,128)(2,1)}), bf16[8,2,256,256]{3,2,1,0:T(8,128)(2,1)}, u32[]{:S(2)}, u32[]{:S(2)}) async-start(bf16[8,2,256,256]{3,2,1,0:T(8,128)(2,1)} %broadcast_in_dim.30), calls=%async_computation.3 | async-start | bytes 4194304 | tf_op jit(solution)/shard_map/all_to_all | solution.py:299
  78.3 4.6 %filter_transform.1.filter_hbm = f32[8,256,256]{2,1,0:T(8,128)} custom-call(f32[64,4096]{1,0:T(8,128)} %filter_ref.1, bf16[512,256]{1,0:T(8,128)(2,1)} %constant.57.clone.first_ref.rest_0_, bf16[256,256]{1,0:T(8,128)(2,1)} %constant.58.clone.second_ref.rest_1_, f32[2,32,128]{2,1,0:T(8,128)} %constant.61.clone.twist_ref), custom_call_target="tpu_custom_call" | custom-call | flops 536870912 | bytes 4194304 | tf_op jit(solution)/shard_map/filter_transform/pallas_call | solution.py:350
  88.4 2.7 %collective-permute-start.10 = (bf16[2,136,256]{2,1,0:T(8,128)(2,1)S(1)}, bf16[2,136,256]{2,1,0:T(8,128)(2,1)S(1)}, u32[]{:S(2)}, u32[]{:S(2)}) collective-permute-start(bf16[2,136,256]{2,1,0:T(8,128)(2,1)S(1)} %slice.35), channel_id=1, source_target_pairs={{0,28},{1,29},{2,30},{3,31},{4,0},{5,1},{6,2},{7,3},{8,4},{9,5},{1... | collective-permute-start | bytes 417800 | tf_op jit(solution)/shard_map/ppermute | solution.py:293
  91.8 2.0 %collective-permute-done.9.last_right_hbm = bf16[2,136,256]{2,1,0:T(8,128)(2,1)S(1)} collective-permute-done((bf16[2,136,256]{2,1,0:T(8,128)(2,1)S(1)}, bf16[2,136,256]{2,1,0:T(8,128)(2,1)S(1)}, u32[]{:S(2)}, u32[]{:S(2)}) %collective-permute-start.9) | collective-permute-done | bytes 139296 | tf_op jit(solution)/shard_map/ppermute | solution.py:293
  95.7 12.9 %long_convolution.1 = (bf16[4,8,64,128]{3,2,1,0:T(8,128)(2,1)}, bf16[64,4096]{1,0:T(8,128)(2,1)}) custom-call(s32[2]{0:T(128)} %pad_add_fusion.place_ref, f32[3,64,128]{2,1,0:T(8,128)} %broadcast_in_dim.24.taps_ref, f32[64,128]{1,0:T(8,128)} %broadcast_in_dim.25.gain_ref, f32[2,32,128]{2,1,0:T(8,128)} %constant.61.clone.twist_ref, ...), custom_call_target="tpu_custom_call" | custom-call | flops 2147483648 | bytes 8388608 | tf_op jit(solution)/shard_map/long_convolution/pallas_call | solution.py:367
  108.7 5.1 %all-to-all-start.2 = ((bf16[4,8,64,128]{3,2,1,0:T(8,128)(2,1)}), bf16[4,8,64,128]{3,2,1,0:T(8,128)(2,1)S(1)}, u32[]{:S(2)}, u32[]{:S(2)}) async-start(bf16[4,8,64,128]{3,2,1,0:T(8,128)(2,1)} %get-tuple-element.18), calls=%async_computation.2 | async-start | bytes 1048576 | tf_op jit(solution)/shard_map/all_to_all | solution.py:388
  115.1 6.5 %all-to-all-done.2.rows_ref = bf16[4,8,64,128]{3,2,1,0:T(8,128)(2,1)S(1)} async-done(((bf16[4,8,64,128]{3,2,1,0:T(8,128)(2,1)}), bf16[4,8,64,128]{3,2,1,0:T(8,128)(2,1)S(1)}, u32[]{:S(2)}, u32[]{:S(2)}) %all-to-all-start.2) | async-done | bytes 524320 | tf_op jit(solution)/shard_map/all_to_all | solution.py:388
  121.6 4.2 %all-to-all-start.5 = ((bf16[8,8,4096]{2,1,0:T(8,128)(2,1)}), bf16[8,8,4096]{2,1,0:T(8,128)(2,1)S(1)}, u32[]{:S(2)}, u32[]{:S(2)}) async-start(bf16[8,8,4096]{2,1,0:T(8,128)(2,1)} %bitcast.20), calls=%async_computation.5 | async-start | bytes 1048576 | tf_op jit(solution)/shard_map/all_to_all | solution.py:389
  127.8 5.7 %read_out.1 = bf16[8,128,256]{2,1,0:T(8,128)(2,1)} custom-call(s32[2]{0:T(128)} %pad_add_fusion.place_ref, bf16[4,8,64,128]{3,2,1,0:T(8,128)(2,1)} %copy-done.3, bf16[8,8,256]{2,1,0:T(8,128)(2,1)} %copy-done.7, bf16[16,256,256]{2,1,0:T(8,128)(2,1)} %bitcast.12.weight_ref), custom_call_target="tpu_custom_call" | custom-call | flops 2147483648 | bytes 6291456 | tf_op jit(solution)/shard_map/read_out/pallas_call | solution.py:393
  133.5 2.7 %all-to-all-done.5 = bf16[8,8,4096]{2,1,0:T(8,128)(2,1)S(1)} async-done(((bf16[8,8,4096]{2,1,0:T(8,128)(2,1)}), bf16[8,8,4096]{2,1,0:T(8,128)(2,1)S(1)}, u32[]{:S(2)}, u32[]{:S(2)}) %all-to-all-start.5) | async-done | bytes 524320 | tf_op jit(solution)/shard_map/all_to_all | solution.py:389
  136.2 4.6 %all-to-all-start.4 = ((bf16[8,128,256]{2,1,0:T(8,128)(2,1)}), bf16[8,128,256]{2,1,0:T(8,128)(2,1)S(1)}, u32[]{:S(2)}, u32[]{:S(2)}) async-start(bf16[8,128,256]{2,1,0:T(8,128)(2,1)} %read_out.1), calls=%async_computation.4 | async-start | bytes 1048576 | tf_op jit(solution)/shard_map/all_to_all | solution.py:402
  140.8 13.1 %all_gather.3 = bf16[64,4096]{1,0:T(8,128)(2,1)S(1)} all-gather(bf16[8,4096]{1,0:T(8,128)(2,1)S(1)} %reduce_sum.35), channel_id=1, replica_groups=mesh['grp'=8,'seq'=32] {'grp'}, dimensions={0}, use_global_device_ids=true | all-gather | bytes 589824 | tf_op jit(solution)/shard_map/all_gather | solution.py:391
  154.0 1.0 convert_element_type.15
  155.0 3.1 %all-to-all-done.4 = bf16[8,128,256]{2,1,0:T(8,128)(2,1)S(1)} async-done(((bf16[8,128,256]{2,1,0:T(8,128)(2,1)}), bf16[8,128,256]{2,1,0:T(8,128)(2,1)S(1)}, u32[]{:S(2)}, u32[]{:S(2)}) %all-to-all-start.4) | async-done | bytes 524320 | tf_op jit(solution)/shard_map/all_to_all | solution.py:402
  (66 shorter events, 14.3 us)
Async XLA Ops:
  0.6 57.6 %copy-start = (bf16[2,2048,256]{2,1,0:T(8,128)(2,1)S(1)}, bf16[2,2048,256]{2,1,0:T(8,128)(2,1)}, u32[]{:S(2)}) copy-start(bf16[2,2048,256]{2,1,0:T(8,128)(2,1)} %param.21) | copy-start | bytes 6291460
  0.7 6.9 %copy-start.13 = (s32[1,128]{1,0:T(1,128)S(1)}, s32[1,128]{1,0:T(1,128)}, u32[]{:S(2)}) copy-start(s32[1,128]{1,0:T(1,128)} %param.15) | copy-start | bytes 1540
  0.7 7.0 %copy-start.14 = (s32[16]{0:T(128)S(1)}, s32[16]{0:T(128)}, u32[]{:S(2)}) copy-start(s32[16]{0:T(128)} %param.16) | copy-start | bytes 196
  0.7 7.2 %copy-start.5 = (bf16[1,128,256]{2,1,0:T(8,128)(2,1)S(1)}, bf16[1,128,256]{2,1,0:T(8,128)(2,1)}, u32[]{:S(2)}) copy-start(bf16[1,128,256]{2,1,0:T(8,128)(2,1)} %param.14) | copy-start | bytes 196612
  3.2 34.8 %all-to-all-start = ((bf16[8,2,256,128]{3,2,1,0:T(8,128)(2,1)}), bf16[8,2,256,128]{3,2,1,0:T(8,128)(2,1)S(1)}, u32[]{:S(2)}, u32[]{:S(2)}) async-start(bf16[8,2,256,128]{3,2,1,0:T(8,128)(2,1)} %broadcast_in_dim.29), calls=%async_computation | async-start | bytes 2097152 | tf_op jit(solution)/shard_map/all_to_all | solution.py:299
  7.9 4.7 %collective-permute-start = (bf16[136,256]{1,0:T(8,128)(2,1)S(1)}, bf16[136,256]{1,0:T(8,128)(2,1)S(1)}, u32[]{:S(2)}, u32[]{:S(2)}) collective-permute-start(bf16[136,256]{1,0:T(8,128)(2,1)S(1)} %get-tuple-element.23), channel_id=1, source_target_pairs={{0,1},{1,2},{2,3},{3,0},{4,5},{5,6},{6,7},{7,4},{8,9},{9,10},{10,1... | collective-permute-start | bytes 208904 | tf_op jit(solution)/shard_map/ppermute | solution.py:289
  9.6 4.3 %collective-permute-start.1 = (bf16[136,256]{1,0:T(8,128)(2,1)S(1)}, bf16[136,256]{1,0:T(8,128)(2,1)S(1)}, u32[]{:S(2)}, u32[]{:S(2)}) collective-permute-start(bf16[136,256]{1,0:T(8,128)(2,1)S(1)} %get-tuple-element.23), channel_id=1, source_target_pairs={{0,3},{1,0},{2,1},{3,2},{4,7},{5,4},{6,5},{7,6},{8,11},{9,8},{10,9... | collective-permute-start | bytes 208904 | tf_op jit(solution)/shard_map/ppermute | solution.py:289
  10.1 6.1 %collective-permute-start.2 = (bf16[136,256]{1,0:T(8,128)(2,1)S(1)}, bf16[136,256]{1,0:T(8,128)(2,1)S(1)}, u32[]{:S(2)}, u32[]{:S(2)}) collective-permute-start(bf16[136,256]{1,0:T(8,128)(2,1)S(1)} %get-tuple-element.23), channel_id=1, source_target_pairs={{0,2},{1,3},{2,0},{3,1},{4,6},{5,7},{6,4},{7,5},{8,10},{9,11},{10,... | collective-permute-start | bytes 208904 | tf_op jit(solution)/shard_map/ppermute | solution.py:289
  16.2 27.2 %copy-start.4 = (bf16[4,136,256]{2,1,0:T(8,128)(2,1)}, bf16[4,136,256]{2,1,0:T(8,128)(2,1)S(1)}, u32[]{:S(2)}) copy-start(bf16[4,136,256]{2,1,0:T(8,128)(2,1)S(1)} %pad_maximum_fusion.rest_0_) | copy-start | bytes 835588
  16.2 12.3 %collective-permute-start.3 = (bf16[4,136,256]{2,1,0:T(8,128)(2,1)S(1)}, bf16[4,136,256]{2,1,0:T(8,128)(2,1)S(1)}, u32[]{:S(2)}, u32[]{:S(2)}) collective-permute-start(bf16[4,136,256]{2,1,0:T(8,128)(2,1)S(1)} %pad_maximum_fusion.rest_0_), channel_id=1, source_target_pairs={{0,4},{1,5},{2,6},{3,7},{4,8},{5,9},{6,10},{7,11},{8,12},{9,13},{1... | collective-permute-start | bytes 835592 | tf_op jit(solution)/shard_map/ppermute | solution.py:293
  18.2 10.3 %collective-permute-start.5 = (bf16[4,136,256]{2,1,0:T(8,128)(2,1)S(1)}, bf16[4,136,256]{2,1,0:T(8,128)(2,1)S(1)}, u32[]{:S(2)}, u32[]{:S(2)}) collective-permute-start(bf16[4,136,256]{2,1,0:T(8,128)(2,1)S(1)} %pad_maximum_fusion.rest_0_), channel_id=1, source_target_pairs={{0,28},{1,29},{2,30},{3,31},{4,0},{5,1},{6,2},{7,3},{8,4},{9,5},{1... | collective-permute-start | bytes 835592 | tf_op jit(solution)/shard_map/ppermute | solution.py:293
  28.5 8.8 %copy-start.10 = (bf16[4,136,256]{2,1,0:T(8,128)(2,1)}, bf16[4,136,256]{2,1,0:T(8,128)(2,1)S(1)}, u32[]{:S(2)}) copy-start(bf16[4,136,256]{2,1,0:T(8,128)(2,1)S(1)} %collective-permute-done.3.rest_1_) | copy-start | bytes 835588
  28.5 8.8 %collective-permute-start.4 = (bf16[4,136,256]{2,1,0:T(8,128)(2,1)S(1)}, bf16[4,136,256]{2,1,0:T(8,128)(2,1)S(1)}, u32[]{:S(2)}, u32[]{:S(2)}) collective-permute-start(bf16[4,136,256]{2,1,0:T(8,128)(2,1)S(1)} %collective-permute-done.3.rest_1_), channel_id=1, source_target_pairs={{0,4},{1,5},{2,6},{3,7},{4,8},{5,9},{6,10},{7,11},{8,12},{9,13},{1... | collective-permute-start | bytes 835592 | tf_op jit(solution)/shard_map/ppermute | solution.py:293
  28.5 8.7 %copy-start.11 = (bf16[4,136,256]{2,1,0:T(8,128)(2,1)}, bf16[4,136,256]{2,1,0:T(8,128)(2,1)S(1)}, u32[]{:S(2)}) copy-start(bf16[4,136,256]{2,1,0:T(8,128)(2,1)S(1)} %collective-permute-done.5.rest_2_) | copy-start | bytes 835588
  28.5 9.5 %collective-permute-start.6 = (bf16[4,136,256]{2,1,0:T(8,128)(2,1)S(1)}, bf16[4,136,256]{2,1,0:T(8,128)(2,1)}, u32[]{:S(2)}, u32[]{:S(2)}) collective-permute-start(bf16[4,136,256]{2,1,0:T(8,128)(2,1)S(1)} %collective-permute-done.5.rest_2_), channel_id=1, source_target_pairs={{0,28},{1,29},{2,30},{3,31},{4,0},{5,1},{6,2},{7,3},{8,4},{9,5},{1... | collective-permute-start | bytes 835592 | tf_op jit(solution)/shard_map/ppermute | solution.py:293
  37.3 0.8 copy-start.9
  38.0 5.4 %copy-start.1 = (bf16[8,2,256,128]{3,2,1,0:T(8,128)(2,1)}, bf16[8,2,256,128]{3,2,1,0:T(8,128)(2,1)S(1)}, u32[]{:S(2)}) copy-start(bf16[8,2,256,128]{3,2,1,0:T(8,128)(2,1)S(1)} %all-to-all-done) | copy-start | bytes 3145732
  38.0 13.3 %collective-permute-start.7 = (bf16[4,136,256]{2,1,0:T(8,128)(2,1)}, bf16[4,136,256]{2,1,0:T(8,128)(2,1)}, u32[]{:S(2)}, u32[]{:S(2)}) collective-permute-start(bf16[4,136,256]{2,1,0:T(8,128)(2,1)} %copy-done.9), channel_id=1, source_target_pairs={{0,4},{1,5},{2,6},{3,7},{4,8},{5,9},{6,10},{7,11},{8,12},{9,13},{1... | collective-permute-start | bytes 835592 | tf_op jit(solution)/shard_map/ppermute | solution.py:293
  38.1 13.3 %collective-permute-start.8 = (bf16[4,136,256]{2,1,0:T(8,128)(2,1)}, bf16[4,136,256]{2,1,0:T(8,128)(2,1)}, u32[]{:S(2)}, u32[]{:S(2)}) collective-permute-start(bf16[4,136,256]{2,1,0:T(8,128)(2,1)} %collective-permute-done.6.rest_4_), channel_id=1, source_target_pairs={{0,28},{1,29},{2,30},{3,31},{4,0},{5,1},{6,2},{7,3},{8,4},{9,5},{1... | collective-permute-start | bytes 835592 | tf_op jit(solution)/shard_map/ppermute | solution.py:293
  51.4 21.1 %all-to-all-start.1 = ((bf16[32,64,128]{2,1,0:T(8,128)(2,1)}), bf16[32,64,128]{2,1,0:T(8,128)(2,1)S(1)}, u32[]{:S(2)}, u32[]{:S(2)}) async-start(bf16[32,64,128]{2,1,0:T(8,128)(2,1)} %bitcast.11), calls=%async_computation.1 | async-start | bytes 1048576 | tf_op jit(solution)/shard_map/all_to_all | solution.py:342
  72.4 1.5 copy-start.2
  74.0 34.7 %all-to-all-start.3 = ((bf16[8,2,256,256]{3,2,1,0:T(8,128)(2,1)}), bf16[8,2,256,256]{3,2,1,0:T(8,128)(2,1)}, u32[]{:S(2)}, u32[]{:S(2)}) async-start(bf16[8,2,256,256]{3,2,1,0:T(8,128)(2,1)} %broadcast_in_dim.30), calls=%async_computation.3 | async-start | bytes 4194304 | tf_op jit(solution)/shard_map/all_to_all | solution.py:299
  78.3 16.7 %copy-start.6 = (f32[64]{0:T(128)S(1)}, f32[64]{0:T(128)}, u32[]{:S(2)}) copy-start(f32[64]{0:T(128)} %param.20) | copy-start | bytes 772
  86.6 7.2 %collective-permute-start.9 = (bf16[2,136,256]{2,1,0:T(8,128)(2,1)S(1)}, bf16[2,136,256]{2,1,0:T(8,128)(2,1)S(1)}, u32[]{:S(2)}, u32[]{:S(2)}) collective-permute-start(bf16[2,136,256]{2,1,0:T(8,128)(2,1)S(1)} %slice.34), channel_id=1, source_target_pairs={{0,4},{1,5},{2,6},{3,7},{4,8},{5,9},{6,10},{7,11},{8,12},{9,13},{1... | collective-permute-start | bytes 417800 | tf_op jit(solution)/shard_map/ppermute | solution.py:293
  88.4 5.9 %collective-permute-start.10 = (bf16[2,136,256]{2,1,0:T(8,128)(2,1)S(1)}, bf16[2,136,256]{2,1,0:T(8,128)(2,1)S(1)}, u32[]{:S(2)}, u32[]{:S(2)}) collective-permute-start(bf16[2,136,256]{2,1,0:T(8,128)(2,1)S(1)} %slice.35), channel_id=1, source_target_pairs={{0,28},{1,29},{2,30},{3,31},{4,0},{5,1},{6,2},{7,3},{8,4},{9,5},{1... | collective-permute-start | bytes 417800 | tf_op jit(solution)/shard_map/ppermute | solution.py:293
  93.8 1.9 %copy-start.8 = (bf16[2,136,256]{2,1,0:T(8,128)(2,1)}, bf16[2,136,256]{2,1,0:T(8,128)(2,1)S(1)}, u32[]{:S(2)}) copy-start(bf16[2,136,256]{2,1,0:T(8,128)(2,1)S(1)} %collective-permute-done.9.last_right_hbm) | copy-start | bytes 417796
  94.3 1.4 copy-start.12
  108.7 12.9 %all-to-all-start.2 = ((bf16[4,8,64,128]{3,2,1,0:T(8,128)(2,1)}), bf16[4,8,64,128]{3,2,1,0:T(8,128)(2,1)S(1)}, u32[]{:S(2)}, u32[]{:S(2)}) async-start(bf16[4,8,64,128]{3,2,1,0:T(8,128)(2,1)} %get-tuple-element.18), calls=%async_computation.2 | async-start | bytes 1048576 | tf_op jit(solution)/shard_map/all_to_all | solution.py:388
  121.6 5.6 %copy-start.3 = (bf16[4,8,64,128]{3,2,1,0:T(8,128)(2,1)}, bf16[4,8,64,128]{3,2,1,0:T(8,128)(2,1)S(1)}, u32[]{:S(2)}) copy-start(bf16[4,8,64,128]{3,2,1,0:T(8,128)(2,1)S(1)} %all-to-all-done.2.rows_ref) | copy-start | bytes 1572868
  121.6 14.6 %all-to-all-start.5 = ((bf16[8,8,4096]{2,1,0:T(8,128)(2,1)}), bf16[8,8,4096]{2,1,0:T(8,128)(2,1)S(1)}, u32[]{:S(2)}, u32[]{:S(2)}) async-start(bf16[8,8,4096]{2,1,0:T(8,128)(2,1)} %bitcast.20), calls=%async_computation.5 | async-start | bytes 1048576 | tf_op jit(solution)/shard_map/all_to_all | solution.py:389
  127.2 0.6 copy-start.7
  136.2 21.9 %all-to-all-start.4 = ((bf16[8,128,256]{2,1,0:T(8,128)(2,1)}), bf16[8,128,256]{2,1,0:T(8,128)(2,1)S(1)}, u32[]{:S(2)}, u32[]{:S(2)}) async-start(bf16[8,128,256]{2,1,0:T(8,128)(2,1)} %read_out.1), calls=%async_computation.4 | async-start | bytes 1048576 | tf_op jit(solution)/shard_map/all_to_all | solution.py:402

commit v3 on v2

v3 whole, which is shorter than its diff:
```python
import jax
import jax.numpy as jnp
import numpy as np
from jax import lax
from jax.experimental import pallas as pl
from jax.experimental.pallas import tpu as pltpu
from jax.sharding import PartitionSpec as P

BLOCK = 128
TRIAL = 16
Z = 8
Y = 4
BLOCKS = Z * Y
CHANS = 64
LANE8 = 8
GROUPS = CHANS // LANE8
LENGTH = BLOCKS * BLOCK
X = 4
CORES = 2
X_STEPS = (0, -1, 1, 2)
f32 = jnp.float32
bf16 = jnp.bfloat16


def transform_tables():
    slow = np.arange(BLOCKS)
    fast = np.arange(BLOCK)
    first = np.exp(-2j * np.pi * (np.outer(slow, slow) / BLOCKS + slow[None, :] / (4.0 * BLOCKS)))
    twist = np.exp(-2j * np.pi * (slow[:, None] + 0.25) * fast[None, :] / LENGTH)
    second = np.exp(-2j * np.pi * np.outer(fast, fast) / BLOCK)
    eye = np.eye(LANE8)
    spread_first = np.concatenate([np.kron(first.real, eye), np.kron(first.imag, eye)], 0)
    forward_second = np.block([[second.real, second.imag], [-second.imag, second.real]])
    back = second.conj()
    back_second = np.block([[back.real, back.imag], [-back.imag, back.real]])
    back_first = first.conj().T / LENGTH
    spread_back = np.concatenate([np.kron(back_first.real, eye), np.kron(-back_first.imag, eye)], 1)
    as_bf16 = lambda table: jnp.asarray(table.astype(np.float32), bf16)
    twists = np.stack([twist.real, twist.imag]).astype(np.float32)
    return (
        as_bf16(spread_first),
        as_bf16(forward_second),
        as_bf16(back_second),
        as_bf16(spread_back),
        jnp.asarray(twists),
    )


def twists_of(twist_ref):
    shape = (BLOCKS, LANE8, BLOCK)
    cosine = jnp.broadcast_to(twist_ref[0][:, None, :], shape).reshape(BLOCKS * LANE8, BLOCK)
    sine = jnp.broadcast_to(twist_ref[1][:, None, :], shape).reshape(BLOCKS * LANE8, BLOCK)
    return cosine, sine


def forward(low, high, first_ref, second_ref, cosine, sine):
    rows = BLOCKS * LANE8
    signals = jnp.concatenate([low, high], 1).astype(bf16)
    part = jnp.dot(first_ref[...], signals, preferred_element_type=f32)
    turned = []
    for lanes in (slice(0, BLOCK), slice(BLOCK, 2 * BLOCK)):
        real, imag = part[:rows, lanes], part[rows:, lanes]
        turned.append(jnp.concatenate([real * cosine - imag * sine, real * sine + imag * cosine], 1))
    return jnp.dot(jnp.concatenate(turned, 0).astype(bf16), second_ref[...], preferred_element_type=f32)


def backward(spectra, back_second_ref, back_first_ref, cosine, sine):
    rows = BLOCKS * LANE8
    part = jnp.dot(spectra.astype(bf16), back_second_ref[...], preferred_element_type=f32)
    turned = []
    for start in (0, rows):
        real, imag = part[start : start + rows, :BLOCK], part[start : start + rows, BLOCK:]
        turned.append(jnp.concatenate([real * cosine + imag * sine, imag * cosine - real * sine], 0))
    return jnp.dot(back_first_ref[...], jnp.concatenate(turned, 1).astype(bf16), preferred_element_type=f32)


def filter_kernel(filter_ref, first_ref, second_ref, twist_ref, spectrum_ref):
    cosine, sine = twists_of(twist_ref)
    rows = BLOCKS * LANE8
    signals = []
    for start in (0, LANE8):
        pieces = [filter_ref[start : start + LANE8, i * BLOCK : (i + 1) * BLOCK] for i in range(BLOCKS)]
        signals.append(jnp.concatenate(pieces, 0))
    spectra = forward(*signals, first_ref, second_ref, cosine, sine)
    spectrum_ref[0] = spectra[:rows]
    spectrum_ref[1] = spectra[rows:]


def start_all(copies):
    for copy in copies:
        copy.start()


def wait_all(copies):
    for copy in copies:
        copy.wait()


def weight_copies(place_ref, weight_hbms, take, sems):
    copies = []
    for other, weight_hbm in enumerate(weight_hbms):
        core = place_ref[3] if other == 0 else 1 - place_ref[3]
        for index, step in enumerate(X_STEPS):
            group = lax.rem(place_ref[2] + (step + X), X) * CORES + core
            for slot in range(2):
                lanes, target = take(group, slot)
                number = (other * X + index) * 2 + slot
                copies.append(pltpu.make_async_copy(weight_hbm.at[index, slot, :, lanes], target, sems.at[number]))
    return copies


def masks_of(marks, width):
    trials = marks.shape[0]
    marks = marks[:, :width].astype(jnp.int32)
    marks = jnp.broadcast_to(marks[:, None, :], (trials, TRIAL, width)).reshape(trials * TRIAL, width)
    return marks


def pick(leaf, marks, count):
    level = 0
    stack = []
    for index in range(count):
        node = leaf(index)
        level = 0
        while stack and stack[-1][0] == level:
            node = jnp.where((marks & (1 << level)) != 0, node, stack.pop()[1])
            level += 1
        stack.append((level, node))
    return stack[0][1]


def project(rows_ref, start, blocks, weight):
    width = 2 * CHANS
    rows = rows_ref[pl.ds(start, blocks), :BLOCK, :].reshape(blocks * BLOCK, rows_ref.shape[2])
    marks = rows_ref[pl.ds(start, blocks), BLOCK:, :].astype(f32).reshape(blocks * BLOCK // TRIAL, rows_ref.shape[2])
    marks = masks_of(marks, width)
    products = {}

    def leaf(slot):
        if slot % 2 == 0:
            products[0] = jnp.dot(rows, weight[slot // 2], preferred_element_type=f32)
            return products[0][:, :width]
        return products[0][:, width:]

    chosen = pick(leaf, marks, 2 * weight.shape[0])
    return [chosen[i * BLOCK : (i + 1) * BLOCK].T.astype(bf16) for i in range(blocks)]


def block_of(place_ref, z_step, y_index):
    y_step = jnp.where(y_index < 2, Y - y_index, y_index - 1)
    return lax.rem(place_ref[0] + z_step, Z) * Y + lax.rem(place_ref[1] + y_step, Y)


def z_step_of(index):
    return jnp.where(index % 2 == 1, Z - (index + 1) // 2, index // 2)


def forward_kernel(place_ref, taps_ref, gain_ref, twist_ref, filter_hbm, own_hbm, other_hbm, *rest):
    chunk_hbms = rest[: Z + 1]
    table_hbms = rest[Z + 1 : Z + 5]
    gated_ref, gate_ref, spectrum_ref, both, rows, weight, spectra, *rest = rest[Z + 5 :]
    tables = rest[:4]
    weight_sems, row_sems, sems = rest[4:]
    half = Y // 2
    width = 2 * CHANS
    place = lambda group, slot: (pl.ds(0, width), weight.at[group, :, pl.ds(slot * width, width)])
    loads = weight_copies(place_ref, (own_hbm, other_hbm), place, weight_sems)
    for index, chunk in enumerate(chunk_hbms[: Z - 1]):
        loads.append(pltpu.make_async_copy(chunk, rows.at[pl.ds(index * Y, Y)], row_sems.at[index]))
    for index, chunk in enumerate(chunk_hbms[Z - 1 :]):
        target = rows.at[pl.ds((Z - 1) * Y + index * half, half)]
        loads.append(pltpu.make_async_copy(chunk, target, row_sems.at[Z - 1 + index]))
    pairs = [(filter_hbm, spectra)] + list(zip(table_hbms, tables))
    others = [pltpu.make_async_copy(source, target, sems.at[index]) for index, (source, target) in enumerate(pairs)]
    start_all(loads)
    start_all(others)
    wait_all(loads)

    def read_in(index, carry):
        blocks = project(rows, index * Y, Y, weight)
        for y_index in range(Y):
            both[block_of(place_ref, z_step_of(index), y_index)] = blocks[y_index]
        return carry

    lax.fori_loop(0, Z, read_in, 0)
    cosine, sine = twists_of(twist_ref)
    lane = lax.broadcasted_iota(jnp.int32, (BLOCKS, LANE8, BLOCK), 2)
    count = BLOCKS * LANE8
    cube = (BLOCKS, LANE8, BLOCK)
    wait_all(others)
    first_ref, second_ref, back_second_ref, back_first_ref = tables

    def short(value, group):
        taps = taps_ref[:, pl.ds(pl.multiple_of(group * LANE8, LANE8), LANE8), :]
        total = taps[0][None] * value
        for shift in (1, 2):
            rolled = pltpu.roll(value.reshape(count, BLOCK), shift, 1).reshape(cube)
            before = jnp.concatenate([jnp.zeros((1, LANE8, BLOCK), f32), rolled[:-1]], 0)
            total = total + taps[shift][None] * jnp.where(lane < shift, before, rolled)
        return total.astype(bf16).astype(f32).reshape(count, BLOCK)

    def step(pair, carry):
        here = pl.ds(pl.multiple_of(pair * 2 * LANE8, 2 * LANE8), 2 * LANE8)
        there = pl.ds(pl.multiple_of(CHANS + pair * 2 * LANE8, 2 * LANE8), 2 * LANE8)
        value = both[:, here, :].astype(f32)
        gate = both[:, there, :]
        signals = [short(value[:, i * LANE8 : (i + 1) * LANE8], pair * 2 + i) for i in range(2)]
        own = forward(*signals, first_ref, second_ref, cosine, sine)
        spectrum_ref[pl.ds(pair * 2, 2)] = own.reshape(2, count, 2 * BLOCK)
        weight = spectra[pl.ds(pair * 2, 2)].reshape(2 * count, 2 * BLOCK)
        own_re, own_im = own[:, :BLOCK], own[:, BLOCK:]
        filter_re, filter_im = weight[:, :BLOCK], weight[:, BLOCK:]
        mix = jnp.concatenate([own_re * filter_re - own_im * filter_im, own_re * filter_im + own_im * filter_re], 1)
        result = backward(mix, back_second_ref, back_first_ref, cosine, sine)
        signal = jnp.concatenate([piece.reshape(cube) for piece in signals], 1)
        long_part = jnp.concatenate([result[:, i * BLOCK : (i + 1) * BLOCK].reshape(cube) for i in range(2)], 1)
        mixed = (long_part + gain_ref[here, :][None] * signal).astype(bf16).astype(f32)
        gated = (gate.astype(f32) * mixed).astype(bf16).reshape(Z, Y, 2 * LANE8, BLOCK)
        for y in range(Y):
            gated_ref[y, :, here, :] = gated[:, y]
        gate_ref[:, here, :] = gate
        return carry

    lax.fori_loop(0, GROUPS // 2, step, 0)


def gradient_kernel(grad_ref, gate_ref, spectrum_ref, first_ref, second_ref, back_second_ref, back_first_ref, twist_ref, out_ref):
    cosine, sine = twists_of(twist_ref)
    count = BLOCKS * LANE8
    products = (grad_ref[...].astype(f32) * gate_ref[...].astype(f32)).astype(bf16).astype(f32)
    signals = [products[:, i * LANE8 : (i + 1) * LANE8].reshape(count, BLOCK) for i in range(2)]
    spectra = forward(*signals, first_ref, second_ref, cosine, sine)
    own = spectrum_ref[...].reshape(2 * count, 2 * BLOCK)
    own_re, own_im = own[:, :BLOCK], own[:, BLOCK:]
    grad_re, grad_im = spectra[:, :BLOCK], spectra[:, BLOCK:]
    lag = jnp.concatenate([own_re * grad_re + own_im * grad_im, own_re * grad_im - own_im * grad_re], 1)
    result = backward(lag, back_second_ref, back_first_ref, cosine, sine)
    both = []
    for half in range(2):
        lanes = slice(half * BLOCK, (half + 1) * BLOCK)
        both.append(jnp.concatenate([result[i * LANE8 : (i + 1) * LANE8, lanes] for i in range(BLOCKS)], 1))
    out_ref[...] = jnp.concatenate(both, 0).astype(bf16)


def read_out_kernel(place_ref, own_hbm, other_hbm, rows_hbm, *rest):
    mark_hbms = rest[:Z]
    out_ref, weight, rows_all, marks_all, weight_sems, mark_sems, row_sem = rest[Z:]
    slots, inner, width = weight.shape
    take = lambda group, slot: (pl.ds(2 * CHANS, width), weight.at[group * 2 + slot])
    loads = [pltpu.make_async_copy(rows_hbm, rows_all, row_sem)]
    for index, mark_hbm in enumerate(mark_hbms):
        source = mark_hbm.at[0, pl.ds(BLOCK, BLOCK // TRIAL), :]
        loads.append(pltpu.make_async_copy(source, marks_all.at[index], mark_sems.at[index]))
    loads += weight_copies(place_ref, (own_hbm, other_hbm), take, weight_sems)
    start_all(loads)
    wait_all(loads)

    def step(quad, carry):
        places = [lax.rem(place_ref[0] + z_step_of(quad * 4 + index), Z) for index in range(4)]
        rows = jnp.concatenate([rows_all[:, block, :, :].reshape(inner, BLOCK).T for block in places], 0)
        marks = marks_all[pl.ds(quad * 4, 4)].astype(f32).reshape(4 * BLOCK // TRIAL, width)
        marks = masks_of(marks, width)
        leaf = lambda slot: jnp.dot(rows, weight[slot], preferred_element_type=f32)
        chosen = pick(leaf, marks, slots)
        for index, block in enumerate(places):
            out_ref[block] = chosen[index * BLOCK : (index + 1) * BLOCK].astype(bf16)
        return carry

    lax.fori_loop(0, Z // 4, step, 0)


def along_y(value, step):
    return lax.ppermute(value, "seq", [(z * Y + y, z * Y + (y + step) % Y) for z in range(Z) for y in range(Y)])


def along_z(value, step):
    return lax.ppermute(value, "seq", [(z * Y + y, (z + step) % Z * Y + y) for z in range(Z) for y in range(Y)])


def along_x(value, step):
    pairs = [(x * CORES + c, (x + step) % X * CORES + c) for x in range(X) for c in range(CORES)]
    return lax.ppermute(value, "grp", pairs)


def other_core(value):
    return lax.ppermute(value, "grp", [(group, group ^ 1) for group in range(X * CORES)])


def whole(count):
    return [pl.BlockSpec(memory_space=pltpu.VMEM)] * count


def local(spikes, session_of_bin, session_slot, readin_weight, short_kernel, long_filter, skip_gain, readout_weight, out_grad):
    groups = lax.axis_size("grp")
    in_chans = spikes.shape[2]
    model_width = short_kernel.shape[1]
    place = lax.axis_index("seq")
    group = lax.axis_index("grp")
    scalar = pl.BlockSpec(memory_space=pltpu.SMEM)
    hbm = pl.BlockSpec(memory_space=pltpu.HBM)
    z_groups = [[z * Y + y for z in range(Z)] for y in range(Y)]
    y_groups = [[z * Y + y for y in range(Y)] for z in range(Z)]
    coords = jnp.stack([place // Y, place % Y, group // CORES, group % CORES]).astype(jnp.int32)
    first, second, back_second, back_first, twists = transform_tables()
    params = pltpu.CompilerParams(vmem_limit_bytes=60 << 20)
    spectrum_shape = jax.ShapeDtypeStruct((GROUPS, BLOCKS * LANE8, 2 * BLOCK), f32)
    plane = (BLOCKS, CHANS, BLOCK)
    work = 2 * GROUPS * (512 * 256 * 128 + 256 * 256 * 256)
    pair = 2 * LANE8
    same = lambda table: pl.BlockSpec(table.shape, lambda i, rank=table.ndim: (0,) * rank)

    sessions = session_of_bin[0, ::TRIAL]
    matches = sessions[:, None] == jnp.arange(session_slot.shape[0], dtype=jnp.int32)[None, :]
    slots = jnp.sum(jnp.where(matches, session_slot[None, :], 0), axis=1)
    marks = jnp.broadcast_to(slots.astype(bf16)[:, None], (slots.shape[0], in_chans))
    block = jnp.concatenate([spikes[0], marks], 0)
    chunk = jnp.stack([block, along_y(block, 1), along_y(block, -1), along_y(block, 2)])
    right, left = along_z(chunk, 1), along_z(chunk, -1)
    chunks = [chunk, right, left]

    pieces = [lax.dynamic_slice_in_dim(readin_weight, start + place * CHANS, CHANS, 2) for start in (0, model_width)]
    pieces.append(lax.dynamic_slice_in_dim(readout_weight, place // Y * (Y * CHANS), Y * CHANS, 1))
    own = jnp.concatenate(pieces, 2)
    own_right, own_left = along_x(own, 1), along_x(own, -1)

    filter_spectrum = pl.pallas_call(
        filter_kernel,
        out_shape=spectrum_shape,
        grid=(GROUPS // 2,),
        in_specs=[pl.BlockSpec((pair, LENGTH), lambda i: (i, 0))] + [same(table) for table in (first, second, twists)],
        out_specs=pl.BlockSpec((2,) + spectrum_shape.shape[1:], lambda i: (i, 0, 0)),
        compiler_params=params,
        cost_estimate=pl.CostEstimate(flops=work, bytes_accessed=4 << 20, transcendentals=0),
        name="filter_transform",
    )(long_filter, first, second, twists)
    turned = out_grad[0].T.reshape(BLOCKS, CHANS, BLOCK)

    right, left, own_right, own_left, filter_spectrum = lax.optimization_barrier((right, left, own_right, own_left, filter_spectrum))
    right, left = along_z(right, 1), along_z(left, -1)
    chunks += [right, left]
    far = jnp.concatenate([along_x(own_right[:1], 1), along_x(own_left[1:], -1)], 0)
    right, left, far, turned = lax.optimization_barrier((right, left, far, turned))
    right, left = along_z(right, 1), along_z(left, -1)
    chunks += [right, left]
    grads = lax.all_to_all(turned, "seq", split_axis=0, concat_axis=0, tiled=True)
    weights = jnp.stack([own, own_right, own_left, far])
    weights_other = other_core(weights)
    taps = lax.dynamic_slice_in_dim(short_kernel, place * CHANS, CHANS, 1)
    taps = jnp.broadcast_to(taps[:, :, None], (short_kernel.shape[0], CHANS, BLOCK))
    gains = jnp.broadcast_to(skip_gain[:, None], (CHANS, BLOCK))
    right, left, weights_other, taps, gains, coords = lax.optimization_barrier((right, left, weights_other, taps, gains, coords))
    last_right, last_left = along_z(right[: Y // 2], 1), along_z(left[Y // 2 :], -1)
    last_right, last_left, grads = lax.optimization_barrier((last_right, last_left, grads))

    tables = (first, second, back_second, back_first)
    slot_count = session_slot.shape[0]
    gated, gates, spectrum = pl.pallas_call(
        forward_kernel,
        out_shape=(
            jax.ShapeDtypeStruct((Y, Z, CHANS, BLOCK), bf16),
            jax.ShapeDtypeStruct(plane, bf16),
            spectrum_shape,
        ),
        in_specs=[scalar] + whole(3) + [hbm] * (3 + Z + 1 + 4),
        out_specs=tuple(whole(3)),
        scratch_shapes=[
            pltpu.VMEM((BLOCKS, 2 * CHANS, BLOCK), bf16),
            pltpu.VMEM((BLOCKS,) + chunk.shape[1:], bf16),
            pltpu.VMEM((slot_count // 2, in_chans, 4 * CHANS), bf16),
            pltpu.VMEM(spectrum_shape.shape, f32),
        ]
        + [pltpu.VMEM(table.shape, bf16) for table in tables]
        + [pltpu.SemaphoreType.DMA((count,)) for count in (slot_count, Z + 1, 5)],
        compiler_params=params,
        cost_estimate=pl.CostEstimate(flops=4 * work, bytes_accessed=8 << 20, transcendentals=0),
        name="long_convolution",
    )(coords, taps, gains, twists, filter_spectrum, weights, weights_other, *chunks, last_right, last_left, *tables)

    arrived = lax.all_to_all(gated, "seq", split_axis=0, concat_axis=0, tiled=True, axis_index_groups=y_groups)
    own_grad = pl.pallas_call(
        gradient_kernel,
        out_shape=jax.ShapeDtypeStruct((CHANS, LENGTH), bf16),
        grid=(GROUPS // 2,),
        in_specs=[pl.BlockSpec((BLOCKS, pair, BLOCK), lambda i: (0, i, 0))] * 2
        + [pl.BlockSpec((2,) + spectrum_shape.shape[1:], lambda i: (i, 0, 0))]
        + [same(table) for table in tables + (twists,)],
        out_specs=pl.BlockSpec((pair, LENGTH), lambda i: (i, 0)),
        compiler_params=params,
        cost_estimate=pl.CostEstimate(flops=2 * work, bytes_accessed=4 << 20, transcendentals=0),
        name="filter_gradient",
    )(grads, gates, spectrum, *tables, twists)
    shares = lax.all_to_all(own_grad.reshape(groups, CHANS // groups, LENGTH), "grp", split_axis=0, concat_axis=0, tiled=True)
    share = jnp.sum(shares.astype(f32), 0).astype(bf16)
    filter_grad = lax.all_gather(share, "grp", axis=0, tiled=True).astype(f32)
    partial = pl.pallas_call(
        read_out_kernel,
        out_shape=jax.ShapeDtypeStruct((Z, BLOCK, in_chans), bf16),
        in_specs=[scalar] + [hbm] * (3 + Z),
        out_specs=whole(1)[0],
        scratch_shapes=[
            pltpu.VMEM((slot_count, Y * CHANS, in_chans), bf16),
            pltpu.VMEM((Y, Z, CHANS, BLOCK), bf16),
            pltpu.VMEM((Z, BLOCK // TRIAL, in_chans), bf16),
        ]
        + [pltpu.SemaphoreType.DMA((count,)) for count in (slot_count, Z)]
        + [pltpu.SemaphoreType.DMA],
        compiler_params=params,
        cost_estimate=pl.CostEstimate(flops=2 * 512 * 512 * 4096, bytes_accessed=6 << 20, transcendentals=0),
        name="read_out",
    )(coords, weights, weights_other, arrived, *chunks, last_right)
    pieces = lax.all_to_all(partial, "seq", split_axis=0, concat_axis=0, tiled=True, axis_index_groups=z_groups)
    denoised = jnp.sum(pieces.astype(f32), 0).astype(bf16)
    return denoised[None], filter_grad


def solution(mesh):
    placed = (
        P("grp", "seq", None),
        P("grp", "seq"),
        P(),
        P("grp", None, None),
        P(),
        P("seq", None),
        P("seq"),
        P("grp", None, None),
        P("grp", "seq", None),
    )
    return jax.shard_map(
        local,
        mesh=mesh,
        in_specs=placed,
        out_specs=(P("grp", "seq", None), P("seq", None)),
        check_vma=False,
    )
```

time: 161 us -> 149 us (0.925)
  waiting for transfers between devices: 44.5 us -> 35.3 us
  local copies, waits for them, and re-layouts: 16.3 us -> 9.17 us
  other arithmetic: 2.82 us -> 8.64 us
  starting transfers between devices: 50 us -> 46.9 us
    all_to_all x1, waiting for transfers between devices: 14.1 us -> 0.01 us  [local(): lax.all_to_all(turned, 'seq', split_axis=0, concat_axis=0, tiled=True)]
    ppermute x8, waiting for transfers between devices: 14.4 us -> 25.6 us  [along_z(): lax.ppermute(value, 'seq', [(z * Y + y, (z + step) % Z * Y + y) for z in...]
    all_to_all x2 -> x0, starting transfers between devices: 8.64 us -> none  [gather_weights(): lax.all_to_all(copies, 'grp', split_axis=0, concat_axis=0, tiled=True)]
    all_to_all x1, waiting for transfers between devices: 6.46 us -> 0.71 us  [local(): lax.all_to_all(gated, 'seq', split_axis=0, concat_axis=0, tiled=True, axi...]
    ppermute x0 -> x5, starting transfers between devices: none -> 5.71 us  [the longest x4 5.71 us: along_x(): return lax.ppermute(value, 'grp', pairs)]
    unnamed x37 -> x22, local copies, waits for them, and re-layouts: 5.48 us -> 1.41 us
    ppermute x3, waiting for transfers between devices: 3.77 us -> 0.01 us  [along_y(): lax.ppermute(value, 'seq', [(z * Y + y, z * Y + (y + step) % Y) for z in...]
    broadcast_in_dim x2 -> x0, local copies, waits for them, and re-layouts: 2.7 us -> none  [gather_weights(): copies = jnp.broadcast_to(own[None], (groups,) + own.shape)]
  transfers between devices with their start and end apart: 17 -> 20, of which waited for: 11 -> 9; matrix products, arithmetic and copies ran while one was open for 8% -> 7% of each run, Pallas kernels for 20% -> 11%
where the time goes in v3:
time: 149 us; the launch traced here: 146 us
  starting transfers between devices  46.9 us (31%)
  waiting for transfers between devices  35.3 us (24%)
  Pallas kernels  32.5 us (22%)
  blocking collectives  13.1 us (9%)
  local copies, waits for them, and re-layouts  9.17 us (6%)
  other arithmetic  8.64 us (6%)
    ppermute x8, waiting for transfers between devices, along_z(): lax.ppermute(value, 'seq', [(z * Y + y, (z + step) % Z * Y + y) for z in...  25.6 us
    pallas_call x1, Pallas kernels, local(): pl.pallas_call(forward_kernel, out_shape=(jax.ShapeDtypeStruct((Y, Z, CHA...  15.8 us
    ppermute x8, starting transfers between devices, along_z(): lax.ppermute(value, 'seq', [(z * Y + y, (z + step) % Z * Y + y) for z in...  14.6 us
    all_gather x1, blocking collectives, local(): filter_grad = lax.all_gather(share, 'grp', axis=0, tiled=True).astype(f32)  13.1 us
    pallas_call x1, Pallas kernels, local(): pl.pallas_call(read_out_kernel, out_shape=jax.ShapeDtypeStruct((Z, BLOCK,...  6.22 us
    pallas_call x1, Pallas kernels, local(): pl.pallas_call(gradient_kernel, out_shape=jax.ShapeDtypeStruct((CHANS, LE...  5.91 us
    all_to_all x1, starting transfers between devices, local(): lax.all_to_all(turned, 'seq', split_axis=0, concat_axis=0, tiled=True)  5.89 us
    all_to_all x1, starting transfers between devices, local(): lax.all_to_all(partial, 'seq', split_axis=0, concat_axis=0, tiled=True, a...  5.76 us
  transfers between devices with their start and end apart: 20, of which 9 were waited for; matrix products, arithmetic and copies ran while one was open for 7% of the time, Pallas kernels for 11%

profile of v3, /device:TPU:8, one launch (start us, length us, event | category | flops | bytes accessed | tf_op | source)
XLA Modules:
  0.0 146.5 jit_solution(741464551933965931)
XLA Ops:
  2.4 0.9 fusion
  3.3 2.3 %collective-permute-start.1 = (bf16[136,256]{1,0:T(8,128)(2,1)S(1)}, bf16[136,256]{1,0:T(8,128)(2,1)S(1)}, u32[]{:S(2)}, u32[]{:S(2)}) collective-permute-start(bf16[136,256]{1,0:T(8,128)(2,1)S(1)} %get-tuple-element.47), channel_id=1, source_target_pairs={{0,3},{1,0},{2,1},{3,2},{4,7},{5,4},{6,5},{7,6},{8,11},{9,8},{10,9... | collective-permute-start | bytes 208904 | tf_op jit(solution)/shard_map/ppermute | solution.py:273
  5.6 3.3 %collective-permute-start.2 = (bf16[136,256]{1,0:T(8,128)(2,1)S(1)}, bf16[136,256]{1,0:T(8,128)(2,1)S(1)}, u32[]{:S(2)}, u32[]{:S(2)}) collective-permute-start(bf16[136,256]{1,0:T(8,128)(2,1)S(1)} %get-tuple-element.47), channel_id=1, source_target_pairs={{0,2},{1,3},{2,0},{3,1},{4,6},{5,7},{6,4},{7,5},{8,10},{9,11},{10,... | collective-permute-start | bytes 208904 | tf_op jit(solution)/shard_map/ppermute | solution.py:273
  9.0 1.1 constant_dynamic-slice_fusion.3
  11.0 2.8 %collective-permute-start.6 = (bf16[2,256,384]{2,1,0:T(8,128)(2,1)}, bf16[2,256,384]{2,1,0:T(8,128)(2,1)S(1)}, u32[]{:S(2)}, u32[]{:S(2)}) collective-permute-start(bf16[2,256,384]{2,1,0:T(8,128)(2,1)} %pad_maximum_fusion.1), channel_id=1, source_target_pairs={{0,192},{32,224},{64,0},{96,32},{128,64},{160,96},{192,128},{224,1... | collective-permute-start | bytes 1179656 | tf_op jit(solution)/shard_map/ppermute | solution.py:282
  14.4 0.9 pad_maximum_fusion.3.rest_0_
  15.3 5.9 %collective-permute-start.4 = (bf16[4,136,256]{2,1,0:T(8,128)(2,1)S(1)}, bf16[4,136,256]{2,1,0:T(8,128)(2,1)}, u32[]{:S(2)}, u32[]{:S(2)}) collective-permute-start(bf16[4,136,256]{2,1,0:T(8,128)(2,1)S(1)} %pad_maximum_fusion.3.rest_0_), channel_id=1, source_target_pairs={{0,28},{1,29},{2,30},{3,31},{4,0},{5,1},{6,2},{7,3},{8,4},{9,5},{1... | collective-permute-start | bytes 835592 | tf_op jit(solution)/shard_map/ppermute | solution.py:277
  21.3 4.6 %filter_transform.1.filter_hbm = f32[8,256,256]{2,1,0:T(8,128)} custom-call(f32[64,4096]{1,0:T(8,128)} %filter_ref.1, bf16[512,256]{1,0:T(8,128)(2,1)} %constant.78.clone.first_ref.rest_9_, bf16[256,256]{1,0:T(8,128)(2,1)} %constant.79.clone.second_ref.rest_10_, f32[2,32,128]{2,1,0:T(8,128)} %constant.82.clone.twist_ref), custom_call_target="tpu_custom_call" | custom-call | flops 536870912 | bytes 4194304 | tf_op jit(solution)/shard_map/filter_transform/pallas_call | solution.py:326
  26.1 3.5 %collective-permute-done.3.rest_1_ = bf16[4,136,256]{2,1,0:T(8,128)(2,1)} collective-permute-done((bf16[4,136,256]{2,1,0:T(8,128)(2,1)S(1)}, bf16[4,136,256]{2,1,0:T(8,128)(2,1)}, u32[]{:S(2)}, u32[]{:S(2)}) %collective-permute-start.3) | collective-permute-done | bytes 278560 | tf_op jit(solution)/shard_map/ppermute | solution.py:277
  31.7 2.9 %collective-permute-start.10 = (bf16[1,256,384]{2,1,0:T(8,128)(2,1)}, bf16[1,256,384]{2,1,0:T(8,128)(2,1)}, u32[]{:S(2)}, u32[]{:S(2)}) collective-permute-start(bf16[1,256,384]{2,1,0:T(8,128)(2,1)} %slice.17), channel_id=1, source_target_pairs={{0,192},{32,224},{64,0},{96,32},{128,64},{160,96},{192,128},{224,1... | collective-permute-start | bytes 589832 | tf_op jit(solution)/shard_map/ppermute | solution.py:282
  34.7 3.2 %collective-permute-start.8 = (bf16[4,136,256]{2,1,0:T(8,128)(2,1)}, bf16[4,136,256]{2,1,0:T(8,128)(2,1)}, u32[]{:S(2)}, u32[]{:S(2)}) collective-permute-start(bf16[4,136,256]{2,1,0:T(8,128)(2,1)} %collective-permute-done.4.rest_2_), channel_id=1, source_target_pairs={{0,28},{1,29},{2,30},{3,31},{4,0},{5,1},{6,2},{7,3},{8,4},{9,5},{1... | collective-permute-start | bytes 835592 | tf_op jit(solution)/shard_map/ppermute | solution.py:277
  37.9 2.0 %copy.17 = bf16[2048,128]{1,0:T(8,128)(2,1)} copy(bf16[2048,128]{0,1:T(8,128)(2,1)} %bitcast.26) | data formatting | bytes 1048576 | tf_op jit(solution)/shard_map/transpose | solution.py:336
  40.1 1.8 %collective-permute-done.9 = bf16[1,256,384]{2,1,0:T(8,128)(2,1)} collective-permute-done((bf16[1,256,384]{2,1,0:T(8,128)(2,1)}, bf16[1,256,384]{2,1,0:T(8,128)(2,1)}, u32[]{:S(2)}, u32[]{:S(2)}) %collective-permute-start.9) | collective-permute-done | bytes 196640 | tf_op jit(solution)/shard_map/ppermute | solution.py:282
  41.9 1.1 pad_maximum_fusion.2
  43.0 1.4 pad_maximum_fusion.own_hbm
  44.4 5.9 %all-to-all-start = ((bf16[32,64,128]{2,1,0:T(8,128)(2,1)}), bf16[32,64,128]{2,1,0:T(8,128)(2,1)S(1)}, u32[]{:S(2)}, u32[]{:S(2)}) async-start(bf16[32,64,128]{2,1,0:T(8,128)(2,1)} %bitcast.8), calls=%async_computation | async-start | bytes 1048576 | tf_op jit(solution)/shard_map/all_to_all | solution.py:345
  50.3 1.5 %collective-permute-start.11 = (bf16[4,136,256]{2,1,0:T(8,128)(2,1)S(1)}, bf16[4,136,256]{2,1,0:T(8,128)(2,1)S(1)}, u32[]{:S(2)}, u32[]{:S(2)}) collective-permute-start(bf16[4,136,256]{2,1,0:T(8,128)(2,1)S(1)} %collective-permute-done.7.rest_3_), channel_id=1, source_target_pairs={{0,4},{1,5},{2,6},{3,7},{4,8},{5,9},{6,10},{7,11},{8,12},{9,13},{1... | collective-permute-start | bytes 835592 | tf_op jit(solution)/shard_map/ppermute | solution.py:277
  51.9 1.8 %collective-permute-start.12 = (bf16[4,136,256]{2,1,0:T(8,128)(2,1)}, bf16[4,136,256]{2,1,0:T(8,128)(2,1)S(1)}, u32[]{:S(2)}, u32[]{:S(2)}) collective-permute-start(bf16[4,136,256]{2,1,0:T(8,128)(2,1)} %collective-permute-done.8.rest_4_), channel_id=1, source_target_pairs={{0,28},{1,29},{2,30},{3,31},{4,0},{5,1},{6,2},{7,3},{8,4},{9,5},{1... | collective-permute-start | bytes 835592 | tf_op jit(solution)/shard_map/ppermute | solution.py:277
  55.0 16.2 %collective-permute-done.11.rest_5_ = bf16[4,136,256]{2,1,0:T(8,128)(2,1)S(1)} collective-permute-done((bf16[4,136,256]{2,1,0:T(8,128)(2,1)S(1)}, bf16[4,136,256]{2,1,0:T(8,128)(2,1)S(1)}, u32[]{:S(2)}, u32[]{:S(2)}) %collective-permute-start.11) | collective-permute-done | bytes 278560 | tf_op jit(solution)/shard_map/ppermute | solution.py:277
  72.7 1.5 %collective-permute-start.15 = (bf16[2,136,256]{2,1,0:T(8,128)(2,1)S(1)}, bf16[2,136,256]{2,1,0:T(8,128)(2,1)}, u32[]{:S(2)}, u32[]{:S(2)}) collective-permute-start(bf16[2,136,256]{2,1,0:T(8,128)(2,1)S(1)} %slice.19), channel_id=1, source_target_pairs={{0,28},{1,29},{2,30},{3,31},{4,0},{5,1},{6,2},{7,3},{8,4},{9,5},{1... | collective-permute-start | bytes 417800 | tf_op jit(solution)/shard_map/ppermute | solution.py:277
  74.8 3.1 %collective-permute-done.15.rest_8_ = bf16[2,136,256]{2,1,0:T(8,128)(2,1)} collective-permute-done((bf16[2,136,256]{2,1,0:T(8,128)(2,1)S(1)}, bf16[2,136,256]{2,1,0:T(8,128)(2,1)}, u32[]{:S(2)}, u32[]{:S(2)}) %collective-permute-start.15) | collective-permute-done | bytes 139296 | tf_op jit(solution)/shard_map/ppermute | solution.py:277
  78.0 2.6 %collective-permute-done.14.rest_7_ = bf16[2,136,256]{2,1,0:T(8,128)(2,1)} collective-permute-done((bf16[2,136,256]{2,1,0:T(8,128)(2,1)S(1)}, bf16[2,136,256]{2,1,0:T(8,128)(2,1)}, u32[]{:S(2)}, u32[]{:S(2)}) %collective-permute-start.14) | collective-permute-done | bytes 139296 | tf_op jit(solution)/shard_map/ppermute | solution.py:277
  80.6 15.8 %long_convolution.1 = (bf16[4,8,64,128]{3,2,1,0:T(8,128)(2,1)}, bf16[32,64,128]{2,1,0:T(8,128)(2,1)}, f32[8,256,256]{2,1,0:T(8,128)}) custom-call(s32[4]{0:T(128)} %pad_add_fusion.place_ref, f32[3,64,128]{2,1,0:T(8,128)} %broadcast_in_dim.38.taps_ref, f32[64,128]{1,0:T(8,128)} %broadcast_in_dim.39.gain_ref, f32[2,32,128]{2,1,0:T(8,128)} %constant.82.clone.twist_ref, ...), custom_call_target="tpu_custom_call" | custom-call | flops 2147483648 | bytes 8388608 | tf_op jit(solution)/shard_map/long_convolution/pallas_call | solution.py:357
  96.4 4.8 %all-to-all-start.1 = ((bf16[4,8,64,128]{3,2,1,0:T(8,128)(2,1)}), bf16[4,8,64,128]{3,2,1,0:T(8,128)(2,1)S(1)}, u32[]{:S(2)}, u32[]{:S(2)}) async-start(bf16[4,8,64,128]{3,2,1,0:T(8,128)(2,1)} %get-tuple-element.40), calls=%async_computation.1 | async-start | bytes 1048576 | tf_op jit(solution)/shard_map/all_to_all | solution.py:379
  101.2 5.9 %filter_gradient.1 = bf16[64,4096]{1,0:T(8,128)(2,1)} custom-call(bf16[32,64,128]{2,1,0:T(8,128)(2,1)} %copy-done.1, bf16[32,64,128]{2,1,0:T(8,128)(2,1)} %get-tuple-element.42.gate_ref, f32[8,256,256]{2,1,0:T(8,128)} %get-tuple-element.43.spectrum_ref, bf16[512,256]{1,0:T(8,128)(2,1)} %constant.78.clone.first_ref.rest_9_, ...), custom_call_target="tpu_custom_call" | custom-call | flops 1073741824 | bytes 4194304 | tf_op jit(solution)/shard_map/filter_gradient/pallas_call | solution.py:380
  107.9 4.5 %all-to-all-start.3 = ((bf16[8,8,4096]{2,1,0:T(8,128)(2,1)}), bf16[8,8,4096]{2,1,0:T(8,128)(2,1)S(1)}, u32[]{:S(2)}, u32[]{:S(2)}) async-start(bf16[8,8,4096]{2,1,0:T(8,128)(2,1)} %bitcast.22), calls=%async_computation.3 | async-start | bytes 1048576 | tf_op jit(solution)/shard_map/all_to_all | solution.py:392
  112.4 6.2 %read_out.1 = bf16[8,128,256]{2,1,0:T(8,128)(2,1)} custom-call(s32[4]{0:T(128)} %pad_add_fusion.place_ref, bf16[4,2,256,384]{3,2,1,0:T(8,128)(2,1)} %pad_maximum_fusion.own_hbm, bf16[4,2,256,384]{3,2,1,0:T(8,128)(2,1)} %collective-permute-done.13.other_hbm, bf16[4,8,64,128]{3,2,1,0:T(8,128)(2,1)} %copy-done.7, bf16[4,136,256]{2,1,0:T(8,128)(2,1)} %copy-done.2, ...), custom_call_target="tpu_custom_call" | custom-call | flops 2147483648 | bytes 6291456 | tf_op jit(solution)/shard_map/read_out/pallas_call | solution.py:395
  118.6 4.1 %all-to-all-done.3 = bf16[8,8,4096]{2,1,0:T(8,128)(2,1)S(1)} async-done(((bf16[8,8,4096]{2,1,0:T(8,128)(2,1)}), bf16[8,8,4096]{2,1,0:T(8,128)(2,1)S(1)}, u32[]{:S(2)}, u32[]{:S(2)}) %all-to-all-start.3) | async-done | bytes 524320 | tf_op jit(solution)/shard_map/all_to_all | solution.py:392
  122.7 5.8 %all-to-all-start.2 = ((bf16[8,128,256]{2,1,0:T(8,128)(2,1)}), bf16[8,128,256]{2,1,0:T(8,128)(2,1)S(1)}, u32[]{:S(2)}, u32[]{:S(2)}) async-start(bf16[8,128,256]{2,1,0:T(8,128)(2,1)} %read_out.1), calls=%async_computation.2 | async-start | bytes 1048576 | tf_op jit(solution)/shard_map/all_to_all | solution.py:411
  128.6 13.1 %all_gather.3 = bf16[64,4096]{1,0:T(8,128)(2,1)S(1)} all-gather(bf16[8,4096]{1,0:T(8,128)(2,1)S(1)} %reduce_sum.35), channel_id=1, replica_groups=mesh['grp'=8,'seq'=32] {'grp'}, dimensions={0}, use_global_device_ids=true | all-gather | bytes 589824 | tf_op jit(solution)/shard_map/all_gather | solution.py:394
  141.7 1.0 convert_element_type.15
  142.7 3.1 %all-to-all-done.2 = bf16[8,128,256]{2,1,0:T(8,128)(2,1)S(1)} async-done(((bf16[8,128,256]{2,1,0:T(8,128)(2,1)}), bf16[8,128,256]{2,1,0:T(8,128)(2,1)S(1)}, u32[]{:S(2)}, u32[]{:S(2)}) %all-to-all-start.2) | async-done | bytes 524320 | tf_op jit(solution)/shard_map/all_to_all | solution.py:411
  (59 shorter events, 10.8 us)
Async XLA Ops:
  0.6 8.3 %copy-start = (bf16[2,2048,256]{2,1,0:T(8,128)(2,1)S(1)}, bf16[2,2048,256]{2,1,0:T(8,128)(2,1)}, u32[]{:S(2)}) copy-start(bf16[2,2048,256]{2,1,0:T(8,128)(2,1)} %param.21) | copy-start | bytes 6291460
  3.3 10.4 %collective-permute-start.1 = (bf16[136,256]{1,0:T(8,128)(2,1)S(1)}, bf16[136,256]{1,0:T(8,128)(2,1)S(1)}, u32[]{:S(2)}, u32[]{:S(2)}) collective-permute-start(bf16[136,256]{1,0:T(8,128)(2,1)S(1)} %get-tuple-element.47), channel_id=1, source_target_pairs={{0,3},{1,0},{2,1},{3,2},{4,7},{5,4},{6,5},{7,6},{8,11},{9,8},{10,9... | collective-permute-start | bytes 208904 | tf_op jit(solution)/shard_map/ppermute | solution.py:273
  5.6 8.2 %collective-permute-start = (bf16[136,256]{1,0:T(8,128)(2,1)S(1)}, bf16[136,256]{1,0:T(8,128)(2,1)S(1)}, u32[]{:S(2)}, u32[]{:S(2)}) collective-permute-start(bf16[136,256]{1,0:T(8,128)(2,1)S(1)} %get-tuple-element.47), channel_id=1, source_target_pairs={{0,1},{1,2},{2,3},{3,0},{4,5},{5,6},{6,7},{7,4},{8,9},{9,10},{10,1... | collective-permute-start | bytes 208904 | tf_op jit(solution)/shard_map/ppermute | solution.py:273
  5.6 8.2 %collective-permute-start.2 = (bf16[136,256]{1,0:T(8,128)(2,1)S(1)}, bf16[136,256]{1,0:T(8,128)(2,1)S(1)}, u32[]{:S(2)}, u32[]{:S(2)}) collective-permute-start(bf16[136,256]{1,0:T(8,128)(2,1)S(1)} %get-tuple-element.47), channel_id=1, source_target_pairs={{0,2},{1,3},{2,0},{3,1},{4,6},{5,7},{6,4},{7,5},{8,10},{9,11},{10,... | collective-permute-start | bytes 208904 | tf_op jit(solution)/shard_map/ppermute | solution.py:273
  11.0 18.6 %collective-permute-start.6 = (bf16[2,256,384]{2,1,0:T(8,128)(2,1)}, bf16[2,256,384]{2,1,0:T(8,128)(2,1)S(1)}, u32[]{:S(2)}, u32[]{:S(2)}) collective-permute-start(bf16[2,256,384]{2,1,0:T(8,128)(2,1)} %pad_maximum_fusion.1), channel_id=1, source_target_pairs={{0,192},{32,224},{64,0},{96,32},{128,64},{160,96},{192,128},{224,1... | collective-permute-start | bytes 1179656 | tf_op jit(solution)/shard_map/ppermute | solution.py:282
  13.7 15.8 %collective-permute-start.5 = (bf16[2,256,384]{2,1,0:T(8,128)(2,1)}, bf16[2,256,384]{2,1,0:T(8,128)(2,1)S(1)}, u32[]{:S(2)}, u32[]{:S(2)}) collective-permute-start(bf16[2,256,384]{2,1,0:T(8,128)(2,1)} %pad_maximum_fusion.1), channel_id=1, source_target_pairs={{0,64},{32,96},{64,128},{96,160},{128,192},{160,224},{192,0},{224,... | collective-permute-start | bytes 1179656 | tf_op jit(solution)/shard_map/ppermute | solution.py:282
  13.8 0.6 copy-start.9
  15.3 10.6 %copy-start.2 = (bf16[4,136,256]{2,1,0:T(8,128)(2,1)}, bf16[4,136,256]{2,1,0:T(8,128)(2,1)S(1)}, u32[]{:S(2)}) copy-start(bf16[4,136,256]{2,1,0:T(8,128)(2,1)S(1)} %pad_maximum_fusion.3.rest_0_) | copy-start | bytes 835588
  15.3 10.7 %collective-permute-start.4 = (bf16[4,136,256]{2,1,0:T(8,128)(2,1)S(1)}, bf16[4,136,256]{2,1,0:T(8,128)(2,1)}, u32[]{:S(2)}, u32[]{:S(2)}) collective-permute-start(bf16[4,136,256]{2,1,0:T(8,128)(2,1)S(1)} %pad_maximum_fusion.3.rest_0_), channel_id=1, source_target_pairs={{0,28},{1,29},{2,30},{3,31},{4,0},{5,1},{6,2},{7,3},{8,4},{9,5},{1... | collective-permute-start | bytes 835592 | tf_op jit(solution)/shard_map/ppermute | solution.py:277
  21.3 8.3 %collective-permute-start.3 = (bf16[4,136,256]{2,1,0:T(8,128)(2,1)S(1)}, bf16[4,136,256]{2,1,0:T(8,128)(2,1)}, u32[]{:S(2)}, u32[]{:S(2)}) collective-permute-start(bf16[4,136,256]{2,1,0:T(8,128)(2,1)S(1)} %pad_maximum_fusion.3.rest_0_), channel_id=1, source_target_pairs={{0,4},{1,5},{2,6},{3,7},{4,8},{5,9},{6,10},{7,11},{8,12},{9,13},{1... | collective-permute-start | bytes 835592 | tf_op jit(solution)/shard_map/ppermute | solution.py:277
  29.6 0.8 copy-start.3
  31.7 8.4 %collective-permute-start.10 = (bf16[1,256,384]{2,1,0:T(8,128)(2,1)}, bf16[1,256,384]{2,1,0:T(8,128)(2,1)}, u32[]{:S(2)}, u32[]{:S(2)}) collective-permute-start(bf16[1,256,384]{2,1,0:T(8,128)(2,1)} %slice.17), channel_id=1, source_target_pairs={{0,192},{32,224},{64,0},{96,32},{128,64},{160,96},{192,128},{224,1... | collective-permute-start | bytes 589832 | tf_op jit(solution)/shard_map/ppermute | solution.py:282
  34.7 7.2 %collective-permute-start.9 = (bf16[1,256,384]{2,1,0:T(8,128)(2,1)}, bf16[1,256,384]{2,1,0:T(8,128)(2,1)}, u32[]{:S(2)}, u32[]{:S(2)}) collective-permute-start(bf16[1,256,384]{2,1,0:T(8,128)(2,1)} %slice.16), channel_id=1, source_target_pairs={{0,64},{32,96},{64,128},{96,160},{128,192},{160,224},{192,0},{224,... | collective-permute-start | bytes 589832 | tf_op jit(solution)/shard_map/ppermute | solution.py:282
  34.7 8.3 %collective-permute-start.7 = (bf16[4,136,256]{2,1,0:T(8,128)(2,1)}, bf16[4,136,256]{2,1,0:T(8,128)(2,1)S(1)}, u32[]{:S(2)}, u32[]{:S(2)}) collective-permute-start(bf16[4,136,256]{2,1,0:T(8,128)(2,1)} %collective-permute-done.3.rest_1_), channel_id=1, source_target_pairs={{0,4},{1,5},{2,6},{3,7},{4,8},{5,9},{6,10},{7,11},{8,12},{9,13},{1... | collective-permute-start | bytes 835592 | tf_op jit(solution)/shard_map/ppermute | solution.py:277
  34.7 8.3 %collective-permute-start.8 = (bf16[4,136,256]{2,1,0:T(8,128)(2,1)}, bf16[4,136,256]{2,1,0:T(8,128)(2,1)}, u32[]{:S(2)}, u32[]{:S(2)}) collective-permute-start(bf16[4,136,256]{2,1,0:T(8,128)(2,1)} %collective-permute-done.4.rest_2_), channel_id=1, source_target_pairs={{0,28},{1,29},{2,30},{3,31},{4,0},{5,1},{6,2},{7,3},{8,4},{9,5},{1... | collective-permute-start | bytes 835592 | tf_op jit(solution)/shard_map/ppermute | solution.py:277
  40.0 3.0 %copy-start.4 = (bf16[2,256,384]{2,1,0:T(8,128)(2,1)S(1)}, bf16[2,256,384]{2,1,0:T(8,128)(2,1)}, u32[]{:S(2)}) copy-start(bf16[2,256,384]{2,1,0:T(8,128)(2,1)} %copy-done.3) | copy-start | bytes 1179652
  43.0 7.4 %copy-start.8 = (bf16[4,136,256]{2,1,0:T(8,128)(2,1)}, bf16[4,136,256]{2,1,0:T(8,128)(2,1)S(1)}, u32[]{:S(2)}) copy-start(bf16[4,136,256]{2,1,0:T(8,128)(2,1)S(1)} %collective-permute-done.7.rest_3_) | copy-start | bytes 835588
  43.0 28.2 %copy-start.10 = (f32[64]{0:T(128)S(1)}, f32[64]{0:T(128)}, u32[]{:S(2)}) copy-start(f32[64]{0:T(128)} %param.20) | copy-start | bytes 772
  44.4 26.8 %collective-permute-start.13 = (bf16[4,2,256,384]{3,2,1,0:T(8,128)(2,1)}, bf16[4,2,256,384]{3,2,1,0:T(8,128)(2,1)}, u32[]{:S(2)}, u32[]{:S(2)}) collective-permute-start(bf16[4,2,256,384]{3,2,1,0:T(8,128)(2,1)} %pad_maximum_fusion.own_hbm), channel_id=1, source_target_pairs={{0,32},{32,0},{64,96},{96,64},{128,160},{160,128},{192,224},{224,1... | collective-permute-start | bytes 4718600 | tf_op jit(solution)/shard_map/ppermute | solution.py:286
  44.4 30.4 %all-to-all-start = ((bf16[32,64,128]{2,1,0:T(8,128)(2,1)}), bf16[32,64,128]{2,1,0:T(8,128)(2,1)S(1)}, u32[]{:S(2)}, u32[]{:S(2)}) async-start(bf16[32,64,128]{2,1,0:T(8,128)(2,1)} %bitcast.8), calls=%async_computation | async-start | bytes 1048576 | tf_op jit(solution)/shard_map/all_to_all | solution.py:345
  50.3 20.8 %collective-permute-start.11 = (bf16[4,136,256]{2,1,0:T(8,128)(2,1)S(1)}, bf16[4,136,256]{2,1,0:T(8,128)(2,1)S(1)}, u32[]{:S(2)}, u32[]{:S(2)}) collective-permute-start(bf16[4,136,256]{2,1,0:T(8,128)(2,1)S(1)} %collective-permute-done.7.rest_3_), channel_id=1, source_target_pairs={{0,4},{1,5},{2,6},{3,7},{4,8},{5,9},{6,10},{7,11},{8,12},{9,13},{1... | collective-permute-start | bytes 835592 | tf_op jit(solution)/shard_map/ppermute | solution.py:277
  51.9 19.3 %collective-permute-start.12 = (bf16[4,136,256]{2,1,0:T(8,128)(2,1)}, bf16[4,136,256]{2,1,0:T(8,128)(2,1)S(1)}, u32[]{:S(2)}, u32[]{:S(2)}) collective-permute-start(bf16[4,136,256]{2,1,0:T(8,128)(2,1)} %collective-permute-done.8.rest_4_), channel_id=1, source_target_pairs={{0,28},{1,29},{2,30},{3,31},{4,0},{5,1},{6,2},{7,3},{8,4},{9,5},{1... | collective-permute-start | bytes 835592 | tf_op jit(solution)/shard_map/ppermute | solution.py:277
  71.2 9.5 %copy-start.5 = (bf16[4,136,256]{2,1,0:T(8,128)(2,1)}, bf16[4,136,256]{2,1,0:T(8,128)(2,1)S(1)}, u32[]{:S(2)}) copy-start(bf16[4,136,256]{2,1,0:T(8,128)(2,1)S(1)} %collective-permute-done.11.rest_5_) | copy-start | bytes 835588
  71.2 9.5 %copy-start.6 = (bf16[4,136,256]{2,1,0:T(8,128)(2,1)}, bf16[4,136,256]{2,1,0:T(8,128)(2,1)S(1)}, u32[]{:S(2)}) copy-start(bf16[4,136,256]{2,1,0:T(8,128)(2,1)S(1)} %collective-permute-done.12.rest_6_) | copy-start | bytes 835588
  72.7 5.2 %collective-permute-start.15 = (bf16[2,136,256]{2,1,0:T(8,128)(2,1)S(1)}, bf16[2,136,256]{2,1,0:T(8,128)(2,1)}, u32[]{:S(2)}, u32[]{:S(2)}) collective-permute-start(bf16[2,136,256]{2,1,0:T(8,128)(2,1)S(1)} %slice.19), channel_id=1, source_target_pairs={{0,28},{1,29},{2,30},{3,31},{4,0},{5,1},{6,2},{7,3},{8,4},{9,5},{1... | collective-permute-start | bytes 417800 | tf_op jit(solution)/shard_map/ppermute | solution.py:277
  74.2 6.4 %collective-permute-start.14 = (bf16[2,136,256]{2,1,0:T(8,128)(2,1)S(1)}, bf16[2,136,256]{2,1,0:T(8,128)(2,1)}, u32[]{:S(2)}, u32[]{:S(2)}) collective-permute-start(bf16[2,136,256]{2,1,0:T(8,128)(2,1)S(1)} %slice.18), channel_id=1, source_target_pairs={{0,4},{1,5},{2,6},{3,7},{4,8},{5,9},{6,10},{7,11},{8,12},{9,13},{1... | collective-permute-start | bytes 417800 | tf_op jit(solution)/shard_map/ppermute | solution.py:277
  74.8 21.6 %copy-start.1 = (bf16[32,64,128]{2,1,0:T(8,128)(2,1)}, bf16[32,64,128]{2,1,0:T(8,128)(2,1)S(1)}, u32[]{:S(2)}) copy-start(bf16[32,64,128]{2,1,0:T(8,128)(2,1)S(1)} %all-to-all-done.grad_ref) | copy-start | bytes 1572868
  96.4 11.4 %all-to-all-start.1 = ((bf16[4,8,64,128]{3,2,1,0:T(8,128)(2,1)}), bf16[4,8,64,128]{3,2,1,0:T(8,128)(2,1)S(1)}, u32[]{:S(2)}, u32[]{:S(2)}) async-start(bf16[4,8,64,128]{3,2,1,0:T(8,128)(2,1)} %get-tuple-element.40), calls=%async_computation.1 | async-start | bytes 1048576 | tf_op jit(solution)/shard_map/all_to_all | solution.py:379
  107.9 4.5 %copy-start.7 = (bf16[4,8,64,128]{3,2,1,0:T(8,128)(2,1)}, bf16[4,8,64,128]{3,2,1,0:T(8,128)(2,1)S(1)}, u32[]{:S(2)}) copy-start(bf16[4,8,64,128]{3,2,1,0:T(8,128)(2,1)S(1)} %all-to-all-done.1.rows_hbm) | copy-start | bytes 1572868
  107.9 14.9 %all-to-all-start.3 = ((bf16[8,8,4096]{2,1,0:T(8,128)(2,1)}), bf16[8,8,4096]{2,1,0:T(8,128)(2,1)S(1)}, u32[]{:S(2)}, u32[]{:S(2)}) async-start(bf16[8,8,4096]{2,1,0:T(8,128)(2,1)} %bitcast.22), calls=%async_computation.3 | async-start | bytes 1048576 | tf_op jit(solution)/shard_map/all_to_all | solution.py:392
  122.7 23.1 %all-to-all-start.2 = ((bf16[8,128,256]{2,1,0:T(8,128)(2,1)}), bf16[8,128,256]{2,1,0:T(8,128)(2,1)S(1)}, u32[]{:S(2)}, u32[]{:S(2)}) async-start(bf16[8,128,256]{2,1,0:T(8,128)(2,1)} %read_out.1), calls=%async_computation.2 | async-start | bytes 1048576 | tf_op jit(solution)/shard_map/all_to_all | solution.py:411

commit v4 on v3

--- a/solution.py
+++ b/solution.py
@@ -109,40 +109,24 @@
     return copies
 
 
-def masks_of(marks, width):
-    trials = marks.shape[0]
-    marks = marks[:, :width].astype(jnp.int32)
-    marks = jnp.broadcast_to(marks[:, None, :], (trials, TRIAL, width)).reshape(trials * TRIAL, width)
-    return marks
-
-
-def pick(leaf, marks, count):
-    level = 0
-    stack = []
-    for index in range(count):
-        node = leaf(index)
-        level = 0
-        while stack and stack[-1][0] == level:
-            node = jnp.where((marks & (1 << level)) != 0, node, stack.pop()[1])
-            level += 1
-        stack.append((level, node))
-    return stack[0][1]
+def spread(rows, marks, count):
+    trials, width = marks.shape
+    marks = jnp.broadcast_to(marks[:, None, :], (trials, TRIAL, width)).reshape(trials * TRIAL, width).astype(bf16)
+    nothing = jnp.zeros_like(rows)
+    return jnp.concatenate([jnp.where(marks == number, rows, nothing) for number in range(count)], 1)
 
 
 def project(rows_ref, start, blocks, weight):
     width = 2 * CHANS
-    rows = rows_ref[pl.ds(start, blocks), :BLOCK, :].reshape(blocks * BLOCK, rows_ref.shape[2])
-    marks = rows_ref[pl.ds(start, blocks), BLOCK:, :].astype(f32).reshape(blocks * BLOCK // TRIAL, rows_ref.shape[2])
-    marks = masks_of(marks, width)
-    products = {}
-
-    def leaf(slot):
-        if slot % 2 == 0:
-            products[0] = jnp.dot(rows, weight[slot // 2], preferred_element_type=f32)
-            return products[0][:, :width]
-        return products[0][:, width:]
-
-    chosen = pick(leaf, marks, 2 * weight.shape[0])
+    in_chans = rows_ref.shape[2]
+    rows = rows_ref[pl.ds(start, blocks), :BLOCK, :].reshape(blocks * BLOCK, in_chans)
+    marks = rows_ref[pl.ds(start, blocks), BLOCK:, :].astype(f32).reshape(blocks * BLOCK // TRIAL, in_chans)
+    wide = spread(rows, jnp.floor(marks * 0.5), weight.shape[0])
+    product = jnp.dot(wide, weight[...].reshape(-1, 2 * width), preferred_element_type=f32)
+    odd = (marks - 2 * jnp.floor(marks * 0.5))[:, :width]
+    trials = odd.shape[0]
+    odd = jnp.broadcast_to(odd[:, None, :], (trials, TRIAL, width)).reshape(trials * TRIAL, width)
+    chosen = jnp.where(odd > 0.5, product[:, width:], product[:, :width])
     return [chosen[i * BLOCK : (i + 1) * BLOCK].T.astype(bf16) for i in range(blocks)]
 
 
@@ -156,25 +140,24 @@
 
 
 def forward_kernel(place_ref, taps_ref, gain_ref, twist_ref, filter_hbm, own_hbm, other_hbm, *rest):
-    chunk_hbms = rest[: Z + 1]
-    table_hbms = rest[Z + 1 : Z + 5]
-    gated_ref, gate_ref, spectrum_ref, both, rows, weight, spectra, *rest = rest[Z + 5 :]
+    chunk_hbms = rest[:Z]
+    table_hbms = rest[Z : Z + 4]
+    gated_ref, gate_ref, spectrum_ref, both, rows, weight, spectra, *rest = rest[Z + 4 :]
     tables = rest[:4]
     weight_sems, row_sems, sems = rest[4:]
-    half = Y // 2
     width = 2 * CHANS
     place = lambda group, slot: (pl.ds(0, width), weight.at[group, :, pl.ds(slot * width, width)])
     loads = weight_copies(place_ref, (own_hbm, other_hbm), place, weight_sems)
-    for index, chunk in enumerate(chunk_hbms[: Z - 1]):
-        loads.append(pltpu.make_async_copy(chunk, rows.at[pl.ds(index * Y, Y)], row_sems.at[index]))
-    for index, chunk in enumerate(chunk_hbms[Z - 1 :]):
-        target = rows.at[pl.ds((Z - 1) * Y + index * half, half)]
-        loads.append(pltpu.make_async_copy(chunk, target, row_sems.at[Z - 1 + index]))
+    chunks = []
+    for index, chunk in enumerate(chunk_hbms):
+        chunks.append(pltpu.make_async_copy(chunk, rows.at[pl.ds(index * Y, Y)], row_sems.at[index]))
     pairs = [(filter_hbm, spectra)] + list(zip(table_hbms, tables))
     others = [pltpu.make_async_copy(source, target, sems.at[index]) for index, (source, target) in enumerate(pairs)]
     start_all(loads)
+    start_all(chunks)
     start_all(others)
     wait_all(loads)
+    wait_all(chunks)
 
     def read_in(index, carry):
         blocks = project(rows, index * Y, Y, weight)
@@ -224,7 +207,7 @@
     lax.fori_loop(0, GROUPS // 2, step, 0)
 
 
-def gradient_kernel(grad_ref, gate_ref, spectrum_ref, first_ref, second_ref, back_second_ref, back_first_ref, twist_ref, out_ref):
+def gradient_kernel(place_ref, grad_ref, gate_ref, spectrum_ref, first_ref, second_ref, back_second_ref, back_first_ref, twist_ref, out_ref):
     cosine, sine = twists_of(twist_ref)
     count = BLOCKS * LANE8
     products = (grad_ref[...].astype(f32) * gate_ref[...].astype(f32)).astype(bf16).astype(f32)
@@ -239,7 +222,7 @@
     for half in range(2):
         lanes = slice(half * BLOCK, (half + 1) * BLOCK)
         both.append(jnp.concatenate([result[i * LANE8 : (i + 1) * LANE8, lanes] for i in range(BLOCKS)], 1))
-    out_ref[...] = jnp.concatenate(both, 0).astype(bf16)
+    out_ref[0] = jnp.concatenate(both, 0).astype(bf16)
 
 
 def read_out_kernel(place_ref, own_hbm, other_hbm, rows_hbm, *rest):
@@ -259,9 +242,8 @@
         places = [lax.rem(place_ref[0] + z_step_of(quad * 4 + index), Z) for index in range(4)]
         rows = jnp.concatenate([rows_all[:, block, :, :].reshape(inner, BLOCK).T for block in places], 0)
         marks = marks_all[pl.ds(quad * 4, 4)].astype(f32).reshape(4 * BLOCK // TRIAL, width)
-        marks = masks_of(marks, width)
-        leaf = lambda slot: jnp.dot(rows, weight[slot], preferred_element_type=f32)
-        chosen = pick(leaf, marks, slots)
+        wide = spread(rows, marks, slots)
+        chosen = jnp.dot(wide, weight[...].reshape(slots * inner, width), preferred_element_type=f32)
         for index, block in enumerate(places):
             out_ref[block] = chosen[index * BLOCK : (index + 1) * BLOCK].astype(bf16)
         return carry
@@ -291,7 +273,6 @@
 
 
 def local(spikes, session_of_bin, session_slot, readin_weight, short_kernel, long_filter, skip_gain, readout_weight, out_grad):
-    groups = lax.axis_size("grp")
     in_chans = spikes.shape[2]
     model_width = short_kernel.shape[1]
     place = lax.axis_index("seq")
@@ -333,24 +314,25 @@
         cost_estimate=pl.CostEstimate(flops=work, bytes_accessed=4 << 20, transcendentals=0),
         name="filter_transform",
     )(long_filter, first, second, twists)
-    turned = out_grad[0].T.reshape(BLOCKS, CHANS, BLOCK)
 
     right, left, own_right, own_left, filter_spectrum = lax.optimization_barrier((right, left, own_right, own_left, filter_spectrum))
     right, left = along_z(right, 1), along_z(left, -1)
     chunks += [right, left]
     far = jnp.concatenate([along_x(own_right[:1], 1), along_x(own_left[1:], -1)], 0)
-    right, left, far, turned = lax.optimization_barrier((right, left, far, turned))
+    right, left, far = lax.optimization_barrier((right, left, far))
     right, left = along_z(right, 1), along_z(left, -1)
     chunks += [right, left]
-    grads = lax.all_to_all(turned, "seq", split_axis=0, concat_axis=0, tiled=True)
     weights = jnp.stack([own, own_right, own_left, far])
     weights_other = other_core(weights)
     taps = lax.dynamic_slice_in_dim(short_kernel, place * CHANS, CHANS, 1)
     taps = jnp.broadcast_to(taps[:, :, None], (short_kernel.shape[0], CHANS, BLOCK))
     gains = jnp.broadcast_to(skip_gain[:, None], (CHANS, BLOCK))
-    right, left, weights_other, taps, gains, coords = lax.optimization_barrier((right, left, weights_other, taps, gains, coords))
-    last_right, last_left = along_z(right[: Y // 2], 1), along_z(left[Y // 2 :], -1)
-    last_right, last_left, grads = lax.optimization_barrier((last_right, last_left, grads))
+    right, left, weights_other = lax.optimization_barrier((right, left, weights_other))
+    turned = out_grad[0].T.reshape(BLOCKS, CHANS, BLOCK)
+    ready = (along_z(right, 1), taps, gains, coords, turned)
+    right, taps, gains, coords, turned = lax.optimization_barrier(ready)
+    chunks.append(right)
+    grads = lax.all_to_all(turned, "seq", split_axis=0, concat_axis=0, tiled=True)
 
     tables = (first, second, back_second, back_first)
     slot_count = session_slot.shape[0]
@@ -361,7 +343,7 @@
             jax.ShapeDtypeStruct(plane, bf16),
             spectrum_shape,
         ),
-        in_specs=[scalar] + whole(3) + [hbm] * (3 + Z + 1 + 4),
+        in_specs=[scalar] + whole(3) + [hbm] * (3 + Z + 4),
         out_specs=tuple(whole(3)),
         scratch_shapes=[
             pltpu.VMEM((BLOCKS, 2 * CHANS, BLOCK), bf16),
@@ -370,28 +352,35 @@
             pltpu.VMEM(spectrum_shape.shape, f32),
         ]
         + [pltpu.VMEM(table.shape, bf16) for table in tables]
-        + [pltpu.SemaphoreType.DMA((count,)) for count in (slot_count, Z + 1, 5)],
+        + [pltpu.SemaphoreType.DMA((count,)) for count in (slot_count, Z, 5)],
         compiler_params=params,
         cost_estimate=pl.CostEstimate(flops=4 * work, bytes_accessed=8 << 20, transcendentals=0),
         name="long_convolution",
-    )(coords, taps, gains, twists, filter_spectrum, weights, weights_other, *chunks, last_right, last_left, *tables)
+    )(coords, taps, gains, twists, filter_spectrum, weights, weights_other, *chunks, *tables)
 
     arrived = lax.all_to_all(gated, "seq", split_axis=0, concat_axis=0, tiled=True, axis_index_groups=y_groups)
-    own_grad = pl.pallas_call(
+    half = CHANS // CORES
+    fixed = lambda table: pl.BlockSpec(table.shape, lambda i, place, rank=table.ndim: (0,) * rank)
+    steps = half // pair
+    halves = pl.pallas_call(
         gradient_kernel,
-        out_shape=jax.ShapeDtypeStruct((CHANS, LENGTH), bf16),
-        grid=(GROUPS // 2,),
-        in_specs=[pl.BlockSpec((BLOCKS, pair, BLOCK), lambda i: (0, i, 0))] * 2
-        + [pl.BlockSpec((2,) + spectrum_shape.shape[1:], lambda i: (i, 0, 0))]
-        + [same(table) for table in tables + (twists,)],
-        out_specs=pl.BlockSpec((pair, LENGTH), lambda i: (i, 0)),
+        out_shape=jax.ShapeDtypeStruct((CORES, half, LENGTH), bf16),
+        grid_spec=pltpu.PrefetchScalarGridSpec(
+            num_scalar_prefetch=1,
+            grid=(GROUPS // 2,),
+            in_specs=[pl.BlockSpec((BLOCKS, pair, BLOCK), lambda i, place: (0, i, 0))] * 2
+            + [pl.BlockSpec((2,) + spectrum_shape.shape[1:], lambda i, place: (i, 0, 0))]
+            + [fixed(table) for table in tables + (twists,)],
+            out_specs=pl.BlockSpec((1, pair, LENGTH), lambda i, place: (lax.rem(i // steps + place[3], 2), i % steps, 0)),
+        ),
         compiler_params=params,
         cost_estimate=pl.CostEstimate(flops=2 * work, bytes_accessed=4 << 20, transcendentals=0),
         name="filter_gradient",
-    )(grads, gates, spectrum, *tables, twists)
-    shares = lax.all_to_all(own_grad.reshape(groups, CHANS // groups, LENGTH), "grp", split_axis=0, concat_axis=0, tiled=True)
-    share = jnp.sum(shares.astype(f32), 0).astype(bf16)
-    filter_grad = lax.all_gather(share, "grp", axis=0, tiled=True).astype(f32)
+    )(coords, grads, gates, spectrum, *tables, twists)
+    came, arrived = lax.optimization_barrier((other_core(halves[1]), arrived))
+    plus = lambda *terms: sum(term.astype(f32) for term in terms).astype(bf16)
+    total = plus(halves[0], came)
+    cames = [along_x(total, step) for step in (1, -1, 2)]
     partial = pl.pallas_call(
         read_out_kernel,
         out_shape=jax.ShapeDtypeStruct((Z, BLOCK, in_chans), bf16),
@@ -407,7 +396,12 @@
         compiler_params=params,
         cost_estimate=pl.CostEstimate(flops=2 * 512 * 512 * 4096, bytes_accessed=6 << 20, transcendentals=0),
         name="read_out",
-    )(coords, weights, weights_other, arrived, *chunks, last_right)
+    )(coords, weights, weights_other, arrived, *chunks)
+    cames, partial = lax.optimization_barrier((cames, partial))
+    total = plus(total, *cames)
+    theirs = other_core(total)
+    lower = coords[3] == 0
+    filter_grad = jnp.concatenate([jnp.where(lower, total, theirs), jnp.where(lower, theirs, total)], 0).astype(f32)
     pieces = lax.all_to_all(partial, "seq", split_axis=0, concat_axis=0, tiled=True, axis_index_groups=z_groups)
     denoised = jnp.sum(pieces.astype(f32), 0).astype(bf16)
     return denoised[None], filter_grad

time: 149 us -> 146 us (0.980)
  blocking collectives: 13.1 us -> 0 us
  waiting for transfers between devices: 35.3 us -> 42.7 us
  starting transfers between devices: 46.9 us -> 49.5 us
  local copies, waits for them, and re-layouts: 9.17 us -> 11 us
  other arithmetic: 8.64 us -> 7.14 us
    all_to_all x1, waiting for transfers between devices: 3.07 us -> 17.1 us  [local(): lax.all_to_all(partial, 'seq', split_axis=0, concat_axis=0, tiled=True, a...]
    all_gather x1 -> x0, blocking collectives: 13.1 us -> none  [local(): filter_grad = lax.all_gather(share, 'grp', axis=0, tiled=True).astype(f32)]
    ppermute x8 -> x7, waiting for transfers between devices: 25.6 us -> 14.8 us  [along_z(): lax.ppermute(value, 'seq', [(z * Y + y, (z + step) % Z * Y + y) for z in...]
    ppermute x4 -> x7, waiting for transfers between devices: 1.76 us -> 9 us  [along_x(): return lax.ppermute(value, 'grp', pairs)]
    ppermute x4 -> x7, starting transfers between devices: 5.71 us -> 10.3 us  [along_x(): return lax.ppermute(value, 'grp', pairs)]
    all_to_all x1 -> x0, starting transfers between devices: 4.51 us -> none  [local(): lax.all_to_all(own_grad.reshape(groups, CHANS // groups, LENGTH), 'grp',...]
    all_to_all x1 -> x0, waiting for transfers between devices: 4.11 us -> none  [local(): lax.all_to_all(own_grad.reshape(groups, CHANS // groups, LENGTH), 'grp',...]
    all_to_all x1, starting transfers between devices: 5.89 us -> 8.46 us  [local(): lax.all_to_all(turned, 'seq', split_axis=0, concat_axis=0, tiled=True)]
  transfers between devices with their start and end apart: 20 -> 23, of which waited for: 9 -> 11; matrix products, arithmetic and copies ran while one was open for 7% -> 5% of each run, Pallas kernels for 11% -> 23%
where the time goes in v4:
time: 146 us; the launch traced here: 145 us
  starting transfers between devices  49.5 us (34%)
  waiting for transfers between devices  42.7 us (29%)
  Pallas kernels  33.1 us (23%)
  local copies, waits for them, and re-layouts  11 us (8%)
  other arithmetic  7.14 us (5%)
  between operations  1.56 us (1%)
    all_to_all x1, waiting for transfers between devices, local(): lax.all_to_all(partial, 'seq', split_axis=0, concat_axis=0, tiled=True, a...  17.1 us
    pallas_call x1, Pallas kernels, local(): pl.pallas_call(forward_kernel, out_shape=(jax.ShapeDtypeStruct((Y, Z, CHA...  15.7 us
    ppermute x7, starting transfers between devices, along_z(): lax.ppermute(value, 'seq', [(z * Y + y, (z + step) % Z * Y + y) for z in...  15 us
    ppermute x7, waiting for transfers between devices, along_z(): lax.ppermute(value, 'seq', [(z * Y + y, (z + step) % Z * Y + y) for z in...  14.8 us
    ppermute x7, starting transfers between devices, along_x(): return lax.ppermute(value, 'grp', pairs)  10.3 us
    ppermute x7, waiting for transfers between devices, along_x(): return lax.ppermute(value, 'grp', pairs)  9 us
    all_to_all x1, starting transfers between devices, local(): lax.all_to_all(turned, 'seq', split_axis=0, concat_axis=0, tiled=True)  8.46 us
    pallas_call x1, Pallas kernels, local(): pl.pallas_call(gradient_kernel, out_shape=jax.ShapeDtypeStruct((CORES, ha...  6.63 us
  transfers between devices with their start and end apart: 23, of which 11 were waited for; matrix products, arithmetic and copies ran while one was open for 5% of the time, Pallas kernels for 23%

profile of v4, /device:TPU:8, one launch (start us, length us, event | category | flops | bytes accessed | tf_op | source)
XLA Modules:
  0.0 145.0 jit_solution(4462830407298590203)
XLA Ops:
  3.3 2.4 %collective-permute-start.2 = (bf16[136,256]{1,0:T(8,128)(2,1)S(1)}, bf16[136,256]{1,0:T(8,128)(2,1)S(1)}, u32[]{:S(2)}, u32[]{:S(2)}) collective-permute-start(bf16[136,256]{1,0:T(8,128)(2,1)S(1)} %get-tuple-element.55), channel_id=1, source_target_pairs={{0,2},{1,3},{2,0},{3,1},{4,6},{5,7},{6,4},{7,5},{8,10},{9,11},{10,... | collective-permute-start | bytes 208904 | tf_op jit(solution)/shard_map/ppermute | solution.py:255
  5.7 1.3 collective-permute-start.1
  7.8 1.1 constant_dynamic-slice_fusion.3
  9.0 1.6 %collective-permute-start.5 = (bf16[2,256,384]{2,1,0:T(8,128)(2,1)S(1)}, bf16[2,256,384]{2,1,0:T(8,128)(2,1)S(1)}, u32[]{:S(2)}, u32[]{:S(2)}) collective-permute-start(bf16[2,256,384]{2,1,0:T(8,128)(2,1)S(1)} %pad_maximum_fusion.1), channel_id=1, source_target_pairs={{0,64},{32,96},{64,128},{96,160},{128,192},{160,224},{192,0},{224,... | collective-permute-start | bytes 1179656 | tf_op jit(solution)/shard_map/ppermute | solution.py:264
  10.6 1.7 %collective-permute-start.6 = (bf16[2,256,384]{2,1,0:T(8,128)(2,1)S(1)}, bf16[2,256,384]{2,1,0:T(8,128)(2,1)}, u32[]{:S(2)}, u32[]{:S(2)}) collective-permute-start(bf16[2,256,384]{2,1,0:T(8,128)(2,1)S(1)} %pad_maximum_fusion.1), channel_id=1, source_target_pairs={{0,192},{32,224},{64,0},{96,32},{128,64},{160,96},{192,128},{224,1... | collective-permute-start | bytes 1179656 | tf_op jit(solution)/shard_map/ppermute | solution.py:264
  12.4 2.0 %collective-permute-start.3 = (bf16[4,136,256]{2,1,0:T(8,128)(2,1)S(1)}, bf16[4,136,256]{2,1,0:T(8,128)(2,1)S(1)}, u32[]{:S(2)}, u32[]{:S(2)}) collective-permute-start(bf16[4,136,256]{2,1,0:T(8,128)(2,1)S(1)} %pad_maximum_fusion.3.rest_0_), channel_id=1, source_target_pairs={{0,4},{1,5},{2,6},{3,7},{4,8},{5,9},{6,10},{7,11},{8,12},{9,13},{1... | collective-permute-start | bytes 835592 | tf_op jit(solution)/shard_map/ppermute | solution.py:259
  14.4 4.0 %collective-permute-start.4 = (bf16[4,136,256]{2,1,0:T(8,128)(2,1)S(1)}, bf16[4,136,256]{2,1,0:T(8,128)(2,1)}, u32[]{:S(2)}, u32[]{:S(2)}) collective-permute-start(bf16[4,136,256]{2,1,0:T(8,128)(2,1)S(1)} %pad_maximum_fusion.3.rest_0_), channel_id=1, source_target_pairs={{0,28},{1,29},{2,30},{3,31},{4,0},{5,1},{6,2},{7,3},{8,4},{9,5},{1... | collective-permute-start | bytes 835592 | tf_op jit(solution)/shard_map/ppermute | solution.py:259
  18.4 4.6 %filter_transform.1.filter_hbm = f32[8,256,256]{2,1,0:T(8,128)} custom-call(f32[64,4096]{1,0:T(8,128)} %filter_ref.1, bf16[512,256]{1,0:T(8,128)(2,1)} %constant.79.clone.first_ref.rest_8_, bf16[256,256]{1,0:T(8,128)(2,1)} %constant.80.clone.second_ref.rest_9_, f32[2,32,128]{2,1,0:T(8,128)} %constant.83.clone.twist_ref), custom_call_target="tpu_custom_call" | custom-call | flops 536870912 | bytes 4194304 | tf_op jit(solution)/shard_map/filter_transform/pallas_call | solution.py:307
  24.7 2.2 %collective-permute-start.10 = (bf16[1,256,384]{2,1,0:T(8,128)(2,1)S(1)}, bf16[1,256,384]{2,1,0:T(8,128)(2,1)S(1)}, u32[]{:S(2)}, u32[]{:S(2)}) collective-permute-start(bf16[1,256,384]{2,1,0:T(8,128)(2,1)S(1)} %slice.20), channel_id=1, source_target_pairs={{0,192},{32,224},{64,0},{96,32},{128,64},{160,96},{192,128},{224,1... | collective-permute-start | bytes 589832 | tf_op jit(solution)/shard_map/ppermute | solution.py:264
  27.1 3.4 %collective-permute-start.8 = (bf16[4,136,256]{2,1,0:T(8,128)(2,1)}, bf16[4,136,256]{2,1,0:T(8,128)(2,1)S(1)}, u32[]{:S(2)}, u32[]{:S(2)}) collective-permute-start(bf16[4,136,256]{2,1,0:T(8,128)(2,1)} %collective-permute-done.4.rest_2_), channel_id=1, source_target_pairs={{0,28},{1,29},{2,30},{3,31},{4,0},{5,1},{6,2},{7,3},{8,4},{9,5},{1... | collective-permute-start | bytes 835592 | tf_op jit(solution)/shard_map/ppermute | solution.py:259
  30.7 3.2 %collective-permute-done.9 = bf16[1,256,384]{2,1,0:T(8,128)(2,1)S(1)} collective-permute-done((bf16[1,256,384]{2,1,0:T(8,128)(2,1)S(1)}, bf16[1,256,384]{2,1,0:T(8,128)(2,1)S(1)}, u32[]{:S(2)}, u32[]{:S(2)}) %collective-permute-start.9) | collective-permute-done | bytes 196640 | tf_op jit(solution)/shard_map/ppermute | solution.py:264
  34.0 1.1 collective-permute-done.7.rest_3_
  35.0 1.5 %pad_maximum_fusion.own_hbm = bf16[4,2,256,384]{3,2,1,0:T(8,128)(2,1)S(1)} fusion(bf16[1,2,256,384]{3,2,1,0:T(8,128)(2,1)S(1)} %bitcast.29, bf16[1,2,256,384]{3,2,1,0:T(8,128)(2,1)} %bitcast.8, bf16[1,2,256,384]{3,2,1,0:T(8,128)(2,1)S(1)} %bitcast.30, bf16[1,2,256,384]{3,2,1,0:T(8,128)(2,1)S(1)} %fusion.2), kind=kLoop, calls=%fused_computation | loop fusion | flops 2359296 | bytes 3145728 | tf_op jit(solution)/shard_map/stack | solution.py:325
  36.5 1.2 copy-done.1
  37.7 2.4 %collective-permute-start.11 = (bf16[4,136,256]{2,1,0:T(8,128)(2,1)S(1)}, bf16[4,136,256]{2,1,0:T(8,128)(2,1)S(1)}, u32[]{:S(2)}, u32[]{:S(2)}) collective-permute-start(bf16[4,136,256]{2,1,0:T(8,128)(2,1)S(1)} %collective-permute-done.7.rest_3_), channel_id=1, source_target_pairs={{0,4},{1,5},{2,6},{3,7},{4,8},{5,9},{6,10},{7,11},{8,12},{9,13},{1... | collective-permute-start | bytes 835592 | tf_op jit(solution)/shard_map/ppermute | solution.py:259
  40.1 1.1 collective-permute-start.12
  41.2 7.2 %collective-permute-done.11.rest_5_ = bf16[4,136,256]{2,1,0:T(8,128)(2,1)S(1)} collective-permute-done((bf16[4,136,256]{2,1,0:T(8,128)(2,1)S(1)}, bf16[4,136,256]{2,1,0:T(8,128)(2,1)S(1)}, u32[]{:S(2)}, u32[]{:S(2)}) %collective-permute-start.11) | collective-permute-done | bytes 278560 | tf_op jit(solution)/shard_map/ppermute | solution.py:259
  49.9 1.1 copy-done.3
  51.0 1.9 %collective-permute-start.14 = (bf16[4,136,256]{2,1,0:T(8,128)(2,1)S(1)}, bf16[4,136,256]{2,1,0:T(8,128)(2,1)S(1)}, u32[]{:S(2)}, u32[]{:S(2)}) collective-permute-start(bf16[4,136,256]{2,1,0:T(8,128)(2,1)S(1)} %collective-permute-done.11.rest_5_), channel_id=1, source_target_pairs={{0,4},{1,5},{2,6},{3,7},{4,8},{5,9},{6,10},{7,11},{8,12},{9,13},{1... | collective-permute-start | bytes 835592 | tf_op jit(solution)/shard_map/ppermute | solution.py:259
  55.4 5.2 %collective-permute-done.14.rest_7_ = bf16[4,136,256]{2,1,0:T(8,128)(2,1)S(1)} collective-permute-done((bf16[4,136,256]{2,1,0:T(8,128)(2,1)S(1)}, bf16[4,136,256]{2,1,0:T(8,128)(2,1)S(1)}, u32[]{:S(2)}, u32[]{:S(2)}) %collective-permute-start.14) | collective-permute-done | bytes 278560 | tf_op jit(solution)/shard_map/ppermute | solution.py:259
  62.0 8.5 %all-to-all-start = ((bf16[32,64,128]{2,1,0:T(8,128)(2,1)}), bf16[32,64,128]{2,1,0:T(8,128)(2,1)S(1)}, u32[]{:S(2)}, u32[]{:S(2)}) async-start(bf16[32,64,128]{2,1,0:T(8,128)(2,1)} %bitcast.16), calls=%async_computation | async-start | bytes 1048576 | tf_op jit(solution)/shard_map/all_to_all | solution.py:335
  70.5 15.7 %long_convolution.1 = (bf16[4,8,64,128]{3,2,1,0:T(8,128)(2,1)}, bf16[32,64,128]{2,1,0:T(8,128)(2,1)}, f32[8,256,256]{2,1,0:T(8,128)}) custom-call(s32[4]{0:T(128)} %pad_add_fusion.place_ref, f32[3,64,128]{2,1,0:T(8,128)} %broadcast_in_dim.38.taps_ref, f32[64,128]{1,0:T(8,128)} %broadcast_in_dim.39.gain_ref, f32[2,32,128]{2,1,0:T(8,128)} %constant.83.clone.twist_ref, ...), custom_call_target="tpu_custom_call" | custom-call | flops 2147483648 | bytes 8388608 | tf_op jit(solution)/shard_map/long_convolution/pallas_call | solution.py:339
  86.5 4.8 %all-to-all-start.1 = ((bf16[4,8,64,128]{3,2,1,0:T(8,128)(2,1)}), bf16[4,8,64,128]{3,2,1,0:T(8,128)(2,1)S(1)}, u32[]{:S(2)}, u32[]{:S(2)}) async-start(bf16[4,8,64,128]{3,2,1,0:T(8,128)(2,1)} %get-tuple-element.43), calls=%async_computation.1 | async-start | bytes 1048576 | tf_op jit(solution)/shard_map/all_to_all | solution.py:361
  91.3 6.6 %filter_gradient.1 = bf16[2,32,4096]{2,1,0:T(8,128)(2,1)} custom-call(s32[4]{0:T(128)} %pad_add_fusion.place_ref, bf16[32,64,128]{2,1,0:T(8,128)(2,1)} %copy-done.2, bf16[32,64,128]{2,1,0:T(8,128)(2,1)} %get-tuple-element.41.gate_ref, f32[8,256,256]{2,1,0:T(8,128)} %get-tuple-element.42.spectrum_ref, bf16[512,256]{1,0:T(8,128)(2,1)} %constant.79.clone.first_ref.rest_8_, ...), custom_call_target="tpu_custom_call" | custom-call | flops 1073741824 | bytes 4194304 | tf_op jit(solution)/shard_map/filter_gradient/pallas_call | solution.py:365
  99.0 1.5 %collective-permute-done.15 = bf16[32,4096]{1,0:T(8,128)(2,1)S(1)} collective-permute-done((bf16[32,4096]{1,0:T(8,128)(2,1)S(1)}, bf16[32,4096]{1,0:T(8,128)(2,1)S(1)}, u32[]{:S(2)}, u32[]{:S(2)}) %collective-permute-start.15) | collective-permute-done | bytes 262176 | tf_op jit(solution)/shard_map/ppermute | solution.py:268
  102.1 2.8 %collective-permute-start.17 = (bf16[32,4096]{1,0:T(8,128)(2,1)S(1)}, bf16[32,4096]{1,0:T(8,128)(2,1)S(1)}, u32[]{:S(2)}, u32[]{:S(2)}) collective-permute-start(bf16[32,4096]{1,0:T(8,128)(2,1)S(1)} %fusion), channel_id=1, source_target_pairs={{0,192},{32,224},{64,0},{96,32},{128,64},{160,96},{192,128},{224,1... | collective-permute-start | bytes 786440 | tf_op jit(solution)/shard_map/ppermute | solution.py:264
  104.9 1.4 collective-permute-start.18
  106.3 6.1 %read_out.1 = bf16[8,128,256]{2,1,0:T(8,128)(2,1)} custom-call(s32[4]{0:T(128)} %pad_add_fusion.place_ref, bf16[4,2,256,384]{3,2,1,0:T(8,128)(2,1)} %copy-done.1, bf16[4,2,256,384]{3,2,1,0:T(8,128)(2,1)} %copy-done.3, bf16[4,8,64,128]{3,2,1,0:T(8,128)(2,1)} %copy-done.6, bf16[4,136,256]{2,1,0:T(8,128)(2,1)} %copy-done.4, bf16[4,136,256]{2,1,0:T(8,128)(2,1)} %copy-done.7, ...), custom_call_target="tpu_custom_call" | custom-call | flops 2147483648 | bytes 6291456 | tf_op jit(solution)/shard_map/read_out/pallas_call | solution.py:384
  112.4 4.0 %collective-permute-done.17 = bf16[32,4096]{1,0:T(8,128)(2,1)S(1)} collective-permute-done((bf16[32,4096]{1,0:T(8,128)(2,1)S(1)}, bf16[32,4096]{1,0:T(8,128)(2,1)S(1)}, u32[]{:S(2)}, u32[]{:S(2)}) %collective-permute-start.17) | collective-permute-done | bytes 262176 | tf_op jit(solution)/shard_map/ppermute | solution.py:264
  116.4 1.8 %collective-permute-done.18 = bf16[32,4096]{1,0:T(8,128)(2,1)S(1)} collective-permute-done((bf16[32,4096]{1,0:T(8,128)(2,1)S(1)}, bf16[32,4096]{1,0:T(8,128)(2,1)S(1)}, u32[]{:S(2)}, u32[]{:S(2)}) %collective-permute-start.18) | collective-permute-done | bytes 262176 | tf_op jit(solution)/shard_map/ppermute | solution.py:264
  119.7 6.4 %all-to-all-start.2 = ((bf16[8,128,256]{2,1,0:T(8,128)(2,1)}), bf16[8,128,256]{2,1,0:T(8,128)(2,1)S(1)}, u32[]{:S(2)}, u32[]{:S(2)}) async-start(bf16[8,128,256]{2,1,0:T(8,128)(2,1)} %read_out.1), calls=%async_computation.2 | async-start | bytes 1048576 | tf_op jit(solution)/shard_map/all_to_all | solution.py:405
  127.2 17.1 %all-to-all-done.2 = bf16[8,128,256]{2,1,0:T(8,128)(2,1)S(1)} async-done(((bf16[8,128,256]{2,1,0:T(8,128)(2,1)}), bf16[8,128,256]{2,1,0:T(8,128)(2,1)S(1)}, u32[]{:S(2)}, u32[]{:S(2)}) %all-to-all-start.2) | async-done | bytes 524320 | tf_op jit(solution)/shard_map/all_to_all | solution.py:405
  (74 shorter events, 16.5 us)
Async XLA Ops:
  0.6 7.1 %copy-start = (bf16[2,2048,256]{2,1,0:T(8,128)(2,1)S(1)}, bf16[2,2048,256]{2,1,0:T(8,128)(2,1)}, u32[]{:S(2)}) copy-start(bf16[2,2048,256]{2,1,0:T(8,128)(2,1)} %param.21) | copy-start | bytes 6291460
  3.3 9.0 %collective-permute-start.2 = (bf16[136,256]{1,0:T(8,128)(2,1)S(1)}, bf16[136,256]{1,0:T(8,128)(2,1)S(1)}, u32[]{:S(2)}, u32[]{:S(2)}) collective-permute-start(bf16[136,256]{1,0:T(8,128)(2,1)S(1)} %get-tuple-element.55), channel_id=1, source_target_pairs={{0,2},{1,3},{2,0},{3,1},{4,6},{5,7},{6,4},{7,5},{8,10},{9,11},{10,... | collective-permute-start | bytes 208904 | tf_op jit(solution)/shard_map/ppermute | solution.py:255
  5.7 6.6 %collective-permute-start.1 = (bf16[136,256]{1,0:T(8,128)(2,1)S(1)}, bf16[136,256]{1,0:T(8,128)(2,1)S(1)}, u32[]{:S(2)}, u32[]{:S(2)}) collective-permute-start(bf16[136,256]{1,0:T(8,128)(2,1)S(1)} %get-tuple-element.55), channel_id=1, source_target_pairs={{0,3},{1,0},{2,1},{3,2},{4,7},{5,4},{6,5},{7,6},{8,11},{9,8},{10,9... | collective-permute-start | bytes 208904 | tf_op jit(solution)/shard_map/ppermute | solution.py:255
  7.1 5.3 %collective-permute-start = (bf16[136,256]{1,0:T(8,128)(2,1)S(1)}, bf16[136,256]{1,0:T(8,128)(2,1)S(1)}, u32[]{:S(2)}, u32[]{:S(2)}) collective-permute-start(bf16[136,256]{1,0:T(8,128)(2,1)S(1)} %get-tuple-element.55), channel_id=1, source_target_pairs={{0,1},{1,2},{2,3},{3,0},{4,5},{5,6},{6,7},{7,4},{8,9},{9,10},{10,1... | collective-permute-start | bytes 208904 | tf_op jit(solution)/shard_map/ppermute | solution.py:255
  9.0 14.6 %collective-permute-start.5 = (bf16[2,256,384]{2,1,0:T(8,128)(2,1)S(1)}, bf16[2,256,384]{2,1,0:T(8,128)(2,1)S(1)}, u32[]{:S(2)}, u32[]{:S(2)}) collective-permute-start(bf16[2,256,384]{2,1,0:T(8,128)(2,1)S(1)} %pad_maximum_fusion.1), channel_id=1, source_target_pairs={{0,64},{32,96},{64,128},{96,160},{128,192},{160,224},{192,0},{224,... | collective-permute-start | bytes 1179656 | tf_op jit(solution)/shard_map/ppermute | solution.py:264
  10.6 13.0 %collective-permute-start.6 = (bf16[2,256,384]{2,1,0:T(8,128)(2,1)S(1)}, bf16[2,256,384]{2,1,0:T(8,128)(2,1)}, u32[]{:S(2)}, u32[]{:S(2)}) collective-permute-start(bf16[2,256,384]{2,1,0:T(8,128)(2,1)S(1)} %pad_maximum_fusion.1), channel_id=1, source_target_pairs={{0,192},{32,224},{64,0},{96,32},{128,64},{160,96},{192,128},{224,1... | collective-permute-start | bytes 1179656 | tf_op jit(solution)/shard_map/ppermute | solution.py:264
  12.4 10.6 %copy-start.4 = (bf16[4,136,256]{2,1,0:T(8,128)(2,1)}, bf16[4,136,256]{2,1,0:T(8,128)(2,1)S(1)}, u32[]{:S(2)}) copy-start(bf16[4,136,256]{2,1,0:T(8,128)(2,1)S(1)} %pad_maximum_fusion.3.rest_0_) | copy-start | bytes 835588
  12.4 11.2 %collective-permute-start.3 = (bf16[4,136,256]{2,1,0:T(8,128)(2,1)S(1)}, bf16[4,136,256]{2,1,0:T(8,128)(2,1)S(1)}, u32[]{:S(2)}, u32[]{:S(2)}) collective-permute-start(bf16[4,136,256]{2,1,0:T(8,128)(2,1)S(1)} %pad_maximum_fusion.3.rest_0_), channel_id=1, source_target_pairs={{0,4},{1,5},{2,6},{3,7},{4,8},{5,9},{6,10},{7,11},{8,12},{9,13},{1... | collective-permute-start | bytes 835592 | tf_op jit(solution)/shard_map/ppermute | solution.py:259
  14.4 9.2 %collective-permute-start.4 = (bf16[4,136,256]{2,1,0:T(8,128)(2,1)S(1)}, bf16[4,136,256]{2,1,0:T(8,128)(2,1)}, u32[]{:S(2)}, u32[]{:S(2)}) collective-permute-start(bf16[4,136,256]{2,1,0:T(8,128)(2,1)S(1)} %pad_maximum_fusion.3.rest_0_), channel_id=1, source_target_pairs={{0,28},{1,29},{2,30},{3,31},{4,0},{5,1},{6,2},{7,3},{8,4},{9,5},{1... | collective-permute-start | bytes 835592 | tf_op jit(solution)/shard_map/ppermute | solution.py:259
  23.6 12.9 %copy-start.7 = (bf16[4,136,256]{2,1,0:T(8,128)(2,1)}, bf16[4,136,256]{2,1,0:T(8,128)(2,1)S(1)}, u32[]{:S(2)}) copy-start(bf16[4,136,256]{2,1,0:T(8,128)(2,1)S(1)} %collective-permute-done.3.rest_1_) | copy-start | bytes 835588
  24.7 6.0 %collective-permute-start.10 = (bf16[1,256,384]{2,1,0:T(8,128)(2,1)S(1)}, bf16[1,256,384]{2,1,0:T(8,128)(2,1)S(1)}, u32[]{:S(2)}, u32[]{:S(2)}) collective-permute-start(bf16[1,256,384]{2,1,0:T(8,128)(2,1)S(1)} %slice.20), channel_id=1, source_target_pairs={{0,192},{32,224},{64,0},{96,32},{128,64},{160,96},{192,128},{224,1... | collective-permute-start | bytes 589832 | tf_op jit(solution)/shard_map/ppermute | solution.py:264
  26.9 7.0 %collective-permute-start.9 = (bf16[1,256,384]{2,1,0:T(8,128)(2,1)S(1)}, bf16[1,256,384]{2,1,0:T(8,128)(2,1)S(1)}, u32[]{:S(2)}, u32[]{:S(2)}) collective-permute-start(bf16[1,256,384]{2,1,0:T(8,128)(2,1)S(1)} %slice.19), channel_id=1, source_target_pairs={{0,64},{32,96},{64,128},{96,160},{128,192},{160,224},{192,0},{224,... | collective-permute-start | bytes 589832 | tf_op jit(solution)/shard_map/ppermute | solution.py:264
  27.0 8.0 %collective-permute-start.7 = (bf16[4,136,256]{2,1,0:T(8,128)(2,1)S(1)}, bf16[4,136,256]{2,1,0:T(8,128)(2,1)S(1)}, u32[]{:S(2)}, u32[]{:S(2)}) collective-permute-start(bf16[4,136,256]{2,1,0:T(8,128)(2,1)S(1)} %collective-permute-done.3.rest_1_), channel_id=1, source_target_pairs={{0,4},{1,5},{2,6},{3,7},{4,8},{5,9},{6,10},{7,11},{8,12},{9,13},{1... | collective-permute-start | bytes 835592 | tf_op jit(solution)/shard_map/ppermute | solution.py:259
  27.1 7.9 %collective-permute-start.8 = (bf16[4,136,256]{2,1,0:T(8,128)(2,1)}, bf16[4,136,256]{2,1,0:T(8,128)(2,1)S(1)}, u32[]{:S(2)}, u32[]{:S(2)}) collective-permute-start(bf16[4,136,256]{2,1,0:T(8,128)(2,1)} %collective-permute-done.4.rest_2_), channel_id=1, source_target_pairs={{0,28},{1,29},{2,30},{3,31},{4,0},{5,1},{6,2},{7,3},{8,4},{9,5},{1... | collective-permute-start | bytes 835592 | tf_op jit(solution)/shard_map/ppermute | solution.py:259
  35.0 5.1 %copy-start.9 = (bf16[4,136,256]{2,1,0:T(8,128)(2,1)}, bf16[4,136,256]{2,1,0:T(8,128)(2,1)S(1)}, u32[]{:S(2)}) copy-start(bf16[4,136,256]{2,1,0:T(8,128)(2,1)S(1)} %collective-permute-done.8.rest_4_) | copy-start | bytes 835588
  35.0 18.0 %copy-start.5 = (bf16[1,128,2048]{2,1,0:T(8,128)(2,1)S(1)}, bf16[1,128,2048]{2,1,0:T(8,128)(2,1)}, u32[]{:S(2)}) copy-start(bf16[1,128,2048]{2,1,0:T(8,128)(2,1)} %param.22) | copy-start | bytes 1572868
  35.0 26.3 %copy-start.14 = (f32[64]{0:T(128)S(1)}, f32[64]{0:T(128)}, u32[]{:S(2)}) copy-start(f32[64]{0:T(128)} %param.20) | copy-start | bytes 772
  37.7 11.5 %collective-permute-start.13 = (bf16[4,2,256,384]{3,2,1,0:T(8,128)(2,1)S(1)}, bf16[4,2,256,384]{3,2,1,0:T(8,128)(2,1)S(1)}, u32[]{:S(2)}, u32[]{:S(2)}) collective-permute-start(bf16[4,2,256,384]{3,2,1,0:T(8,128)(2,1)S(1)} %pad_maximum_fusion.own_hbm), channel_id=1, source_target_pairs={{0,32},{32,0},{64,96},{96,64},{128,160},{160,128},{192,224},{224,1... | collective-permute-start | bytes 4718600 | tf_op jit(solution)/shard_map/ppermute | solution.py:268
  37.7 10.8 %collective-permute-start.11 = (bf16[4,136,256]{2,1,0:T(8,128)(2,1)S(1)}, bf16[4,136,256]{2,1,0:T(8,128)(2,1)S(1)}, u32[]{:S(2)}, u32[]{:S(2)}) collective-permute-start(bf16[4,136,256]{2,1,0:T(8,128)(2,1)S(1)} %collective-permute-done.7.rest_3_), channel_id=1, source_target_pairs={{0,4},{1,5},{2,6},{3,7},{4,8},{5,9},{6,10},{7,11},{8,12},{9,13},{1... | collective-permute-start | bytes 835592 | tf_op jit(solution)/shard_map/ppermute | solution.py:259
  40.1 9.1 %collective-permute-start.12 = (bf16[4,136,256]{2,1,0:T(8,128)(2,1)S(1)}, bf16[4,136,256]{2,1,0:T(8,128)(2,1)S(1)}, u32[]{:S(2)}, u32[]{:S(2)}) collective-permute-start(bf16[4,136,256]{2,1,0:T(8,128)(2,1)S(1)} %collective-permute-done.8.rest_4_), channel_id=1, source_target_pairs={{0,28},{1,29},{2,30},{3,31},{4,0},{5,1},{6,2},{7,3},{8,4},{9,5},{1... | collective-permute-start | bytes 835592 | tf_op jit(solution)/shard_map/ppermute | solution.py:259
  48.4 22.0 %copy-start.10 = (bf16[4,136,256]{2,1,0:T(8,128)(2,1)}, bf16[4,136,256]{2,1,0:T(8,128)(2,1)S(1)}, u32[]{:S(2)}) copy-start(bf16[4,136,256]{2,1,0:T(8,128)(2,1)S(1)} %collective-permute-done.11.rest_5_) | copy-start | bytes 835588
  51.0 9.5 %collective-permute-start.14 = (bf16[4,136,256]{2,1,0:T(8,128)(2,1)S(1)}, bf16[4,136,256]{2,1,0:T(8,128)(2,1)S(1)}, u32[]{:S(2)}, u32[]{:S(2)}) collective-permute-start(bf16[4,136,256]{2,1,0:T(8,128)(2,1)S(1)} %collective-permute-done.11.rest_5_), channel_id=1, source_target_pairs={{0,4},{1,5},{2,6},{3,7},{4,8},{5,9},{6,10},{7,11},{8,12},{9,13},{1... | collective-permute-start | bytes 835592 | tf_op jit(solution)/shard_map/ppermute | solution.py:259
  62.0 24.5 %all-to-all-start = ((bf16[32,64,128]{2,1,0:T(8,128)(2,1)}), bf16[32,64,128]{2,1,0:T(8,128)(2,1)S(1)}, u32[]{:S(2)}, u32[]{:S(2)}) async-start(bf16[32,64,128]{2,1,0:T(8,128)(2,1)} %bitcast.16), calls=%async_computation | async-start | bytes 1048576 | tf_op jit(solution)/shard_map/all_to_all | solution.py:335
  86.5 12.5 %all-to-all-start.1 = ((bf16[4,8,64,128]{3,2,1,0:T(8,128)(2,1)}), bf16[4,8,64,128]{3,2,1,0:T(8,128)(2,1)S(1)}, u32[]{:S(2)}, u32[]{:S(2)}) async-start(bf16[4,8,64,128]{3,2,1,0:T(8,128)(2,1)} %get-tuple-element.43), calls=%async_computation.1 | async-start | bytes 1048576 | tf_op jit(solution)/shard_map/all_to_all | solution.py:361
  98.9 1.6 %collective-permute-start.15 = (bf16[32,4096]{1,0:T(8,128)(2,1)S(1)}, bf16[32,4096]{1,0:T(8,128)(2,1)S(1)}, u32[]{:S(2)}, u32[]{:S(2)}) collective-permute-start(bf16[32,4096]{1,0:T(8,128)(2,1)S(1)} %slice_bitcast_fusion), channel_id=1, source_target_pairs={{0,32},{32,0},{64,96},{96,64},{128,160},{160,128},{192,224},{224,1... | collective-permute-start | bytes 786440 | tf_op jit(solution)/shard_map/ppermute | solution.py:268
  99.0 7.2 %copy-start.6 = (bf16[4,8,64,128]{3,2,1,0:T(8,128)(2,1)}, bf16[4,8,64,128]{3,2,1,0:T(8,128)(2,1)S(1)}, u32[]{:S(2)}) copy-start(bf16[4,8,64,128]{3,2,1,0:T(8,128)(2,1)S(1)} %all-to-all-done.1.rows_hbm) | copy-start | bytes 1572868
  101.6 16.9 %copy-start.13 = (s32[4]{0:T(128)S(1)}, s32[4]{0:T(128)}, u32[]{:S(2)}) copy-start(s32[4]{0:T(128)} %pad_add_fusion.place_ref) | copy-start | bytes 52
  101.6 10.8 %collective-permute-start.16 = (bf16[32,4096]{1,0:T(8,128)(2,1)S(1)}, bf16[32,4096]{1,0:T(8,128)(2,1)S(1)}, u32[]{:S(2)}, u32[]{:S(2)}) collective-permute-start(bf16[32,4096]{1,0:T(8,128)(2,1)S(1)} %fusion), channel_id=1, source_target_pairs={{0,64},{32,96},{64,128},{96,160},{128,192},{160,224},{192,0},{224,... | collective-permute-start | bytes 786440 | tf_op jit(solution)/shard_map/ppermute | solution.py:264
  102.1 14.2 %collective-permute-start.17 = (bf16[32,4096]{1,0:T(8,128)(2,1)S(1)}, bf16[32,4096]{1,0:T(8,128)(2,1)S(1)}, u32[]{:S(2)}, u32[]{:S(2)}) collective-permute-start(bf16[32,4096]{1,0:T(8,128)(2,1)S(1)} %fusion), channel_id=1, source_target_pairs={{0,192},{32,224},{64,0},{96,32},{128,64},{160,96},{192,128},{224,1... | collective-permute-start | bytes 786440 | tf_op jit(solution)/shard_map/ppermute | solution.py:264
  104.9 13.3 %collective-permute-start.18 = (bf16[32,4096]{1,0:T(8,128)(2,1)S(1)}, bf16[32,4096]{1,0:T(8,128)(2,1)S(1)}, u32[]{:S(2)}, u32[]{:S(2)}) collective-permute-start(bf16[32,4096]{1,0:T(8,128)(2,1)S(1)} %fusion), channel_id=1, source_target_pairs={{0,128},{32,160},{64,192},{96,224},{128,0},{160,32},{192,64},{224,... | collective-permute-start | bytes 786440 | tf_op jit(solution)/shard_map/ppermute | solution.py:264
  118.3 7.7 %collective-permute-start.19 = (bf16[32,4096]{1,0:T(8,128)(2,1)S(1)}, bf16[32,4096]{1,0:T(8,128)(2,1)S(1)}, u32[]{:S(2)}, u32[]{:S(2)}) collective-permute-start(bf16[32,4096]{1,0:T(8,128)(2,1)S(1)} %add_convert_fusion), channel_id=1, source_target_pairs={{0,32},{32,0},{64,96},{96,64},{128,160},{160,128},{192,224},{224,1... | collective-permute-start | bytes 786440 | tf_op jit(solution)/shard_map/ppermute | solution.py:268
  119.7 24.6 %all-to-all-start.2 = ((bf16[8,128,256]{2,1,0:T(8,128)(2,1)}), bf16[8,128,256]{2,1,0:T(8,128)(2,1)S(1)}, u32[]{:S(2)}, u32[]{:S(2)}) async-start(bf16[8,128,256]{2,1,0:T(8,128)(2,1)} %read_out.1), calls=%async_computation.2 | async-start | bytes 1048576 | tf_op jit(solution)/shard_map/all_to_all | solution.py:405
  (6 other events, 12.0 us)

commit v5 on v4

--- a/solution.py
+++ b/solution.py
@@ -82,8 +82,7 @@
         pieces = [filter_ref[start : start + LANE8, i * BLOCK : (i + 1) * BLOCK] for i in range(BLOCKS)]
         signals.append(jnp.concatenate(pieces, 0))
     spectra = forward(*signals, first_ref, second_ref, cosine, sine)
-    spectrum_ref[0] = spectra[:rows]
-    spectrum_ref[1] = spectra[rows:]
+    spectrum_ref[...] = spectra.astype(bf16).reshape(2, rows, 2 * BLOCK)
 
 
 def start_all(copies):
@@ -96,16 +95,14 @@
         copy.wait()
 
 
-def weight_copies(place_ref, weight_hbms, take, sems):
+def weight_copies(place_ref, weight_hbms, take):
     copies = []
-    for other, weight_hbm in enumerate(weight_hbms):
-        core = place_ref[3] if other == 0 else 1 - place_ref[3]
-        for index, step in enumerate(X_STEPS):
-            group = lax.rem(place_ref[2] + (step + X), X) * CORES + core
-            for slot in range(2):
-                lanes, target = take(group, slot)
-                number = (other * X + index) * 2 + slot
-                copies.append(pltpu.make_async_copy(weight_hbm.at[index, slot, :, lanes], target, sems.at[number]))
+    for number, weight_hbm in enumerate(weight_hbms):
+        core = place_ref[3] if number < X else 1 - place_ref[3]
+        group = lax.rem(place_ref[2] + (X_STEPS[number % X] + X), X) * CORES + core
+        for slot in range(2):
+            for lanes, target, sem in take(number * 2 + slot, group, slot):
+                copies.append(pltpu.make_async_copy(weight_hbm.at[slot, :, lanes], target, sem))
     return copies
 
 
@@ -139,15 +136,19 @@
     return jnp.where(index % 2 == 1, Z - (index + 1) // 2, index // 2)
 
 
-def forward_kernel(place_ref, taps_ref, gain_ref, twist_ref, filter_hbm, own_hbm, other_hbm, *rest):
-    chunk_hbms = rest[:Z]
-    table_hbms = rest[Z : Z + 4]
-    gated_ref, gate_ref, spectrum_ref, both, rows, weight, spectra, *rest = rest[Z + 4 :]
+def forward_kernel(place_ref, taps_ref, gain_ref, twist_ref, filter_hbm, *rest):
+    devices = X * CORES
+    weight_hbms = rest[:devices]
+    chunk_hbms = rest[devices : devices + Z]
+    table_hbms = rest[devices + Z : devices + Z + 4]
+    gated_ref, gate_ref, spectrum_ref, both, rows, weight, spectra, *rest = rest[devices + Z + 4 :]
     tables = rest[:4]
     weight_sems, row_sems, sems = rest[4:]
     width = 2 * CHANS
-    place = lambda group, slot: (pl.ds(0, width), weight.at[group, :, pl.ds(slot * width, width)])
-    loads = weight_copies(place_ref, (own_hbm, other_hbm), place, weight_sems)
+    take = lambda number, group, slot: [
+        (pl.ds(0, width), weight.at[group, :, pl.ds(slot * width, width)], weight_sems.at[number])
+    ]
+    loads = weight_copies(place_ref, weight_hbms, take)
     chunks = []
     for index, chunk in enumerate(chunk_hbms):
         chunks.append(pltpu.make_async_copy(chunk, rows.at[pl.ds(index * Y, Y)], row_sems.at[index]))
@@ -165,7 +166,7 @@
             both[block_of(place_ref, z_step_of(index), y_index)] = blocks[y_index]
         return carry
 
-    lax.fori_loop(0, Z, read_in, 0)
+    lax.fori_loop(0, Z, read_in, 0, unroll=2)
     cosine, sine = twists_of(twist_ref)
     lane = lax.broadcasted_iota(jnp.int32, (BLOCKS, LANE8, BLOCK), 2)
     count = BLOCKS * LANE8
@@ -189,8 +190,8 @@
         gate = both[:, there, :]
         signals = [short(value[:, i * LANE8 : (i + 1) * LANE8], pair * 2 + i) for i in range(2)]
         own = forward(*signals, first_ref, second_ref, cosine, sine)
-        spectrum_ref[pl.ds(pair * 2, 2)] = own.reshape(2, count, 2 * BLOCK)
-        weight = spectra[pl.ds(pair * 2, 2)].reshape(2 * count, 2 * BLOCK)
+        spectrum_ref[pl.ds(pair * 2, 2)] = own.reshape(2, count, 2 * BLOCK).astype(bf16)
+        weight = spectra[pl.ds(pair * 2, 2)].reshape(2 * count, 2 * BLOCK).astype(f32)
         own_re, own_im = own[:, :BLOCK], own[:, BLOCK:]
         filter_re, filter_im = weight[:, :BLOCK], weight[:, BLOCK:]
         mix = jnp.concatenate([own_re * filter_re - own_im * filter_im, own_re * filter_im + own_im * filter_re], 1)
@@ -198,9 +199,7 @@
         signal = jnp.concatenate([piece.reshape(cube) for piece in signals], 1)
         long_part = jnp.concatenate([result[:, i * BLOCK : (i + 1) * BLOCK].reshape(cube) for i in range(2)], 1)
         mixed = (long_part + gain_ref[here, :][None] * signal).astype(bf16).astype(f32)
-        gated = (gate.astype(f32) * mixed).astype(bf16).reshape(Z, Y, 2 * LANE8, BLOCK)
-        for y in range(Y):
-            gated_ref[y, :, here, :] = gated[:, y]
+        gated_ref[:, here, :] = (gate.astype(f32) * mixed).astype(bf16)
         gate_ref[:, here, :] = gate
         return carry
 
@@ -213,7 +212,7 @@
     products = (grad_ref[...].astype(f32) * gate_ref[...].astype(f32)).astype(bf16).astype(f32)
     signals = [products[:, i * LANE8 : (i + 1) * LANE8].reshape(count, BLOCK) for i in range(2)]
     spectra = forward(*signals, first_ref, second_ref, cosine, sine)
-    own = spectrum_ref[...].reshape(2 * count, 2 * BLOCK)
+    own = spectrum_ref[...].reshape(2 * count, 2 * BLOCK).astype(f32)
     own_re, own_im = own[:, :BLOCK], own[:, BLOCK:]
     grad_re, grad_im = spectra[:, :BLOCK], spectra[:, BLOCK:]
     lag = jnp.concatenate([own_re * grad_re + own_im * grad_im, own_re * grad_im - own_im * grad_re], 1)
@@ -225,30 +224,47 @@
     out_ref[0] = jnp.concatenate(both, 0).astype(bf16)
 
 
-def read_out_kernel(place_ref, own_hbm, other_hbm, rows_hbm, *rest):
-    mark_hbms = rest[:Z]
-    out_ref, weight, rows_all, marks_all, weight_sems, mark_sems, row_sem = rest[Z:]
+def read_out_kernel(place_ref, rows_hbm, marks_hbm, *rest):
+    devices = X * CORES
+    weight_hbms = rest[:devices]
+    out_ref, weight, rows_all, chunk_all, weight_sems, sems = rest[devices:]
     slots, inner, width = weight.shape
-    take = lambda group, slot: (pl.ds(2 * CHANS, width), weight.at[group * 2 + slot])
-    loads = [pltpu.make_async_copy(rows_hbm, rows_all, row_sem)]
-    for index, mark_hbm in enumerate(mark_hbms):
-        source = mark_hbm.at[0, pl.ds(BLOCK, BLOCK // TRIAL), :]
-        loads.append(pltpu.make_async_copy(source, marks_all.at[index], mark_sems.at[index]))
-    loads += weight_copies(place_ref, (own_hbm, other_hbm), take, weight_sems)
+    trials = BLOCK // TRIAL
+    top = inner // 2
+    take = lambda number, group, slot: [
+        (
+            pl.ds(2 * CHANS + half * width, width),
+            weight.at[group * 2 + slot, pl.ds(half * top, top), :],
+            weight_sems.at[number * 2 + half],
+        )
+        for half in range(2)
+    ]
+    first = [pltpu.make_async_copy(rows_hbm, rows_all, sems.at[0]), pltpu.make_async_copy(marks_hbm, chunk_all, sems.at[1])]
+    loads = weight_copies(place_ref, weight_hbms, take)
+    start_all(first)
     start_all(loads)
-    wait_all(loads)
-
-    def step(quad, carry):
-        places = [lax.rem(place_ref[0] + z_step_of(quad * 4 + index), Z) for index in range(4)]
-        rows = jnp.concatenate([rows_all[:, block, :, :].reshape(inner, BLOCK).T for block in places], 0)
-        marks = marks_all[pl.ds(quad * 4, 4)].astype(f32).reshape(4 * BLOCK // TRIAL, width)
-        wide = spread(rows, marks, slots)
-        chosen = jnp.dot(wide, weight[...].reshape(slots * inner, width), preferred_element_type=f32)
-        for index, block in enumerate(places):
-            out_ref[block] = chosen[index * BLOCK : (index + 1) * BLOCK].astype(bf16)
-        return carry
-
-    lax.fori_loop(0, Z // 4, step, 0)
+    wait_all(first)
+    places = [block_of(place_ref, 0, index) - place_ref[0] * Y for index in range(Y)]
+    rows = jnp.concatenate([rows_all[:, block, :, :].reshape(inner, BLOCK).T for block in places], 0)
+    marks = chunk_all[...].astype(f32).reshape(Y * trials, chunk_all.shape[2])
+    marks = jnp.concatenate([marks] * (inner // width), 1)
+    marks = jnp.broadcast_to(marks[:, None, :], (Y * trials, TRIAL, inner)).reshape(Y * BLOCK, inner).astype(bf16)
+    nothing = jnp.zeros_like(rows)
+    total = jnp.zeros((Y * BLOCK, width), f32)
+    for number in range(0, devices, 2):
+        for load in loads[number * 4 : number * 4 + 8]:
+            load.wait()
+        for offset in range(2):
+            core = place_ref[3] if number + offset < X else 1 - place_ref[3]
+            group = lax.rem(place_ref[2] + (X_STEPS[(number + offset) % X] + X), X) * CORES + core
+            wide = []
+            for slot in range(2):
+                mark = (group * 2 + slot).astype(f32).astype(bf16)
+                wide.append(jnp.where(marks == mark, rows, nothing))
+            pair = weight[pl.ds(group * 2, 2)].reshape(2 * inner, width)
+            total = total + jnp.dot(jnp.concatenate(wide, 1), pair, preferred_element_type=f32)
+    for index, block in enumerate(places):
+        out_ref[block] = total[index * BLOCK : (index + 1) * BLOCK].astype(bf16)
 
 
 def along_y(value, step):
@@ -284,7 +300,7 @@
     coords = jnp.stack([place // Y, place % Y, group // CORES, group % CORES]).astype(jnp.int32)
     first, second, back_second, back_first, twists = transform_tables()
     params = pltpu.CompilerParams(vmem_limit_bytes=60 << 20)
-    spectrum_shape = jax.ShapeDtypeStruct((GROUPS, BLOCKS * LANE8, 2 * BLOCK), f32)
+    spectrum_shape = jax.ShapeDtypeStruct((GROUPS, BLOCKS * LANE8, 2 * BLOCK), bf16)
     plane = (BLOCKS, CHANS, BLOCK)
     work = 2 * GROUPS * (512 * 256 * 128 + 256 * 256 * 256)
     pair = 2 * LANE8
@@ -295,14 +311,18 @@
     slots = jnp.sum(jnp.where(matches, session_slot[None, :], 0), axis=1)
     marks = jnp.broadcast_to(slots.astype(bf16)[:, None], (slots.shape[0], in_chans))
     block = jnp.concatenate([spikes[0], marks], 0)
+    block, readin_weight, readout_weight = lax.optimization_barrier((block, readin_weight, readout_weight))
     chunk = jnp.stack([block, along_y(block, 1), along_y(block, -1), along_y(block, 2)])
+    own_marks = chunk[:, BLOCK:, :]
     right, left = along_z(chunk, 1), along_z(chunk, -1)
     chunks = [chunk, right, left]
 
     pieces = [lax.dynamic_slice_in_dim(readin_weight, start + place * CHANS, CHANS, 2) for start in (0, model_width)]
-    pieces.append(lax.dynamic_slice_in_dim(readout_weight, place // Y * (Y * CHANS), Y * CHANS, 1))
-    own = jnp.concatenate(pieces, 2)
+    split = readout_weight.reshape(2, 2, Z // 2, Y, CHANS, in_chans)
+    split = lax.dynamic_index_in_dim(split, place % Y, 3, keepdims=False).reshape(2, 2, Z // 2 * CHANS, in_chans)
+    own = jnp.concatenate(pieces + [split[:, 0], split[:, 1]], 2)
     own_right, own_left = along_x(own, 1), along_x(own, -1)
+    own_other = other_core(own)
 
     filter_spectrum = pl.pallas_call(
         filter_kernel,
@@ -315,22 +335,24 @@
         name="filter_transform",
     )(long_filter, first, second, twists)
 
-    right, left, own_right, own_left, filter_spectrum = lax.optimization_barrier((right, left, own_right, own_left, filter_spectrum))
+    right, left, filter_spectrum, own_marks = lax.optimization_barrier((right, left, filter_spectrum, own_marks))
     right, left = along_z(right, 1), along_z(left, -1)
     chunks += [right, left]
-    far = jnp.concatenate([along_x(own_right[:1], 1), along_x(own_left[1:], -1)], 0)
-    right, left, far = lax.optimization_barrier((right, left, far))
+    ready = (right, left, own_right, own_left, own_other)
+    right, left, own_right, own_left, own_other = lax.optimization_barrier(ready)
     right, left = along_z(right, 1), along_z(left, -1)
     chunks += [right, left]
-    weights = jnp.stack([own, own_right, own_left, far])
-    weights_other = other_core(weights)
+    far = along_x(own_right, 1)
+    right_other, left_other = other_core(own_right), other_core(own_left)
     taps = lax.dynamic_slice_in_dim(short_kernel, place * CHANS, CHANS, 1)
     taps = jnp.broadcast_to(taps[:, :, None], (short_kernel.shape[0], CHANS, BLOCK))
     gains = jnp.broadcast_to(skip_gain[:, None], (CHANS, BLOCK))
-    right, left, weights_other = lax.optimization_barrier((right, left, weights_other))
+    right, left, far, right_other, left_other = lax.optimization_barrier((right, left, far, right_other, left_other))
+    far_other = other_core(far)
+    weights = [own, own_right, own_left, far, own_other, right_other, left_other, far_other]
     turned = out_grad[0].T.reshape(BLOCKS, CHANS, BLOCK)
-    ready = (along_z(right, 1), taps, gains, coords, turned)
-    right, taps, gains, coords, turned = lax.optimization_barrier(ready)
+    ready = (along_z(right, 1), taps, gains, coords, turned, weights[-1])
+    right, taps, gains, coords, turned, weights[-1] = lax.optimization_barrier(ready)
     chunks.append(right)
     grads = lax.all_to_all(turned, "seq", split_axis=0, concat_axis=0, tiled=True)
 
@@ -339,26 +361,27 @@
     gated, gates, spectrum = pl.pallas_call(
         forward_kernel,
         out_shape=(
-            jax.ShapeDtypeStruct((Y, Z, CHANS, BLOCK), bf16),
+            jax.ShapeDtypeStruct(plane, bf16),
             jax.ShapeDtypeStruct(plane, bf16),
             spectrum_shape,
         ),
-        in_specs=[scalar] + whole(3) + [hbm] * (3 + Z + 4),
+        in_specs=[scalar] + whole(3) + [hbm] * (1 + X * CORES + Z + 4),
         out_specs=tuple(whole(3)),
         scratch_shapes=[
             pltpu.VMEM((BLOCKS, 2 * CHANS, BLOCK), bf16),
             pltpu.VMEM((BLOCKS,) + chunk.shape[1:], bf16),
             pltpu.VMEM((slot_count // 2, in_chans, 4 * CHANS), bf16),
-            pltpu.VMEM(spectrum_shape.shape, f32),
+            pltpu.VMEM(spectrum_shape.shape, bf16),
         ]
         + [pltpu.VMEM(table.shape, bf16) for table in tables]
         + [pltpu.SemaphoreType.DMA((count,)) for count in (slot_count, Z, 5)],
         compiler_params=params,
         cost_estimate=pl.CostEstimate(flops=4 * work, bytes_accessed=8 << 20, transcendentals=0),
         name="long_convolution",
-    )(coords, taps, gains, twists, filter_spectrum, weights, weights_other, *chunks, *tables)
-
-    arrived = lax.all_to_all(gated, "seq", split_axis=0, concat_axis=0, tiled=True, axis_index_groups=y_groups)
+    )(coords, taps, gains, twists, filter_spectrum, *weights, *chunks, *tables)
+
+    gated = gated.reshape(Z, Y, CHANS, BLOCK)
+    arrived = lax.all_to_all(gated, "seq", split_axis=0, concat_axis=0, tiled=True, axis_index_groups=z_groups)
     half = CHANS // CORES
     fixed = lambda table: pl.BlockSpec(table.shape, lambda i, place, rank=table.ndim: (0,) * rank)
     steps = half // pair
@@ -377,32 +400,32 @@
         cost_estimate=pl.CostEstimate(flops=2 * work, bytes_accessed=4 << 20, transcendentals=0),
         name="filter_gradient",
     )(coords, grads, gates, spectrum, *tables, twists)
-    came, arrived = lax.optimization_barrier((other_core(halves[1]), arrived))
+    came = other_core(halves[1])
     plus = lambda *terms: sum(term.astype(f32) for term in terms).astype(bf16)
+    came, arrived = lax.optimization_barrier((came, arrived))
     total = plus(halves[0], came)
     cames = [along_x(total, step) for step in (1, -1, 2)]
     partial = pl.pallas_call(
         read_out_kernel,
-        out_shape=jax.ShapeDtypeStruct((Z, BLOCK, in_chans), bf16),
-        in_specs=[scalar] + [hbm] * (3 + Z),
+        out_shape=jax.ShapeDtypeStruct((Y, BLOCK, in_chans), bf16),
+        in_specs=[scalar] + [hbm] * (2 + X * CORES),
         out_specs=whole(1)[0],
         scratch_shapes=[
-            pltpu.VMEM((slot_count, Y * CHANS, in_chans), bf16),
-            pltpu.VMEM((Y, Z, CHANS, BLOCK), bf16),
-            pltpu.VMEM((Z, BLOCK // TRIAL, in_chans), bf16),
+            pltpu.VMEM((slot_count, Z * CHANS, in_chans), bf16),
+            pltpu.VMEM((Z, Y, CHANS, BLOCK), bf16),
+            pltpu.VMEM((Y, BLOCK // TRIAL, in_chans), bf16),
         ]
-        + [pltpu.SemaphoreType.DMA((count,)) for count in (slot_count, Z)]
-        + [pltpu.SemaphoreType.DMA],
+        + [pltpu.SemaphoreType.DMA((count,)) for count in (2 * slot_count, 2)],
         compiler_params=params,
         cost_estimate=pl.CostEstimate(flops=2 * 512 * 512 * 4096, bytes_accessed=6 << 20, transcendentals=0),
         name="read_out",
-    )(coords, weights, weights_other, arrived, *chunks)
+    )(coords, arrived, own_marks, *weights)
     cames, partial = lax.optimization_barrier((cames, partial))
     total = plus(total, *cames)
     theirs = other_core(total)
     lower = coords[3] == 0
     filter_grad = jnp.concatenate([jnp.where(lower, total, theirs), jnp.where(lower, theirs, total)], 0).astype(f32)
-    pieces = lax.all_to_all(partial, "seq", split_axis=0, concat_axis=0, tiled=True, axis_index_groups=z_groups)
+    pieces = lax.all_to_all(partial, "seq", split_axis=0, concat_axis=0, tiled=True, axis_index_groups=y_groups)
     denoised = jnp.sum(pieces.astype(f32), 0).astype(bf16)
     return denoised[None], filter_grad
 

time: 146 us -> 143 us (0.979)
  starting transfers between devices: 49.5 us -> 43.3 us
  waiting for transfers between devices: 42.7 us -> 46.2 us
  other arithmetic: 7.14 us -> 5.65 us
    all_to_all x1, waiting for transfers between devices: 17.1 us -> 4.62 us  [local(): lax.all_to_all(partial, 'seq', split_axis=0, concat_axis=0, tiled=True, a...]
    all_to_all x1, waiting for transfers between devices: 0.01 us -> 9.27 us  [local(): lax.all_to_all(gated, 'seq', split_axis=0, concat_axis=0, tiled=True, axi...]
    ppermute x7, waiting for transfers between devices: 14.8 us -> 22.7 us  [along_z(): lax.ppermute(value, 'seq', [(z * Y + y, (z + step) % Z * Y + y) for z in...]
    ppermute x7 -> x6, starting transfers between devices: 10.3 us -> 6.81 us  [along_x(): return lax.ppermute(value, 'grp', pairs)]
    all_to_all x1, waiting for transfers between devices: 0.3 us -> 2.32 us  [local(): lax.all_to_all(turned, 'seq', split_axis=0, concat_axis=0, tiled=True)]
    ppermute x7 -> x6, waiting for transfers between devices: 9 us -> 7.27 us  [along_x(): return lax.ppermute(value, 'grp', pairs)]
    another operation x2 -> x0, other arithmetic: 1.59 us -> none  [local(): weights = jnp.stack([own, own_right, own_left, far])]
    all_to_all x1, starting transfers between devices: 6.4 us -> 4.81 us  [local(): lax.all_to_all(partial, 'seq', split_axis=0, concat_axis=0, tiled=True, a...]
  transfers between devices with their start and end apart: 23 -> 25, of which waited for: 11 -> 10; matrix products, arithmetic and copies ran while one was open for 5% -> 5% of each run, Pallas kernels for 23% -> 24%
where the time goes in v5:
time: 143 us; the launch traced here: 141 us
  waiting for transfers between devices  46.2 us (32%)
  starting transfers between devices  43.3 us (30%)
  Pallas kernels  34.3 us (24%)
  local copies, waits for them, and re-layouts  9.91 us (7%)
  other arithmetic  5.65 us (4%)
  between operations  1.56 us (1%)
    ppermute x7, waiting for transfers between devices, along_z(): lax.ppermute(value, 'seq', [(z * Y + y, (z + step) % Z * Y + y) for z in...  22.7 us
    pallas_call x1, Pallas kernels, local(): pl.pallas_call(forward_kernel, out_shape=(jax.ShapeDtypeStruct(plane, bf1...  14.4 us
    ppermute x7, starting transfers between devices, along_z(): lax.ppermute(value, 'seq', [(z * Y + y, (z + step) % Z * Y + y) for z in...  13.9 us
    all_to_all x1, waiting for transfers between devices, local(): lax.all_to_all(gated, 'seq', split_axis=0, concat_axis=0, tiled=True, axi...  9.27 us
    pallas_call x1, Pallas kernels, local(): pl.pallas_call(read_out_kernel, out_shape=jax.ShapeDtypeStruct((Y, BLOCK,...  9.06 us
    all_to_all x1, starting transfers between devices, local(): lax.all_to_all(turned, 'seq', split_axis=0, concat_axis=0, tiled=True)  8.33 us
    ppermute x6, waiting for transfers between devices, along_x(): return lax.ppermute(value, 'grp', pairs)  7.27 us
    ppermute x6, starting transfers between devices, along_x(): return lax.ppermute(value, 'grp', pairs)  6.81 us
  transfers between devices with their start and end apart: 25, of which 10 were waited for; matrix products, arithmetic and copies ran while one was open for 5% of the time, Pallas kernels for 24%

profile of v5, /device:TPU:8, one launch (start us, length us, event | category | flops | bytes accessed | tf_op | source)
XLA Modules:
  0.0 141.0 jit_solution(4197691789555265396)
XLA Ops:
  3.3 2.4 %collective-permute-start.2 = (bf16[136,256]{1,0:T(8,128)(2,1)S(1)}, bf16[136,256]{1,0:T(8,128)(2,1)S(1)}, u32[]{:S(2)}, u32[]{:S(2)}) collective-permute-start(bf16[136,256]{1,0:T(8,128)(2,1)S(1)} %pad_maximum_fusion.2), channel_id=1, source_target_pairs={{0,2},{1,3},{2,0},{3,1},{4,6},{5,7},{6,4},{7,5},{8,10},{9,11},{10,... | collective-permute-start | bytes 208904 | tf_op jit(solution)/shard_map/ppermute | solution.py:271
  5.7 1.3 collective-permute-start.1
  7.9 1.1 constant_dynamic-slice_fusion.3
  9.2 1.6 %collective-permute-start.7 = (bf16[2,256,640]{2,1,0:T(8,128)(2,1)S(1)}, bf16[2,256,640]{2,1,0:T(8,128)(2,1)}, u32[]{:S(2)}, u32[]{:S(2)}) collective-permute-start(bf16[2,256,640]{2,1,0:T(8,128)(2,1)S(1)} %pad_maximum_fusion.rest_0_), channel_id=1, source_target_pairs={{0,64},{32,96},{64,128},{96,160},{128,192},{160,224},{192,0},{224,... | collective-permute-start | bytes 1966088 | tf_op jit(solution)/shard_map/ppermute | solution.py:280
  10.7 1.7 %collective-permute-start.8 = (bf16[2,256,640]{2,1,0:T(8,128)(2,1)S(1)}, bf16[2,256,640]{2,1,0:T(8,128)(2,1)}, u32[]{:S(2)}, u32[]{:S(2)}) collective-permute-start(bf16[2,256,640]{2,1,0:T(8,128)(2,1)S(1)} %pad_maximum_fusion.rest_0_), channel_id=1, source_target_pairs={{0,192},{32,224},{64,0},{96,32},{128,64},{160,96},{192,128},{224,1... | collective-permute-start | bytes 1966088 | tf_op jit(solution)/shard_map/ppermute | solution.py:280
  12.6 2.0 %collective-permute-start.3 = (bf16[4,136,256]{2,1,0:T(8,128)(2,1)S(1)}, bf16[4,136,256]{2,1,0:T(8,128)(2,1)S(1)}, u32[]{:S(2)}, u32[]{:S(2)}) collective-permute-start(bf16[4,136,256]{2,1,0:T(8,128)(2,1)S(1)} %pad_maximum_fusion.1.rest_8_), channel_id=1, source_target_pairs={{0,4},{1,5},{2,6},{3,7},{4,8},{5,9},{6,10},{7,11},{8,12},{9,13},{1... | collective-permute-start | bytes 835592 | tf_op jit(solution)/shard_map/ppermute | solution.py:275
  14.6 4.0 %collective-permute-start.4 = (bf16[4,136,256]{2,1,0:T(8,128)(2,1)S(1)}, bf16[4,136,256]{2,1,0:T(8,128)(2,1)S(1)}, u32[]{:S(2)}, u32[]{:S(2)}) collective-permute-start(bf16[4,136,256]{2,1,0:T(8,128)(2,1)S(1)} %pad_maximum_fusion.1.rest_8_), channel_id=1, source_target_pairs={{0,28},{1,29},{2,30},{3,31},{4,0},{5,1},{6,2},{7,3},{8,4},{9,5},{1... | collective-permute-start | bytes 835592 | tf_op jit(solution)/shard_map/ppermute | solution.py:275
  18.6 4.4 %filter_transform.1.filter_hbm = bf16[8,256,256]{2,1,0:T(8,128)(2,1)} custom-call(f32[64,4096]{1,0:T(8,128)} %filter_ref.1, bf16[512,256]{1,0:T(8,128)(2,1)} %constant.81.clone.first_ref.rest_16_, bf16[256,256]{1,0:T(8,128)(2,1)} %constant.82.clone.second_ref.rest_17_, f32[2,32,128]{2,1,0:T(8,128)} %constant.85.clone.twist_ref), custom_call_target="tpu_custom_call" | custom-call | flops 536870912 | bytes 4194304 | tf_op jit(solution)/shard_map/filter_transform/pallas_call | solution.py:327
  23.6 2.2 %collective-permute-done.3.rest_9_ = bf16[4,136,256]{2,1,0:T(8,128)(2,1)S(1)} collective-permute-done((bf16[4,136,256]{2,1,0:T(8,128)(2,1)S(1)}, bf16[4,136,256]{2,1,0:T(8,128)(2,1)S(1)}, u32[]{:S(2)}, u32[]{:S(2)}) %collective-permute-start.3) | collective-permute-done | bytes 278560 | tf_op jit(solution)/shard_map/ppermute | solution.py:275
  25.9 3.2 %collective-permute-start.6 = (bf16[4,136,256]{2,1,0:T(8,128)(2,1)S(1)}, bf16[4,136,256]{2,1,0:T(8,128)(2,1)S(1)}, u32[]{:S(2)}, u32[]{:S(2)}) collective-permute-start(bf16[4,136,256]{2,1,0:T(8,128)(2,1)S(1)} %collective-permute-done.4.rest_10_), channel_id=1, source_target_pairs={{0,28},{1,29},{2,30},{3,31},{4,0},{5,1},{6,2},{7,3},{8,4},{9,5},{1... | collective-permute-start | bytes 835592 | tf_op jit(solution)/shard_map/ppermute | solution.py:275
  29.2 6.6 %collective-permute-done.5.rest_11_ = bf16[4,136,256]{2,1,0:T(8,128)(2,1)S(1)} collective-permute-done((bf16[4,136,256]{2,1,0:T(8,128)(2,1)S(1)}, bf16[4,136,256]{2,1,0:T(8,128)(2,1)S(1)}, u32[]{:S(2)}, u32[]{:S(2)}) %collective-permute-start.5) | collective-permute-done | bytes 278560 | tf_op jit(solution)/shard_map/ppermute | solution.py:275
  36.5 1.8 %collective-permute-start.10 = (bf16[4,136,256]{2,1,0:T(8,128)(2,1)S(1)}, bf16[4,136,256]{2,1,0:T(8,128)(2,1)}, u32[]{:S(2)}, u32[]{:S(2)}) collective-permute-start(bf16[4,136,256]{2,1,0:T(8,128)(2,1)S(1)} %collective-permute-done.5.rest_11_), channel_id=1, source_target_pairs={{0,4},{1,5},{2,6},{3,7},{4,8},{5,9},{6,10},{7,11},{8,12},{9,13},{1... | collective-permute-start | bytes 835592 | tf_op jit(solution)/shard_map/ppermute | solution.py:275
  38.3 1.4 collective-permute-start.11
  39.7 6.7 %collective-permute-done.10.rest_13_ = bf16[4,136,256]{2,1,0:T(8,128)(2,1)} collective-permute-done((bf16[4,136,256]{2,1,0:T(8,128)(2,1)S(1)}, bf16[4,136,256]{2,1,0:T(8,128)(2,1)}, u32[]{:S(2)}, u32[]{:S(2)}) %collective-permute-start.10) | collective-permute-done | bytes 278560 | tf_op jit(solution)/shard_map/ppermute | solution.py:275
  46.7 6.4 %collective-permute-done.12.rest_3_ = bf16[2,256,640]{2,1,0:T(8,128)(2,1)S(1)} collective-permute-done((bf16[2,256,640]{2,1,0:T(8,128)(2,1)}, bf16[2,256,640]{2,1,0:T(8,128)(2,1)S(1)}, u32[]{:S(2)}, u32[]{:S(2)}) %collective-permute-start.12) | collective-permute-done | bytes 655392 | tf_op jit(solution)/shard_map/ppermute | solution.py:280
  54.9 1.3 collective-permute-start.15
  56.2 1.0 copy.19
  58.6 7.0 %collective-permute-done.15.rest_15_ = bf16[4,136,256]{2,1,0:T(8,128)(2,1)} collective-permute-done((bf16[4,136,256]{2,1,0:T(8,128)(2,1)}, bf16[4,136,256]{2,1,0:T(8,128)(2,1)}, u32[]{:S(2)}, u32[]{:S(2)}) %collective-permute-start.15) | collective-permute-done | bytes 278560 | tf_op jit(solution)/shard_map/ppermute | solution.py:275
  66.3 1.3 broadcast_in_dim.39.gain_ref
  67.6 8.3 %all-to-all-start = ((bf16[32,64,128]{2,1,0:T(8,128)(2,1)}), bf16[32,64,128]{2,1,0:T(8,128)(2,1)S(1)}, u32[]{:S(2)}, u32[]{:S(2)}) async-start(bf16[32,64,128]{2,1,0:T(8,128)(2,1)} %bitcast.16), calls=%async_computation | async-start | bytes 1048576 | tf_op jit(solution)/shard_map/all_to_all | solution.py:357
  75.9 14.4 %long_convolution.1 = (bf16[32,64,128]{2,1,0:T(8,128)(2,1)}, bf16[32,64,128]{2,1,0:T(8,128)(2,1)}, bf16[8,256,256]{2,1,0:T(8,128)(2,1)}) custom-call(s32[4]{0:T(128)} %pad_add_fusion.place_ref, f32[3,64,128]{2,1,0:T(8,128)} %broadcast_in_dim.38.taps_ref, f32[64,128]{1,0:T(8,128)} %broadcast_in_dim.39.gain_ref, f32[2,32,128]{2,1,0:T(8,128)} %constant.85.clone.twist_ref, ...), custom_call_target="tpu_custom_call" | custom-call | flops 2147483648 | bytes 8388608 | tf_op jit(solution)/shard_map/long_convolution/pallas_call | solution.py:361
  90.3 2.3 %all-to-all-done.grad_ref = bf16[32,64,128]{2,1,0:T(8,128)(2,1)S(1)} async-done(((bf16[32,64,128]{2,1,0:T(8,128)(2,1)}), bf16[32,64,128]{2,1,0:T(8,128)(2,1)S(1)}, u32[]{:S(2)}, u32[]{:S(2)}) %all-to-all-start) | async-done | bytes 524320 | tf_op jit(solution)/shard_map/all_to_all | solution.py:357
  92.6 4.4 %all-to-all-start.1 = ((bf16[8,4,64,128]{3,2,1,0:T(8,128)(2,1)}), bf16[8,4,64,128]{3,2,1,0:T(8,128)(2,1)S(1)}, u32[]{:S(2)}, u32[]{:S(2)}) async-start(bf16[8,4,64,128]{3,2,1,0:T(8,128)(2,1)} %bitcast.33), calls=%async_computation.1 | async-start | bytes 1048576 | tf_op jit(solution)/shard_map/all_to_all | solution.py:384
  97.0 6.5 %filter_gradient.1 = bf16[2,32,4096]{2,1,0:T(8,128)(2,1)} custom-call(s32[4]{0:T(128)} %pad_add_fusion.place_ref, bf16[32,64,128]{2,1,0:T(8,128)(2,1)} %copy-done.8, bf16[32,64,128]{2,1,0:T(8,128)(2,1)} %get-tuple-element.54.gate_ref, bf16[8,256,256]{2,1,0:T(8,128)(2,1)} %get-tuple-element.55.spectrum_ref, ...), custom_call_target="tpu_custom_call" | custom-call | flops 1073741824 | bytes 4194304 | tf_op jit(solution)/shard_map/filter_gradient/pallas_call | solution.py:388
  103.5 1.0 slice_bitcast_fusion
  104.5 9.3 %all-to-all-done.1.rows_hbm = bf16[8,4,64,128]{3,2,1,0:T(8,128)(2,1)S(1)} async-done(((bf16[8,4,64,128]{3,2,1,0:T(8,128)(2,1)}), bf16[8,4,64,128]{3,2,1,0:T(8,128)(2,1)S(1)}, u32[]{:S(2)}, u32[]{:S(2)}) %all-to-all-start.1) | async-done | bytes 524320 | tf_op jit(solution)/shard_map/all_to_all | solution.py:384
  113.8 1.2 fusion
  115.1 3.2 %collective-permute-start.19 = (bf16[32,4096]{1,0:T(8,128)(2,1)S(1)}, bf16[32,4096]{1,0:T(8,128)(2,1)S(1)}, u32[]{:S(2)}, u32[]{:S(2)}) collective-permute-start(bf16[32,4096]{1,0:T(8,128)(2,1)S(1)} %fusion), channel_id=1, source_target_pairs={{0,192},{32,224},{64,0},{96,32},{128,64},{160,96},{192,128},{224,1... | collective-permute-start | bytes 786440 | tf_op jit(solution)/shard_map/ppermute | solution.py:280
  118.3 9.1 %read_out.1 = bf16[4,128,256]{2,1,0:T(8,128)(2,1)} custom-call(s32[4]{0:T(128)} %pad_add_fusion.place_ref, bf16[8,4,64,128]{3,2,1,0:T(8,128)(2,1)} %copy-done.7, bf16[4,8,256]{2,1,0:T(8,128)(2,1)} %slice.28.marks_hbm, bf16[2,256,640]{2,1,0:T(8,128)(2,1)} %copy-done.1, bf16[2,256,640]{2,1,0:T(8,128)(2,1)} %collective-permute-done.7.rest_1_, ...), custom_call_target="tpu_custom_call" | custom-call | flops 2147483648 | bytes 6291456 | tf_op jit(solution)/shard_map/read_out/pallas_call | solution.py:408
  128.5 4.8 %all-to-all-start.2 = ((bf16[4,128,256]{2,1,0:T(8,128)(2,1)}), bf16[4,128,256]{2,1,0:T(8,128)(2,1)S(1)}, u32[]{:S(2)}, u32[]{:S(2)}) async-start(bf16[4,128,256]{2,1,0:T(8,128)(2,1)} %read_out.1), calls=%async_computation.2 | async-start | bytes 524288 | tf_op jit(solution)/shard_map/all_to_all | solution.py:428
  134.6 4.6 %all-to-all-done.2 = bf16[4,128,256]{2,1,0:T(8,128)(2,1)S(1)} async-done(((bf16[4,128,256]{2,1,0:T(8,128)(2,1)}), bf16[4,128,256]{2,1,0:T(8,128)(2,1)S(1)}, u32[]{:S(2)}, u32[]{:S(2)}) %all-to-all-start.2) | async-done | bytes 262176 | tf_op jit(solution)/shard_map/all_to_all | solution.py:428
  139.9 1.0 maximum_convert_fusion
  (76 shorter events, 11.8 us)
Async XLA Ops:
  3.3 9.2 %collective-permute-start.2 = (bf16[136,256]{1,0:T(8,128)(2,1)S(1)}, bf16[136,256]{1,0:T(8,128)(2,1)S(1)}, u32[]{:S(2)}, u32[]{:S(2)}) collective-permute-start(bf16[136,256]{1,0:T(8,128)(2,1)S(1)} %pad_maximum_fusion.2), channel_id=1, source_target_pairs={{0,2},{1,3},{2,0},{3,1},{4,6},{5,7},{6,4},{7,5},{8,10},{9,11},{10,... | collective-permute-start | bytes 208904 | tf_op jit(solution)/shard_map/ppermute | solution.py:271
  5.7 6.8 %collective-permute-start.1 = (bf16[136,256]{1,0:T(8,128)(2,1)S(1)}, bf16[136,256]{1,0:T(8,128)(2,1)S(1)}, u32[]{:S(2)}, u32[]{:S(2)}) collective-permute-start(bf16[136,256]{1,0:T(8,128)(2,1)S(1)} %pad_maximum_fusion.2), channel_id=1, source_target_pairs={{0,3},{1,0},{2,1},{3,2},{4,7},{5,4},{6,5},{7,6},{8,11},{9,8},{10,9... | collective-permute-start | bytes 208904 | tf_op jit(solution)/shard_map/ppermute | solution.py:271
  7.1 5.4 %collective-permute-start = (bf16[136,256]{1,0:T(8,128)(2,1)S(1)}, bf16[136,256]{1,0:T(8,128)(2,1)S(1)}, u32[]{:S(2)}, u32[]{:S(2)}) collective-permute-start(bf16[136,256]{1,0:T(8,128)(2,1)S(1)} %pad_maximum_fusion.2), channel_id=1, source_target_pairs={{0,1},{1,2},{2,3},{3,0},{4,5},{5,6},{6,7},{7,4},{8,9},{9,10},{10,1... | collective-permute-start | bytes 208904 | tf_op jit(solution)/shard_map/ppermute | solution.py:271
  9.2 13.9 %copy-start.1 = (bf16[2,256,640]{2,1,0:T(8,128)(2,1)}, bf16[2,256,640]{2,1,0:T(8,128)(2,1)S(1)}, u32[]{:S(2)}) copy-start(bf16[2,256,640]{2,1,0:T(8,128)(2,1)S(1)} %pad_maximum_fusion.rest_0_) | copy-start | bytes 1966084
  9.2 26.5 %collective-permute-start.7 = (bf16[2,256,640]{2,1,0:T(8,128)(2,1)S(1)}, bf16[2,256,640]{2,1,0:T(8,128)(2,1)}, u32[]{:S(2)}, u32[]{:S(2)}) collective-permute-start(bf16[2,256,640]{2,1,0:T(8,128)(2,1)S(1)} %pad_maximum_fusion.rest_0_), channel_id=1, source_target_pairs={{0,64},{32,96},{64,128},{96,160},{128,192},{160,224},{192,0},{224,... | collective-permute-start | bytes 1966088 | tf_op jit(solution)/shard_map/ppermute | solution.py:280
  10.7 25.0 %collective-permute-start.8 = (bf16[2,256,640]{2,1,0:T(8,128)(2,1)S(1)}, bf16[2,256,640]{2,1,0:T(8,128)(2,1)}, u32[]{:S(2)}, u32[]{:S(2)}) collective-permute-start(bf16[2,256,640]{2,1,0:T(8,128)(2,1)S(1)} %pad_maximum_fusion.rest_0_), channel_id=1, source_target_pairs={{0,192},{32,224},{64,0},{96,32},{128,64},{160,96},{192,128},{224,1... | collective-permute-start | bytes 1966088 | tf_op jit(solution)/shard_map/ppermute | solution.py:280
  12.5 23.3 %collective-permute-start.9 = (bf16[2,256,640]{2,1,0:T(8,128)(2,1)S(1)}, bf16[2,256,640]{2,1,0:T(8,128)(2,1)}, u32[]{:S(2)}, u32[]{:S(2)}) collective-permute-start(bf16[2,256,640]{2,1,0:T(8,128)(2,1)S(1)} %pad_maximum_fusion.rest_0_), channel_id=1, source_target_pairs={{0,32},{32,0},{64,96},{96,64},{128,160},{160,128},{192,224},{224,1... | collective-permute-start | bytes 1966088 | tf_op jit(solution)/shard_map/ppermute | solution.py:284
  12.6 44.6 %copy-start.2 = (bf16[4,136,256]{2,1,0:T(8,128)(2,1)}, bf16[4,136,256]{2,1,0:T(8,128)(2,1)S(1)}, u32[]{:S(2)}) copy-start(bf16[4,136,256]{2,1,0:T(8,128)(2,1)S(1)} %pad_maximum_fusion.1.rest_8_) | copy-start | bytes 835588
  12.6 43.6 %copy-start.6 = (bf16[1,128,2048]{2,1,0:T(8,128)(2,1)S(1)}, bf16[1,128,2048]{2,1,0:T(8,128)(2,1)}, u32[]{:S(2)}) copy-start(bf16[1,128,2048]{2,1,0:T(8,128)(2,1)} %param.22) | copy-start | bytes 1572868
  12.6 13.2 %collective-permute-start.3 = (bf16[4,136,256]{2,1,0:T(8,128)(2,1)S(1)}, bf16[4,136,256]{2,1,0:T(8,128)(2,1)S(1)}, u32[]{:S(2)}, u32[]{:S(2)}) collective-permute-start(bf16[4,136,256]{2,1,0:T(8,128)(2,1)S(1)} %pad_maximum_fusion.1.rest_8_), channel_id=1, source_target_pairs={{0,4},{1,5},{2,6},{3,7},{4,8},{5,9},{6,10},{7,11},{8,12},{9,13},{1... | collective-permute-start | bytes 835592 | tf_op jit(solution)/shard_map/ppermute | solution.py:275
  14.6 11.3 %collective-permute-start.4 = (bf16[4,136,256]{2,1,0:T(8,128)(2,1)S(1)}, bf16[4,136,256]{2,1,0:T(8,128)(2,1)S(1)}, u32[]{:S(2)}, u32[]{:S(2)}) collective-permute-start(bf16[4,136,256]{2,1,0:T(8,128)(2,1)S(1)} %pad_maximum_fusion.1.rest_8_), channel_id=1, source_target_pairs={{0,28},{1,29},{2,30},{3,31},{4,0},{5,1},{6,2},{7,3},{8,4},{9,5},{1... | collective-permute-start | bytes 835592 | tf_op jit(solution)/shard_map/ppermute | solution.py:275
  25.8 9.9 %copy-start.10 = (bf16[4,136,256]{2,1,0:T(8,128)(2,1)}, bf16[4,136,256]{2,1,0:T(8,128)(2,1)S(1)}, u32[]{:S(2)}) copy-start(bf16[4,136,256]{2,1,0:T(8,128)(2,1)S(1)} %collective-permute-done.4.rest_10_) | copy-start | bytes 835588
  25.8 9.9 %collective-permute-start.5 = (bf16[4,136,256]{2,1,0:T(8,128)(2,1)S(1)}, bf16[4,136,256]{2,1,0:T(8,128)(2,1)S(1)}, u32[]{:S(2)}, u32[]{:S(2)}) collective-permute-start(bf16[4,136,256]{2,1,0:T(8,128)(2,1)S(1)} %collective-permute-done.3.rest_9_), channel_id=1, source_target_pairs={{0,4},{1,5},{2,6},{3,7},{4,8},{5,9},{6,10},{7,11},{8,12},{9,13},{1... | collective-permute-start | bytes 835592 | tf_op jit(solution)/shard_map/ppermute | solution.py:275
  25.9 9.8 %collective-permute-start.6 = (bf16[4,136,256]{2,1,0:T(8,128)(2,1)S(1)}, bf16[4,136,256]{2,1,0:T(8,128)(2,1)S(1)}, u32[]{:S(2)}, u32[]{:S(2)}) collective-permute-start(bf16[4,136,256]{2,1,0:T(8,128)(2,1)S(1)} %collective-permute-done.4.rest_10_), channel_id=1, source_target_pairs={{0,28},{1,29},{2,30},{3,31},{4,0},{5,1},{6,2},{7,3},{8,4},{9,5},{1... | collective-permute-start | bytes 835592 | tf_op jit(solution)/shard_map/ppermute | solution.py:275
  35.7 19.1 %copy-start.11 = (bf16[4,136,256]{2,1,0:T(8,128)(2,1)}, bf16[4,136,256]{2,1,0:T(8,128)(2,1)S(1)}, u32[]{:S(2)}) copy-start(bf16[4,136,256]{2,1,0:T(8,128)(2,1)S(1)} %collective-permute-done.5.rest_11_) | copy-start | bytes 835588
  35.7 19.1 %copy-start.12 = (bf16[4,136,256]{2,1,0:T(8,128)(2,1)}, bf16[4,136,256]{2,1,0:T(8,128)(2,1)S(1)}, u32[]{:S(2)}) copy-start(bf16[4,136,256]{2,1,0:T(8,128)(2,1)S(1)} %collective-permute-done.6.rest_12_) | copy-start | bytes 835588
  35.8 17.3 %collective-permute-start.12 = (bf16[2,256,640]{2,1,0:T(8,128)(2,1)}, bf16[2,256,640]{2,1,0:T(8,128)(2,1)S(1)}, u32[]{:S(2)}, u32[]{:S(2)}) collective-permute-start(bf16[2,256,640]{2,1,0:T(8,128)(2,1)} %collective-permute-done.7.rest_1_), channel_id=1, source_target_pairs={{0,64},{32,96},{64,128},{96,160},{128,192},{160,224},{192,0},{224,... | collective-permute-start | bytes 1966088 | tf_op jit(solution)/shard_map/ppermute | solution.py:280
  36.0 17.1 %collective-permute-start.13 = (bf16[2,256,640]{2,1,0:T(8,128)(2,1)}, bf16[2,256,640]{2,1,0:T(8,128)(2,1)S(1)}, u32[]{:S(2)}, u32[]{:S(2)}) collective-permute-start(bf16[2,256,640]{2,1,0:T(8,128)(2,1)} %collective-permute-done.7.rest_1_), channel_id=1, source_target_pairs={{0,32},{32,0},{64,96},{96,64},{128,160},{160,128},{192,224},{224,1... | collective-permute-start | bytes 1966088 | tf_op jit(solution)/shard_map/ppermute | solution.py:284
  36.0 18.0 %collective-permute-start.14 = (bf16[2,256,640]{2,1,0:T(8,128)(2,1)}, bf16[2,256,640]{2,1,0:T(8,128)(2,1)S(1)}, u32[]{:S(2)}, u32[]{:S(2)}) collective-permute-start(bf16[2,256,640]{2,1,0:T(8,128)(2,1)} %collective-permute-done.8.rest_2_), channel_id=1, source_target_pairs={{0,32},{32,0},{64,96},{96,64},{128,160},{160,128},{192,224},{224,1... | collective-permute-start | bytes 1966088 | tf_op jit(solution)/shard_map/ppermute | solution.py:284
  36.5 10.0 %collective-permute-start.10 = (bf16[4,136,256]{2,1,0:T(8,128)(2,1)S(1)}, bf16[4,136,256]{2,1,0:T(8,128)(2,1)}, u32[]{:S(2)}, u32[]{:S(2)}) collective-permute-start(bf16[4,136,256]{2,1,0:T(8,128)(2,1)S(1)} %collective-permute-done.5.rest_11_), channel_id=1, source_target_pairs={{0,4},{1,5},{2,6},{3,7},{4,8},{5,9},{6,10},{7,11},{8,12},{9,13},{1... | collective-permute-start | bytes 835592 | tf_op jit(solution)/shard_map/ppermute | solution.py:275
  38.3 8.4 %collective-permute-start.11 = (bf16[4,136,256]{2,1,0:T(8,128)(2,1)S(1)}, bf16[4,136,256]{2,1,0:T(8,128)(2,1)S(1)}, u32[]{:S(2)}, u32[]{:S(2)}) collective-permute-start(bf16[4,136,256]{2,1,0:T(8,128)(2,1)S(1)} %collective-permute-done.6.rest_12_), channel_id=1, source_target_pairs={{0,28},{1,29},{2,30},{3,31},{4,0},{5,1},{6,2},{7,3},{8,4},{9,5},{1... | collective-permute-start | bytes 835592 | tf_op jit(solution)/shard_map/ppermute | solution.py:275
  53.1 22.9 %copy-start.3 = (bf16[2,256,640]{2,1,0:T(8,128)(2,1)}, bf16[2,256,640]{2,1,0:T(8,128)(2,1)S(1)}, u32[]{:S(2)}) copy-start(bf16[2,256,640]{2,1,0:T(8,128)(2,1)S(1)} %collective-permute-done.12.rest_3_) | copy-start | bytes 1966084
  54.8 10.7 %collective-permute-start.16 = (bf16[2,256,640]{2,1,0:T(8,128)(2,1)S(1)}, bf16[2,256,640]{2,1,0:T(8,128)(2,1)}, u32[]{:S(2)}, u32[]{:S(2)}) collective-permute-start(bf16[2,256,640]{2,1,0:T(8,128)(2,1)S(1)} %collective-permute-done.12.rest_3_), channel_id=1, source_target_pairs={{0,32},{32,0},{64,96},{96,64},{128,160},{160,128},{192,224},{224,1... | collective-permute-start | bytes 1966088 | tf_op jit(solution)/shard_map/ppermute | solution.py:284
  54.9 10.7 %collective-permute-start.15 = (bf16[4,136,256]{2,1,0:T(8,128)(2,1)}, bf16[4,136,256]{2,1,0:T(8,128)(2,1)}, u32[]{:S(2)}, u32[]{:S(2)}) collective-permute-start(bf16[4,136,256]{2,1,0:T(8,128)(2,1)} %collective-permute-done.10.rest_13_), channel_id=1, source_target_pairs={{0,4},{1,5},{2,6},{3,7},{4,8},{5,9},{6,10},{7,11},{8,12},{9,13},{1... | collective-permute-start | bytes 835592 | tf_op jit(solution)/shard_map/ppermute | solution.py:275
  67.6 25.0 %all-to-all-start = ((bf16[32,64,128]{2,1,0:T(8,128)(2,1)}), bf16[32,64,128]{2,1,0:T(8,128)(2,1)S(1)}, u32[]{:S(2)}, u32[]{:S(2)}) async-start(bf16[32,64,128]{2,1,0:T(8,128)(2,1)} %bitcast.16), calls=%async_computation | async-start | bytes 1048576 | tf_op jit(solution)/shard_map/all_to_all | solution.py:357
  92.6 21.2 %all-to-all-start.1 = ((bf16[8,4,64,128]{3,2,1,0:T(8,128)(2,1)}), bf16[8,4,64,128]{3,2,1,0:T(8,128)(2,1)S(1)}, u32[]{:S(2)}, u32[]{:S(2)}) async-start(bf16[8,4,64,128]{3,2,1,0:T(8,128)(2,1)} %bitcast.33), calls=%async_computation.1 | async-start | bytes 1048576 | tf_op jit(solution)/shard_map/all_to_all | solution.py:384
  104.4 9.4 %collective-permute-start.17 = (bf16[32,4096]{1,0:T(8,128)(2,1)S(1)}, bf16[32,4096]{1,0:T(8,128)(2,1)S(1)}, u32[]{:S(2)}, u32[]{:S(2)}) collective-permute-start(bf16[32,4096]{1,0:T(8,128)(2,1)S(1)} %slice_bitcast_fusion), channel_id=1, source_target_pairs={{0,32},{32,0},{64,96},{96,64},{128,160},{160,128},{192,224},{224,1... | collective-permute-start | bytes 786440 | tf_op jit(solution)/shard_map/ppermute | solution.py:284
  115.0 13.3 %collective-permute-start.18 = (bf16[32,4096]{1,0:T(8,128)(2,1)S(1)}, bf16[32,4096]{1,0:T(8,128)(2,1)S(1)}, u32[]{:S(2)}, u32[]{:S(2)}) collective-permute-start(bf16[32,4096]{1,0:T(8,128)(2,1)S(1)} %fusion), channel_id=1, source_target_pairs={{0,64},{32,96},{64,128},{96,160},{128,192},{160,224},{192,0},{224,... | collective-permute-start | bytes 786440 | tf_op jit(solution)/shard_map/ppermute | solution.py:280
  115.1 13.2 %collective-permute-start.19 = (bf16[32,4096]{1,0:T(8,128)(2,1)S(1)}, bf16[32,4096]{1,0:T(8,128)(2,1)S(1)}, u32[]{:S(2)}, u32[]{:S(2)}) collective-permute-start(bf16[32,4096]{1,0:T(8,128)(2,1)S(1)} %fusion), channel_id=1, source_target_pairs={{0,192},{32,224},{64,0},{96,32},{128,64},{160,96},{192,128},{224,1... | collective-permute-start | bytes 786440 | tf_op jit(solution)/shard_map/ppermute | solution.py:280
  118.3 10.0 %collective-permute-start.20 = (bf16[32,4096]{1,0:T(8,128)(2,1)S(1)}, bf16[32,4096]{1,0:T(8,128)(2,1)S(1)}, u32[]{:S(2)}, u32[]{:S(2)}) collective-permute-start(bf16[32,4096]{1,0:T(8,128)(2,1)S(1)} %fusion), channel_id=1, source_target_pairs={{0,128},{32,160},{64,192},{96,224},{128,0},{160,32},{192,64},{224,... | collective-permute-start | bytes 786440 | tf_op jit(solution)/shard_map/ppermute | solution.py:280
  128.4 11.4 %collective-permute-start.21 = (bf16[32,4096]{1,0:T(8,128)(2,1)S(1)}, bf16[32,4096]{1,0:T(8,128)(2,1)S(1)}, u32[]{:S(2)}, u32[]{:S(2)}) collective-permute-start(bf16[32,4096]{1,0:T(8,128)(2,1)S(1)} %add_convert_fusion), channel_id=1, source_target_pairs={{0,32},{32,0},{64,96},{96,64},{128,160},{160,128},{192,224},{224,1... | collective-permute-start | bytes 786440 | tf_op jit(solution)/shard_map/ppermute | solution.py:284
  128.5 10.7 %all-to-all-start.2 = ((bf16[4,128,256]{2,1,0:T(8,128)(2,1)}), bf16[4,128,256]{2,1,0:T(8,128)(2,1)S(1)}, u32[]{:S(2)}, u32[]{:S(2)}) async-start(bf16[4,128,256]{2,1,0:T(8,128)(2,1)} %read_out.1), calls=%async_computation.2 | async-start | bytes 524288 | tf_op jit(solution)/shard_map/all_to_all | solution.py:428
  (8 other events, 41.8 us)

commit v6 on v5

--- a/solution.py
+++ b/solution.py
@@ -15,9 +15,6 @@
 LANE8 = 8
 GROUPS = CHANS // LANE8
 LENGTH = BLOCKS * BLOCK
-X = 4
-CORES = 2
-X_STEPS = (0, -1, 1, 2)
 f32 = jnp.float32
 bf16 = jnp.bfloat16
 
@@ -95,14 +92,11 @@
         copy.wait()
 
 
-def weight_copies(place_ref, weight_hbms, take):
+def weight_copies(weight_hbm, weight, sems):
     copies = []
-    for number, weight_hbm in enumerate(weight_hbms):
-        core = place_ref[3] if number < X else 1 - place_ref[3]
-        group = lax.rem(place_ref[2] + (X_STEPS[number % X] + X), X) * CORES + core
-        for slot in range(2):
-            for lanes, target, sem in take(number * 2 + slot, group, slot):
-                copies.append(pltpu.make_async_copy(weight_hbm.at[slot, :, lanes], target, sem))
+    for slot in range(weight_hbm.shape[0]):
+        lanes = pl.ds(slot % 2 * 2 * CHANS, 2 * CHANS)
+        copies.append(pltpu.make_async_copy(weight_hbm.at[slot], weight.at[slot // 2, :, lanes], sems.at[slot]))
     return copies
 
 
@@ -136,37 +130,51 @@
     return jnp.where(index % 2 == 1, Z - (index + 1) // 2, index // 2)
 
 
-def forward_kernel(place_ref, taps_ref, gain_ref, twist_ref, filter_hbm, *rest):
-    devices = X * CORES
-    weight_hbms = rest[:devices]
-    chunk_hbms = rest[devices : devices + Z]
-    table_hbms = rest[devices + Z : devices + Z + 4]
-    gated_ref, gate_ref, spectrum_ref, both, rows, weight, spectra, *rest = rest[devices + Z + 4 :]
+def read_in_kernel(weight_hbm, *rest):
+    chunk_hbms = rest[:-5]
+    out_ref, rows, weight, weight_sems, sems = rest[-5:]
+    loads = weight_copies(weight_hbm, weight, weight_sems)
+    for index, chunk in enumerate(chunk_hbms):
+        loads.append(pltpu.make_async_copy(chunk, rows.at[pl.ds(index * Y, Y)], sems.at[index]))
+    start_all(loads)
+    wait_all(loads)
+
+    def step(index, carry):
+        blocks = project(rows, index * Y, Y, weight)
+        for y_index in range(Y):
+            out_ref[index * Y + y_index] = blocks[y_index]
+        return carry
+
+    lax.fori_loop(0, len(chunk_hbms), step, 0)
+
+
+def forward_kernel(place_ref, taps_ref, gain_ref, twist_ref, filter_hbm, weight_hbm, early_hbm, *rest):
+    late = Z - early_hbm.shape[0] // Y
+    chunk_hbms = rest[:late]
+    table_hbms = rest[late : late + 4]
+    gated_ref, gate_ref, spectrum_ref, both, rows, weight, spectra, *rest = rest[late + 4 :]
     tables = rest[:4]
-    weight_sems, row_sems, sems = rest[4:]
-    width = 2 * CHANS
-    take = lambda number, group, slot: [
-        (pl.ds(0, width), weight.at[group, :, pl.ds(slot * width, width)], weight_sems.at[number])
-    ]
-    loads = weight_copies(place_ref, weight_hbms, take)
-    chunks = []
+    weight_sems, row_sems, early_sems, sems = rest[4:]
+    loads = weight_copies(weight_hbm, weight, weight_sems)
     for index, chunk in enumerate(chunk_hbms):
-        chunks.append(pltpu.make_async_copy(chunk, rows.at[pl.ds(index * Y, Y)], row_sems.at[index]))
+        loads.append(pltpu.make_async_copy(chunk, rows.at[pl.ds(index * Y, Y)], row_sems.at[index]))
+    others = []
+    for index in range(early_hbm.shape[0]):
+        target = both.at[block_of(place_ref, z_step_of(index // Y), index % Y)]
+        others.append(pltpu.make_async_copy(early_hbm.at[index], target, early_sems.at[index]))
     pairs = [(filter_hbm, spectra)] + list(zip(table_hbms, tables))
-    others = [pltpu.make_async_copy(source, target, sems.at[index]) for index, (source, target) in enumerate(pairs)]
+    others += [pltpu.make_async_copy(source, target, sems.at[index]) for index, (source, target) in enumerate(pairs)]
     start_all(loads)
-    start_all(chunks)
     start_all(others)
     wait_all(loads)
-    wait_all(chunks)
 
     def read_in(index, carry):
         blocks = project(rows, index * Y, Y, weight)
         for y_index in range(Y):
-            both[block_of(place_ref, z_step_of(index), y_index)] = blocks[y_index]
+            both[block_of(place_ref, z_step_of(index + Z - late), y_index)] = blocks[y_index]
         return carry
 
-    lax.fori_loop(0, Z, read_in, 0, unroll=2)
+    lax.fori_loop(0, late, read_in, 0)
     cosine, sine = twists_of(twist_ref)
     lane = lax.broadcasted_iota(jnp.int32, (BLOCKS, LANE8, BLOCK), 2)
     count = BLOCKS * LANE8
@@ -206,7 +214,7 @@
     lax.fori_loop(0, GROUPS // 2, step, 0)
 
 
-def gradient_kernel(place_ref, grad_ref, gate_ref, spectrum_ref, first_ref, second_ref, back_second_ref, back_first_ref, twist_ref, out_ref):
+def gradient_kernel(grad_ref, gate_ref, spectrum_ref, first_ref, second_ref, back_second_ref, back_first_ref, twist_ref, out_ref):
     cosine, sine = twists_of(twist_ref)
     count = BLOCKS * LANE8
     products = (grad_ref[...].astype(f32) * gate_ref[...].astype(f32)).astype(bf16).astype(f32)
@@ -221,26 +229,14 @@
     for half in range(2):
         lanes = slice(half * BLOCK, (half + 1) * BLOCK)
         both.append(jnp.concatenate([result[i * LANE8 : (i + 1) * LANE8, lanes] for i in range(BLOCKS)], 1))
-    out_ref[0] = jnp.concatenate(both, 0).astype(bf16)
-
-
-def read_out_kernel(place_ref, rows_hbm, marks_hbm, *rest):
-    devices = X * CORES
-    weight_hbms = rest[:devices]
-    out_ref, weight, rows_all, chunk_all, weight_sems, sems = rest[devices:]
+    out_ref[...] = jnp.concatenate(both, 0).astype(bf16)
+
+
+def read_out_kernel(place_ref, rows_hbm, marks_hbm, weight_hbm, out_ref, weight, rows_all, chunk_all, weight_sems, sems):
     slots, inner, width = weight.shape
     trials = BLOCK // TRIAL
-    top = inner // 2
-    take = lambda number, group, slot: [
-        (
-            pl.ds(2 * CHANS + half * width, width),
-            weight.at[group * 2 + slot, pl.ds(half * top, top), :],
-            weight_sems.at[number * 2 + half],
-        )
-        for half in range(2)
-    ]
     first = [pltpu.make_async_copy(rows_hbm, rows_all, sems.at[0]), pltpu.make_async_copy(marks_hbm, chunk_all, sems.at[1])]
-    loads = weight_copies(place_ref, weight_hbms, take)
+    loads = [pltpu.make_async_copy(weight_hbm.at[slot], weight.at[slot], weight_sems.at[slot]) for slot in range(slots)]
     start_all(first)
     start_all(loads)
     wait_all(first)
@@ -248,40 +244,29 @@
     rows = jnp.concatenate([rows_all[:, block, :, :].reshape(inner, BLOCK).T for block in places], 0)
     marks = chunk_all[...].astype(f32).reshape(Y * trials, chunk_all.shape[2])
     marks = jnp.concatenate([marks] * (inner // width), 1)
-    marks = jnp.broadcast_to(marks[:, None, :], (Y * trials, TRIAL, inner)).reshape(Y * BLOCK, inner).astype(bf16)
-    nothing = jnp.zeros_like(rows)
     total = jnp.zeros((Y * BLOCK, width), f32)
-    for number in range(0, devices, 2):
-        for load in loads[number * 4 : number * 4 + 8]:
-            load.wait()
-        for offset in range(2):
-            core = place_ref[3] if number + offset < X else 1 - place_ref[3]
-            group = lax.rem(place_ref[2] + (X_STEPS[(number + offset) % X] + X), X) * CORES + core
-            wide = []
-            for slot in range(2):
-                mark = (group * 2 + slot).astype(f32).astype(bf16)
-                wide.append(jnp.where(marks == mark, rows, nothing))
-            pair = weight[pl.ds(group * 2, 2)].reshape(2 * inner, width)
-            total = total + jnp.dot(jnp.concatenate(wide, 1), pair, preferred_element_type=f32)
+    part = slots // 2
+    for start in range(0, slots, part):
+        wait_all(loads[start : start + part])
+        wide = spread(rows, marks - start, part)
+        total = total + jnp.dot(wide, weight[start : start + part].reshape(part * inner, width), preferred_element_type=f32)
     for index, block in enumerate(places):
         out_ref[block] = total[index * BLOCK : (index + 1) * BLOCK].astype(bf16)
 
 
+def sum_kernel(parts_ref, out_ref):
+    total = parts_ref[0].astype(f32)
+    for index in range(1, parts_ref.shape[0]):
+        total = total + parts_ref[index].astype(f32)
+    out_ref[...] = total
+
+
 def along_y(value, step):
     return lax.ppermute(value, "seq", [(z * Y + y, z * Y + (y + step) % Y) for z in range(Z) for y in range(Y)])
 
 
 def along_z(value, step):
     return lax.ppermute(value, "seq", [(z * Y + y, (z + step) % Z * Y + y) for z in range(Z) for y in range(Y)])
-
-
-def along_x(value, step):
-    pairs = [(x * CORES + c, (x + step) % X * CORES + c) for x in range(X) for c in range(CORES)]
-    return lax.ppermute(value, "grp", pairs)
-
-
-def other_core(value):
-    return lax.ppermute(value, "grp", [(group, group ^ 1) for group in range(X * CORES)])
 
 
 def whole(count):
@@ -292,12 +277,11 @@
     in_chans = spikes.shape[2]
     model_width = short_kernel.shape[1]
     place = lax.axis_index("seq")
-    group = lax.axis_index("grp")
     scalar = pl.BlockSpec(memory_space=pltpu.SMEM)
     hbm = pl.BlockSpec(memory_space=pltpu.HBM)
     z_groups = [[z * Y + y for z in range(Z)] for y in range(Y)]
     y_groups = [[z * Y + y for y in range(Y)] for z in range(Z)]
-    coords = jnp.stack([place // Y, place % Y, group // CORES, group % CORES]).astype(jnp.int32)
+    coords = jnp.stack([place // Y, place % Y]).astype(jnp.int32)
     first, second, back_second, back_first, twists = transform_tables()
     params = pltpu.CompilerParams(vmem_limit_bytes=60 << 20)
     spectrum_shape = jax.ShapeDtypeStruct((GROUPS, BLOCKS * LANE8, 2 * BLOCK), bf16)
@@ -311,18 +295,16 @@
     slots = jnp.sum(jnp.where(matches, session_slot[None, :], 0), axis=1)
     marks = jnp.broadcast_to(slots.astype(bf16)[:, None], (slots.shape[0], in_chans))
     block = jnp.concatenate([spikes[0], marks], 0)
-    block, readin_weight, readout_weight = lax.optimization_barrier((block, readin_weight, readout_weight))
     chunk = jnp.stack([block, along_y(block, 1), along_y(block, -1), along_y(block, 2)])
     own_marks = chunk[:, BLOCK:, :]
     right, left = along_z(chunk, 1), along_z(chunk, -1)
     chunks = [chunk, right, left]
 
     pieces = [lax.dynamic_slice_in_dim(readin_weight, start + place * CHANS, CHANS, 2) for start in (0, model_width)]
-    split = readout_weight.reshape(2, 2, Z // 2, Y, CHANS, in_chans)
-    split = lax.dynamic_index_in_dim(split, place % Y, 3, keepdims=False).reshape(2, 2, Z // 2 * CHANS, in_chans)
-    own = jnp.concatenate(pieces + [split[:, 0], split[:, 1]], 2)
-    own_right, own_left = along_x(own, 1), along_x(own, -1)
-    own_other = other_core(own)
+    in_weights = lax.all_gather(jnp.concatenate(pieces, 2), "grp", axis=0, tiled=True)
+    split = readout_weight.reshape(2, Z, Y, CHANS, in_chans)
+    split = lax.dynamic_index_in_dim(split, place % Y, 2, keepdims=False).reshape(2, Z * CHANS, in_chans)
+    out_weights = lax.all_gather(split, "grp", axis=0, tiled=True)
 
     filter_spectrum = pl.pallas_call(
         filter_kernel,
@@ -338,26 +320,37 @@
     right, left, filter_spectrum, own_marks = lax.optimization_barrier((right, left, filter_spectrum, own_marks))
     right, left = along_z(right, 1), along_z(left, -1)
     chunks += [right, left]
-    ready = (right, left, own_right, own_left, own_other)
-    right, left, own_right, own_left, own_other = lax.optimization_barrier(ready)
-    right, left = along_z(right, 1), along_z(left, -1)
-    chunks += [right, left]
-    far = along_x(own_right, 1)
-    right_other, left_other = other_core(own_right), other_core(own_left)
+    turned = out_grad[0].T.reshape(BLOCKS, CHANS, BLOCK)
     taps = lax.dynamic_slice_in_dim(short_kernel, place * CHANS, CHANS, 1)
     taps = jnp.broadcast_to(taps[:, :, None], (short_kernel.shape[0], CHANS, BLOCK))
     gains = jnp.broadcast_to(skip_gain[:, None], (CHANS, BLOCK))
-    right, left, far, right_other, left_other = lax.optimization_barrier((right, left, far, right_other, left_other))
-    far_other = other_core(far)
-    weights = [own, own_right, own_left, far, own_other, right_other, left_other, far_other]
-    turned = out_grad[0].T.reshape(BLOCKS, CHANS, BLOCK)
-    ready = (along_z(right, 1), taps, gains, coords, turned, weights[-1])
-    right, taps, gains, coords, turned, weights[-1] = lax.optimization_barrier(ready)
-    chunks.append(right)
+    ready = (right, left, taps, gains, coords, turned)
+    right, left, taps, gains, coords, turned = lax.optimization_barrier(ready)
+    right, left = along_z(right, 1), along_z(left, -1)
+    slot_count = session_slot.shape[0]
+    width = 2 * CHANS
+    early_blocks = len(chunks) * Y
+    early = pl.pallas_call(
+        read_in_kernel,
+        out_shape=jax.ShapeDtypeStruct((early_blocks, width, BLOCK), bf16),
+        in_specs=[hbm] * (1 + len(chunks)),
+        out_specs=whole(1)[0],
+        scratch_shapes=[
+            pltpu.VMEM((early_blocks,) + chunk.shape[1:], bf16),
+            pltpu.VMEM((slot_count // 2, in_chans, 2 * width), bf16),
+            pltpu.SemaphoreType.DMA((slot_count,)),
+            pltpu.SemaphoreType.DMA((len(chunks),)),
+        ],
+        compiler_params=params,
+        cost_estimate=pl.CostEstimate(flops=work, bytes_accessed=4 << 20, transcendentals=0),
+        name="read_in",
+    )(in_weights, *chunks)
+    right, left, early = lax.optimization_barrier((right, left, early))
+    late = [right, left, along_z(right, 1)]
+    late[2], turned = lax.optimization_barrier((late[2], turned))
     grads = lax.all_to_all(turned, "seq", split_axis=0, concat_axis=0, tiled=True)
 
     tables = (first, second, back_second, back_first)
-    slot_count = session_slot.shape[0]
     gated, gates, spectrum = pl.pallas_call(
         forward_kernel,
         out_shape=(
@@ -365,66 +358,62 @@
             jax.ShapeDtypeStruct(plane, bf16),
             spectrum_shape,
         ),
-        in_specs=[scalar] + whole(3) + [hbm] * (1 + X * CORES + Z + 4),
+        in_specs=[scalar] + whole(3) + [hbm] * (3 + len(late) + 4),
         out_specs=tuple(whole(3)),
         scratch_shapes=[
             pltpu.VMEM((BLOCKS, 2 * CHANS, BLOCK), bf16),
-            pltpu.VMEM((BLOCKS,) + chunk.shape[1:], bf16),
+            pltpu.VMEM((len(late) * Y,) + chunk.shape[1:], bf16),
             pltpu.VMEM((slot_count // 2, in_chans, 4 * CHANS), bf16),
             pltpu.VMEM(spectrum_shape.shape, bf16),
         ]
         + [pltpu.VMEM(table.shape, bf16) for table in tables]
-        + [pltpu.SemaphoreType.DMA((count,)) for count in (slot_count, Z, 5)],
+        + [pltpu.SemaphoreType.DMA((count,)) for count in (slot_count, len(late), early_blocks, 5)],
         compiler_params=params,
         cost_estimate=pl.CostEstimate(flops=4 * work, bytes_accessed=8 << 20, transcendentals=0),
         name="long_convolution",
-    )(coords, taps, gains, twists, filter_spectrum, *weights, *chunks, *tables)
+    )(coords, taps, gains, twists, filter_spectrum, in_weights, early, *late, *tables)
 
     gated = gated.reshape(Z, Y, CHANS, BLOCK)
     arrived = lax.all_to_all(gated, "seq", split_axis=0, concat_axis=0, tiled=True, axis_index_groups=z_groups)
-    half = CHANS // CORES
-    fixed = lambda table: pl.BlockSpec(table.shape, lambda i, place, rank=table.ndim: (0,) * rank)
-    steps = half // pair
-    halves = pl.pallas_call(
+    own_grad = pl.pallas_call(
         gradient_kernel,
-        out_shape=jax.ShapeDtypeStruct((CORES, half, LENGTH), bf16),
-        grid_spec=pltpu.PrefetchScalarGridSpec(
-            num_scalar_prefetch=1,
-            grid=(GROUPS // 2,),
-            in_specs=[pl.BlockSpec((BLOCKS, pair, BLOCK), lambda i, place: (0, i, 0))] * 2
-            + [pl.BlockSpec((2,) + spectrum_shape.shape[1:], lambda i, place: (i, 0, 0))]
-            + [fixed(table) for table in tables + (twists,)],
-            out_specs=pl.BlockSpec((1, pair, LENGTH), lambda i, place: (lax.rem(i // steps + place[3], 2), i % steps, 0)),
-        ),
+        out_shape=jax.ShapeDtypeStruct((CHANS, LENGTH), bf16),
+        grid=(GROUPS // 2,),
+        in_specs=[pl.BlockSpec((BLOCKS, pair, BLOCK), lambda i: (0, i, 0))] * 2
+        + [pl.BlockSpec((2,) + spectrum_shape.shape[1:], lambda i: (i, 0, 0))]
+        + [same(table) for table in tables + (twists,)],
+        out_specs=pl.BlockSpec((pair, LENGTH), lambda i: (i, 0)),
         compiler_params=params,
         cost_estimate=pl.CostEstimate(flops=2 * work, bytes_accessed=4 << 20, transcendentals=0),
         name="filter_gradient",
-    )(coords, grads, gates, spectrum, *tables, twists)
-    came = other_core(halves[1])
-    plus = lambda *terms: sum(term.astype(f32) for term in terms).astype(bf16)
-    came, arrived = lax.optimization_barrier((came, arrived))
-    total = plus(halves[0], came)
-    cames = [along_x(total, step) for step in (1, -1, 2)]
+    )(grads, gates, spectrum, *tables, twists)
+    all_grads = lax.all_gather(own_grad, "grp", axis=0, tiled=False)
+    lanes = LENGTH // 8
+    filter_grad = pl.pallas_call(
+        sum_kernel,
+        out_shape=jax.ShapeDtypeStruct((CHANS, LENGTH), f32),
+        grid=(LENGTH // lanes,),
+        in_specs=[pl.BlockSpec((all_grads.shape[0], CHANS, lanes), lambda i: (0, 0, i))],
+        out_specs=pl.BlockSpec((CHANS, lanes), lambda i: (0, i)),
+        compiler_params=params,
+        cost_estimate=pl.CostEstimate(flops=all_grads.size, bytes_accessed=5 << 20, transcendentals=0),
+        name="sum_gradients",
+    )(all_grads)
     partial = pl.pallas_call(
         read_out_kernel,
         out_shape=jax.ShapeDtypeStruct((Y, BLOCK, in_chans), bf16),
-        in_specs=[scalar] + [hbm] * (2 + X * CORES),
+        in_specs=[scalar] + [hbm] * 3,
         out_specs=whole(1)[0],
         scratch_shapes=[
-            pltpu.VMEM((slot_count, Z * CHANS, in_chans), bf16),
+            pltpu.VMEM(out_weights.shape, bf16),
             pltpu.VMEM((Z, Y, CHANS, BLOCK), bf16),
             pltpu.VMEM((Y, BLOCK // TRIAL, in_chans), bf16),
         ]
-        + [pltpu.SemaphoreType.DMA((count,)) for count in (2 * slot_count, 2)],
+        + [pltpu.SemaphoreType.DMA((count,)) for count in (slot_count, 2)],
         compiler_params=params,
         cost_estimate=pl.CostEstimate(flops=2 * 512 * 512 * 4096, bytes_accessed=6 << 20, transcendentals=0),
         name="read_out",
-    )(coords, arrived, own_marks, *weights)
-    cames, partial = lax.optimization_barrier((cames, partial))
-    total = plus(total, *cames)
-    theirs = other_core(total)
-    lower = coords[3] == 0
-    filter_grad = jnp.concatenate([jnp.where(lower, total, theirs), jnp.where(lower, theirs, total)], 0).astype(f32)
+    )(coords, arrived, own_marks, out_weights)
     pieces = lax.all_to_all(partial, "seq", split_axis=0, concat_axis=0, tiled=True, axis_index_groups=y_groups)
     denoised = jnp.sum(pieces.astype(f32), 0).astype(bf16)
     return denoised[None], filter_grad

time: 143 us -> 138 us (0.965)
  waiting for transfers between devices: 46.2 us -> 14.2 us
  blocking collectives: 0 us -> 28.8 us
  starting transfers between devices: 43.3 us -> 26.9 us
  between operations: 1.56 us -> 13.9 us
  Pallas kernels: 34.3 us -> 41.1 us
  local copies, waits for them, and re-layouts: 9.91 us -> 7.53 us
  other arithmetic: 5.65 us -> 3.9 us
    all_to_all x0 -> x2, blocking collectives: none -> 28.8 us  [the longest x1 18.7 us: local(): lax.all_to_all(gated, 'seq', split_axis=0, concat_axis=0, tiled=True, axi...]
    all_to_all x2 -> x0, waiting for transfers between devices: 13.9 us -> none  [the longest x1 9.27 us: local(): lax.all_to_all(gated, 'seq', split_axis=0, concat_axis=0, tiled=True, axi...]
    ppermute x7, waiting for transfers between devices: 22.7 us -> 9.25 us  [along_z(): lax.ppermute(value, 'seq', [(z * Y + y, (z + step) % Z * Y + y) for z in...]
    pallas_call x1 -> x3, Pallas kernels: 6.46 us -> 18.4 us  [the longest x1 6.69 us: local(): pl.pallas_call(read_in_kernel, out_shape=jax.ShapeDtypeStruct((early_bloc...]
    all_to_all x2 -> x0, starting transfers between devices: 9.18 us -> none  [the longest x1 4.81 us: local(): lax.all_to_all(partial, 'seq', split_axis=0, concat_axis=0, tiled=True, a...]
    ppermute x12 -> x0, starting transfers between devices: 7.52 us -> none  [the longest x6 6.81 us: along_x(): return lax.ppermute(value, 'grp', pairs)]
    ppermute x12 -> x0, waiting for transfers between devices: 7.29 us -> none  [the longest x6 7.27 us: along_x(): return lax.ppermute(value, 'grp', pairs)]
    ppermute x3, waiting for transfers between devices: 0.01 us -> 3.77 us  [along_y(): lax.ppermute(value, 'seq', [(z * Y + y, z * Y + (y + step) % Y) for z in...]
  transfers between devices with their start and end apart: 25 -> 14, of which waited for: 10 -> 7; matrix products, arithmetic and copies ran while one was open for 5% -> 6% of each run, Pallas kernels for 24% -> 26%
where the time goes in v6:
time: 138 us; the launch traced here: 136 us
  Pallas kernels  41.1 us (30%)
  blocking collectives  28.8 us (21%)
  starting transfers between devices  26.9 us (19%)
  waiting for transfers between devices  14.2 us (10%)
  between operations  13.9 us (10%)
  local copies, waits for them, and re-layouts  7.53 us (5%)
  other arithmetic  3.9 us (3%)
    all_to_all x1, blocking collectives, local(): lax.all_to_all(gated, 'seq', split_axis=0, concat_axis=0, tiled=True, axi...  18.7 us
    ppermute x7, starting transfers between devices, along_z(): lax.ppermute(value, 'seq', [(z * Y + y, (z + step) % Z * Y + y) for z in...  13.5 us
    pallas_call x1, Pallas kernels, local(): pl.pallas_call(forward_kernel, out_shape=(jax.ShapeDtypeStruct(plane, bf1...  11.2 us
    all_to_all x1, blocking collectives, local(): lax.all_to_all(partial, 'seq', split_axis=0, concat_axis=0, tiled=True, a...  10 us
    ppermute x7, waiting for transfers between devices, along_z(): lax.ppermute(value, 'seq', [(z * Y + y, (z + step) % Z * Y + y) for z in...  9.25 us
    all_to_all x1, starting transfers between devices, local(): lax.all_to_all(turned, 'seq', split_axis=0, concat_axis=0, tiled=True)  8.67 us
    pallas_call x1, Pallas kernels, local(): pl.pallas_call(read_out_kernel, out_shape=jax.ShapeDtypeStruct((Y, BLOCK,...  7.01 us
    pallas_call x1, Pallas kernels, local(): pl.pallas_call(read_in_kernel, out_shape=jax.ShapeDtypeStruct((early_bloc...  6.69 us
  transfers between devices with their start and end apart: 14, of which 7 were waited for; matrix products, arithmetic and copies ran while one was open for 6% of the time, Pallas kernels for 26%

profile of v6, /device:TPU:8, one launch (start us, length us, event | category | flops | bytes accessed | tf_op | source)
XLA Modules:
  0.0 136.3 jit_solution(3691112861080787244)
XLA Ops:
  7.3 1.3 constant_dynamic-slice_fusion.2
  8.5 0.8 pad_maximum_fusion.1
  9.4 0.9 constant_dynamic-slice_fusion
  10.3 0.7 slice.6
  11.1 0.8 select_reduce_fusion
  11.9 0.9 fusion
  12.9 1.7 %collective-permute-start = (bf16[136,256]{1,0:T(8,128)(2,1)S(1)}, bf16[136,256]{1,0:T(8,128)(2,1)S(1)}, u32[]{:S(2)}, u32[]{:S(2)}) collective-permute-start(bf16[136,256]{1,0:T(8,128)(2,1)S(1)} %get-tuple-element.41), channel_id=1, source_target_pairs={{0,1},{1,2},{2,3},{3,0},{4,5},{5,6},{6,7},{7,4},{8,9},{9,10},{10,1... | collective-permute-start | bytes 208904 | tf_op jit(solution)/shard_map/ppermute | solution.py:265
  15.2 2.0 %collective-permute-start.2 = (bf16[136,256]{1,0:T(8,128)(2,1)S(1)}, bf16[136,256]{1,0:T(8,128)(2,1)S(1)}, u32[]{:S(2)}, u32[]{:S(2)}) collective-permute-start(bf16[136,256]{1,0:T(8,128)(2,1)S(1)} %get-tuple-element.41), channel_id=1, source_target_pairs={{0,2},{1,3},{2,0},{3,1},{4,6},{5,7},{6,4},{7,5},{8,10},{9,11},{10,... | collective-permute-start | bytes 208904 | tf_op jit(solution)/shard_map/ppermute | solution.py:265
  17.4 2.2 %collective-permute-done.1 = bf16[136,256]{1,0:T(8,128)(2,1)S(1)} collective-permute-done((bf16[136,256]{1,0:T(8,128)(2,1)S(1)}, bf16[136,256]{1,0:T(8,128)(2,1)S(1)}, u32[]{:S(2)}, u32[]{:S(2)}) %collective-permute-start.1) | collective-permute-done | bytes 69664 | tf_op jit(solution)/shard_map/ppermute | solution.py:265
  19.6 1.5 %collective-permute-done.2 = bf16[136,256]{1,0:T(8,128)(2,1)S(1)} collective-permute-done((bf16[136,256]{1,0:T(8,128)(2,1)S(1)}, bf16[136,256]{1,0:T(8,128)(2,1)S(1)}, u32[]{:S(2)}, u32[]{:S(2)}) %collective-permute-start.2) | collective-permute-done | bytes 69664 | tf_op jit(solution)/shard_map/ppermute | solution.py:265
  21.1 1.7 %collective-permute-start.3 = (bf16[4,136,256]{2,1,0:T(8,128)(2,1)S(1)}, bf16[4,136,256]{2,1,0:T(8,128)(2,1)S(1)}, u32[]{:S(2)}, u32[]{:S(2)}) collective-permute-start(bf16[4,136,256]{2,1,0:T(8,128)(2,1)S(1)} %pad_maximum_fusion.rest_0_), channel_id=1, source_target_pairs={{0,4},{1,5},{2,6},{3,7},{4,8},{5,9},{6,10},{7,11},{8,12},{9,13},{1... | collective-permute-start | bytes 835592 | tf_op jit(solution)/shard_map/ppermute | solution.py:269
  22.8 4.0 %collective-permute-start.4 = (bf16[4,136,256]{2,1,0:T(8,128)(2,1)S(1)}, bf16[4,136,256]{2,1,0:T(8,128)(2,1)S(1)}, u32[]{:S(2)}, u32[]{:S(2)}) collective-permute-start(bf16[4,136,256]{2,1,0:T(8,128)(2,1)S(1)} %pad_maximum_fusion.rest_0_), channel_id=1, source_target_pairs={{0,28},{1,29},{2,30},{3,31},{4,0},{5,1},{6,2},{7,3},{8,4},{9,5},{1... | collective-permute-start | bytes 835592 | tf_op jit(solution)/shard_map/ppermute | solution.py:269
  26.9 4.4 %filter_transform.1.filter_hbm = bf16[8,256,256]{2,1,0:T(8,128)(2,1)} custom-call(f32[64,4096]{1,0:T(8,128)} %filter_ref.1, bf16[512,256]{1,0:T(8,128)(2,1)} %constant.58.clone.first_ref.rest_3_, bf16[256,256]{1,0:T(8,128)(2,1)} %constant.59.clone.second_ref.rest_4_, f32[2,32,128]{2,1,0:T(8,128)} %constant.62.clone.twist_ref), custom_call_target="tpu_custom_call" | custom-call | flops 536870912 | bytes 4194304 | tf_op jit(solution)/shard_map/filter_transform/pallas_call | solution.py:309
  32.2 3.2 %collective-permute-start.6 = (bf16[4,136,256]{2,1,0:T(8,128)(2,1)S(1)}, bf16[4,136,256]{2,1,0:T(8,128)(2,1)}, u32[]{:S(2)}, u32[]{:S(2)}) collective-permute-start(bf16[4,136,256]{2,1,0:T(8,128)(2,1)S(1)} %collective-permute-done.4.rest_2_), channel_id=1, source_target_pairs={{0,28},{1,29},{2,30},{3,31},{4,0},{5,1},{6,2},{7,3},{8,4},{9,5},{1... | collective-permute-start | bytes 835592 | tf_op jit(solution)/shard_map/ppermute | solution.py:269
  35.4 1.0 copy.20
  37.0 0.8 constant_dynamic-slice_fusion.3
  37.8 2.4 %collective-permute-done.5.rest_3_ = bf16[4,136,256]{2,1,0:T(8,128)(2,1)} collective-permute-done((bf16[4,136,256]{2,1,0:T(8,128)(2,1)S(1)}, bf16[4,136,256]{2,1,0:T(8,128)(2,1)}, u32[]{:S(2)}, u32[]{:S(2)}) %collective-permute-start.5) | collective-permute-done | bytes 278560 | tf_op jit(solution)/shard_map/ppermute | solution.py:269
  40.2 0.7 broadcast_in_dim.38.taps_ref
  41.6 2.3 %collective-permute-start.7 = (bf16[4,136,256]{2,1,0:T(8,128)(2,1)}, bf16[4,136,256]{2,1,0:T(8,128)(2,1)S(1)}, u32[]{:S(2)}, u32[]{:S(2)}) collective-permute-start(bf16[4,136,256]{2,1,0:T(8,128)(2,1)} %collective-permute-done.5.rest_3_), channel_id=1, source_target_pairs={{0,4},{1,5},{2,6},{3,7},{4,8},{5,9},{6,10},{7,11},{8,12},{9,13},{1... | collective-permute-start | bytes 835592 | tf_op jit(solution)/shard_map/ppermute | solution.py:269
  43.8 1.0 collective-permute-start.8
  44.8 6.7 %read_in.1.early_hbm = bf16[20,128,128]{2,1,0:T(8,128)(2,1)} custom-call(bf16[16,256,128]{2,1,0:T(8,128)(2,1)} %all-gather.5.cloned.1.call-done.weight_hbm, bf16[4,136,256]{2,1,0:T(8,128)(2,1)} %copy-done.1, bf16[4,136,256]{2,1,0:T(8,128)(2,1)} %copy-done.5, bf16[4,136,256]{2,1,0:T(8,128)(2,1)} %copy-done.6, ...), custom_call_target="tpu_custom_call" | custom-call | flops 536870912 | bytes 4194304 | tf_op jit(solution)/shard_map/read_in/pallas_call | solution.py:333
  51.6 1.2 collective-permute-start.9
  52.7 6.7 %collective-permute-done.9.rest_2_ = bf16[4,136,256]{2,1,0:T(8,128)(2,1)S(1)} collective-permute-done((bf16[4,136,256]{2,1,0:T(8,128)(2,1)S(1)}, bf16[4,136,256]{2,1,0:T(8,128)(2,1)S(1)}, u32[]{:S(2)}, u32[]{:S(2)}) %collective-permute-start.9) | collective-permute-done | bytes 278560 | tf_op jit(solution)/shard_map/ppermute | solution.py:269
  59.4 8.7 %all-to-all-start.2 = ((bf16[32,64,128]{2,1,0:T(8,128)(2,1)}), bf16[32,64,128]{2,1,0:T(8,128)(2,1)S(1)}, u32[]{:S(2)}, u32[]{:S(2)}) async-start(bf16[32,64,128]{2,1,0:T(8,128)(2,1)} %bitcast.10), calls=%async_computation.2 | async-start | bytes 1048576 | tf_op jit(solution)/shard_map/all_to_all | solution.py:351
  68.3 11.2 %long_convolution.1 = (bf16[32,64,128]{2,1,0:T(8,128)(2,1)}, bf16[32,64,128]{2,1,0:T(8,128)(2,1)}, bf16[8,256,256]{2,1,0:T(8,128)(2,1)}) custom-call(s32[2]{0:T(128)} %pad_add_fusion.place_ref, f32[3,64,128]{2,1,0:T(8,128)} %broadcast_in_dim.38.taps_ref, f32[64,128]{1,0:T(8,128)} %broadcast_in_dim.39.gain_ref, f32[2,32,128]{2,1,0:T(8,128)} %constant.62.clone.twist_ref, ...), custom_call_target="tpu_custom_call" | custom-call | flops 2147483648 | bytes 8388608 | tf_op jit(solution)/shard_map/long_convolution/pallas_call | solution.py:354
  79.6 1.1 all-to-all-done.2.grad_ref
  80.7 0.8 copy-done.4
  81.5 5.7 %filter_gradient.1 = bf16[64,4096]{1,0:T(8,128)(2,1)} custom-call(bf16[32,64,128]{2,1,0:T(8,128)(2,1)} %copy-done.4, bf16[32,64,128]{2,1,0:T(8,128)(2,1)} %get-tuple-element.36.gate_ref, bf16[8,256,256]{2,1,0:T(8,128)(2,1)} %get-tuple-element.37.spectrum_ref, bf16[512,256]{1,0:T(8,128)(2,1)} %constant.58.clone.first_ref.rest_3_, ...), custom_call_target="tpu_custom_call" | custom-call | flops 1073741824 | bytes 4194304 | tf_op jit(solution)/shard_map/filter_gradient/pallas_call | solution.py:378
  87.3 18.7 %all_to_all.15.rows_hbm = bf16[8,4,64,128]{3,2,1,0:T(8,128)(2,1)} all-to-all(bf16[8,4,64,128]{3,2,1,0:T(8,128)(2,1)S(1)} %bitcast.24), channel_id=1, replica_groups={{0,4,8,12,16,20,24,28},{1,5,9,13,17,21,25,29},{2,6,10,14,18,22,26,30},{..., dimensions={0} | all-to-all | bytes 1048576 | tf_op jit(solution)/shard_map/all_to_all | solution.py:377
  106.0 7.0 %read_out.1 = bf16[4,128,256]{2,1,0:T(8,128)(2,1)} custom-call(s32[2]{0:T(128)} %pad_add_fusion.place_ref, bf16[8,4,64,128]{3,2,1,0:T(8,128)(2,1)} %all_to_all.15.rows_hbm, bf16[4,8,256]{2,1,0:T(8,128)(2,1)} %slice.8.marks_hbm, bf16[16,512,256]{2,1,0:T(8,128)(2,1)} %all-gather.7.cloned.1.call-done.weight_hbm), custom_call_target="tpu_custom_call" | custom-call | flops 2147483648 | bytes 6291456 | tf_op jit(solution)/shard_map/read_out/pallas_call | solution.py:402
  113.0 10.0 %all_to_all.16 = bf16[4,128,256]{2,1,0:T(8,128)(2,1)S(1)} all-to-all(bf16[4,128,256]{2,1,0:T(8,128)(2,1)} %read_out.1), channel_id=1, replica_groups={{0,1,2,3},{4,5,6,7},{8,9,10,11},{12,13,14,15},{16,17,18,19},{20,21,22,2..., dimensions={0} | all-to-all | bytes 524288 | tf_op jit(solution)/shard_map/all_to_all | solution.py:417
  123.7 6.0 %sum_gradients.1 = f32[64,4096]{1,0:T(8,128)} custom-call(bf16[8,64,4096]{2,1,0:T(8,128)(2,1)} %bitcast.21), custom_call_target="tpu_custom_call" | custom-call | flops 2097152 | bytes 5242880 | tf_op jit(solution)/shard_map/sum_gradients/pallas_call | solution.py:392
  (43 shorter events, 4.2 us)
Async XLA Ops:
  7.2 2.2 %copy-start = (bf16[2,2048,256]{2,1,0:T(8,128)(2,1)S(1)}, bf16[2,2048,256]{2,1,0:T(8,128)(2,1)}, u32[]{:S(2)}) copy-start(bf16[2,2048,256]{2,1,0:T(8,128)(2,1)} %param.21) | copy-start | bytes 6291460
  7.2 28.2 %copy-start.2 = (bf16[1,128,2048]{2,1,0:T(8,128)(2,1)S(1)}, bf16[1,128,2048]{2,1,0:T(8,128)(2,1)}, u32[]{:S(2)}) copy-start(bf16[1,128,2048]{2,1,0:T(8,128)(2,1)} %param.22) | copy-start | bytes 1572868
  7.2 33.7 %copy-start.7 = (f32[64]{0:T(128)S(1)}, f32[64]{0:T(128)}, u32[]{:S(2)}) copy-start(f32[64]{0:T(128)} %param.20) | copy-start | bytes 772
  7.2 37.6 %all-gather.5.cloned.1.call-start = ((), (), s32[]{:S(2)}) async-start(), calls=%async_computation.3 | async-start | bytes 1179648 | tf_op jit(solution)/shard_map/all_gather | solution.py:304
  9.3 96.7 %all-gather.7.cloned.1.call-start = ((), (), s32[]{:S(2)}) async-start(), calls=%async_computation.4 | async-start | bytes 4718592 | tf_op jit(solution)/shard_map/all_gather | solution.py:307
  12.9 4.6 %collective-permute-start = (bf16[136,256]{1,0:T(8,128)(2,1)S(1)}, bf16[136,256]{1,0:T(8,128)(2,1)S(1)}, u32[]{:S(2)}, u32[]{:S(2)}) collective-permute-start(bf16[136,256]{1,0:T(8,128)(2,1)S(1)} %get-tuple-element.41), channel_id=1, source_target_pairs={{0,1},{1,2},{2,3},{3,0},{4,5},{5,6},{6,7},{7,4},{8,9},{9,10},{10,1... | collective-permute-start | bytes 208904 | tf_op jit(solution)/shard_map/ppermute | solution.py:265
  14.5 5.1 %collective-permute-start.1 = (bf16[136,256]{1,0:T(8,128)(2,1)S(1)}, bf16[136,256]{1,0:T(8,128)(2,1)S(1)}, u32[]{:S(2)}, u32[]{:S(2)}) collective-permute-start(bf16[136,256]{1,0:T(8,128)(2,1)S(1)} %get-tuple-element.41), channel_id=1, source_target_pairs={{0,3},{1,0},{2,1},{3,2},{4,7},{5,4},{6,5},{7,6},{8,11},{9,8},{10,9... | collective-permute-start | bytes 208904 | tf_op jit(solution)/shard_map/ppermute | solution.py:265
  15.2 5.8 %collective-permute-start.2 = (bf16[136,256]{1,0:T(8,128)(2,1)S(1)}, bf16[136,256]{1,0:T(8,128)(2,1)S(1)}, u32[]{:S(2)}, u32[]{:S(2)}) collective-permute-start(bf16[136,256]{1,0:T(8,128)(2,1)S(1)} %get-tuple-element.41), channel_id=1, source_target_pairs={{0,2},{1,3},{2,0},{3,1},{4,6},{5,7},{6,4},{7,5},{8,10},{9,11},{10,... | collective-permute-start | bytes 208904 | tf_op jit(solution)/shard_map/ppermute | solution.py:265
  21.1 23.7 %copy-start.1 = (bf16[4,136,256]{2,1,0:T(8,128)(2,1)}, bf16[4,136,256]{2,1,0:T(8,128)(2,1)S(1)}, u32[]{:S(2)}) copy-start(bf16[4,136,256]{2,1,0:T(8,128)(2,1)S(1)} %pad_maximum_fusion.rest_0_) | copy-start | bytes 835588
  21.1 11.0 %collective-permute-start.3 = (bf16[4,136,256]{2,1,0:T(8,128)(2,1)S(1)}, bf16[4,136,256]{2,1,0:T(8,128)(2,1)S(1)}, u32[]{:S(2)}, u32[]{:S(2)}) collective-permute-start(bf16[4,136,256]{2,1,0:T(8,128)(2,1)S(1)} %pad_maximum_fusion.rest_0_), channel_id=1, source_target_pairs={{0,4},{1,5},{2,6},{3,7},{4,8},{5,9},{6,10},{7,11},{8,12},{9,13},{1... | collective-permute-start | bytes 835592 | tf_op jit(solution)/shard_map/ppermute | solution.py:269
  22.8 9.3 %collective-permute-start.4 = (bf16[4,136,256]{2,1,0:T(8,128)(2,1)S(1)}, bf16[4,136,256]{2,1,0:T(8,128)(2,1)S(1)}, u32[]{:S(2)}, u32[]{:S(2)}) collective-permute-start(bf16[4,136,256]{2,1,0:T(8,128)(2,1)S(1)} %pad_maximum_fusion.rest_0_), channel_id=1, source_target_pairs={{0,28},{1,29},{2,30},{3,31},{4,0},{5,1},{6,2},{7,3},{8,4},{9,5},{1... | collective-permute-start | bytes 835592 | tf_op jit(solution)/shard_map/ppermute | solution.py:269
  32.1 12.7 %copy-start.5 = (bf16[4,136,256]{2,1,0:T(8,128)(2,1)}, bf16[4,136,256]{2,1,0:T(8,128)(2,1)S(1)}, u32[]{:S(2)}) copy-start(bf16[4,136,256]{2,1,0:T(8,128)(2,1)S(1)} %collective-permute-done.3.rest_1_) | copy-start | bytes 835588
  32.1 12.7 %copy-start.6 = (bf16[4,136,256]{2,1,0:T(8,128)(2,1)}, bf16[4,136,256]{2,1,0:T(8,128)(2,1)S(1)}, u32[]{:S(2)}) copy-start(bf16[4,136,256]{2,1,0:T(8,128)(2,1)S(1)} %collective-permute-done.4.rest_2_) | copy-start | bytes 835588
  32.1 8.1 %collective-permute-start.5 = (bf16[4,136,256]{2,1,0:T(8,128)(2,1)S(1)}, bf16[4,136,256]{2,1,0:T(8,128)(2,1)}, u32[]{:S(2)}, u32[]{:S(2)}) collective-permute-start(bf16[4,136,256]{2,1,0:T(8,128)(2,1)S(1)} %collective-permute-done.3.rest_1_), channel_id=1, source_target_pairs={{0,4},{1,5},{2,6},{3,7},{4,8},{5,9},{6,10},{7,11},{8,12},{9,13},{1... | collective-permute-start | bytes 835592 | tf_op jit(solution)/shard_map/ppermute | solution.py:269
  32.2 8.0 %collective-permute-start.6 = (bf16[4,136,256]{2,1,0:T(8,128)(2,1)S(1)}, bf16[4,136,256]{2,1,0:T(8,128)(2,1)}, u32[]{:S(2)}, u32[]{:S(2)}) collective-permute-start(bf16[4,136,256]{2,1,0:T(8,128)(2,1)S(1)} %collective-permute-done.4.rest_2_), channel_id=1, source_target_pairs={{0,28},{1,29},{2,30},{3,31},{4,0},{5,1},{6,2},{7,3},{8,4},{9,5},{1... | collective-permute-start | bytes 835592 | tf_op jit(solution)/shard_map/ppermute | solution.py:269
  41.6 9.9 %collective-permute-start.7 = (bf16[4,136,256]{2,1,0:T(8,128)(2,1)}, bf16[4,136,256]{2,1,0:T(8,128)(2,1)S(1)}, u32[]{:S(2)}, u32[]{:S(2)}) collective-permute-start(bf16[4,136,256]{2,1,0:T(8,128)(2,1)} %collective-permute-done.5.rest_3_), channel_id=1, source_target_pairs={{0,4},{1,5},{2,6},{3,7},{4,8},{5,9},{6,10},{7,11},{8,12},{9,13},{1... | collective-permute-start | bytes 835592 | tf_op jit(solution)/shard_map/ppermute | solution.py:269
  43.8 7.7 %collective-permute-start.8 = (bf16[4,136,256]{2,1,0:T(8,128)(2,1)}, bf16[4,136,256]{2,1,0:T(8,128)(2,1)}, u32[]{:S(2)}, u32[]{:S(2)}) collective-permute-start(bf16[4,136,256]{2,1,0:T(8,128)(2,1)} %collective-permute-done.6.rest_4_), channel_id=1, source_target_pairs={{0,28},{1,29},{2,30},{3,31},{4,0},{5,1},{6,2},{7,3},{8,4},{9,5},{1... | collective-permute-start | bytes 835592 | tf_op jit(solution)/shard_map/ppermute | solution.py:269
  51.5 16.8 %copy-start.8 = (bf16[4,136,256]{2,1,0:T(8,128)(2,1)}, bf16[4,136,256]{2,1,0:T(8,128)(2,1)S(1)}, u32[]{:S(2)}) copy-start(bf16[4,136,256]{2,1,0:T(8,128)(2,1)S(1)} %collective-permute-done.7.rest_0_) | copy-start | bytes 835588
  51.6 7.8 %collective-permute-start.9 = (bf16[4,136,256]{2,1,0:T(8,128)(2,1)S(1)}, bf16[4,136,256]{2,1,0:T(8,128)(2,1)S(1)}, u32[]{:S(2)}, u32[]{:S(2)}) collective-permute-start(bf16[4,136,256]{2,1,0:T(8,128)(2,1)S(1)} %collective-permute-done.7.rest_0_), channel_id=1, source_target_pairs={{0,4},{1,5},{2,6},{3,7},{4,8},{5,9},{6,10},{7,11},{8,12},{9,13},{1... | collective-permute-start | bytes 835592 | tf_op jit(solution)/shard_map/ppermute | solution.py:269
  59.4 8.9 %copy-start.9 = (bf16[4,136,256]{2,1,0:T(8,128)(2,1)}, bf16[4,136,256]{2,1,0:T(8,128)(2,1)S(1)}, u32[]{:S(2)}) copy-start(bf16[4,136,256]{2,1,0:T(8,128)(2,1)S(1)} %collective-permute-done.9.rest_2_) | copy-start | bytes 835588
  59.4 21.3 %all-to-all-start.2 = ((bf16[32,64,128]{2,1,0:T(8,128)(2,1)}), bf16[32,64,128]{2,1,0:T(8,128)(2,1)S(1)}, u32[]{:S(2)}, u32[]{:S(2)}) async-start(bf16[32,64,128]{2,1,0:T(8,128)(2,1)} %bitcast.10), calls=%async_computation.2 | async-start | bytes 1048576 | tf_op jit(solution)/shard_map/all_to_all | solution.py:351
  68.1 55.6 %all-gather.9.cloned.1.call-start = ((), (), s32[]{:S(2)}) async-start(), calls=%async_computation.5 | async-start | bytes 4718592 | tf_op jit(solution)/shard_map/all_gather | solution.py:390
  79.6 7.7 %copy-start.3 = (bf16[32,64,128]{2,1,0:T(8,128)(2,1)S(1)}, bf16[32,64,128]{2,1,0:T(8,128)(2,1)}, u32[]{:S(2)}) copy-start(bf16[32,64,128]{2,1,0:T(8,128)(2,1)} %get-tuple-element.33) | copy-start | bytes 1572868
  80.7 0.8 copy-start.4
Sparse Core Ops, SparseCore 0:
  9.9 28.7 all-gather.4
  40.6 34.5 all-gather.6
  87.4 34.4 all-gather.8

commit v7 on v6

--- a/solution.py
+++ b/solution.py
@@ -211,25 +211,28 @@
         gate_ref[:, here, :] = gate
         return carry
 
-    lax.fori_loop(0, GROUPS // 2, step, 0)
+    lax.fori_loop(0, GROUPS // 2, step, 0, unroll=2)
 
 
 def gradient_kernel(grad_ref, gate_ref, spectrum_ref, first_ref, second_ref, back_second_ref, back_first_ref, twist_ref, out_ref):
     cosine, sine = twists_of(twist_ref)
     count = BLOCKS * LANE8
-    products = (grad_ref[...].astype(f32) * gate_ref[...].astype(f32)).astype(bf16).astype(f32)
-    signals = [products[:, i * LANE8 : (i + 1) * LANE8].reshape(count, BLOCK) for i in range(2)]
-    spectra = forward(*signals, first_ref, second_ref, cosine, sine)
-    own = spectrum_ref[...].reshape(2 * count, 2 * BLOCK).astype(f32)
-    own_re, own_im = own[:, :BLOCK], own[:, BLOCK:]
-    grad_re, grad_im = spectra[:, :BLOCK], spectra[:, BLOCK:]
-    lag = jnp.concatenate([own_re * grad_re + own_im * grad_im, own_re * grad_im - own_im * grad_re], 1)
-    result = backward(lag, back_second_ref, back_first_ref, cosine, sine)
-    both = []
-    for half in range(2):
-        lanes = slice(half * BLOCK, (half + 1) * BLOCK)
-        both.append(jnp.concatenate([result[i * LANE8 : (i + 1) * LANE8, lanes] for i in range(BLOCKS)], 1))
-    out_ref[...] = jnp.concatenate(both, 0).astype(bf16)
+    pair = 2 * LANE8
+    for start in range(0, grad_ref.shape[1], pair):
+        here = slice(start, start + pair)
+        products = (grad_ref[:, here, :].astype(f32) * gate_ref[:, here, :].astype(f32)).astype(bf16).astype(f32)
+        signals = [products[:, i * LANE8 : (i + 1) * LANE8].reshape(count, BLOCK) for i in range(2)]
+        spectra = forward(*signals, first_ref, second_ref, cosine, sine)
+        own = spectrum_ref[start // LANE8 : start // LANE8 + 2].reshape(2 * count, 2 * BLOCK).astype(f32)
+        own_re, own_im = own[:, :BLOCK], own[:, BLOCK:]
+        grad_re, grad_im = spectra[:, :BLOCK], spectra[:, BLOCK:]
+        lag = jnp.concatenate([own_re * grad_re + own_im * grad_im, own_re * grad_im - own_im * grad_re], 1)
+        result = backward(lag, back_second_ref, back_first_ref, cosine, sine)
+        both = []
+        for half in range(2):
+            lanes = slice(half * BLOCK, (half + 1) * BLOCK)
+            both.append(jnp.concatenate([result[i * LANE8 : (i + 1) * LANE8, lanes] for i in range(BLOCKS)], 1))
+        out_ref[here, :] = jnp.concatenate(both, 0).astype(bf16)
 
 
 def read_out_kernel(place_ref, rows_hbm, marks_hbm, weight_hbm, out_ref, weight, rows_all, chunk_all, weight_sems, sems):
@@ -245,7 +248,7 @@
     marks = chunk_all[...].astype(f32).reshape(Y * trials, chunk_all.shape[2])
     marks = jnp.concatenate([marks] * (inner // width), 1)
     total = jnp.zeros((Y * BLOCK, width), f32)
-    part = slots // 2
+    part = slots // 4
     for start in range(0, slots, part):
         wait_all(loads[start : start + part])
         wide = spread(rows, marks - start, part)
@@ -254,11 +257,9 @@
         out_ref[block] = total[index * BLOCK : (index + 1) * BLOCK].astype(bf16)
 
 
-def sum_kernel(parts_ref, out_ref):
-    total = parts_ref[0].astype(f32)
-    for index in range(1, parts_ref.shape[0]):
-        total = total + parts_ref[index].astype(f32)
-    out_ref[...] = total
+def sum_kernel(parts_ref, pick_ref, out_ref):
+    count, rows, lanes = parts_ref.shape
+    out_ref[...] = jnp.dot(pick_ref[...], parts_ref[...].reshape(count * rows, lanes), preferred_element_type=f32)
 
 
 def along_y(value, step):
@@ -296,6 +297,7 @@
     marks = jnp.broadcast_to(slots.astype(bf16)[:, None], (slots.shape[0], in_chans))
     block = jnp.concatenate([spikes[0], marks], 0)
     chunk = jnp.stack([block, along_y(block, 1), along_y(block, -1), along_y(block, 2)])
+    chunk, readout_weight = lax.optimization_barrier((chunk, readout_weight))
     own_marks = chunk[:, BLOCK:, :]
     right, left = along_z(chunk, 1), along_z(chunk, -1)
     chunks = [chunk, right, left]
@@ -378,27 +380,28 @@
     own_grad = pl.pallas_call(
         gradient_kernel,
         out_shape=jax.ShapeDtypeStruct((CHANS, LENGTH), bf16),
-        grid=(GROUPS // 2,),
-        in_specs=[pl.BlockSpec((BLOCKS, pair, BLOCK), lambda i: (0, i, 0))] * 2
-        + [pl.BlockSpec((2,) + spectrum_shape.shape[1:], lambda i: (i, 0, 0))]
+        grid=(GROUPS // 4,),
+        in_specs=[pl.BlockSpec((BLOCKS, 2 * pair, BLOCK), lambda i: (0, i, 0))] * 2
+        + [pl.BlockSpec((4,) + spectrum_shape.shape[1:], lambda i: (i, 0, 0))]
         + [same(table) for table in tables + (twists,)],
-        out_specs=pl.BlockSpec((pair, LENGTH), lambda i: (i, 0)),
+        out_specs=pl.BlockSpec((2 * pair, LENGTH), lambda i: (i, 0)),
         compiler_params=params,
         cost_estimate=pl.CostEstimate(flops=2 * work, bytes_accessed=4 << 20, transcendentals=0),
         name="filter_gradient",
     )(grads, gates, spectrum, *tables, twists)
     all_grads = lax.all_gather(own_grad, "grp", axis=0, tiled=False)
-    lanes = LENGTH // 8
+    devices = all_grads.shape[0]
+    picks = jnp.asarray(np.tile(np.eye(pair, dtype=np.float32), (1, devices)), bf16)
     filter_grad = pl.pallas_call(
         sum_kernel,
         out_shape=jax.ShapeDtypeStruct((CHANS, LENGTH), f32),
-        grid=(LENGTH // lanes,),
-        in_specs=[pl.BlockSpec((all_grads.shape[0], CHANS, lanes), lambda i: (0, 0, i))],
-        out_specs=pl.BlockSpec((CHANS, lanes), lambda i: (0, i)),
+        grid=(CHANS // pair,),
+        in_specs=[pl.BlockSpec((devices, pair, LENGTH), lambda i: (0, i, 0)), same(picks)],
+        out_specs=pl.BlockSpec((pair, LENGTH), lambda i: (i, 0)),
         compiler_params=params,
         cost_estimate=pl.CostEstimate(flops=all_grads.size, bytes_accessed=5 << 20, transcendentals=0),
         name="sum_gradients",
-    )(all_grads)
+    )(all_grads, picks)
     partial = pl.pallas_call(
         read_out_kernel,
         out_shape=jax.ShapeDtypeStruct((Y, BLOCK, in_chans), bf16),

time: 138 us -> 137 us (level)
  Pallas kernels: 41.1 us -> 39.7 us
    pallas_call x1, Pallas kernels: 7.01 us -> 8.97 us  [local(): pl.pallas_call(read_out_kernel, out_shape=jax.ShapeDtypeStruct((Y, BLOCK,...]
    pallas_call x1, Pallas kernels: 6.01 us -> 4.44 us  [local(): pl.pallas_call(sum_kernel, out_shape=jax.ShapeDtypeStruct((CHANS, LENGTH)...]
where the time goes in v7:
time: 137 us; the launch traced here: 135 us
  Pallas kernels  39.7 us (29%)
  blocking collectives  27.9 us (20%)
  starting transfers between devices  26.9 us (20%)
  waiting for transfers between devices  15.1 us (11%)
  between operations  13.9 us (10%)
  local copies, waits for them, and re-layouts  7.57 us (6%)
  other arithmetic  3.9 us (3%)
    all_to_all x1, blocking collectives, local(): lax.all_to_all(gated, 'seq', split_axis=0, concat_axis=0, tiled=True, axi...  17.8 us
    ppermute x7, starting transfers between devices, along_z(): lax.ppermute(value, 'seq', [(z * Y + y, (z + step) % Z * Y + y) for z in...  13.5 us
    pallas_call x1, Pallas kernels, local(): pl.pallas_call(forward_kernel, out_shape=(jax.ShapeDtypeStruct(plane, bf1...  10.3 us
    all_to_all x1, blocking collectives, local(): lax.all_to_all(partial, 'seq', split_axis=0, concat_axis=0, tiled=True, a...  10 us
    ppermute x7, waiting for transfers between devices, along_z(): lax.ppermute(value, 'seq', [(z * Y + y, (z + step) % Z * Y + y) for z in...  9.25 us
    pallas_call x1, Pallas kernels, local(): pl.pallas_call(read_out_kernel, out_shape=jax.ShapeDtypeStruct((Y, BLOCK,...  8.97 us
    all_to_all x1, starting transfers between devices, local(): lax.all_to_all(turned, 'seq', split_axis=0, concat_axis=0, tiled=True)  8.68 us
    pallas_call x1, Pallas kernels, local(): pl.pallas_call(read_in_kernel, out_shape=jax.ShapeDtypeStruct((early_bloc...  6.68 us
  transfers between devices with their start and end apart: 14, of which 7 were waited for; matrix products, arithmetic and copies ran while one was open for 6% of the time, Pallas kernels for 26%

profile of v7, /device:TPU:8, one launch (start us, length us, event | category | flops | bytes accessed | tf_op | source)
XLA Modules:
  0.0 135.0 jit_solution(1672868834497580324)
XLA Ops:
  7.3 1.3 constant_dynamic-slice_fusion.2
  8.5 0.8 pad_maximum_fusion.1
  9.4 0.7 slice.6
  10.1 0.8 select_reduce_fusion
  11.0 0.9 fusion
  11.9 1.7 %collective-permute-start = (bf16[136,256]{1,0:T(8,128)(2,1)S(1)}, bf16[136,256]{1,0:T(8,128)(2,1)S(1)}, u32[]{:S(2)}, u32[]{:S(2)}) collective-permute-start(bf16[136,256]{1,0:T(8,128)(2,1)S(1)} %get-tuple-element.45), channel_id=1, source_target_pairs={{0,1},{1,2},{2,3},{3,0},{4,5},{5,6},{6,7},{7,4},{8,9},{9,10},{10,1... | collective-permute-start | bytes 208904 | tf_op jit(solution)/shard_map/ppermute | solution.py:266
  14.3 2.0 %collective-permute-start.2 = (bf16[136,256]{1,0:T(8,128)(2,1)S(1)}, bf16[136,256]{1,0:T(8,128)(2,1)S(1)}, u32[]{:S(2)}, u32[]{:S(2)}) collective-permute-start(bf16[136,256]{1,0:T(8,128)(2,1)S(1)} %get-tuple-element.45), channel_id=1, source_target_pairs={{0,2},{1,3},{2,0},{3,1},{4,6},{5,7},{6,4},{7,5},{8,10},{9,11},{10,... | collective-permute-start | bytes 208904 | tf_op jit(solution)/shard_map/ppermute | solution.py:266
  16.5 2.2 %collective-permute-done.1 = bf16[136,256]{1,0:T(8,128)(2,1)S(1)} collective-permute-done((bf16[136,256]{1,0:T(8,128)(2,1)S(1)}, bf16[136,256]{1,0:T(8,128)(2,1)S(1)}, u32[]{:S(2)}, u32[]{:S(2)}) %collective-permute-start.1) | collective-permute-done | bytes 69664 | tf_op jit(solution)/shard_map/ppermute | solution.py:266
  18.6 1.5 %collective-permute-done.2 = bf16[136,256]{1,0:T(8,128)(2,1)S(1)} collective-permute-done((bf16[136,256]{1,0:T(8,128)(2,1)S(1)}, bf16[136,256]{1,0:T(8,128)(2,1)S(1)}, u32[]{:S(2)}, u32[]{:S(2)}) %collective-permute-start.2) | collective-permute-done | bytes 69664 | tf_op jit(solution)/shard_map/ppermute | solution.py:266
  20.1 1.0 constant_dynamic-slice_fusion
  21.1 1.7 %collective-permute-start.3 = (bf16[4,136,256]{2,1,0:T(8,128)(2,1)S(1)}, bf16[4,136,256]{2,1,0:T(8,128)(2,1)S(1)}, u32[]{:S(2)}, u32[]{:S(2)}) collective-permute-start(bf16[4,136,256]{2,1,0:T(8,128)(2,1)S(1)} %pad_maximum_fusion.rest_0_), channel_id=1, source_target_pairs={{0,4},{1,5},{2,6},{3,7},{4,8},{5,9},{6,10},{7,11},{8,12},{9,13},{1... | collective-permute-start | bytes 835592 | tf_op jit(solution)/shard_map/ppermute | solution.py:270
  22.9 4.0 %collective-permute-start.4 = (bf16[4,136,256]{2,1,0:T(8,128)(2,1)S(1)}, bf16[4,136,256]{2,1,0:T(8,128)(2,1)S(1)}, u32[]{:S(2)}, u32[]{:S(2)}) collective-permute-start(bf16[4,136,256]{2,1,0:T(8,128)(2,1)S(1)} %pad_maximum_fusion.rest_0_), channel_id=1, source_target_pairs={{0,28},{1,29},{2,30},{3,31},{4,0},{5,1},{6,2},{7,3},{8,4},{9,5},{1... | collective-permute-start | bytes 835592 | tf_op jit(solution)/shard_map/ppermute | solution.py:270
  26.9 4.4 %filter_transform.1.filter_hbm = bf16[8,256,256]{2,1,0:T(8,128)(2,1)} custom-call(f32[64,4096]{1,0:T(8,128)} %filter_ref.1, bf16[512,256]{1,0:T(8,128)(2,1)} %constant.60.clone.first_ref.rest_3_, bf16[256,256]{1,0:T(8,128)(2,1)} %constant.61.clone.second_ref.rest_4_, f32[2,32,128]{2,1,0:T(8,128)} %constant.64.clone.twist_ref), custom_call_target="tpu_custom_call" | custom-call | flops 536870912 | bytes 4194304 | tf_op jit(solution)/shard_map/filter_transform/pallas_call | solution.py:311
  32.2 3.2 %collective-permute-start.6 = (bf16[4,136,256]{2,1,0:T(8,128)(2,1)S(1)}, bf16[4,136,256]{2,1,0:T(8,128)(2,1)}, u32[]{:S(2)}, u32[]{:S(2)}) collective-permute-start(bf16[4,136,256]{2,1,0:T(8,128)(2,1)S(1)} %collective-permute-done.4.rest_2_), channel_id=1, source_target_pairs={{0,28},{1,29},{2,30},{3,31},{4,0},{5,1},{6,2},{7,3},{8,4},{9,5},{1... | collective-permute-start | bytes 835592 | tf_op jit(solution)/shard_map/ppermute | solution.py:270
  35.4 1.0 copy.21
  37.1 0.8 constant_dynamic-slice_fusion.3
  37.8 2.4 %collective-permute-done.5.rest_3_ = bf16[4,136,256]{2,1,0:T(8,128)(2,1)} collective-permute-done((bf16[4,136,256]{2,1,0:T(8,128)(2,1)S(1)}, bf16[4,136,256]{2,1,0:T(8,128)(2,1)}, u32[]{:S(2)}, u32[]{:S(2)}) %collective-permute-start.5) | collective-permute-done | bytes 278560 | tf_op jit(solution)/shard_map/ppermute | solution.py:270
  40.2 0.7 broadcast_in_dim.38.taps_ref
  41.6 2.3 %collective-permute-start.7 = (bf16[4,136,256]{2,1,0:T(8,128)(2,1)}, bf16[4,136,256]{2,1,0:T(8,128)(2,1)S(1)}, u32[]{:S(2)}, u32[]{:S(2)}) collective-permute-start(bf16[4,136,256]{2,1,0:T(8,128)(2,1)} %collective-permute-done.5.rest_3_), channel_id=1, source_target_pairs={{0,4},{1,5},{2,6},{3,7},{4,8},{5,9},{6,10},{7,11},{8,12},{9,13},{1... | collective-permute-start | bytes 835592 | tf_op jit(solution)/shard_map/ppermute | solution.py:270
  43.9 1.0 collective-permute-start.8
  44.9 6.7 %read_in.1.early_hbm = bf16[20,128,128]{2,1,0:T(8,128)(2,1)} custom-call(bf16[16,256,128]{2,1,0:T(8,128)(2,1)} %all-gather.5.cloned.1.call-done.weight_hbm, bf16[4,136,256]{2,1,0:T(8,128)(2,1)} %copy-done.1, bf16[4,136,256]{2,1,0:T(8,128)(2,1)} %copy-done.5, bf16[4,136,256]{2,1,0:T(8,128)(2,1)} %copy-done.6, ...), custom_call_target="tpu_custom_call" | custom-call | flops 536870912 | bytes 4194304 | tf_op jit(solution)/shard_map/read_in/pallas_call | solution.py:335
  51.6 1.2 collective-permute-start.9
  52.8 6.7 %collective-permute-done.9.rest_2_ = bf16[4,136,256]{2,1,0:T(8,128)(2,1)S(1)} collective-permute-done((bf16[4,136,256]{2,1,0:T(8,128)(2,1)S(1)}, bf16[4,136,256]{2,1,0:T(8,128)(2,1)S(1)}, u32[]{:S(2)}, u32[]{:S(2)}) %collective-permute-start.9) | collective-permute-done | bytes 278560 | tf_op jit(solution)/shard_map/ppermute | solution.py:270
  59.4 8.7 %all-to-all-start.2 = ((bf16[32,64,128]{2,1,0:T(8,128)(2,1)}), bf16[32,64,128]{2,1,0:T(8,128)(2,1)S(1)}, u32[]{:S(2)}, u32[]{:S(2)}) async-start(bf16[32,64,128]{2,1,0:T(8,128)(2,1)} %bitcast.10), calls=%async_computation.2 | async-start | bytes 1048576 | tf_op jit(solution)/shard_map/all_to_all | solution.py:353
  68.4 10.3 %long_convolution.1 = (bf16[32,64,128]{2,1,0:T(8,128)(2,1)}, bf16[32,64,128]{2,1,0:T(8,128)(2,1)}, bf16[8,256,256]{2,1,0:T(8,128)(2,1)}) custom-call(s32[2]{0:T(128)} %pad_add_fusion.place_ref, f32[3,64,128]{2,1,0:T(8,128)} %broadcast_in_dim.38.taps_ref, f32[64,128]{1,0:T(8,128)} %broadcast_in_dim.39.gain_ref, f32[2,32,128]{2,1,0:T(8,128)} %constant.64.clone.twist_ref, ...), custom_call_target="tpu_custom_call" | custom-call | flops 2147483648 | bytes 8388608 | tf_op jit(solution)/shard_map/long_convolution/pallas_call | solution.py:356
  78.7 2.0 %all-to-all-done.2.grad_ref = bf16[32,64,128]{2,1,0:T(8,128)(2,1)S(1)} async-done(((bf16[32,64,128]{2,1,0:T(8,128)(2,1)}), bf16[32,64,128]{2,1,0:T(8,128)(2,1)S(1)}, u32[]{:S(2)}, u32[]{:S(2)}) %all-to-all-start.2) | async-done | bytes 524320 | tf_op jit(solution)/shard_map/all_to_all | solution.py:353
  80.7 0.8 copy-done.4
  81.5 4.9 %filter_gradient.1 = bf16[64,4096]{1,0:T(8,128)(2,1)} custom-call(bf16[32,64,128]{2,1,0:T(8,128)(2,1)} %copy-done.4, bf16[32,64,128]{2,1,0:T(8,128)(2,1)} %get-tuple-element.40.gate_ref, bf16[8,256,256]{2,1,0:T(8,128)(2,1)} %get-tuple-element.41.spectrum_ref, bf16[512,256]{1,0:T(8,128)(2,1)} %constant.60.clone.first_ref.rest_3_, ...), custom_call_target="tpu_custom_call" | custom-call | flops 1073741824 | bytes 4194304 | tf_op jit(solution)/shard_map/filter_gradient/pallas_call | solution.py:380
  86.5 17.8 %all_to_all.15.rows_hbm = bf16[8,4,64,128]{3,2,1,0:T(8,128)(2,1)} all-to-all(bf16[8,4,64,128]{3,2,1,0:T(8,128)(2,1)S(1)} %bitcast.24), channel_id=1, replica_groups={{0,4,8,12,16,20,24,28},{1,5,9,13,17,21,25,29},{2,6,10,14,18,22,26,30},{..., dimensions={0} | all-to-all | bytes 1048576 | tf_op jit(solution)/shard_map/all_to_all | solution.py:379
  104.3 9.0 %read_out.1 = bf16[4,128,256]{2,1,0:T(8,128)(2,1)} custom-call(s32[2]{0:T(128)} %pad_add_fusion.place_ref, bf16[8,4,64,128]{3,2,1,0:T(8,128)(2,1)} %all_to_all.15.rows_hbm, bf16[4,8,256]{2,1,0:T(8,128)(2,1)} %slice.7.marks_hbm, bf16[16,512,256]{2,1,0:T(8,128)(2,1)} %all-gather.7.cloned.1.call-done.weight_hbm), custom_call_target="tpu_custom_call" | custom-call | flops 2147483648 | bytes 6291456 | tf_op jit(solution)/shard_map/read_out/pallas_call | solution.py:405
  113.3 10.0 %all_to_all.16 = bf16[4,128,256]{2,1,0:T(8,128)(2,1)S(1)} all-to-all(bf16[4,128,256]{2,1,0:T(8,128)(2,1)} %read_out.1), channel_id=1, replica_groups={{0,1,2,3},{4,5,6,7},{8,9,10,11},{12,13,14,15},{16,17,18,19},{20,21,22,2..., dimensions={0} | all-to-all | bytes 524288 | tf_op jit(solution)/shard_map/all_to_all | solution.py:420
  124.0 4.4 %sum_gradients.1 = f32[64,4096]{1,0:T(8,128)} custom-call(bf16[8,64,4096]{2,1,0:T(8,128)(2,1)} %bitcast.21, bf16[16,128]{1,0:T(8,128)(2,1)} %constant.65.clone.pick_ref), custom_call_target="tpu_custom_call" | custom-call | flops 2097152 | bytes 5242880 | tf_op jit(solution)/shard_map/sum_gradients/pallas_call | solution.py:395
  (43 shorter events, 4.2 us)
Async XLA Ops:
  7.2 13.0 %copy-start = (bf16[2,2048,256]{2,1,0:T(8,128)(2,1)S(1)}, bf16[2,2048,256]{2,1,0:T(8,128)(2,1)}, u32[]{:S(2)}) copy-start(bf16[2,2048,256]{2,1,0:T(8,128)(2,1)} %param.22) | copy-start | bytes 6291460
  7.2 28.3 %copy-start.2 = (bf16[1,128,2048]{2,1,0:T(8,128)(2,1)S(1)}, bf16[1,128,2048]{2,1,0:T(8,128)(2,1)}, u32[]{:S(2)}) copy-start(bf16[1,128,2048]{2,1,0:T(8,128)(2,1)} %param.23) | copy-start | bytes 1572868
  7.2 33.7 %copy-start.7 = (f32[64]{0:T(128)S(1)}, f32[64]{0:T(128)}, u32[]{:S(2)}) copy-start(f32[64]{0:T(128)} %param.21) | copy-start | bytes 772
  7.2 37.7 %all-gather.5.cloned.1.call-start = ((), (), s32[]{:S(2)}) async-start(), calls=%async_computation.3 | async-start | bytes 1179648 | tf_op jit(solution)/shard_map/all_gather | solution.py:306
  9.3 95.0 %all-gather.7.cloned.1.call-start = ((), (), s32[]{:S(2)}) async-start(), calls=%async_computation.4 | async-start | bytes 4718592 | tf_op jit(solution)/shard_map/all_gather | solution.py:309
  11.9 4.6 %collective-permute-start = (bf16[136,256]{1,0:T(8,128)(2,1)S(1)}, bf16[136,256]{1,0:T(8,128)(2,1)S(1)}, u32[]{:S(2)}, u32[]{:S(2)}) collective-permute-start(bf16[136,256]{1,0:T(8,128)(2,1)S(1)} %get-tuple-element.45), channel_id=1, source_target_pairs={{0,1},{1,2},{2,3},{3,0},{4,5},{5,6},{6,7},{7,4},{8,9},{9,10},{10,1... | collective-permute-start | bytes 208904 | tf_op jit(solution)/shard_map/ppermute | solution.py:266
  13.6 5.1 %collective-permute-start.1 = (bf16[136,256]{1,0:T(8,128)(2,1)S(1)}, bf16[136,256]{1,0:T(8,128)(2,1)S(1)}, u32[]{:S(2)}, u32[]{:S(2)}) collective-permute-start(bf16[136,256]{1,0:T(8,128)(2,1)S(1)} %get-tuple-element.45), channel_id=1, source_target_pairs={{0,3},{1,0},{2,1},{3,2},{4,7},{5,4},{6,5},{7,6},{8,11},{9,8},{10,9... | collective-permute-start | bytes 208904 | tf_op jit(solution)/shard_map/ppermute | solution.py:266
  14.3 5.8 %collective-permute-start.2 = (bf16[136,256]{1,0:T(8,128)(2,1)S(1)}, bf16[136,256]{1,0:T(8,128)(2,1)S(1)}, u32[]{:S(2)}, u32[]{:S(2)}) collective-permute-start(bf16[136,256]{1,0:T(8,128)(2,1)S(1)} %get-tuple-element.45), channel_id=1, source_target_pairs={{0,2},{1,3},{2,0},{3,1},{4,6},{5,7},{6,4},{7,5},{8,10},{9,11},{10,... | collective-permute-start | bytes 208904 | tf_op jit(solution)/shard_map/ppermute | solution.py:266
  20.1 24.7 %copy-start.1 = (bf16[4,136,256]{2,1,0:T(8,128)(2,1)}, bf16[4,136,256]{2,1,0:T(8,128)(2,1)S(1)}, u32[]{:S(2)}) copy-start(bf16[4,136,256]{2,1,0:T(8,128)(2,1)S(1)} %pad_maximum_fusion.rest_0_) | copy-start | bytes 835588
  21.1 11.0 %collective-permute-start.3 = (bf16[4,136,256]{2,1,0:T(8,128)(2,1)S(1)}, bf16[4,136,256]{2,1,0:T(8,128)(2,1)S(1)}, u32[]{:S(2)}, u32[]{:S(2)}) collective-permute-start(bf16[4,136,256]{2,1,0:T(8,128)(2,1)S(1)} %pad_maximum_fusion.rest_0_), channel_id=1, source_target_pairs={{0,4},{1,5},{2,6},{3,7},{4,8},{5,9},{6,10},{7,11},{8,12},{9,13},{1... | collective-permute-start | bytes 835592 | tf_op jit(solution)/shard_map/ppermute | solution.py:270
  22.9 9.3 %collective-permute-start.4 = (bf16[4,136,256]{2,1,0:T(8,128)(2,1)S(1)}, bf16[4,136,256]{2,1,0:T(8,128)(2,1)S(1)}, u32[]{:S(2)}, u32[]{:S(2)}) collective-permute-start(bf16[4,136,256]{2,1,0:T(8,128)(2,1)S(1)} %pad_maximum_fusion.rest_0_), channel_id=1, source_target_pairs={{0,28},{1,29},{2,30},{3,31},{4,0},{5,1},{6,2},{7,3},{8,4},{9,5},{1... | collective-permute-start | bytes 835592 | tf_op jit(solution)/shard_map/ppermute | solution.py:270
  32.1 12.7 %copy-start.5 = (bf16[4,136,256]{2,1,0:T(8,128)(2,1)}, bf16[4,136,256]{2,1,0:T(8,128)(2,1)S(1)}, u32[]{:S(2)}) copy-start(bf16[4,136,256]{2,1,0:T(8,128)(2,1)S(1)} %collective-permute-done.3.rest_1_) | copy-start | bytes 835588
  32.1 12.7 %copy-start.6 = (bf16[4,136,256]{2,1,0:T(8,128)(2,1)}, bf16[4,136,256]{2,1,0:T(8,128)(2,1)S(1)}, u32[]{:S(2)}) copy-start(bf16[4,136,256]{2,1,0:T(8,128)(2,1)S(1)} %collective-permute-done.4.rest_2_) | copy-start | bytes 835588
  32.1 8.1 %collective-permute-start.5 = (bf16[4,136,256]{2,1,0:T(8,128)(2,1)S(1)}, bf16[4,136,256]{2,1,0:T(8,128)(2,1)}, u32[]{:S(2)}, u32[]{:S(2)}) collective-permute-start(bf16[4,136,256]{2,1,0:T(8,128)(2,1)S(1)} %collective-permute-done.3.rest_1_), channel_id=1, source_target_pairs={{0,4},{1,5},{2,6},{3,7},{4,8},{5,9},{6,10},{7,11},{8,12},{9,13},{1... | collective-permute-start | bytes 835592 | tf_op jit(solution)/shard_map/ppermute | solution.py:270
  32.2 8.0 %collective-permute-start.6 = (bf16[4,136,256]{2,1,0:T(8,128)(2,1)S(1)}, bf16[4,136,256]{2,1,0:T(8,128)(2,1)}, u32[]{:S(2)}, u32[]{:S(2)}) collective-permute-start(bf16[4,136,256]{2,1,0:T(8,128)(2,1)S(1)} %collective-permute-done.4.rest_2_), channel_id=1, source_target_pairs={{0,28},{1,29},{2,30},{3,31},{4,0},{5,1},{6,2},{7,3},{8,4},{9,5},{1... | collective-permute-start | bytes 835592 | tf_op jit(solution)/shard_map/ppermute | solution.py:270
  41.6 9.9 %collective-permute-start.7 = (bf16[4,136,256]{2,1,0:T(8,128)(2,1)}, bf16[4,136,256]{2,1,0:T(8,128)(2,1)S(1)}, u32[]{:S(2)}, u32[]{:S(2)}) collective-permute-start(bf16[4,136,256]{2,1,0:T(8,128)(2,1)} %collective-permute-done.5.rest_3_), channel_id=1, source_target_pairs={{0,4},{1,5},{2,6},{3,7},{4,8},{5,9},{6,10},{7,11},{8,12},{9,13},{1... | collective-permute-start | bytes 835592 | tf_op jit(solution)/shard_map/ppermute | solution.py:270
  43.9 7.7 %collective-permute-start.8 = (bf16[4,136,256]{2,1,0:T(8,128)(2,1)}, bf16[4,136,256]{2,1,0:T(8,128)(2,1)}, u32[]{:S(2)}, u32[]{:S(2)}) collective-permute-start(bf16[4,136,256]{2,1,0:T(8,128)(2,1)} %collective-permute-done.6.rest_4_), channel_id=1, source_target_pairs={{0,28},{1,29},{2,30},{3,31},{4,0},{5,1},{6,2},{7,3},{8,4},{9,5},{1... | collective-permute-start | bytes 835592 | tf_op jit(solution)/shard_map/ppermute | solution.py:270
  51.6 16.8 %copy-start.8 = (bf16[4,136,256]{2,1,0:T(8,128)(2,1)}, bf16[4,136,256]{2,1,0:T(8,128)(2,1)S(1)}, u32[]{:S(2)}) copy-start(bf16[4,136,256]{2,1,0:T(8,128)(2,1)S(1)} %collective-permute-done.7.rest_0_) | copy-start | bytes 835588
  51.6 7.8 %collective-permute-start.9 = (bf16[4,136,256]{2,1,0:T(8,128)(2,1)S(1)}, bf16[4,136,256]{2,1,0:T(8,128)(2,1)S(1)}, u32[]{:S(2)}, u32[]{:S(2)}) collective-permute-start(bf16[4,136,256]{2,1,0:T(8,128)(2,1)S(1)} %collective-permute-done.7.rest_0_), channel_id=1, source_target_pairs={{0,4},{1,5},{2,6},{3,7},{4,8},{5,9},{6,10},{7,11},{8,12},{9,13},{1... | collective-permute-start | bytes 835592 | tf_op jit(solution)/shard_map/ppermute | solution.py:270
  59.4 8.9 %copy-start.9 = (bf16[4,136,256]{2,1,0:T(8,128)(2,1)}, bf16[4,136,256]{2,1,0:T(8,128)(2,1)S(1)}, u32[]{:S(2)}) copy-start(bf16[4,136,256]{2,1,0:T(8,128)(2,1)S(1)} %collective-permute-done.9.rest_2_) | copy-start | bytes 835588
  59.4 21.3 %all-to-all-start.2 = ((bf16[32,64,128]{2,1,0:T(8,128)(2,1)}), bf16[32,64,128]{2,1,0:T(8,128)(2,1)S(1)}, u32[]{:S(2)}, u32[]{:S(2)}) async-start(bf16[32,64,128]{2,1,0:T(8,128)(2,1)} %bitcast.10), calls=%async_computation.2 | async-start | bytes 1048576 | tf_op jit(solution)/shard_map/all_to_all | solution.py:353
  68.1 55.9 %all-gather.9.cloned.1.call-start = ((), (), s32[]{:S(2)}) async-start(), calls=%async_computation.5 | async-start | bytes 4718592 | tf_op jit(solution)/shard_map/all_gather | solution.py:392
  78.7 7.8 %copy-start.3 = (bf16[32,64,128]{2,1,0:T(8,128)(2,1)S(1)}, bf16[32,64,128]{2,1,0:T(8,128)(2,1)}, u32[]{:S(2)}) copy-start(bf16[32,64,128]{2,1,0:T(8,128)(2,1)} %get-tuple-element.36) | copy-start | bytes 1572868
  80.7 0.8 copy-start.4
Sparse Core Ops, SparseCore 0:
  9.9 28.7 all-gather.4
  40.6 34.5 all-gather.6
  86.6 33.5 all-gather.8

commit v8 on v7

--- a/solution.py
+++ b/solution.py
@@ -245,21 +245,64 @@
     wait_all(first)
     places = [block_of(place_ref, 0, index) - place_ref[0] * Y for index in range(Y)]
     rows = jnp.concatenate([rows_all[:, block, :, :].reshape(inner, BLOCK).T for block in places], 0)
-    marks = chunk_all[...].astype(f32).reshape(Y * trials, chunk_all.shape[2])
-    marks = jnp.concatenate([marks] * (inner // width), 1)
+    marks = chunk_all[...].astype(f32).reshape(Y * trials, width)
+    marks = jnp.broadcast_to(marks[:, None, :], (Y * trials, TRIAL, width)).reshape(Y * BLOCK, width)
+    wait_all(loads)
     total = jnp.zeros((Y * BLOCK, width), f32)
-    part = slots // 4
-    for start in range(0, slots, part):
-        wait_all(loads[start : start + part])
-        wide = spread(rows, marks - start, part)
-        total = total + jnp.dot(wide, weight[start : start + part].reshape(part * inner, width), preferred_element_type=f32)
+    for slot in range(slots):
+        product = jnp.dot(rows, weight[slot], preferred_element_type=f32)
+        total = jnp.where(marks == slot, product, total)
     for index, block in enumerate(places):
         out_ref[block] = total[index * BLOCK : (index + 1) * BLOCK].astype(bf16)
 
 
-def sum_kernel(parts_ref, pick_ref, out_ref):
-    count, rows, lanes = parts_ref.shape
-    out_ref[...] = jnp.dot(pick_ref[...], parts_ref[...].reshape(count * rows, lanes), preferred_element_type=f32)
+def sum_kernel(parts_hbm, out_hbm, parts, total, in_sems, out_sems):
+    count, rows, _ = parts.shape
+    step = 2 * LANE8
+    loads = []
+    stores = []
+    for index in range(rows // step):
+        here = pl.ds(index * step, step)
+        for part in range(count):
+            load = pltpu.make_async_copy(parts_hbm.at[part, here, :], parts.at[part, here, :], in_sems.at[index, part])
+            loads.append(load)
+        stores.append(pltpu.make_async_copy(total.at[here, :], out_hbm.at[here, :], out_sems.at[index]))
+    start_all(loads)
+    for index in range(rows // step):
+        wait_all(loads[index * count : (index + 1) * count])
+        here = slice(index * step, (index + 1) * step)
+        running = parts[0, here, :].astype(f32)
+        for part in range(1, count):
+            running = running + parts[part, here, :].astype(f32)
+        total[here, :] = running
+        stores[index].start()
+    wait_all(stores)
+
+
+def prepare_kernel(place_ref, session_ref, slot_ref, spikes_ref, weight_hbm, block_ref, own_ref, value, gate, sems):
+    place = place_ref[0]
+    half = weight_hbm.shape[2] // 2
+    window = pl.multiple_of(place // 2 * 2 * CHANS, 2 * CHANS)
+    loads = [
+        pltpu.make_async_copy(weight_hbm.at[:, :, pl.ds(window, 2 * CHANS)], value, sems.at[0]),
+        pltpu.make_async_copy(weight_hbm.at[:, :, pl.ds(half + window, 2 * CHANS)], gate, sems.at[1]),
+    ]
+    start_all(loads)
+    trials = BLOCK // TRIAL
+    width = block_ref.shape[1]
+    row = lax.broadcasted_iota(jnp.int32, (trials, width), 0)
+    marks = jnp.zeros((trials, width), jnp.int32)
+    for trial in range(trials):
+        marks = jnp.where(row == trial, slot_ref[session_ref[0, trial * TRIAL]], marks)
+    block_ref[:BLOCK, :] = spikes_ref[0]
+    block_ref[BLOCK:, :] = marks.astype(f32).astype(bf16)
+    wait_all(loads)
+    slots, inner, lanes = own_ref.shape
+    odd = place % 2
+    low = pltpu.roll(value[...].astype(f32).reshape(slots * inner, lanes), odd * CHANS, 1)
+    high = pltpu.roll(gate[...].astype(f32).reshape(slots * inner, lanes), (1 - odd) * CHANS, 1)
+    lane = lax.broadcasted_iota(jnp.int32, (slots * inner, lanes), 1)
+    own_ref[...] = jnp.where(lane < CHANS, low, high).astype(bf16).reshape(slots, inner, lanes)
 
 
 def along_y(value, step):
@@ -276,7 +319,6 @@
 
 def local(spikes, session_of_bin, session_slot, readin_weight, short_kernel, long_filter, skip_gain, readout_weight, out_grad):
     in_chans = spikes.shape[2]
-    model_width = short_kernel.shape[1]
     place = lax.axis_index("seq")
     scalar = pl.BlockSpec(memory_space=pltpu.SMEM)
     hbm = pl.BlockSpec(memory_space=pltpu.HBM)
@@ -291,19 +333,24 @@
     pair = 2 * LANE8
     same = lambda table: pl.BlockSpec(table.shape, lambda i, rank=table.ndim: (0,) * rank)
 
-    sessions = session_of_bin[0, ::TRIAL]
-    matches = sessions[:, None] == jnp.arange(session_slot.shape[0], dtype=jnp.int32)[None, :]
-    slots = jnp.sum(jnp.where(matches, session_slot[None, :], 0), axis=1)
-    marks = jnp.broadcast_to(slots.astype(bf16)[:, None], (slots.shape[0], in_chans))
-    block = jnp.concatenate([spikes[0], marks], 0)
+    own_shape = (2, in_chans, 2 * CHANS)
+    block, own_weights = pl.pallas_call(
+        prepare_kernel,
+        out_shape=(jax.ShapeDtypeStruct((BLOCK + BLOCK // TRIAL, in_chans), bf16), jax.ShapeDtypeStruct(own_shape, bf16)),
+        in_specs=[scalar] * 3 + whole(1) + [hbm],
+        out_specs=tuple(whole(2)),
+        scratch_shapes=[pltpu.VMEM(own_shape, bf16), pltpu.VMEM(own_shape, bf16), pltpu.SemaphoreType.DMA((2,))],
+        compiler_params=params,
+        cost_estimate=pl.CostEstimate(flops=1 << 16, bytes_accessed=1 << 19, transcendentals=0),
+        name="prepare",
+    )(place.astype(jnp.int32)[None], session_of_bin, session_slot, spikes, readin_weight)
     chunk = jnp.stack([block, along_y(block, 1), along_y(block, -1), along_y(block, 2)])
     chunk, readout_weight = lax.optimization_barrier((chunk, readout_weight))
     own_marks = chunk[:, BLOCK:, :]
     right, left = along_z(chunk, 1), along_z(chunk, -1)
     chunks = [chunk, right, left]
 
-    pieces = [lax.dynamic_slice_in_dim(readin_weight, start + place * CHANS, CHANS, 2) for start in (0, model_width)]
-    in_weights = lax.all_gather(jnp.concatenate(pieces, 2), "grp", axis=0, tiled=True)
+    in_weights = lax.all_gather(own_weights, "grp", axis=0, tiled=True)
     split = readout_weight.reshape(2, Z, Y, CHANS, in_chans)
     split = lax.dynamic_index_in_dim(split, place % Y, 2, keepdims=False).reshape(2, Z * CHANS, in_chans)
     out_weights = lax.all_gather(split, "grp", axis=0, tiled=True)
@@ -391,17 +438,21 @@
     )(grads, gates, spectrum, *tables, twists)
     all_grads = lax.all_gather(own_grad, "grp", axis=0, tiled=False)
     devices = all_grads.shape[0]
-    picks = jnp.asarray(np.tile(np.eye(pair, dtype=np.float32), (1, devices)), bf16)
     filter_grad = pl.pallas_call(
         sum_kernel,
         out_shape=jax.ShapeDtypeStruct((CHANS, LENGTH), f32),
-        grid=(CHANS // pair,),
-        in_specs=[pl.BlockSpec((devices, pair, LENGTH), lambda i: (0, i, 0)), same(picks)],
-        out_specs=pl.BlockSpec((pair, LENGTH), lambda i: (i, 0)),
+        in_specs=[hbm],
+        out_specs=hbm,
+        scratch_shapes=[
+            pltpu.VMEM(all_grads.shape, bf16),
+            pltpu.VMEM((CHANS, LENGTH), f32),
+            pltpu.SemaphoreType.DMA((CHANS // pair, devices)),
+            pltpu.SemaphoreType.DMA((CHANS // pair,)),
+        ],
         compiler_params=params,
         cost_estimate=pl.CostEstimate(flops=all_grads.size, bytes_accessed=5 << 20, transcendentals=0),
         name="sum_gradients",
-    )(all_grads, picks)
+    )(all_grads)
     partial = pl.pallas_call(
         read_out_kernel,
         out_shape=jax.ShapeDtypeStruct((Y, BLOCK, in_chans), bf16),

time: 137 us -> 132 us (0.964)
  local copies, waits for them, and re-layouts: 7.57 us -> 5.57 us
  other arithmetic: 3.9 us -> 2.23 us
    pallas_call x0 -> x1, Pallas kernels: none -> 2.81 us  [local(): pl.pallas_call(prepare_kernel, out_shape=(jax.ShapeDtypeStruct((BLOCK + B...]
    pallas_call x1, Pallas kernels: 8.97 us -> 6.35 us  [local(): pl.pallas_call(read_out_kernel, out_shape=jax.ShapeDtypeStruct((Y, BLOCK,...]
  transfers between devices with their start and end apart: 14 -> 14, of which waited for: 7 -> 7; matrix products, arithmetic and copies ran while one was open for 6% -> 5% of each run, Pallas kernels for 26% -> 25%
where the time goes in v8:
time: 132 us; the launch traced here: 131 us
  Pallas kernels  38.9 us (29%)
  blocking collectives  27.9 us (21%)
  starting transfers between devices  27 us (20%)
  waiting for transfers between devices  15.1 us (11%)
  between operations  13.9 us (11%)
  local copies, waits for them, and re-layouts  5.57 us (4%)
  other arithmetic  2.23 us (2%)
    all_to_all x1, blocking collectives, local(): lax.all_to_all(gated, 'seq', split_axis=0, concat_axis=0, tiled=True, axi...  17.9 us
    ppermute x7, starting transfers between devices, along_z(): lax.ppermute(value, 'seq', [(z * Y + y, (z + step) % Z * Y + y) for z in...  13.6 us
    pallas_call x1, Pallas kernels, local(): pl.pallas_call(forward_kernel, out_shape=(jax.ShapeDtypeStruct(plane, bf1...  10.4 us
    all_to_all x1, blocking collectives, local(): lax.all_to_all(partial, 'seq', split_axis=0, concat_axis=0, tiled=True, a...  10 us
    ppermute x7, waiting for transfers between devices, along_z(): lax.ppermute(value, 'seq', [(z * Y + y, (z + step) % Z * Y + y) for z in...  9.09 us
    all_to_all x1, starting transfers between devices, local(): lax.all_to_all(turned, 'seq', split_axis=0, concat_axis=0, tiled=True)  8.78 us
    pallas_call x1, Pallas kernels, local(): pl.pallas_call(read_in_kernel, out_shape=jax.ShapeDtypeStruct((early_bloc...  6.67 us
    pallas_call x1, Pallas kernels, local(): pl.pallas_call(read_out_kernel, out_shape=jax.ShapeDtypeStruct((Y, BLOCK,...  6.35 us
  transfers between devices with their start and end apart: 14, of which 7 were waited for; matrix products, arithmetic and copies ran while one was open for 5% of the time, Pallas kernels for 25%

profile of v8, /device:TPU:8, one launch (start us, length us, event | category | flops | bytes accessed | tf_op | source)
XLA Modules:
  0.0 130.7 jit_solution(16376680190083219535)
XLA Ops:
  7.3 2.8 %prepare.1 = (bf16[136,256]{1,0:T(8,128)(2,1)}, bf16[2,256,128]{2,1,0:T(8,128)(2,1)}) custom-call(s32[1]{0:T(128)} %bitcast.place_ref, s32[1,128]{1,0:T(1,128)} %session_ref.1, s32[16]{0:T(128)} %slot_ref.1, bf16[1,128,256]{2,1,0:T(8,128)(2,1)} %spikes_ref.1, bf16[2,256,4096]{2,1,0:T(8,128)(2,1)} %weight_hbm.1), custom_call_target="tpu_custom_call" | custom-call | flops 65536 | bytes 524288 | tf_op jit(solution)/shard_map/prepare/pallas_call | solution.py:337
  10.1 1.7 %collective-permute-start = (bf16[136,256]{1,0:T(8,128)(2,1)}, bf16[136,256]{1,0:T(8,128)(2,1)S(1)}, u32[]{:S(2)}, u32[]{:S(2)}) collective-permute-start(bf16[136,256]{1,0:T(8,128)(2,1)} %get-tuple-element.24), channel_id=1, source_target_pairs={{0,1},{1,2},{2,3},{3,0},{4,5},{5,6},{6,7},{7,4},{8,9},{9,10},{10,1... | collective-permute-start | bytes 208904 | tf_op jit(solution)/shard_map/ppermute | solution.py:309
  11.8 0.7 collective-permute-start.1
  12.5 2.0 %collective-permute-start.2 = (bf16[136,256]{1,0:T(8,128)(2,1)}, bf16[136,256]{1,0:T(8,128)(2,1)S(1)}, u32[]{:S(2)}, u32[]{:S(2)}) collective-permute-start(bf16[136,256]{1,0:T(8,128)(2,1)} %get-tuple-element.24), channel_id=1, source_target_pairs={{0,2},{1,3},{2,0},{3,1},{4,6},{5,7},{6,4},{7,5},{8,10},{9,11},{10,... | collective-permute-start | bytes 208904 | tf_op jit(solution)/shard_map/ppermute | solution.py:309
  14.9 2.2 %collective-permute-done.1 = bf16[136,256]{1,0:T(8,128)(2,1)S(1)} collective-permute-done((bf16[136,256]{1,0:T(8,128)(2,1)}, bf16[136,256]{1,0:T(8,128)(2,1)S(1)}, u32[]{:S(2)}, u32[]{:S(2)}) %collective-permute-start.1) | collective-permute-done | bytes 69664 | tf_op jit(solution)/shard_map/ppermute | solution.py:309
  17.1 1.5 %collective-permute-done.2 = bf16[136,256]{1,0:T(8,128)(2,1)S(1)} collective-permute-done((bf16[136,256]{1,0:T(8,128)(2,1)}, bf16[136,256]{1,0:T(8,128)(2,1)S(1)}, u32[]{:S(2)}, u32[]{:S(2)}) %collective-permute-start.2) | collective-permute-done | bytes 69664 | tf_op jit(solution)/shard_map/ppermute | solution.py:309
  18.5 0.9 pad_maximum_fusion.rest_0_
  19.5 1.0 constant_dynamic-slice_fusion
  20.5 1.7 %collective-permute-start.3 = (bf16[4,136,256]{2,1,0:T(8,128)(2,1)S(1)}, bf16[4,136,256]{2,1,0:T(8,128)(2,1)S(1)}, u32[]{:S(2)}, u32[]{:S(2)}) collective-permute-start(bf16[4,136,256]{2,1,0:T(8,128)(2,1)S(1)} %pad_maximum_fusion.rest_0_), channel_id=1, source_target_pairs={{0,4},{1,5},{2,6},{3,7},{4,8},{5,9},{6,10},{7,11},{8,12},{9,13},{1... | collective-permute-start | bytes 835592 | tf_op jit(solution)/shard_map/ppermute | solution.py:313
  22.2 4.0 %collective-permute-start.4 = (bf16[4,136,256]{2,1,0:T(8,128)(2,1)S(1)}, bf16[4,136,256]{2,1,0:T(8,128)(2,1)S(1)}, u32[]{:S(2)}, u32[]{:S(2)}) collective-permute-start(bf16[4,136,256]{2,1,0:T(8,128)(2,1)S(1)} %pad_maximum_fusion.rest_0_), channel_id=1, source_target_pairs={{0,28},{1,29},{2,30},{3,31},{4,0},{5,1},{6,2},{7,3},{8,4},{9,5},{1... | collective-permute-start | bytes 835592 | tf_op jit(solution)/shard_map/ppermute | solution.py:313
  26.2 4.4 %filter_transform.1.filter_hbm = bf16[8,256,256]{2,1,0:T(8,128)(2,1)} custom-call(f32[64,4096]{1,0:T(8,128)} %filter_ref.1, bf16[512,256]{1,0:T(8,128)(2,1)} %constant.54.clone.first_ref.rest_3_, bf16[256,256]{1,0:T(8,128)(2,1)} %constant.55.clone.second_ref.rest_4_, f32[2,32,128]{2,1,0:T(8,128)} %constant.58.clone.twist_ref), custom_call_target="tpu_custom_call" | custom-call | flops 536870912 | bytes 4194304 | tf_op jit(solution)/shard_map/filter_transform/pallas_call | solution.py:358
  31.6 3.2 %collective-permute-start.6 = (bf16[4,136,256]{2,1,0:T(8,128)(2,1)S(1)}, bf16[4,136,256]{2,1,0:T(8,128)(2,1)}, u32[]{:S(2)}, u32[]{:S(2)}) collective-permute-start(bf16[4,136,256]{2,1,0:T(8,128)(2,1)S(1)} %collective-permute-done.4.rest_2_), channel_id=1, source_target_pairs={{0,28},{1,29},{2,30},{3,31},{4,0},{5,1},{6,2},{7,3},{8,4},{9,5},{1... | collective-permute-start | bytes 835592 | tf_op jit(solution)/shard_map/ppermute | solution.py:313
  34.8 1.0 copy.18
  36.4 0.8 constant_dynamic-slice_fusion.1
  37.2 2.3 %collective-permute-done.5.rest_3_ = bf16[4,136,256]{2,1,0:T(8,128)(2,1)} collective-permute-done((bf16[4,136,256]{2,1,0:T(8,128)(2,1)S(1)}, bf16[4,136,256]{2,1,0:T(8,128)(2,1)}, u32[]{:S(2)}, u32[]{:S(2)}) %collective-permute-start.5) | collective-permute-done | bytes 278560 | tf_op jit(solution)/shard_map/ppermute | solution.py:313
  39.5 0.7 broadcast_in_dim.9.taps_ref
  40.2 0.7 broadcast_in_dim.20.gain_ref
  40.9 2.3 %collective-permute-start.7 = (bf16[4,136,256]{2,1,0:T(8,128)(2,1)}, bf16[4,136,256]{2,1,0:T(8,128)(2,1)S(1)}, u32[]{:S(2)}, u32[]{:S(2)}) collective-permute-start(bf16[4,136,256]{2,1,0:T(8,128)(2,1)} %collective-permute-done.5.rest_3_), channel_id=1, source_target_pairs={{0,4},{1,5},{2,6},{3,7},{4,8},{5,9},{6,10},{7,11},{8,12},{9,13},{1... | collective-permute-start | bytes 835592 | tf_op jit(solution)/shard_map/ppermute | solution.py:313
  43.2 0.9 collective-permute-start.8
  44.1 6.7 %read_in.1.early_hbm = bf16[20,128,128]{2,1,0:T(8,128)(2,1)} custom-call(bf16[16,256,128]{2,1,0:T(8,128)(2,1)} %all-gather.5.cloned.1.call-done.weight_hbm, bf16[4,136,256]{2,1,0:T(8,128)(2,1)} %copy-done.1, bf16[4,136,256]{2,1,0:T(8,128)(2,1)} %copy-done.5, bf16[4,136,256]{2,1,0:T(8,128)(2,1)} %copy-done.6, ...), custom_call_target="tpu_custom_call" | custom-call | flops 536870912 | bytes 4194304 | tf_op jit(solution)/shard_map/read_in/pallas_call | solution.py:382
  50.8 1.2 collective-permute-start.9
  52.1 6.6 %collective-permute-done.9.rest_2_ = bf16[4,136,256]{2,1,0:T(8,128)(2,1)S(1)} collective-permute-done((bf16[4,136,256]{2,1,0:T(8,128)(2,1)S(1)}, bf16[4,136,256]{2,1,0:T(8,128)(2,1)S(1)}, u32[]{:S(2)}, u32[]{:S(2)}) %collective-permute-start.9) | collective-permute-done | bytes 278560 | tf_op jit(solution)/shard_map/ppermute | solution.py:313
  58.7 8.8 %all-to-all-start.2 = ((bf16[32,64,128]{2,1,0:T(8,128)(2,1)}), bf16[32,64,128]{2,1,0:T(8,128)(2,1)S(1)}, u32[]{:S(2)}, u32[]{:S(2)}) async-start(bf16[32,64,128]{2,1,0:T(8,128)(2,1)} %bitcast.9), calls=%async_computation.2 | async-start | bytes 1048576 | tf_op jit(solution)/shard_map/all_to_all | solution.py:400
  67.7 10.4 %long_convolution.1 = (bf16[32,64,128]{2,1,0:T(8,128)(2,1)}, bf16[32,64,128]{2,1,0:T(8,128)(2,1)}, bf16[8,256,256]{2,1,0:T(8,128)(2,1)}) custom-call(s32[2]{0:T(128)} %pad_add_fusion.place_ref, f32[3,64,128]{2,1,0:T(8,128)} %broadcast_in_dim.9.taps_ref, f32[64,128]{1,0:T(8,128)} %broadcast_in_dim.20.gain_ref, f32[2,32,128]{2,1,0:T(8,128)} %constant.58.clone.twist_ref, ...), custom_call_target="tpu_custom_call" | custom-call | flops 2147483648 | bytes 8388608 | tf_op jit(solution)/shard_map/long_convolution/pallas_call | solution.py:403
  78.1 2.0 %all-to-all-done.2.grad_ref = bf16[32,64,128]{2,1,0:T(8,128)(2,1)S(1)} async-done(((bf16[32,64,128]{2,1,0:T(8,128)(2,1)}), bf16[32,64,128]{2,1,0:T(8,128)(2,1)S(1)}, u32[]{:S(2)}, u32[]{:S(2)}) %all-to-all-start.2) | async-done | bytes 524320 | tf_op jit(solution)/shard_map/all_to_all | solution.py:400
  80.1 0.8 copy-done.4
  80.9 4.9 %filter_gradient.1 = bf16[64,4096]{1,0:T(8,128)(2,1)} custom-call(bf16[32,64,128]{2,1,0:T(8,128)(2,1)} %copy-done.4, bf16[32,64,128]{2,1,0:T(8,128)(2,1)} %get-tuple-element.44.gate_ref, bf16[8,256,256]{2,1,0:T(8,128)(2,1)} %get-tuple-element.45.spectrum_ref, bf16[512,256]{1,0:T(8,128)(2,1)} %constant.54.clone.first_ref.rest_3_, ...), custom_call_target="tpu_custom_call" | custom-call | flops 1073741824 | bytes 4194304 | tf_op jit(solution)/shard_map/filter_gradient/pallas_call | solution.py:427
  85.8 17.9 %all_to_all.15.rows_hbm = bf16[8,4,64,128]{3,2,1,0:T(8,128)(2,1)} all-to-all(bf16[8,4,64,128]{3,2,1,0:T(8,128)(2,1)S(1)} %bitcast.22), channel_id=1, replica_groups={{0,4,8,12,16,20,24,28},{1,5,9,13,17,21,25,29},{2,6,10,14,18,22,26,30},{..., dimensions={0} | all-to-all | bytes 1048576 | tf_op jit(solution)/shard_map/all_to_all | solution.py:426
  103.7 6.3 %read_out.1 = bf16[4,128,256]{2,1,0:T(8,128)(2,1)} custom-call(s32[2]{0:T(128)} %pad_add_fusion.place_ref, bf16[8,4,64,128]{3,2,1,0:T(8,128)(2,1)} %all_to_all.15.rows_hbm, bf16[4,8,256]{2,1,0:T(8,128)(2,1)} %slice.3.marks_hbm, bf16[16,512,256]{2,1,0:T(8,128)(2,1)} %all-gather.7.cloned.1.call-done.weight_hbm), custom_call_target="tpu_custom_call" | custom-call | flops 2147483648 | bytes 6291456 | tf_op jit(solution)/shard_map/read_out/pallas_call | solution.py:456
  110.1 10.0 %all_to_all.16 = bf16[4,128,256]{2,1,0:T(8,128)(2,1)S(1)} all-to-all(bf16[4,128,256]{2,1,0:T(8,128)(2,1)} %read_out.1), channel_id=1, replica_groups={{0,1,2,3},{4,5,6,7},{8,9,10,11},{12,13,14,15},{16,17,18,19},{20,21,22,2..., dimensions={0} | all-to-all | bytes 524288 | tf_op jit(solution)/shard_map/all_to_all | solution.py:471
  120.1 0.7 reduce_sum.12
  120.8 3.4 %sum_gradients.1 = f32[64,4096]{1,0:T(8,128)} custom-call(bf16[8,64,4096]{2,1,0:T(8,128)(2,1)} %bitcast.19), custom_call_target="tpu_custom_call" | custom-call | flops 2097152 | bytes 5242880 | tf_op jit(solution)/shard_map/sum_gradients/pallas_call | solution.py:441
  (37 shorter events, 2.3 us)
Async XLA Ops:
  7.2 12.3 %copy-start = (bf16[2,2048,256]{2,1,0:T(8,128)(2,1)S(1)}, bf16[2,2048,256]{2,1,0:T(8,128)(2,1)}, u32[]{:S(2)}) copy-start(bf16[2,2048,256]{2,1,0:T(8,128)(2,1)} %param.21) | copy-start | bytes 6291460
  7.2 36.9 %all-gather.5.cloned.1.call-start = ((), (), s32[]{:S(2)}) async-start(), calls=%async_computation.3 | async-start | bytes 1179648 | tf_op jit(solution)/shard_map/all_gather | solution.py:353
  7.2 27.6 %copy-start.2 = (bf16[1,128,2048]{2,1,0:T(8,128)(2,1)S(1)}, bf16[1,128,2048]{2,1,0:T(8,128)(2,1)}, u32[]{:S(2)}) copy-start(bf16[1,128,2048]{2,1,0:T(8,128)(2,1)} %param.22) | copy-start | bytes 1572868
  7.2 33.0 %copy-start.7 = (f32[64]{0:T(128)S(1)}, f32[64]{0:T(128)}, u32[]{:S(2)}) copy-start(f32[64]{0:T(128)} %param.20) | copy-start | bytes 772
  10.1 93.6 %all-gather.7.cloned.1.call-start = ((), (), s32[]{:S(2)}) async-start(), calls=%async_computation.4 | async-start | bytes 4718592 | tf_op jit(solution)/shard_map/all_gather | solution.py:356
  10.1 4.8 %collective-permute-start = (bf16[136,256]{1,0:T(8,128)(2,1)}, bf16[136,256]{1,0:T(8,128)(2,1)S(1)}, u32[]{:S(2)}, u32[]{:S(2)}) collective-permute-start(bf16[136,256]{1,0:T(8,128)(2,1)} %get-tuple-element.24), channel_id=1, source_target_pairs={{0,1},{1,2},{2,3},{3,0},{4,5},{5,6},{6,7},{7,4},{8,9},{9,10},{10,1... | collective-permute-start | bytes 208904 | tf_op jit(solution)/shard_map/ppermute | solution.py:309
  11.8 5.3 %collective-permute-start.1 = (bf16[136,256]{1,0:T(8,128)(2,1)}, bf16[136,256]{1,0:T(8,128)(2,1)S(1)}, u32[]{:S(2)}, u32[]{:S(2)}) collective-permute-start(bf16[136,256]{1,0:T(8,128)(2,1)} %get-tuple-element.24), channel_id=1, source_target_pairs={{0,3},{1,0},{2,1},{3,2},{4,7},{5,4},{6,5},{7,6},{8,11},{9,8},{10,9... | collective-permute-start | bytes 208904 | tf_op jit(solution)/shard_map/ppermute | solution.py:309
  12.5 6.0 %collective-permute-start.2 = (bf16[136,256]{1,0:T(8,128)(2,1)}, bf16[136,256]{1,0:T(8,128)(2,1)S(1)}, u32[]{:S(2)}, u32[]{:S(2)}) collective-permute-start(bf16[136,256]{1,0:T(8,128)(2,1)} %get-tuple-element.24), channel_id=1, source_target_pairs={{0,2},{1,3},{2,0},{3,1},{4,6},{5,7},{6,4},{7,5},{8,10},{9,11},{10,... | collective-permute-start | bytes 208904 | tf_op jit(solution)/shard_map/ppermute | solution.py:309
  19.5 24.7 %copy-start.1 = (bf16[4,136,256]{2,1,0:T(8,128)(2,1)}, bf16[4,136,256]{2,1,0:T(8,128)(2,1)S(1)}, u32[]{:S(2)}) copy-start(bf16[4,136,256]{2,1,0:T(8,128)(2,1)S(1)} %pad_maximum_fusion.rest_0_) | copy-start | bytes 835588
  20.5 11.0 %collective-permute-start.3 = (bf16[4,136,256]{2,1,0:T(8,128)(2,1)S(1)}, bf16[4,136,256]{2,1,0:T(8,128)(2,1)S(1)}, u32[]{:S(2)}, u32[]{:S(2)}) collective-permute-start(bf16[4,136,256]{2,1,0:T(8,128)(2,1)S(1)} %pad_maximum_fusion.rest_0_), channel_id=1, source_target_pairs={{0,4},{1,5},{2,6},{3,7},{4,8},{5,9},{6,10},{7,11},{8,12},{9,13},{1... | collective-permute-start | bytes 835592 | tf_op jit(solution)/shard_map/ppermute | solution.py:313
  22.2 9.3 %collective-permute-start.4 = (bf16[4,136,256]{2,1,0:T(8,128)(2,1)S(1)}, bf16[4,136,256]{2,1,0:T(8,128)(2,1)S(1)}, u32[]{:S(2)}, u32[]{:S(2)}) collective-permute-start(bf16[4,136,256]{2,1,0:T(8,128)(2,1)S(1)} %pad_maximum_fusion.rest_0_), channel_id=1, source_target_pairs={{0,28},{1,29},{2,30},{3,31},{4,0},{5,1},{6,2},{7,3},{8,4},{9,5},{1... | collective-permute-start | bytes 835592 | tf_op jit(solution)/shard_map/ppermute | solution.py:313
  31.5 12.7 %copy-start.5 = (bf16[4,136,256]{2,1,0:T(8,128)(2,1)}, bf16[4,136,256]{2,1,0:T(8,128)(2,1)S(1)}, u32[]{:S(2)}) copy-start(bf16[4,136,256]{2,1,0:T(8,128)(2,1)S(1)} %collective-permute-done.3.rest_1_) | copy-start | bytes 835588
  31.5 12.7 %copy-start.6 = (bf16[4,136,256]{2,1,0:T(8,128)(2,1)}, bf16[4,136,256]{2,1,0:T(8,128)(2,1)S(1)}, u32[]{:S(2)}) copy-start(bf16[4,136,256]{2,1,0:T(8,128)(2,1)S(1)} %collective-permute-done.4.rest_2_) | copy-start | bytes 835588
  31.5 8.0 %collective-permute-start.5 = (bf16[4,136,256]{2,1,0:T(8,128)(2,1)S(1)}, bf16[4,136,256]{2,1,0:T(8,128)(2,1)}, u32[]{:S(2)}, u32[]{:S(2)}) collective-permute-start(bf16[4,136,256]{2,1,0:T(8,128)(2,1)S(1)} %collective-permute-done.3.rest_1_), channel_id=1, source_target_pairs={{0,4},{1,5},{2,6},{3,7},{4,8},{5,9},{6,10},{7,11},{8,12},{9,13},{1... | collective-permute-start | bytes 835592 | tf_op jit(solution)/shard_map/ppermute | solution.py:313
  31.6 7.9 %collective-permute-start.6 = (bf16[4,136,256]{2,1,0:T(8,128)(2,1)S(1)}, bf16[4,136,256]{2,1,0:T(8,128)(2,1)}, u32[]{:S(2)}, u32[]{:S(2)}) collective-permute-start(bf16[4,136,256]{2,1,0:T(8,128)(2,1)S(1)} %collective-permute-done.4.rest_2_), channel_id=1, source_target_pairs={{0,28},{1,29},{2,30},{3,31},{4,0},{5,1},{6,2},{7,3},{8,4},{9,5},{1... | collective-permute-start | bytes 835592 | tf_op jit(solution)/shard_map/ppermute | solution.py:313
  40.9 9.9 %collective-permute-start.7 = (bf16[4,136,256]{2,1,0:T(8,128)(2,1)}, bf16[4,136,256]{2,1,0:T(8,128)(2,1)S(1)}, u32[]{:S(2)}, u32[]{:S(2)}) collective-permute-start(bf16[4,136,256]{2,1,0:T(8,128)(2,1)} %collective-permute-done.5.rest_3_), channel_id=1, source_target_pairs={{0,4},{1,5},{2,6},{3,7},{4,8},{5,9},{6,10},{7,11},{8,12},{9,13},{1... | collective-permute-start | bytes 835592 | tf_op jit(solution)/shard_map/ppermute | solution.py:313
  43.2 7.6 %collective-permute-start.8 = (bf16[4,136,256]{2,1,0:T(8,128)(2,1)}, bf16[4,136,256]{2,1,0:T(8,128)(2,1)}, u32[]{:S(2)}, u32[]{:S(2)}) collective-permute-start(bf16[4,136,256]{2,1,0:T(8,128)(2,1)} %collective-permute-done.6.rest_4_), channel_id=1, source_target_pairs={{0,28},{1,29},{2,30},{3,31},{4,0},{5,1},{6,2},{7,3},{8,4},{9,5},{1... | collective-permute-start | bytes 835592 | tf_op jit(solution)/shard_map/ppermute | solution.py:313
  50.8 16.9 %copy-start.8 = (bf16[4,136,256]{2,1,0:T(8,128)(2,1)}, bf16[4,136,256]{2,1,0:T(8,128)(2,1)S(1)}, u32[]{:S(2)}) copy-start(bf16[4,136,256]{2,1,0:T(8,128)(2,1)S(1)} %collective-permute-done.7.rest_0_) | copy-start | bytes 835588
  50.8 7.8 %collective-permute-start.9 = (bf16[4,136,256]{2,1,0:T(8,128)(2,1)S(1)}, bf16[4,136,256]{2,1,0:T(8,128)(2,1)S(1)}, u32[]{:S(2)}, u32[]{:S(2)}) collective-permute-start(bf16[4,136,256]{2,1,0:T(8,128)(2,1)S(1)} %collective-permute-done.7.rest_0_), channel_id=1, source_target_pairs={{0,4},{1,5},{2,6},{3,7},{4,8},{5,9},{6,10},{7,11},{8,12},{9,13},{1... | collective-permute-start | bytes 835592 | tf_op jit(solution)/shard_map/ppermute | solution.py:313
  58.7 9.0 %copy-start.9 = (bf16[4,136,256]{2,1,0:T(8,128)(2,1)}, bf16[4,136,256]{2,1,0:T(8,128)(2,1)S(1)}, u32[]{:S(2)}) copy-start(bf16[4,136,256]{2,1,0:T(8,128)(2,1)S(1)} %collective-permute-done.9.rest_2_) | copy-start | bytes 835588
  58.7 21.4 %all-to-all-start.2 = ((bf16[32,64,128]{2,1,0:T(8,128)(2,1)}), bf16[32,64,128]{2,1,0:T(8,128)(2,1)S(1)}, u32[]{:S(2)}, u32[]{:S(2)}) async-start(bf16[32,64,128]{2,1,0:T(8,128)(2,1)} %bitcast.9), calls=%async_computation.2 | async-start | bytes 1048576 | tf_op jit(solution)/shard_map/all_to_all | solution.py:400
  67.5 53.3 %all-gather.9.cloned.1.call-start = ((), (), s32[]{:S(2)}) async-start(), calls=%async_computation.5 | async-start | bytes 4718592 | tf_op jit(solution)/shard_map/all_gather | solution.py:439
  78.1 7.8 %copy-start.3 = (bf16[32,64,128]{2,1,0:T(8,128)(2,1)S(1)}, bf16[32,64,128]{2,1,0:T(8,128)(2,1)}, u32[]{:S(2)}) copy-start(bf16[32,64,128]{2,1,0:T(8,128)(2,1)} %get-tuple-element.40) | copy-start | bytes 1572868
  80.1 0.8 copy-start.4
Sparse Core Ops, SparseCore 0:
  10.2 28.7 all-gather.4
  40.9 34.5 all-gather.6
  86.0 33.5 all-gather.8

commit v9 on v8

--- a/solution.py
+++ b/solution.py
@@ -148,39 +148,44 @@
     lax.fori_loop(0, len(chunk_hbms), step, 0)
 
 
-def forward_kernel(place_ref, taps_ref, gain_ref, twist_ref, filter_hbm, weight_hbm, early_hbm, *rest):
-    late = Z - early_hbm.shape[0] // Y
-    chunk_hbms = rest[:late]
-    table_hbms = rest[late : late + 4]
-    gated_ref, gate_ref, spectrum_ref, both, rows, weight, spectra, *rest = rest[late + 4 :]
+def forward_kernel(place_ref, taps_ref, gain_ref, twist_ref, filter_hbm, weight_hbm, *rest):
+    early_hbms, (chunk_hbm, *rest) = rest[:2], rest[2:]
+    table_hbms, rest = rest[:4], rest[4:]
+    gated_hbm, gate_hbm, spectrum_hbm, both, rows, weight, spectra, gated_all, spectrum_all, *rest = rest
     tables = rest[:4]
-    weight_sems, row_sems, early_sems, sems = rest[4:]
+    weight_sems, early_sems, sems, store_sems = rest[4:]
     loads = weight_copies(weight_hbm, weight, weight_sems)
-    for index, chunk in enumerate(chunk_hbms):
-        loads.append(pltpu.make_async_copy(chunk, rows.at[pl.ds(index * Y, Y)], row_sems.at[index]))
     others = []
-    for index in range(early_hbm.shape[0]):
-        target = both.at[block_of(place_ref, z_step_of(index // Y), index % Y)]
-        others.append(pltpu.make_async_copy(early_hbm.at[index], target, early_sems.at[index]))
+    for early_hbm in early_hbms:
+        for index in range(early_hbm.shape[0]):
+            number = len(others)
+            target = both.at[block_of(place_ref, z_step_of(number // Y), number % Y)]
+            others.append(pltpu.make_async_copy(early_hbm.at[index], target, early_sems.at[number]))
     pairs = [(filter_hbm, spectra)] + list(zip(table_hbms, tables))
     others += [pltpu.make_async_copy(source, target, sems.at[index]) for index, (source, target) in enumerate(pairs)]
+    loads.append(pltpu.make_async_copy(chunk_hbm, rows, sems.at[len(pairs)]))
     start_all(loads)
     start_all(others)
     wait_all(loads)
-
-    def read_in(index, carry):
-        blocks = project(rows, index * Y, Y, weight)
-        for y_index in range(Y):
-            both[block_of(place_ref, z_step_of(index + Z - late), y_index)] = blocks[y_index]
-        return carry
-
-    lax.fori_loop(0, late, read_in, 0)
+    last = project(rows, 0, Y, weight)
+    for y_index in range(Y):
+        both[block_of(place_ref, z_step_of(Z - 1), y_index)] = last[y_index]
     cosine, sine = twists_of(twist_ref)
     lane = lax.broadcasted_iota(jnp.int32, (BLOCKS, LANE8, BLOCK), 2)
     count = BLOCKS * LANE8
     cube = (BLOCKS, LANE8, BLOCK)
     wait_all(others)
+    gate_store = pltpu.make_async_copy(both.at[:, pl.ds(CHANS, CHANS), :], gate_hbm, store_sems.at[0, GROUPS // 2])
+    gate_store.start()
     first_ref, second_ref, back_second_ref, back_first_ref = tables
+
+    def stores_of(pair):
+        here = pl.ds(pl.multiple_of(pair * 2 * LANE8, 2 * LANE8), 2 * LANE8)
+        groups = pl.ds(pair * 2, 2)
+        return [
+            pltpu.make_async_copy(gated_all.at[:, here, :], gated_hbm.at[:, here, :], store_sems.at[0, pair]),
+            pltpu.make_async_copy(spectrum_all.at[groups], spectrum_hbm.at[groups], store_sems.at[1, pair]),
+        ]
 
     def short(value, group):
         taps = taps_ref[:, pl.ds(pl.multiple_of(group * LANE8, LANE8), LANE8), :]
@@ -198,7 +203,7 @@
         gate = both[:, there, :]
         signals = [short(value[:, i * LANE8 : (i + 1) * LANE8], pair * 2 + i) for i in range(2)]
         own = forward(*signals, first_ref, second_ref, cosine, sine)
-        spectrum_ref[pl.ds(pair * 2, 2)] = own.reshape(2, count, 2 * BLOCK).astype(bf16)
+        spectrum_all[pl.ds(pair * 2, 2)] = own.reshape(2, count, 2 * BLOCK).astype(bf16)
         weight = spectra[pl.ds(pair * 2, 2)].reshape(2 * count, 2 * BLOCK).astype(f32)
         own_re, own_im = own[:, :BLOCK], own[:, BLOCK:]
         filter_re, filter_im = weight[:, :BLOCK], weight[:, BLOCK:]
@@ -207,11 +212,14 @@
         signal = jnp.concatenate([piece.reshape(cube) for piece in signals], 1)
         long_part = jnp.concatenate([result[:, i * BLOCK : (i + 1) * BLOCK].reshape(cube) for i in range(2)], 1)
         mixed = (long_part + gain_ref[here, :][None] * signal).astype(bf16).astype(f32)
-        gated_ref[:, here, :] = (gate.astype(f32) * mixed).astype(bf16)
-        gate_ref[:, here, :] = gate
+        gated_all[:, here, :] = (gate.astype(f32) * mixed).astype(bf16)
+        start_all(stores_of(pair))
         return carry
 
     lax.fori_loop(0, GROUPS // 2, step, 0, unroll=2)
+    for pair in range(GROUPS // 2):
+        wait_all(stores_of(pair))
+    gate_store.wait()
 
 
 def gradient_kernel(grad_ref, gate_ref, spectrum_ref, first_ref, second_ref, back_second_ref, back_first_ref, twist_ref, out_ref):
@@ -279,7 +287,7 @@
     wait_all(stores)
 
 
-def prepare_kernel(place_ref, session_ref, slot_ref, spikes_ref, weight_hbm, block_ref, own_ref, value, gate, sems):
+def prepare_kernel(place_ref, session_ref, slot_ref, spikes_ref, weight_hbm, out_hbm, block_ref, own_ref, own_out_hbm, value, gate, sems):
     place = place_ref[0]
     half = weight_hbm.shape[2] // 2
     window = pl.multiple_of(place // 2 * 2 * CHANS, 2 * CHANS)
@@ -288,6 +296,8 @@
         pltpu.make_async_copy(weight_hbm.at[:, :, pl.ds(half + window, 2 * CHANS)], gate, sems.at[1]),
     ]
     start_all(loads)
+    moved = pltpu.make_async_copy(out_hbm.at[:, :, lax.rem(place, Y)], own_out_hbm, sems.at[2])
+    moved.start()
     trials = BLOCK // TRIAL
     width = block_ref.shape[1]
     row = lax.broadcasted_iota(jnp.int32, (trials, width), 0)
@@ -303,6 +313,7 @@
     high = pltpu.roll(gate[...].astype(f32).reshape(slots * inner, lanes), (1 - odd) * CHANS, 1)
     lane = lax.broadcasted_iota(jnp.int32, (slots * inner, lanes), 1)
     own_ref[...] = jnp.where(lane < CHANS, low, high).astype(bf16).reshape(slots, inner, lanes)
+    moved.wait()
 
 
 def along_y(value, step):
@@ -334,39 +345,30 @@
     same = lambda table: pl.BlockSpec(table.shape, lambda i, rank=table.ndim: (0,) * rank)
 
     own_shape = (2, in_chans, 2 * CHANS)
-    block, own_weights = pl.pallas_call(
+    out_split = readout_weight.reshape(2, Z, Y, CHANS, in_chans)
+    block, own_weights, own_out = pl.pallas_call(
         prepare_kernel,
-        out_shape=(jax.ShapeDtypeStruct((BLOCK + BLOCK // TRIAL, in_chans), bf16), jax.ShapeDtypeStruct(own_shape, bf16)),
-        in_specs=[scalar] * 3 + whole(1) + [hbm],
-        out_specs=tuple(whole(2)),
-        scratch_shapes=[pltpu.VMEM(own_shape, bf16), pltpu.VMEM(own_shape, bf16), pltpu.SemaphoreType.DMA((2,))],
+        out_shape=(
+            jax.ShapeDtypeStruct((BLOCK + BLOCK // TRIAL, in_chans), bf16),
+            jax.ShapeDtypeStruct(own_shape, bf16),
+            jax.ShapeDtypeStruct((2, Z, CHANS, in_chans), bf16),
+        ),
+        in_specs=[scalar] * 3 + whole(1) + [hbm] * 2,
+        out_specs=tuple(whole(2)) + (hbm,),
+        scratch_shapes=[pltpu.VMEM(own_shape, bf16), pltpu.VMEM(own_shape, bf16), pltpu.SemaphoreType.DMA((3,))],
         compiler_params=params,
         cost_estimate=pl.CostEstimate(flops=1 << 16, bytes_accessed=1 << 19, transcendentals=0),
         name="prepare",
-    )(place.astype(jnp.int32)[None], session_of_bin, session_slot, spikes, readin_weight)
+    )(place.astype(jnp.int32)[None], session_of_bin, session_slot, spikes, readin_weight, out_split)
     chunk = jnp.stack([block, along_y(block, 1), along_y(block, -1), along_y(block, 2)])
-    chunk, readout_weight = lax.optimization_barrier((chunk, readout_weight))
     own_marks = chunk[:, BLOCK:, :]
     right, left = along_z(chunk, 1), along_z(chunk, -1)
     chunks = [chunk, right, left]
 
     in_weights = lax.all_gather(own_weights, "grp", axis=0, tiled=True)
-    split = readout_weight.reshape(2, Z, Y, CHANS, in_chans)
-    split = lax.dynamic_index_in_dim(split, place % Y, 2, keepdims=False).reshape(2, Z * CHANS, in_chans)
+    right, left, own_marks, own_out = lax.optimization_barrier((right, left, own_marks, own_out))
+    split = own_out.reshape(2, Z * CHANS, in_chans)
     out_weights = lax.all_gather(split, "grp", axis=0, tiled=True)
-
-    filter_spectrum = pl.pallas_call(
-        filter_kernel,
-        out_shape=spectrum_shape,
-        grid=(GROUPS // 2,),
-        in_specs=[pl.BlockSpec((pair, LENGTH), lambda i: (i, 0))] + [same(table) for table in (first, second, twists)],
-        out_specs=pl.BlockSpec((2,) + spectrum_shape.shape[1:], lambda i: (i, 0, 0)),
-        compiler_params=params,
-        cost_estimate=pl.CostEstimate(flops=work, bytes_accessed=4 << 20, transcendentals=0),
-        name="filter_transform",
-    )(long_filter, first, second, twists)
-
-    right, left, filter_spectrum, own_marks = lax.optimization_barrier((right, left, filter_spectrum, own_marks))
     right, left = along_z(right, 1), along_z(left, -1)
     chunks += [right, left]
     turned = out_grad[0].T.reshape(BLOCKS, CHANS, BLOCK)
@@ -378,25 +380,40 @@
     right, left = along_z(right, 1), along_z(left, -1)
     slot_count = session_slot.shape[0]
     width = 2 * CHANS
-    early_blocks = len(chunks) * Y
-    early = pl.pallas_call(
-        read_in_kernel,
-        out_shape=jax.ShapeDtypeStruct((early_blocks, width, BLOCK), bf16),
-        in_specs=[hbm] * (1 + len(chunks)),
-        out_specs=whole(1)[0],
-        scratch_shapes=[
-            pltpu.VMEM((early_blocks,) + chunk.shape[1:], bf16),
-            pltpu.VMEM((slot_count // 2, in_chans, 2 * width), bf16),
-            pltpu.SemaphoreType.DMA((slot_count,)),
-            pltpu.SemaphoreType.DMA((len(chunks),)),
-        ],
+
+    def read_in(pieces):
+        blocks = len(pieces) * Y
+        return pl.pallas_call(
+            read_in_kernel,
+            out_shape=jax.ShapeDtypeStruct((blocks, width, BLOCK), bf16),
+            in_specs=[hbm] * (1 + len(pieces)),
+            out_specs=whole(1)[0],
+            scratch_shapes=[
+                pltpu.VMEM((blocks,) + chunk.shape[1:], bf16),
+                pltpu.VMEM((slot_count // 2, in_chans, 2 * width), bf16),
+                pltpu.SemaphoreType.DMA((slot_count,)),
+                pltpu.SemaphoreType.DMA((len(pieces),)),
+            ],
+            compiler_params=params,
+            cost_estimate=pl.CostEstimate(flops=work, bytes_accessed=4 << 20, transcendentals=0),
+            name="read_in",
+        )(in_weights, *pieces)
+
+    early = read_in(chunks)
+    right, left, early, long_filter = lax.optimization_barrier((right, left, early, long_filter))
+    last = along_z(right, 1)
+    later = read_in([right, left])
+    filter_spectrum = pl.pallas_call(
+        filter_kernel,
+        out_shape=spectrum_shape,
+        grid=(GROUPS // 2,),
+        in_specs=[pl.BlockSpec((pair, LENGTH), lambda i: (i, 0))] + [same(table) for table in (first, second, twists)],
+        out_specs=pl.BlockSpec((2,) + spectrum_shape.shape[1:], lambda i: (i, 0, 0)),
         compiler_params=params,
         cost_estimate=pl.CostEstimate(flops=work, bytes_accessed=4 << 20, transcendentals=0),
-        name="read_in",
-    )(in_weights, *chunks)
-    right, left, early = lax.optimization_barrier((right, left, early))
-    late = [right, left, along_z(right, 1)]
-    late[2], turned = lax.optimization_barrier((late[2], turned))
+        name="filter_transform",
+    )(long_filter, first, second, twists)
+    last, later, filter_spectrum, turned = lax.optimization_barrier((last, later, filter_spectrum, turned))
     grads = lax.all_to_all(turned, "seq", split_axis=0, concat_axis=0, tiled=True)
 
     tables = (first, second, back_second, back_first)
@@ -407,20 +424,23 @@
             jax.ShapeDtypeStruct(plane, bf16),
             spectrum_shape,
         ),
-        in_specs=[scalar] + whole(3) + [hbm] * (3 + len(late) + 4),
-        out_specs=tuple(whole(3)),
+        in_specs=[scalar] + whole(3) + [hbm] * (5 + 4),
+        out_specs=(hbm,) * 3,
         scratch_shapes=[
             pltpu.VMEM((BLOCKS, 2 * CHANS, BLOCK), bf16),
-            pltpu.VMEM((len(late) * Y,) + chunk.shape[1:], bf16),
+            pltpu.VMEM(chunk.shape, bf16),
             pltpu.VMEM((slot_count // 2, in_chans, 4 * CHANS), bf16),
+            pltpu.VMEM(spectrum_shape.shape, bf16),
+            pltpu.VMEM(plane, bf16),
             pltpu.VMEM(spectrum_shape.shape, bf16),
         ]
         + [pltpu.VMEM(table.shape, bf16) for table in tables]
-        + [pltpu.SemaphoreType.DMA((count,)) for count in (slot_count, len(late), early_blocks, 5)],
+        + [pltpu.SemaphoreType.DMA((count,)) for count in (slot_count, (Z - 1) * Y, 6)]
+        + [pltpu.SemaphoreType.DMA((2, GROUPS // 2 + 1))],
         compiler_params=params,
         cost_estimate=pl.CostEstimate(flops=4 * work, bytes_accessed=8 << 20, transcendentals=0),
         name="long_convolution",
-    )(coords, taps, gains, twists, filter_spectrum, in_weights, early, *late, *tables)
+    )(coords, taps, gains, twists, filter_spectrum, in_weights, early, later, last, *tables)
 
     gated = gated.reshape(Z, Y, CHANS, BLOCK)
     arrived = lax.all_to_all(gated, "seq", split_axis=0, concat_axis=0, tiled=True, axis_index_groups=z_groups)

time: 132 us -> 148 us (1.12)
  Pallas kernels: 38.9 us -> 56.6 us
  waiting for transfers between devices: 15.1 us -> 17.5 us
  local copies, waits for them, and re-layouts: 5.57 us -> 4.04 us
    pallas_call x1, Pallas kernels: 2.81 us -> 18.6 us  [local(): pl.pallas_call(prepare_kernel, out_shape=(jax.ShapeDtypeStruct((BLOCK + B...]
    all_to_all x1, waiting for transfers between devices: 2 us -> 6.04 us  [local(): lax.all_to_all(turned, 'seq', split_axis=0, concat_axis=0, tiled=True)]
    pallas_call x1 -> x2, Pallas kernels: 6.67 us -> 10.6 us  [read_in(): pl.pallas_call(read_in_kernel, out_shape=jax.ShapeDtypeStruct((blocks, wi...]
    pallas_call x1, Pallas kernels: 10.4 us -> 8.29 us  [local(): pl.pallas_call(forward_kernel, out_shape=(jax.ShapeDtypeStruct(plane, bf1...]
    ppermute x7, waiting for transfers between devices: 9.09 us -> 7.47 us  [along_z(): lax.ppermute(value, 'seq', [(z * Y + y, (z + step) % Z * Y + y) for z in...]
  transfers between devices with their start and end apart: 14 -> 14, of which waited for: 7 -> 6; matrix products, arithmetic and copies ran while one was open for 5% -> 4% of each run, Pallas kernels for 25% -> 23%
where the time goes in v9:
time: 148 us
  Pallas kernels  56.6 us (38%)
  blocking collectives  27.2 us (18%)
  starting transfers between devices  26.2 us (18%)
  waiting for transfers between devices  17.5 us (12%)
  between operations  14 us (9%)
  local copies, waits for them, and re-layouts  4.04 us (3%)
  other arithmetic  2.21 us (1%)
    pallas_call x1, Pallas kernels, local(): pl.pallas_call(prepare_kernel, out_shape=(jax.ShapeDtypeStruct((BLOCK + B...  18.6 us
    all_to_all x1, blocking collectives, local(): lax.all_to_all(gated, 'seq', split_axis=0, concat_axis=0, tiled=True, axi...  17 us
    ppermute x7, starting transfers between devices, along_z(): lax.ppermute(value, 'seq', [(z * Y + y, (z + step) % Z * Y + y) for z in...  13.5 us
    pallas_call x2, Pallas kernels, read_in(): pl.pallas_call(read_in_kernel, out_shape=jax.ShapeDtypeStruct((blocks, wi...  10.6 us
    all_to_all x1, blocking collectives, local(): lax.all_to_all(partial, 'seq', split_axis=0, concat_axis=0, tiled=True, a...  10.2 us
    pallas_call x1, Pallas kernels, local(): pl.pallas_call(forward_kernel, out_shape=(jax.ShapeDtypeStruct(plane, bf1...  8.29 us
    all_to_all x1, starting transfers between devices, local(): lax.all_to_all(turned, 'seq', split_axis=0, concat_axis=0, tiled=True)  7.94 us
    ppermute x7, waiting for transfers between devices, along_z(): lax.ppermute(value, 'seq', [(z * Y + y, (z + step) % Z * Y + y) for z in...  7.47 us
  transfers between devices with their start and end apart: 14, of which 6 were waited for; matrix products, arithmetic and copies ran while one was open for 4% of the time, Pallas kernels for 23%

profile of v9, /device:TPU:8, one launch (start us, length us, event | category | flops | bytes accessed | tf_op | source)
XLA Modules:
  0.0 147.8 jit_solution(5272057301138603655)
XLA Ops:
  7.3 18.6 %prepare.1 = (bf16[136,256]{1,0:T(8,128)(2,1)}, bf16[2,256,128]{2,1,0:T(8,128)(2,1)}, bf16[2,8,64,256]{3,2,1,0:T(8,128)(2,1)}) custom-call(s32[1]{0:T(128)} %bitcast.place_ref, s32[1,128]{1,0:T(1,128)} %session_ref.1, s32[16]{0:T(128)} %slot_ref.1, bf16[1,128,256]{2,1,0:T(8,128)(2,1)} %spikes_ref.1, bf16[2,256,4096]{2,1,0:T(8,128)(2,1)} %weight_hbm.1, ...), custom_call_target="tpu_custom_call" | custom-call | flops 65536 | bytes 524288 | tf_op jit(solution)/shard_map/prepare/pallas_call | solution.py:349
  26.0 1.7 %collective-permute-start = (bf16[136,256]{1,0:T(8,128)(2,1)}, bf16[136,256]{1,0:T(8,128)(2,1)S(1)}, u32[]{:S(2)}, u32[]{:S(2)}) collective-permute-start(bf16[136,256]{1,0:T(8,128)(2,1)} %get-tuple-element.26), channel_id=1, source_target_pairs={{0,1},{1,2},{2,3},{3,0},{4,5},{5,6},{6,7},{7,4},{8,9},{9,10},{10,1... | collective-permute-start | bytes 208904 | tf_op jit(solution)/shard_map/ppermute | solution.py:320
  27.6 0.7 collective-permute-start.1
  28.3 2.0 %collective-permute-start.2 = (bf16[136,256]{1,0:T(8,128)(2,1)}, bf16[136,256]{1,0:T(8,128)(2,1)S(1)}, u32[]{:S(2)}, u32[]{:S(2)}) collective-permute-start(bf16[136,256]{1,0:T(8,128)(2,1)} %get-tuple-element.26), channel_id=1, source_target_pairs={{0,2},{1,3},{2,0},{3,1},{4,6},{5,7},{6,4},{7,5},{8,10},{9,11},{10,... | collective-permute-start | bytes 208904 | tf_op jit(solution)/shard_map/ppermute | solution.py:320
  30.7 2.2 %collective-permute-done.1 = bf16[136,256]{1,0:T(8,128)(2,1)S(1)} collective-permute-done((bf16[136,256]{1,0:T(8,128)(2,1)}, bf16[136,256]{1,0:T(8,128)(2,1)S(1)}, u32[]{:S(2)}, u32[]{:S(2)}) %collective-permute-start.1) | collective-permute-done | bytes 69664 | tf_op jit(solution)/shard_map/ppermute | solution.py:320
  32.9 1.5 collective-permute-done.2
  34.3 0.9 pad_maximum_fusion.rest_0_
  35.3 1.7 %collective-permute-start.3 = (bf16[4,136,256]{2,1,0:T(8,128)(2,1)S(1)}, bf16[4,136,256]{2,1,0:T(8,128)(2,1)S(1)}, u32[]{:S(2)}, u32[]{:S(2)}) collective-permute-start(bf16[4,136,256]{2,1,0:T(8,128)(2,1)S(1)} %pad_maximum_fusion.rest_0_), channel_id=1, source_target_pairs={{0,4},{1,5},{2,6},{3,7},{4,8},{5,9},{6,10},{7,11},{8,12},{9,13},{1... | collective-permute-start | bytes 835592 | tf_op jit(solution)/shard_map/ppermute | solution.py:324
  37.0 4.0 %collective-permute-start.4 = (bf16[4,136,256]{2,1,0:T(8,128)(2,1)S(1)}, bf16[4,136,256]{2,1,0:T(8,128)(2,1)S(1)}, u32[]{:S(2)}, u32[]{:S(2)}) collective-permute-start(bf16[4,136,256]{2,1,0:T(8,128)(2,1)S(1)} %pad_maximum_fusion.rest_0_), channel_id=1, source_target_pairs={{0,28},{1,29},{2,30},{3,31},{4,0},{5,1},{6,2},{7,3},{8,4},{9,5},{1... | collective-permute-start | bytes 835592 | tf_op jit(solution)/shard_map/ppermute | solution.py:324
  41.6 4.6 %collective-permute-done.3.rest_1_ = bf16[4,136,256]{2,1,0:T(8,128)(2,1)S(1)} collective-permute-done((bf16[4,136,256]{2,1,0:T(8,128)(2,1)S(1)}, bf16[4,136,256]{2,1,0:T(8,128)(2,1)S(1)}, u32[]{:S(2)}, u32[]{:S(2)}) %collective-permute-start.3) | collective-permute-done | bytes 278560 | tf_op jit(solution)/shard_map/ppermute | solution.py:324
  46.4 3.2 %collective-permute-start.6 = (bf16[4,136,256]{2,1,0:T(8,128)(2,1)S(1)}, bf16[4,136,256]{2,1,0:T(8,128)(2,1)S(1)}, u32[]{:S(2)}, u32[]{:S(2)}) collective-permute-start(bf16[4,136,256]{2,1,0:T(8,128)(2,1)S(1)} %collective-permute-done.4.rest_2_), channel_id=1, source_target_pairs={{0,28},{1,29},{2,30},{3,31},{4,0},{5,1},{6,2},{7,3},{8,4},{9,5},{1... | collective-permute-start | bytes 835592 | tf_op jit(solution)/shard_map/ppermute | solution.py:324
  49.6 1.0 copy.17
  50.6 0.6 pad_add_fusion.place_ref
  51.3 2.8 %collective-permute-done.5.rest_3_ = bf16[4,136,256]{2,1,0:T(8,128)(2,1)S(1)} collective-permute-done((bf16[4,136,256]{2,1,0:T(8,128)(2,1)S(1)}, bf16[4,136,256]{2,1,0:T(8,128)(2,1)S(1)}, u32[]{:S(2)}, u32[]{:S(2)}) %collective-permute-start.5) | collective-permute-done | bytes 278560 | tf_op jit(solution)/shard_map/ppermute | solution.py:324
  54.1 0.8 broadcast_in_dim.9.taps_ref
  55.0 0.7 broadcast_in_dim.20.gain_ref
  55.7 2.4 %collective-permute-start.7 = (bf16[4,136,256]{2,1,0:T(8,128)(2,1)S(1)}, bf16[4,136,256]{2,1,0:T(8,128)(2,1)S(1)}, u32[]{:S(2)}, u32[]{:S(2)}) collective-permute-start(bf16[4,136,256]{2,1,0:T(8,128)(2,1)S(1)} %collective-permute-done.5.rest_3_), channel_id=1, source_target_pairs={{0,4},{1,5},{2,6},{3,7},{4,8},{5,9},{6,10},{7,11},{8,12},{9,13},{1... | collective-permute-start | bytes 835592 | tf_op jit(solution)/shard_map/ppermute | solution.py:324
  58.0 0.9 collective-permute-start.8
  58.9 6.7 %read_in.2.rest_0_ = bf16[20,128,128]{2,1,0:T(8,128)(2,1)} custom-call(bf16[16,256,128]{2,1,0:T(8,128)(2,1)} %all-gather.5.cloned.1.call-done.weight_hbm, bf16[4,136,256]{2,1,0:T(8,128)(2,1)} %copy-done.1, bf16[4,136,256]{2,1,0:T(8,128)(2,1)} %copy-done.5, bf16[4,136,256]{2,1,0:T(8,128)(2,1)} %copy-done.6, bf16[4,136,256]{2,1,0:T(8,128)(2,1)} %copy-done.7, ...), custom_call_target="tpu_custom_call" | custom-call | flops 536870912 | bytes 4194304 | tf_op jit(solution)/shard_map/read_in/pallas_call | solution.py:386
  65.7 1.2 collective-permute-start.9
  66.9 4.5 %filter_transform.1.filter_hbm = bf16[8,256,256]{2,1,0:T(8,128)(2,1)} custom-call(f32[64,4096]{1,0:T(8,128)} %filter_ref, bf16[512,256]{1,0:T(8,128)(2,1)} %constant.48.clone.first_ref.rest_3_, bf16[256,256]{1,0:T(8,128)(2,1)} %constant.49.clone.second_ref.rest_4_, f32[2,32,128]{2,1,0:T(8,128)} %constant.52.clone.twist_ref), custom_call_target="tpu_custom_call" | custom-call | flops 536870912 | bytes 4194304 | tf_op jit(solution)/shard_map/filter_transform/pallas_call | solution.py:406
  71.4 3.9 %read_in.3.rest_1_ = bf16[8,128,128]{2,1,0:T(8,128)(2,1)} custom-call(bf16[16,256,128]{2,1,0:T(8,128)(2,1)} %all-gather.5.cloned.1.call-done.weight_hbm, bf16[4,136,256]{2,1,0:T(8,128)(2,1)} %copy-done.10, bf16[4,136,256]{2,1,0:T(8,128)(2,1)} %copy-done.11), custom_call_target="tpu_custom_call" | custom-call | flops 536870912 | bytes 4194304 | tf_op jit(solution)/shard_map/read_in/pallas_call | solution.py:386
  75.3 7.9 %all-to-all-start.2 = ((bf16[32,64,128]{2,1,0:T(8,128)(2,1)}), bf16[32,64,128]{2,1,0:T(8,128)(2,1)S(1)}, u32[]{:S(2)}, u32[]{:S(2)}) async-start(bf16[32,64,128]{2,1,0:T(8,128)(2,1)} %bitcast.10), calls=%async_computation.2 | async-start | bytes 1048576 | tf_op jit(solution)/shard_map/all_to_all | solution.py:417
  83.5 8.3 %long_convolution.1 = (bf16[32,64,128]{2,1,0:T(8,128)(2,1)}, bf16[32,64,128]{2,1,0:T(8,128)(2,1)}, bf16[8,256,256]{2,1,0:T(8,128)(2,1)}) custom-call(s32[2]{0:T(128)} %pad_add_fusion.place_ref, f32[3,64,128]{2,1,0:T(8,128)} %broadcast_in_dim.9.taps_ref, f32[64,128]{1,0:T(8,128)} %broadcast_in_dim.20.gain_ref, f32[2,32,128]{2,1,0:T(8,128)} %constant.52.clone.twist_ref, ...), custom_call_target="tpu_custom_call" | custom-call | flops 2147483648 | bytes 8388608 | tf_op jit(solution)/shard_map/long_convolution/pallas_call | solution.py:420
  91.8 6.0 %all-to-all-done.2.grad_ref = bf16[32,64,128]{2,1,0:T(8,128)(2,1)S(1)} async-done(((bf16[32,64,128]{2,1,0:T(8,128)(2,1)}), bf16[32,64,128]{2,1,0:T(8,128)(2,1)S(1)}, u32[]{:S(2)}, u32[]{:S(2)}) %all-to-all-start.2) | async-done | bytes 524320 | tf_op jit(solution)/shard_map/all_to_all | solution.py:417
  97.9 0.8 copy-done.4
  98.7 4.9 %filter_gradient.1 = bf16[64,4096]{1,0:T(8,128)(2,1)} custom-call(bf16[32,64,128]{2,1,0:T(8,128)(2,1)} %copy-done.4, bf16[32,64,128]{2,1,0:T(8,128)(2,1)} %get-tuple-element.48.gate_ref, bf16[8,256,256]{2,1,0:T(8,128)(2,1)} %get-tuple-element.49.spectrum_ref, bf16[512,256]{1,0:T(8,128)(2,1)} %constant.48.clone.first_ref.rest_3_, ...), custom_call_target="tpu_custom_call" | custom-call | flops 1073741824 | bytes 4194304 | tf_op jit(solution)/shard_map/filter_gradient/pallas_call | solution.py:447
  103.6 17.0 %all_to_all.15.rows_hbm = bf16[8,4,64,128]{3,2,1,0:T(8,128)(2,1)} all-to-all(bf16[8,4,64,128]{3,2,1,0:T(8,128)(2,1)S(1)} %bitcast.20), channel_id=1, replica_groups={{0,4,8,12,16,20,24,28},{1,5,9,13,17,21,25,29},{2,6,10,14,18,22,26,30},{..., dimensions={0} | all-to-all | bytes 1048576 | tf_op jit(solution)/shard_map/all_to_all | solution.py:446
  120.6 6.3 %read_out.1 = bf16[4,128,256]{2,1,0:T(8,128)(2,1)} custom-call(s32[2]{0:T(128)} %pad_add_fusion.place_ref, bf16[8,4,64,128]{3,2,1,0:T(8,128)(2,1)} %all_to_all.15.rows_hbm, bf16[4,8,256]{2,1,0:T(8,128)(2,1)} %slice.4.marks_hbm, bf16[16,512,256]{2,1,0:T(8,128)(2,1)} %all-gather.7.cloned.1.call-done.weight_hbm), custom_call_target="tpu_custom_call" | custom-call | flops 2147483648 | bytes 6291456 | tf_op jit(solution)/shard_map/read_out/pallas_call | solution.py:476
  126.9 10.2 %all_to_all.16 = bf16[4,128,256]{2,1,0:T(8,128)(2,1)S(1)} all-to-all(bf16[4,128,256]{2,1,0:T(8,128)(2,1)} %read_out.1), channel_id=1, replica_groups={{0,1,2,3},{4,5,6,7},{8,9,10,11},{12,13,14,15},{16,17,18,19},{20,21,22,2..., dimensions={0} | all-to-all | bytes 524288 | tf_op jit(solution)/shard_map/all_to_all | solution.py:491
  137.2 0.7 reduce_sum.12
  137.8 3.4 %sum_gradients.1 = f32[64,4096]{1,0:T(8,128)} custom-call(bf16[8,64,4096]{2,1,0:T(8,128)(2,1)} %bitcast.16), custom_call_target="tpu_custom_call" | custom-call | flops 2097152 | bytes 5242880 | tf_op jit(solution)/shard_map/sum_gradients/pallas_call | solution.py:461
  (43 shorter events, 1.5 us)
Async XLA Ops:
  7.2 44.1 %copy-start = (f32[3,2048]{1,0:T(4,128)S(1)}, f32[3,2048]{1,0:T(4,128)}, u32[]{:S(2)}) copy-start(f32[3,2048]{1,0:T(4,128)} %param.18) | copy-start | bytes 73732
  7.2 42.4 %copy-start.2 = (bf16[1,128,2048]{2,1,0:T(8,128)(2,1)S(1)}, bf16[1,128,2048]{2,1,0:T(8,128)(2,1)}, u32[]{:S(2)}) copy-start(bf16[1,128,2048]{2,1,0:T(8,128)(2,1)} %param.22) | copy-start | bytes 1572868
  7.2 51.7 %all-gather.5.cloned.1.call-start = ((), (), s32[]{:S(2)}) async-start(), calls=%async_computation.3 | async-start | bytes 1179648 | tf_op jit(solution)/shard_map/all_gather | solution.py:368
  7.2 47.7 %copy-start.9 = (f32[64]{0:T(128)S(1)}, f32[64]{0:T(128)}, u32[]{:S(2)}) copy-start(f32[64]{0:T(128)} %param.20) | copy-start | bytes 772
  25.9 94.7 %all-gather.7.cloned.1.call-start = ((), (), s32[]{:S(2)}) async-start(), calls=%async_computation.4 | async-start | bytes 4718592 | tf_op jit(solution)/shard_map/all_gather | solution.py:371
  26.0 4.8 %collective-permute-start = (bf16[136,256]{1,0:T(8,128)(2,1)}, bf16[136,256]{1,0:T(8,128)(2,1)S(1)}, u32[]{:S(2)}, u32[]{:S(2)}) collective-permute-start(bf16[136,256]{1,0:T(8,128)(2,1)} %get-tuple-element.26), channel_id=1, source_target_pairs={{0,1},{1,2},{2,3},{3,0},{4,5},{5,6},{6,7},{7,4},{8,9},{9,10},{10,1... | collective-permute-start | bytes 208904 | tf_op jit(solution)/shard_map/ppermute | solution.py:320
  27.6 5.3 %collective-permute-start.1 = (bf16[136,256]{1,0:T(8,128)(2,1)}, bf16[136,256]{1,0:T(8,128)(2,1)S(1)}, u32[]{:S(2)}, u32[]{:S(2)}) collective-permute-start(bf16[136,256]{1,0:T(8,128)(2,1)} %get-tuple-element.26), channel_id=1, source_target_pairs={{0,3},{1,0},{2,1},{3,2},{4,7},{5,4},{6,5},{7,6},{8,11},{9,8},{10,9... | collective-permute-start | bytes 208904 | tf_op jit(solution)/shard_map/ppermute | solution.py:320
  28.3 6.0 %collective-permute-start.2 = (bf16[136,256]{1,0:T(8,128)(2,1)}, bf16[136,256]{1,0:T(8,128)(2,1)S(1)}, u32[]{:S(2)}, u32[]{:S(2)}) collective-permute-start(bf16[136,256]{1,0:T(8,128)(2,1)} %get-tuple-element.26), channel_id=1, source_target_pairs={{0,2},{1,3},{2,0},{3,1},{4,6},{5,7},{6,4},{7,5},{8,10},{9,11},{10,... | collective-permute-start | bytes 208904 | tf_op jit(solution)/shard_map/ppermute | solution.py:320
  35.3 23.7 %copy-start.1 = (bf16[4,136,256]{2,1,0:T(8,128)(2,1)}, bf16[4,136,256]{2,1,0:T(8,128)(2,1)S(1)}, u32[]{:S(2)}) copy-start(bf16[4,136,256]{2,1,0:T(8,128)(2,1)S(1)} %pad_maximum_fusion.rest_0_) | copy-start | bytes 835588
  35.3 11.0 %collective-permute-start.3 = (bf16[4,136,256]{2,1,0:T(8,128)(2,1)S(1)}, bf16[4,136,256]{2,1,0:T(8,128)(2,1)S(1)}, u32[]{:S(2)}, u32[]{:S(2)}) collective-permute-start(bf16[4,136,256]{2,1,0:T(8,128)(2,1)S(1)} %pad_maximum_fusion.rest_0_), channel_id=1, source_target_pairs={{0,4},{1,5},{2,6},{3,7},{4,8},{5,9},{6,10},{7,11},{8,12},{9,13},{1... | collective-permute-start | bytes 835592 | tf_op jit(solution)/shard_map/ppermute | solution.py:324
  37.0 9.3 %collective-permute-start.4 = (bf16[4,136,256]{2,1,0:T(8,128)(2,1)S(1)}, bf16[4,136,256]{2,1,0:T(8,128)(2,1)S(1)}, u32[]{:S(2)}, u32[]{:S(2)}) collective-permute-start(bf16[4,136,256]{2,1,0:T(8,128)(2,1)S(1)} %pad_maximum_fusion.rest_0_), channel_id=1, source_target_pairs={{0,28},{1,29},{2,30},{3,31},{4,0},{5,1},{6,2},{7,3},{8,4},{9,5},{1... | collective-permute-start | bytes 835592 | tf_op jit(solution)/shard_map/ppermute | solution.py:324
  46.3 12.7 %copy-start.5 = (bf16[4,136,256]{2,1,0:T(8,128)(2,1)}, bf16[4,136,256]{2,1,0:T(8,128)(2,1)S(1)}, u32[]{:S(2)}) copy-start(bf16[4,136,256]{2,1,0:T(8,128)(2,1)S(1)} %collective-permute-done.3.rest_1_) | copy-start | bytes 835588
  46.3 12.7 %copy-start.6 = (bf16[4,136,256]{2,1,0:T(8,128)(2,1)}, bf16[4,136,256]{2,1,0:T(8,128)(2,1)S(1)}, u32[]{:S(2)}) copy-start(bf16[4,136,256]{2,1,0:T(8,128)(2,1)S(1)} %collective-permute-done.4.rest_2_) | copy-start | bytes 835588
  46.3 7.8 %collective-permute-start.5 = (bf16[4,136,256]{2,1,0:T(8,128)(2,1)S(1)}, bf16[4,136,256]{2,1,0:T(8,128)(2,1)S(1)}, u32[]{:S(2)}, u32[]{:S(2)}) collective-permute-start(bf16[4,136,256]{2,1,0:T(8,128)(2,1)S(1)} %collective-permute-done.3.rest_1_), channel_id=1, source_target_pairs={{0,4},{1,5},{2,6},{3,7},{4,8},{5,9},{6,10},{7,11},{8,12},{9,13},{1... | collective-permute-start | bytes 835592 | tf_op jit(solution)/shard_map/ppermute | solution.py:324
  46.4 7.8 %collective-permute-start.6 = (bf16[4,136,256]{2,1,0:T(8,128)(2,1)S(1)}, bf16[4,136,256]{2,1,0:T(8,128)(2,1)S(1)}, u32[]{:S(2)}, u32[]{:S(2)}) collective-permute-start(bf16[4,136,256]{2,1,0:T(8,128)(2,1)S(1)} %collective-permute-done.4.rest_2_), channel_id=1, source_target_pairs={{0,28},{1,29},{2,30},{3,31},{4,0},{5,1},{6,2},{7,3},{8,4},{9,5},{1... | collective-permute-start | bytes 835592 | tf_op jit(solution)/shard_map/ppermute | solution.py:324
  54.1 4.8 %copy-start.7 = (bf16[4,136,256]{2,1,0:T(8,128)(2,1)}, bf16[4,136,256]{2,1,0:T(8,128)(2,1)S(1)}, u32[]{:S(2)}) copy-start(bf16[4,136,256]{2,1,0:T(8,128)(2,1)S(1)} %collective-permute-done.5.rest_3_) | copy-start | bytes 835588
  54.1 4.8 %copy-start.8 = (bf16[4,136,256]{2,1,0:T(8,128)(2,1)}, bf16[4,136,256]{2,1,0:T(8,128)(2,1)S(1)}, u32[]{:S(2)}) copy-start(bf16[4,136,256]{2,1,0:T(8,128)(2,1)S(1)} %collective-permute-done.6.rest_4_) | copy-start | bytes 835588
  55.7 10.0 %collective-permute-start.7 = (bf16[4,136,256]{2,1,0:T(8,128)(2,1)S(1)}, bf16[4,136,256]{2,1,0:T(8,128)(2,1)S(1)}, u32[]{:S(2)}, u32[]{:S(2)}) collective-permute-start(bf16[4,136,256]{2,1,0:T(8,128)(2,1)S(1)} %collective-permute-done.5.rest_3_), channel_id=1, source_target_pairs={{0,4},{1,5},{2,6},{3,7},{4,8},{5,9},{6,10},{7,11},{8,12},{9,13},{1... | collective-permute-start | bytes 835592 | tf_op jit(solution)/shard_map/ppermute | solution.py:324
  58.0 7.6 %collective-permute-start.8 = (bf16[4,136,256]{2,1,0:T(8,128)(2,1)S(1)}, bf16[4,136,256]{2,1,0:T(8,128)(2,1)S(1)}, u32[]{:S(2)}, u32[]{:S(2)}) collective-permute-start(bf16[4,136,256]{2,1,0:T(8,128)(2,1)S(1)} %collective-permute-done.6.rest_4_), channel_id=1, source_target_pairs={{0,28},{1,29},{2,30},{3,31},{4,0},{5,1},{6,2},{7,3},{8,4},{9,5},{1... | collective-permute-start | bytes 835592 | tf_op jit(solution)/shard_map/ppermute | solution.py:324
  65.6 5.7 %copy-start.10 = (bf16[4,136,256]{2,1,0:T(8,128)(2,1)}, bf16[4,136,256]{2,1,0:T(8,128)(2,1)S(1)}, u32[]{:S(2)}) copy-start(bf16[4,136,256]{2,1,0:T(8,128)(2,1)S(1)} %collective-permute-done.7.rest_0_) | copy-start | bytes 835588
  65.7 5.7 %copy-start.11 = (bf16[4,136,256]{2,1,0:T(8,128)(2,1)}, bf16[4,136,256]{2,1,0:T(8,128)(2,1)S(1)}, u32[]{:S(2)}) copy-start(bf16[4,136,256]{2,1,0:T(8,128)(2,1)S(1)} %collective-permute-done.8.rest_1_) | copy-start | bytes 835588
  65.7 9.6 %collective-permute-start.9 = (bf16[4,136,256]{2,1,0:T(8,128)(2,1)S(1)}, bf16[4,136,256]{2,1,0:T(8,128)(2,1)S(1)}, u32[]{:S(2)}, u32[]{:S(2)}) collective-permute-start(bf16[4,136,256]{2,1,0:T(8,128)(2,1)S(1)} %collective-permute-done.7.rest_0_), channel_id=1, source_target_pairs={{0,4},{1,5},{2,6},{3,7},{4,8},{5,9},{6,10},{7,11},{8,12},{9,13},{1... | collective-permute-start | bytes 835592 | tf_op jit(solution)/shard_map/ppermute | solution.py:324
  75.3 8.2 %copy-start.12 = (bf16[4,136,256]{2,1,0:T(8,128)(2,1)}, bf16[4,136,256]{2,1,0:T(8,128)(2,1)S(1)}, u32[]{:S(2)}) copy-start(bf16[4,136,256]{2,1,0:T(8,128)(2,1)S(1)} %collective-permute-done.9.rest_2_) | copy-start | bytes 835588
  75.3 22.5 %all-to-all-start.2 = ((bf16[32,64,128]{2,1,0:T(8,128)(2,1)}), bf16[32,64,128]{2,1,0:T(8,128)(2,1)S(1)}, u32[]{:S(2)}, u32[]{:S(2)}) async-start(bf16[32,64,128]{2,1,0:T(8,128)(2,1)} %bitcast.10), calls=%async_computation.2 | async-start | bytes 1048576 | tf_op jit(solution)/shard_map/all_to_all | solution.py:417
  83.3 54.6 %all-gather.9.cloned.1.call-start = ((), (), s32[]{:S(2)}) async-start(), calls=%async_computation.5 | async-start | bytes 4718592 | tf_op jit(solution)/shard_map/all_gather | solution.py:459
  91.8 11.8 %copy-start.3 = (bf16[32,64,128]{2,1,0:T(8,128)(2,1)S(1)}, bf16[32,64,128]{2,1,0:T(8,128)(2,1)}, u32[]{:S(2)}) copy-start(bf16[32,64,128]{2,1,0:T(8,128)(2,1)} %get-tuple-element.44) | copy-start | bytes 1572868
  97.9 0.8 copy-start.4
Sparse Core Ops, SparseCore 0:
  26.0 28.7 all-gather.4
  56.7 34.5 all-gather.6
  103.7 29.8 all-gather.8

commit v10 on v9

--- a/solution.py
+++ b/solution.py
@@ -287,7 +287,7 @@
     wait_all(stores)
 
 
-def prepare_kernel(place_ref, session_ref, slot_ref, spikes_ref, weight_hbm, out_hbm, block_ref, own_ref, own_out_hbm, value, gate, sems):
+def prepare_kernel(place_ref, session_ref, slot_ref, spikes_ref, weight_hbm, out_hbm, block_ref, own_ref, own_out_ref, value, gate, sems):
     place = place_ref[0]
     half = weight_hbm.shape[2] // 2
     window = pl.multiple_of(place // 2 * 2 * CHANS, 2 * CHANS)
@@ -296,7 +296,7 @@
         pltpu.make_async_copy(weight_hbm.at[:, :, pl.ds(half + window, 2 * CHANS)], gate, sems.at[1]),
     ]
     start_all(loads)
-    moved = pltpu.make_async_copy(out_hbm.at[:, :, lax.rem(place, Y)], own_out_hbm, sems.at[2])
+    moved = pltpu.make_async_copy(out_hbm.at[:, :, lax.rem(place, Y)], own_out_ref, sems.at[2])
     moved.start()
     trials = BLOCK // TRIAL
     width = block_ref.shape[1]
@@ -354,7 +354,7 @@
             jax.ShapeDtypeStruct((2, Z, CHANS, in_chans), bf16),
         ),
         in_specs=[scalar] * 3 + whole(1) + [hbm] * 2,
-        out_specs=tuple(whole(2)) + (hbm,),
+        out_specs=tuple(whole(3)),
         scratch_shapes=[pltpu.VMEM(own_shape, bf16), pltpu.VMEM(own_shape, bf16), pltpu.SemaphoreType.DMA((3,))],
         compiler_params=params,
         cost_estimate=pl.CostEstimate(flops=1 << 16, bytes_accessed=1 << 19, transcendentals=0),
@@ -400,7 +400,9 @@
         )(in_weights, *pieces)
 
     early = read_in(chunks)
-    right, left, early, long_filter = lax.optimization_barrier((right, left, early, long_filter))
+    ready = (right, left, early, long_filter, turned)
+    right, left, early, long_filter, turned = lax.optimization_barrier(ready)
+    grads = lax.all_to_all(turned, "seq", split_axis=0, concat_axis=0, tiled=True)
     last = along_z(right, 1)
     later = read_in([right, left])
     filter_spectrum = pl.pallas_call(
@@ -413,8 +415,7 @@
         cost_estimate=pl.CostEstimate(flops=work, bytes_accessed=4 << 20, transcendentals=0),
         name="filter_transform",
     )(long_filter, first, second, twists)
-    last, later, filter_spectrum, turned = lax.optimization_barrier((last, later, filter_spectrum, turned))
-    grads = lax.all_to_all(turned, "seq", split_axis=0, concat_axis=0, tiled=True)
+    last, later, filter_spectrum = lax.optimization_barrier((last, later, filter_spectrum))
 
     tables = (first, second, back_second, back_first)
     gated, gates, spectrum = pl.pallas_call(

time: 148 us -> 140 us (0.946)
  Pallas kernels: 56.6 us -> 40.9 us
  blocking collectives: 27.2 us -> 30.8 us
  waiting for transfers between devices: 17.5 us -> 19.6 us
    pallas_call x1, Pallas kernels: 18.6 us -> 3.03 us  [local(): pl.pallas_call(prepare_kernel, out_shape=(jax.ShapeDtypeStruct((BLOCK + B...]
    ppermute x7, waiting for transfers between devices: 7.47 us -> 15.5 us  [along_z(): lax.ppermute(value, 'seq', [(z * Y + y, (z + step) % Z * Y + y) for z in...]
    all_to_all x1, waiting for transfers between devices: 6.04 us -> 0.01 us  [local(): lax.all_to_all(turned, 'seq', split_axis=0, concat_axis=0, tiled=True)]
    all_to_all x1, blocking collectives: 17 us -> 21 us  [local(): lax.all_to_all(gated, 'seq', split_axis=0, concat_axis=0, tiled=True, axi...]
  transfers between devices with their start and end apart: 14 -> 14, of which waited for: 6 -> 6; matrix products, arithmetic and copies ran while one was open for 4% -> 4% of each run, Pallas kernels for 23% -> 25%
where the time goes in v10:
time: 140 us; the launch traced here: 139 us
  Pallas kernels  40.9 us (29%)
  blocking collectives  30.8 us (22%)
  starting transfers between devices  27 us (19%)
  waiting for transfers between devices  19.6 us (14%)
  between operations  14 us (10%)
  local copies, waits for them, and re-layouts  4.79 us (3%)
  other arithmetic  2.21 us (2%)
    all_to_all x1, blocking collectives, local(): lax.all_to_all(gated, 'seq', split_axis=0, concat_axis=0, tiled=True, axi...  21 us
    ppermute x7, waiting for transfers between devices, along_z(): lax.ppermute(value, 'seq', [(z * Y + y, (z + step) % Z * Y + y) for z in...  15.5 us
    ppermute x7, starting transfers between devices, along_z(): lax.ppermute(value, 'seq', [(z * Y + y, (z + step) % Z * Y + y) for z in...  14 us
    pallas_call x2, Pallas kernels, read_in(): pl.pallas_call(read_in_kernel, out_shape=jax.ShapeDtypeStruct((blocks, wi...  10.7 us
    all_to_all x1, blocking collectives, local(): lax.all_to_all(partial, 'seq', split_axis=0, concat_axis=0, tiled=True, a...  9.86 us
    all_to_all x1, starting transfers between devices, local(): lax.all_to_all(turned, 'seq', split_axis=0, concat_axis=0, tiled=True)  8.46 us
    pallas_call x1, Pallas kernels, local(): pl.pallas_call(forward_kernel, out_shape=(jax.ShapeDtypeStruct(plane, bf1...  8.19 us
    pallas_call x1, Pallas kernels, local(): pl.pallas_call(read_out_kernel, out_shape=jax.ShapeDtypeStruct((Y, BLOCK,...  6.34 us
  transfers between devices with their start and end apart: 14, of which 6 were waited for; matrix products, arithmetic and copies ran while one was open for 4% of the time, Pallas kernels for 25%

profile of v10, /device:TPU:8, one launch (start us, length us, event | category | flops | bytes accessed | tf_op | source)
XLA Modules:
  0.0 139.3 jit_solution(17453934669971516619)
XLA Ops:
  7.3 3.0 %prepare.1 = (bf16[136,256]{1,0:T(8,128)(2,1)}, bf16[2,256,128]{2,1,0:T(8,128)(2,1)}, bf16[2,8,64,256]{3,2,1,0:T(8,128)(2,1)}) custom-call(s32[1]{0:T(128)} %bitcast.place_ref, s32[1,128]{1,0:T(1,128)} %session_ref.1, s32[16]{0:T(128)} %slot_ref.1, bf16[1,128,256]{2,1,0:T(8,128)(2,1)} %spikes_ref.1, bf16[2,256,4096]{2,1,0:T(8,128)(2,1)} %weight_hbm.1, ...), custom_call_target="tpu_custom_call" | custom-call | flops 65536 | bytes 524288 | tf_op jit(solution)/shard_map/prepare/pallas_call | solution.py:349
  10.4 1.7 %collective-permute-start = (bf16[136,256]{1,0:T(8,128)(2,1)}, bf16[136,256]{1,0:T(8,128)(2,1)S(1)}, u32[]{:S(2)}, u32[]{:S(2)}) collective-permute-start(bf16[136,256]{1,0:T(8,128)(2,1)} %get-tuple-element.26), channel_id=1, source_target_pairs={{0,1},{1,2},{2,3},{3,0},{4,5},{5,6},{6,7},{7,4},{8,9},{9,10},{10,1... | collective-permute-start | bytes 208904 | tf_op jit(solution)/shard_map/ppermute | solution.py:320
  12.0 0.7 collective-permute-start.1
  12.7 2.0 %collective-permute-start.2 = (bf16[136,256]{1,0:T(8,128)(2,1)}, bf16[136,256]{1,0:T(8,128)(2,1)S(1)}, u32[]{:S(2)}, u32[]{:S(2)}) collective-permute-start(bf16[136,256]{1,0:T(8,128)(2,1)} %get-tuple-element.26), channel_id=1, source_target_pairs={{0,2},{1,3},{2,0},{3,1},{4,6},{5,7},{6,4},{7,5},{8,10},{9,11},{10,... | collective-permute-start | bytes 208904 | tf_op jit(solution)/shard_map/ppermute | solution.py:320
  15.1 2.2 %collective-permute-done.1 = bf16[136,256]{1,0:T(8,128)(2,1)S(1)} collective-permute-done((bf16[136,256]{1,0:T(8,128)(2,1)}, bf16[136,256]{1,0:T(8,128)(2,1)S(1)}, u32[]{:S(2)}, u32[]{:S(2)}) %collective-permute-start.1) | collective-permute-done | bytes 69664 | tf_op jit(solution)/shard_map/ppermute | solution.py:320
  17.3 1.5 %collective-permute-done.2 = bf16[136,256]{1,0:T(8,128)(2,1)S(1)} collective-permute-done((bf16[136,256]{1,0:T(8,128)(2,1)}, bf16[136,256]{1,0:T(8,128)(2,1)S(1)}, u32[]{:S(2)}, u32[]{:S(2)}) %collective-permute-start.2) | collective-permute-done | bytes 69664 | tf_op jit(solution)/shard_map/ppermute | solution.py:320
  18.7 0.9 pad_maximum_fusion.rest_0_
  19.7 1.7 %collective-permute-start.3 = (bf16[4,136,256]{2,1,0:T(8,128)(2,1)S(1)}, bf16[4,136,256]{2,1,0:T(8,128)(2,1)S(1)}, u32[]{:S(2)}, u32[]{:S(2)}) collective-permute-start(bf16[4,136,256]{2,1,0:T(8,128)(2,1)S(1)} %pad_maximum_fusion.rest_0_), channel_id=1, source_target_pairs={{0,4},{1,5},{2,6},{3,7},{4,8},{5,9},{6,10},{7,11},{8,12},{9,13},{1... | collective-permute-start | bytes 835592 | tf_op jit(solution)/shard_map/ppermute | solution.py:324
  21.4 4.0 %collective-permute-start.4 = (bf16[4,136,256]{2,1,0:T(8,128)(2,1)S(1)}, bf16[4,136,256]{2,1,0:T(8,128)(2,1)S(1)}, u32[]{:S(2)}, u32[]{:S(2)}) collective-permute-start(bf16[4,136,256]{2,1,0:T(8,128)(2,1)S(1)} %pad_maximum_fusion.rest_0_), channel_id=1, source_target_pairs={{0,28},{1,29},{2,30},{3,31},{4,0},{5,1},{6,2},{7,3},{8,4},{9,5},{1... | collective-permute-start | bytes 835592 | tf_op jit(solution)/shard_map/ppermute | solution.py:324
  26.0 4.6 %collective-permute-done.3.rest_1_ = bf16[4,136,256]{2,1,0:T(8,128)(2,1)S(1)} collective-permute-done((bf16[4,136,256]{2,1,0:T(8,128)(2,1)S(1)}, bf16[4,136,256]{2,1,0:T(8,128)(2,1)S(1)}, u32[]{:S(2)}, u32[]{:S(2)}) %collective-permute-start.3) | collective-permute-done | bytes 278560 | tf_op jit(solution)/shard_map/ppermute | solution.py:324
  30.8 3.2 %collective-permute-start.6 = (bf16[4,136,256]{2,1,0:T(8,128)(2,1)S(1)}, bf16[4,136,256]{2,1,0:T(8,128)(2,1)S(1)}, u32[]{:S(2)}, u32[]{:S(2)}) collective-permute-start(bf16[4,136,256]{2,1,0:T(8,128)(2,1)S(1)} %collective-permute-done.4.rest_2_), channel_id=1, source_target_pairs={{0,28},{1,29},{2,30},{3,31},{4,0},{5,1},{6,2},{7,3},{8,4},{9,5},{1... | collective-permute-start | bytes 835592 | tf_op jit(solution)/shard_map/ppermute | solution.py:324
  34.0 1.0 copy.17
  35.7 2.8 %collective-permute-done.5.rest_3_ = bf16[4,136,256]{2,1,0:T(8,128)(2,1)S(1)} collective-permute-done((bf16[4,136,256]{2,1,0:T(8,128)(2,1)S(1)}, bf16[4,136,256]{2,1,0:T(8,128)(2,1)S(1)}, u32[]{:S(2)}, u32[]{:S(2)}) %collective-permute-start.5) | collective-permute-done | bytes 278560 | tf_op jit(solution)/shard_map/ppermute | solution.py:324
  38.5 0.8 broadcast_in_dim.9.taps_ref
  39.4 0.7 broadcast_in_dim.20.gain_ref
  40.1 2.4 %collective-permute-start.7 = (bf16[4,136,256]{2,1,0:T(8,128)(2,1)S(1)}, bf16[4,136,256]{2,1,0:T(8,128)(2,1)S(1)}, u32[]{:S(2)}, u32[]{:S(2)}) collective-permute-start(bf16[4,136,256]{2,1,0:T(8,128)(2,1)S(1)} %collective-permute-done.5.rest_3_), channel_id=1, source_target_pairs={{0,4},{1,5},{2,6},{3,7},{4,8},{5,9},{6,10},{7,11},{8,12},{9,13},{1... | collective-permute-start | bytes 835592 | tf_op jit(solution)/shard_map/ppermute | solution.py:324
  42.4 0.9 collective-permute-start.8
  43.4 6.7 %read_in.2.rest_0_ = bf16[20,128,128]{2,1,0:T(8,128)(2,1)} custom-call(bf16[16,256,128]{2,1,0:T(8,128)(2,1)} %all-gather.5.cloned.1.call-done.weight_hbm, bf16[4,136,256]{2,1,0:T(8,128)(2,1)} %copy-done.1, bf16[4,136,256]{2,1,0:T(8,128)(2,1)} %copy-done.5, bf16[4,136,256]{2,1,0:T(8,128)(2,1)} %copy-done.6, bf16[4,136,256]{2,1,0:T(8,128)(2,1)} %copy-done.7, ...), custom_call_target="tpu_custom_call" | custom-call | flops 536870912 | bytes 4194304 | tf_op jit(solution)/shard_map/read_in/pallas_call | solution.py:386
  50.1 8.5 %all-to-all-start.2 = ((bf16[32,64,128]{2,1,0:T(8,128)(2,1)}), bf16[32,64,128]{2,1,0:T(8,128)(2,1)S(1)}, u32[]{:S(2)}, u32[]{:S(2)}) async-start(bf16[32,64,128]{2,1,0:T(8,128)(2,1)} %bitcast.10), calls=%async_computation.2 | async-start | bytes 1048576 | tf_op jit(solution)/shard_map/all_to_all | solution.py:405
  58.6 1.7 %collective-permute-start.9 = (bf16[4,136,256]{2,1,0:T(8,128)(2,1)S(1)}, bf16[4,136,256]{2,1,0:T(8,128)(2,1)S(1)}, u32[]{:S(2)}, u32[]{:S(2)}) collective-permute-start(bf16[4,136,256]{2,1,0:T(8,128)(2,1)S(1)} %collective-permute-done.7.rest_0_), channel_id=1, source_target_pairs={{0,4},{1,5},{2,6},{3,7},{4,8},{5,9},{6,10},{7,11},{8,12},{9,13},{1... | collective-permute-start | bytes 835592 | tf_op jit(solution)/shard_map/ppermute | solution.py:324
  60.3 4.4 %filter_transform.1.filter_hbm = bf16[8,256,256]{2,1,0:T(8,128)(2,1)} custom-call(f32[64,4096]{1,0:T(8,128)} %filter_ref, bf16[512,256]{1,0:T(8,128)(2,1)} %constant.48.clone.first_ref.rest_3_, bf16[256,256]{1,0:T(8,128)(2,1)} %constant.49.clone.second_ref.rest_4_, f32[2,32,128]{2,1,0:T(8,128)} %constant.52.clone.twist_ref), custom_call_target="tpu_custom_call" | custom-call | flops 536870912 | bytes 4194304 | tf_op jit(solution)/shard_map/filter_transform/pallas_call | solution.py:408
  64.7 4.0 %read_in.3.rest_1_ = bf16[8,128,128]{2,1,0:T(8,128)(2,1)} custom-call(bf16[16,256,128]{2,1,0:T(8,128)(2,1)} %all-gather.5.cloned.1.call-done.weight_hbm, bf16[4,136,256]{2,1,0:T(8,128)(2,1)} %copy-done.10, bf16[4,136,256]{2,1,0:T(8,128)(2,1)} %copy-done.11), custom_call_target="tpu_custom_call" | custom-call | flops 536870912 | bytes 4194304 | tf_op jit(solution)/shard_map/read_in/pallas_call | solution.py:386
  68.7 8.1 %collective-permute-done.9.rest_2_ = bf16[4,136,256]{2,1,0:T(8,128)(2,1)S(1)} collective-permute-done((bf16[4,136,256]{2,1,0:T(8,128)(2,1)S(1)}, bf16[4,136,256]{2,1,0:T(8,128)(2,1)S(1)}, u32[]{:S(2)}, u32[]{:S(2)}) %collective-permute-start.9) | collective-permute-done | bytes 278560 | tf_op jit(solution)/shard_map/ppermute | solution.py:324
  76.8 0.8 copy-done.12
  77.6 8.2 %long_convolution.1 = (bf16[32,64,128]{2,1,0:T(8,128)(2,1)}, bf16[32,64,128]{2,1,0:T(8,128)(2,1)}, bf16[8,256,256]{2,1,0:T(8,128)(2,1)}) custom-call(s32[2]{0:T(128)} %pad_add_fusion.place_ref, f32[3,64,128]{2,1,0:T(8,128)} %broadcast_in_dim.9.taps_ref, f32[64,128]{1,0:T(8,128)} %broadcast_in_dim.20.gain_ref, f32[2,32,128]{2,1,0:T(8,128)} %constant.52.clone.twist_ref, ...), custom_call_target="tpu_custom_call" | custom-call | flops 2147483648 | bytes 8388608 | tf_op jit(solution)/shard_map/long_convolution/pallas_call | solution.py:421
  85.8 0.8 copy-done.3
  86.6 4.9 %filter_gradient.1 = bf16[64,4096]{1,0:T(8,128)(2,1)} custom-call(bf16[32,64,128]{2,1,0:T(8,128)(2,1)} %copy-done.3, bf16[32,64,128]{2,1,0:T(8,128)(2,1)} %get-tuple-element.48.gate_ref, bf16[8,256,256]{2,1,0:T(8,128)(2,1)} %get-tuple-element.49.spectrum_ref, bf16[512,256]{1,0:T(8,128)(2,1)} %constant.48.clone.first_ref.rest_3_, ...), custom_call_target="tpu_custom_call" | custom-call | flops 1073741824 | bytes 4194304 | tf_op jit(solution)/shard_map/filter_gradient/pallas_call | solution.py:448
  91.5 21.0 %all_to_all.15.rows_hbm = bf16[8,4,64,128]{3,2,1,0:T(8,128)(2,1)} all-to-all(bf16[8,4,64,128]{3,2,1,0:T(8,128)(2,1)S(1)} %bitcast.20), channel_id=1, replica_groups={{0,4,8,12,16,20,24,28},{1,5,9,13,17,21,25,29},{2,6,10,14,18,22,26,30},{..., dimensions={0} | all-to-all | bytes 1048576 | tf_op jit(solution)/shard_map/all_to_all | solution.py:447
  112.5 6.3 %read_out.1 = bf16[4,128,256]{2,1,0:T(8,128)(2,1)} custom-call(s32[2]{0:T(128)} %pad_add_fusion.place_ref, bf16[8,4,64,128]{3,2,1,0:T(8,128)(2,1)} %all_to_all.15.rows_hbm, bf16[4,8,256]{2,1,0:T(8,128)(2,1)} %slice.4.marks_hbm, bf16[16,512,256]{2,1,0:T(8,128)(2,1)} %all-gather.7.cloned.1.call-done.weight_hbm), custom_call_target="tpu_custom_call" | custom-call | flops 2147483648 | bytes 6291456 | tf_op jit(solution)/shard_map/read_out/pallas_call | solution.py:477
  118.8 9.9 %all_to_all.16 = bf16[4,128,256]{2,1,0:T(8,128)(2,1)S(1)} all-to-all(bf16[4,128,256]{2,1,0:T(8,128)(2,1)} %read_out.1), channel_id=1, replica_groups={{0,1,2,3},{4,5,6,7},{8,9,10,11},{12,13,14,15},{16,17,18,19},{20,21,22,2..., dimensions={0} | all-to-all | bytes 524288 | tf_op jit(solution)/shard_map/all_to_all | solution.py:492
  128.7 0.7 reduce_sum.12
  129.3 3.4 %sum_gradients.1 = f32[64,4096]{1,0:T(8,128)} custom-call(bf16[8,64,4096]{2,1,0:T(8,128)(2,1)} %bitcast.16), custom_call_target="tpu_custom_call" | custom-call | flops 2097152 | bytes 5242880 | tf_op jit(solution)/shard_map/sum_gradients/pallas_call | solution.py:462
  (43 shorter events, 2.0 us)
Async XLA Ops:
  7.2 28.5 %copy-start = (f32[3,2048]{1,0:T(4,128)S(1)}, f32[3,2048]{1,0:T(4,128)}, u32[]{:S(2)}) copy-start(f32[3,2048]{1,0:T(4,128)} %param.18) | copy-start | bytes 73732
  7.2 26.8 %copy-start.2 = (bf16[1,128,2048]{2,1,0:T(8,128)(2,1)S(1)}, bf16[1,128,2048]{2,1,0:T(8,128)(2,1)}, u32[]{:S(2)}) copy-start(bf16[1,128,2048]{2,1,0:T(8,128)(2,1)} %param.22) | copy-start | bytes 1572868
  7.2 36.1 %all-gather.5.cloned.1.call-start = ((), (), s32[]{:S(2)}) async-start(), calls=%async_computation.3 | async-start | bytes 1179648 | tf_op jit(solution)/shard_map/all_gather | solution.py:368
  7.2 32.2 %copy-start.9 = (f32[64]{0:T(128)S(1)}, f32[64]{0:T(128)}, u32[]{:S(2)}) copy-start(f32[64]{0:T(128)} %param.20) | copy-start | bytes 772
  10.3 102.2 %all-gather.7.cloned.1.call-start = ((), (), s32[]{:S(2)}) async-start(), calls=%async_computation.4 | async-start | bytes 4718592 | tf_op jit(solution)/shard_map/all_gather | solution.py:371
  10.4 4.8 %collective-permute-start = (bf16[136,256]{1,0:T(8,128)(2,1)}, bf16[136,256]{1,0:T(8,128)(2,1)S(1)}, u32[]{:S(2)}, u32[]{:S(2)}) collective-permute-start(bf16[136,256]{1,0:T(8,128)(2,1)} %get-tuple-element.26), channel_id=1, source_target_pairs={{0,1},{1,2},{2,3},{3,0},{4,5},{5,6},{6,7},{7,4},{8,9},{9,10},{10,1... | collective-permute-start | bytes 208904 | tf_op jit(solution)/shard_map/ppermute | solution.py:320
  12.0 5.3 %collective-permute-start.1 = (bf16[136,256]{1,0:T(8,128)(2,1)}, bf16[136,256]{1,0:T(8,128)(2,1)S(1)}, u32[]{:S(2)}, u32[]{:S(2)}) collective-permute-start(bf16[136,256]{1,0:T(8,128)(2,1)} %get-tuple-element.26), channel_id=1, source_target_pairs={{0,3},{1,0},{2,1},{3,2},{4,7},{5,4},{6,5},{7,6},{8,11},{9,8},{10,9... | collective-permute-start | bytes 208904 | tf_op jit(solution)/shard_map/ppermute | solution.py:320
  12.7 6.0 %collective-permute-start.2 = (bf16[136,256]{1,0:T(8,128)(2,1)}, bf16[136,256]{1,0:T(8,128)(2,1)S(1)}, u32[]{:S(2)}, u32[]{:S(2)}) collective-permute-start(bf16[136,256]{1,0:T(8,128)(2,1)} %get-tuple-element.26), channel_id=1, source_target_pairs={{0,2},{1,3},{2,0},{3,1},{4,6},{5,7},{6,4},{7,5},{8,10},{9,11},{10,... | collective-permute-start | bytes 208904 | tf_op jit(solution)/shard_map/ppermute | solution.py:320
  19.7 23.7 %copy-start.1 = (bf16[4,136,256]{2,1,0:T(8,128)(2,1)}, bf16[4,136,256]{2,1,0:T(8,128)(2,1)S(1)}, u32[]{:S(2)}) copy-start(bf16[4,136,256]{2,1,0:T(8,128)(2,1)S(1)} %pad_maximum_fusion.rest_0_) | copy-start | bytes 835588
  19.7 11.0 %collective-permute-start.3 = (bf16[4,136,256]{2,1,0:T(8,128)(2,1)S(1)}, bf16[4,136,256]{2,1,0:T(8,128)(2,1)S(1)}, u32[]{:S(2)}, u32[]{:S(2)}) collective-permute-start(bf16[4,136,256]{2,1,0:T(8,128)(2,1)S(1)} %pad_maximum_fusion.rest_0_), channel_id=1, source_target_pairs={{0,4},{1,5},{2,6},{3,7},{4,8},{5,9},{6,10},{7,11},{8,12},{9,13},{1... | collective-permute-start | bytes 835592 | tf_op jit(solution)/shard_map/ppermute | solution.py:324
  21.4 9.3 %collective-permute-start.4 = (bf16[4,136,256]{2,1,0:T(8,128)(2,1)S(1)}, bf16[4,136,256]{2,1,0:T(8,128)(2,1)S(1)}, u32[]{:S(2)}, u32[]{:S(2)}) collective-permute-start(bf16[4,136,256]{2,1,0:T(8,128)(2,1)S(1)} %pad_maximum_fusion.rest_0_), channel_id=1, source_target_pairs={{0,28},{1,29},{2,30},{3,31},{4,0},{5,1},{6,2},{7,3},{8,4},{9,5},{1... | collective-permute-start | bytes 835592 | tf_op jit(solution)/shard_map/ppermute | solution.py:324
  30.7 12.7 %copy-start.5 = (bf16[4,136,256]{2,1,0:T(8,128)(2,1)}, bf16[4,136,256]{2,1,0:T(8,128)(2,1)S(1)}, u32[]{:S(2)}) copy-start(bf16[4,136,256]{2,1,0:T(8,128)(2,1)S(1)} %collective-permute-done.3.rest_1_) | copy-start | bytes 835588
  30.7 12.7 %copy-start.6 = (bf16[4,136,256]{2,1,0:T(8,128)(2,1)}, bf16[4,136,256]{2,1,0:T(8,128)(2,1)S(1)}, u32[]{:S(2)}) copy-start(bf16[4,136,256]{2,1,0:T(8,128)(2,1)S(1)} %collective-permute-done.4.rest_2_) | copy-start | bytes 835588
  30.7 7.8 %collective-permute-start.5 = (bf16[4,136,256]{2,1,0:T(8,128)(2,1)S(1)}, bf16[4,136,256]{2,1,0:T(8,128)(2,1)S(1)}, u32[]{:S(2)}, u32[]{:S(2)}) collective-permute-start(bf16[4,136,256]{2,1,0:T(8,128)(2,1)S(1)} %collective-permute-done.3.rest_1_), channel_id=1, source_target_pairs={{0,4},{1,5},{2,6},{3,7},{4,8},{5,9},{6,10},{7,11},{8,12},{9,13},{1... | collective-permute-start | bytes 835592 | tf_op jit(solution)/shard_map/ppermute | solution.py:324
  30.8 7.8 %collective-permute-start.6 = (bf16[4,136,256]{2,1,0:T(8,128)(2,1)S(1)}, bf16[4,136,256]{2,1,0:T(8,128)(2,1)S(1)}, u32[]{:S(2)}, u32[]{:S(2)}) collective-permute-start(bf16[4,136,256]{2,1,0:T(8,128)(2,1)S(1)} %collective-permute-done.4.rest_2_), channel_id=1, source_target_pairs={{0,28},{1,29},{2,30},{3,31},{4,0},{5,1},{6,2},{7,3},{8,4},{9,5},{1... | collective-permute-start | bytes 835592 | tf_op jit(solution)/shard_map/ppermute | solution.py:324
  38.5 4.8 %copy-start.7 = (bf16[4,136,256]{2,1,0:T(8,128)(2,1)}, bf16[4,136,256]{2,1,0:T(8,128)(2,1)S(1)}, u32[]{:S(2)}) copy-start(bf16[4,136,256]{2,1,0:T(8,128)(2,1)S(1)} %collective-permute-done.5.rest_3_) | copy-start | bytes 835588
  38.5 4.8 %copy-start.8 = (bf16[4,136,256]{2,1,0:T(8,128)(2,1)}, bf16[4,136,256]{2,1,0:T(8,128)(2,1)S(1)}, u32[]{:S(2)}) copy-start(bf16[4,136,256]{2,1,0:T(8,128)(2,1)S(1)} %collective-permute-done.6.rest_4_) | copy-start | bytes 835588
  40.1 9.9 %collective-permute-start.7 = (bf16[4,136,256]{2,1,0:T(8,128)(2,1)S(1)}, bf16[4,136,256]{2,1,0:T(8,128)(2,1)S(1)}, u32[]{:S(2)}, u32[]{:S(2)}) collective-permute-start(bf16[4,136,256]{2,1,0:T(8,128)(2,1)S(1)} %collective-permute-done.5.rest_3_), channel_id=1, source_target_pairs={{0,4},{1,5},{2,6},{3,7},{4,8},{5,9},{6,10},{7,11},{8,12},{9,13},{1... | collective-permute-start | bytes 835592 | tf_op jit(solution)/shard_map/ppermute | solution.py:324
  42.4 7.6 %collective-permute-start.8 = (bf16[4,136,256]{2,1,0:T(8,128)(2,1)S(1)}, bf16[4,136,256]{2,1,0:T(8,128)(2,1)S(1)}, u32[]{:S(2)}, u32[]{:S(2)}) collective-permute-start(bf16[4,136,256]{2,1,0:T(8,128)(2,1)S(1)} %collective-permute-done.6.rest_4_), channel_id=1, source_target_pairs={{0,28},{1,29},{2,30},{3,31},{4,0},{5,1},{6,2},{7,3},{8,4},{9,5},{1... | collective-permute-start | bytes 835592 | tf_op jit(solution)/shard_map/ppermute | solution.py:324
  50.0 14.7 %copy-start.10 = (bf16[4,136,256]{2,1,0:T(8,128)(2,1)}, bf16[4,136,256]{2,1,0:T(8,128)(2,1)S(1)}, u32[]{:S(2)}) copy-start(bf16[4,136,256]{2,1,0:T(8,128)(2,1)S(1)} %collective-permute-done.7.rest_0_) | copy-start | bytes 835588
  50.1 14.7 %copy-start.11 = (bf16[4,136,256]{2,1,0:T(8,128)(2,1)}, bf16[4,136,256]{2,1,0:T(8,128)(2,1)S(1)}, u32[]{:S(2)}) copy-start(bf16[4,136,256]{2,1,0:T(8,128)(2,1)S(1)} %collective-permute-done.8.rest_1_) | copy-start | bytes 835588
  50.1 35.7 %all-to-all-start.2 = ((bf16[32,64,128]{2,1,0:T(8,128)(2,1)}), bf16[32,64,128]{2,1,0:T(8,128)(2,1)S(1)}, u32[]{:S(2)}, u32[]{:S(2)}) async-start(bf16[32,64,128]{2,1,0:T(8,128)(2,1)} %bitcast.10), calls=%async_computation.2 | async-start | bytes 1048576 | tf_op jit(solution)/shard_map/all_to_all | solution.py:405
  58.5 70.8 %all-gather.9.cloned.1.call-start = ((), (), s32[]{:S(2)}) async-start(), calls=%async_computation.5 | async-start | bytes 4718592 | tf_op jit(solution)/shard_map/all_gather | solution.py:460
  58.6 18.2 %collective-permute-start.9 = (bf16[4,136,256]{2,1,0:T(8,128)(2,1)S(1)}, bf16[4,136,256]{2,1,0:T(8,128)(2,1)S(1)}, u32[]{:S(2)}, u32[]{:S(2)}) collective-permute-start(bf16[4,136,256]{2,1,0:T(8,128)(2,1)S(1)} %collective-permute-done.7.rest_0_), channel_id=1, source_target_pairs={{0,4},{1,5},{2,6},{3,7},{4,8},{5,9},{6,10},{7,11},{8,12},{9,13},{1... | collective-permute-start | bytes 835592 | tf_op jit(solution)/shard_map/ppermute | solution.py:324
  76.8 0.8 copy-start.12
  85.8 5.8 %copy-start.4 = (bf16[32,64,128]{2,1,0:T(8,128)(2,1)S(1)}, bf16[32,64,128]{2,1,0:T(8,128)(2,1)}, u32[]{:S(2)}) copy-start(bf16[32,64,128]{2,1,0:T(8,128)(2,1)} %get-tuple-element.44) | copy-start | bytes 1572868
  85.8 0.8 copy-start.3
Sparse Core Ops, SparseCore 0:
  10.4 28.7 all-gather.4
  41.1 34.5 all-gather.6
  91.6 31.8 all-gather.8

commit v11 on v10

--- a/solution.py
+++ b/solution.py
@@ -148,13 +148,11 @@
     lax.fori_loop(0, len(chunk_hbms), step, 0)
 
 
-def forward_kernel(place_ref, taps_ref, gain_ref, twist_ref, filter_hbm, weight_hbm, *rest):
-    early_hbms, (chunk_hbm, *rest) = rest[:2], rest[2:]
-    table_hbms, rest = rest[:4], rest[4:]
-    gated_hbm, gate_hbm, spectrum_hbm, both, rows, weight, spectra, gated_all, spectrum_all, *rest = rest
+def forward_kernel(place_ref, taps_ref, gain_ref, twist_ref, filter_hbm, *rest):
+    early_hbms, table_hbms, rest = rest[:2], rest[2:6], rest[6:]
+    gated_hbm, gate_hbm, spectrum_hbm, both, spectra, gated_all, spectrum_all, *rest = rest
     tables = rest[:4]
-    weight_sems, early_sems, sems, store_sems = rest[4:]
-    loads = weight_copies(weight_hbm, weight, weight_sems)
+    early_sems, sems, store_sems = rest[4:]
     others = []
     for early_hbm in early_hbms:
         for index in range(early_hbm.shape[0]):
@@ -163,13 +161,7 @@
             others.append(pltpu.make_async_copy(early_hbm.at[index], target, early_sems.at[number]))
     pairs = [(filter_hbm, spectra)] + list(zip(table_hbms, tables))
     others += [pltpu.make_async_copy(source, target, sems.at[index]) for index, (source, target) in enumerate(pairs)]
-    loads.append(pltpu.make_async_copy(chunk_hbm, rows, sems.at[len(pairs)]))
-    start_all(loads)
     start_all(others)
-    wait_all(loads)
-    last = project(rows, 0, Y, weight)
-    for y_index in range(Y):
-        both[block_of(place_ref, z_step_of(Z - 1), y_index)] = last[y_index]
     cosine, sine = twists_of(twist_ref)
     lane = lax.broadcasted_iota(jnp.int32, (BLOCKS, LANE8, BLOCK), 2)
     count = BLOCKS * LANE8
@@ -400,11 +392,8 @@
         )(in_weights, *pieces)
 
     early = read_in(chunks)
-    ready = (right, left, early, long_filter, turned)
-    right, left, early, long_filter, turned = lax.optimization_barrier(ready)
-    grads = lax.all_to_all(turned, "seq", split_axis=0, concat_axis=0, tiled=True)
+    right, left, early, long_filter = lax.optimization_barrier((right, left, early, long_filter))
     last = along_z(right, 1)
-    later = read_in([right, left])
     filter_spectrum = pl.pallas_call(
         filter_kernel,
         out_shape=spectrum_shape,
@@ -415,7 +404,10 @@
         cost_estimate=pl.CostEstimate(flops=work, bytes_accessed=4 << 20, transcendentals=0),
         name="filter_transform",
     )(long_filter, first, second, twists)
-    last, later, filter_spectrum = lax.optimization_barrier((last, later, filter_spectrum))
+    ready = (right, left, last, filter_spectrum, turned)
+    right, left, last, filter_spectrum, turned = lax.optimization_barrier(ready)
+    grads = lax.all_to_all(turned, "seq", split_axis=0, concat_axis=0, tiled=True)
+    later = read_in([right, left, last])
 
     tables = (first, second, back_second, back_first)
     gated, gates, spectrum = pl.pallas_call(
@@ -425,23 +417,21 @@
             jax.ShapeDtypeStruct(plane, bf16),
             spectrum_shape,
         ),
-        in_specs=[scalar] + whole(3) + [hbm] * (5 + 4),
+        in_specs=[scalar] + whole(3) + [hbm] * (3 + 4),
         out_specs=(hbm,) * 3,
         scratch_shapes=[
             pltpu.VMEM((BLOCKS, 2 * CHANS, BLOCK), bf16),
-            pltpu.VMEM(chunk.shape, bf16),
-            pltpu.VMEM((slot_count // 2, in_chans, 4 * CHANS), bf16),
             pltpu.VMEM(spectrum_shape.shape, bf16),
             pltpu.VMEM(plane, bf16),
             pltpu.VMEM(spectrum_shape.shape, bf16),
         ]
         + [pltpu.VMEM(table.shape, bf16) for table in tables]
-        + [pltpu.SemaphoreType.DMA((count,)) for count in (slot_count, (Z - 1) * Y, 6)]
+        + [pltpu.SemaphoreType.DMA((count,)) for count in (BLOCKS, 5)]
         + [pltpu.SemaphoreType.DMA((2, GROUPS // 2 + 1))],
         compiler_params=params,
         cost_estimate=pl.CostEstimate(flops=4 * work, bytes_accessed=8 << 20, transcendentals=0),
         name="long_convolution",
-    )(coords, taps, gains, twists, filter_spectrum, in_weights, early, later, last, *tables)
+    )(coords, taps, gains, twists, filter_spectrum, early, later, *tables)
 
     gated = gated.reshape(Z, Y, CHANS, BLOCK)
     arrived = lax.all_to_all(gated, "seq", split_axis=0, concat_axis=0, tiled=True, axis_index_groups=z_groups)

time: 140 us -> 133 us (0.950)
  waiting for transfers between devices: 19.6 us -> 15.1 us
  blocking collectives: 30.8 us -> 29 us
    ppermute x7, waiting for transfers between devices: 15.5 us -> 9.54 us  [along_z(): lax.ppermute(value, 'seq', [(z * Y + y, (z + step) % Z * Y + y) for z in...]
    all_to_all x1, blocking collectives: 21 us -> 19 us  [local(): lax.all_to_all(gated, 'seq', split_axis=0, concat_axis=0, tiled=True, axi...]
    all_to_all x1, waiting for transfers between devices: 0.01 us -> 1.5 us  [local(): lax.all_to_all(turned, 'seq', split_axis=0, concat_axis=0, tiled=True)]
  transfers between devices with their start and end apart: 14 -> 14, of which waited for: 6 -> 7; matrix products, arithmetic and copies ran while one was open for 4% -> 4% of each run, Pallas kernels for 25% -> 26%
where the time goes in v11:
time: 133 us; the launch traced here: 132 us
  Pallas kernels  40.7 us (31%)
  blocking collectives  29 us (22%)
  starting transfers between devices  26.7 us (20%)
  waiting for transfers between devices  15.1 us (11%)
  between operations  14 us (11%)
  local copies, waits for them, and re-layouts  4.08 us (3%)
  other arithmetic  2.21 us (2%)
    all_to_all x1, blocking collectives, local(): lax.all_to_all(gated, 'seq', split_axis=0, concat_axis=0, tiled=True, axi...  19 us
    ppermute x7, starting transfers between devices, along_z(): lax.ppermute(value, 'seq', [(z * Y + y, (z + step) % Z * Y + y) for z in...  13.6 us
    pallas_call x2, Pallas kernels, read_in(): pl.pallas_call(read_in_kernel, out_shape=jax.ShapeDtypeStruct((blocks, wi...  11.5 us
    all_to_all x1, blocking collectives, local(): lax.all_to_all(partial, 'seq', split_axis=0, concat_axis=0, tiled=True, a...  10 us
    ppermute x7, waiting for transfers between devices, along_z(): lax.ppermute(value, 'seq', [(z * Y + y, (z + step) % Z * Y + y) for z in...  9.54 us
    all_to_all x1, starting transfers between devices, local(): lax.all_to_all(turned, 'seq', split_axis=0, concat_axis=0, tiled=True)  8.45 us
    pallas_call x1, Pallas kernels, local(): pl.pallas_call(forward_kernel, out_shape=(jax.ShapeDtypeStruct(plane, bf1...  7.1 us
    pallas_call x1, Pallas kernels, local(): pl.pallas_call(read_out_kernel, out_shape=jax.ShapeDtypeStruct((Y, BLOCK,...  6.34 us
  transfers between devices with their start and end apart: 14, of which 7 were waited for; matrix products, arithmetic and copies ran while one was open for 4% of the time, Pallas kernels for 26%

profile of v11, /device:TPU:8, one launch (start us, length us, event | category | flops | bytes accessed | tf_op | source)
XLA Modules:
  0.0 131.8 jit_solution(2461558358258000453)
XLA Ops:
  7.3 3.0 %prepare.1 = (bf16[136,256]{1,0:T(8,128)(2,1)}, bf16[2,256,128]{2,1,0:T(8,128)(2,1)}, bf16[2,8,64,256]{3,2,1,0:T(8,128)(2,1)}) custom-call(s32[1]{0:T(128)} %bitcast.place_ref, s32[1,128]{1,0:T(1,128)} %session_ref.1, s32[16]{0:T(128)} %slot_ref.1, bf16[1,128,256]{2,1,0:T(8,128)(2,1)} %spikes_ref.1, bf16[2,256,4096]{2,1,0:T(8,128)(2,1)} %weight_hbm.1, ...), custom_call_target="tpu_custom_call" | custom-call | flops 65536 | bytes 524288 | tf_op jit(solution)/shard_map/prepare/pallas_call | solution.py:341
  10.4 1.7 %collective-permute-start = (bf16[136,256]{1,0:T(8,128)(2,1)}, bf16[136,256]{1,0:T(8,128)(2,1)S(1)}, u32[]{:S(2)}, u32[]{:S(2)}) collective-permute-start(bf16[136,256]{1,0:T(8,128)(2,1)} %get-tuple-element.27), channel_id=1, source_target_pairs={{0,1},{1,2},{2,3},{3,0},{4,5},{5,6},{6,7},{7,4},{8,9},{9,10},{10,1... | collective-permute-start | bytes 208904 | tf_op jit(solution)/shard_map/ppermute | solution.py:312
  12.0 0.7 collective-permute-start.1
  12.7 2.0 %collective-permute-start.2 = (bf16[136,256]{1,0:T(8,128)(2,1)}, bf16[136,256]{1,0:T(8,128)(2,1)S(1)}, u32[]{:S(2)}, u32[]{:S(2)}) collective-permute-start(bf16[136,256]{1,0:T(8,128)(2,1)} %get-tuple-element.27), channel_id=1, source_target_pairs={{0,2},{1,3},{2,0},{3,1},{4,6},{5,7},{6,4},{7,5},{8,10},{9,11},{10,... | collective-permute-start | bytes 208904 | tf_op jit(solution)/shard_map/ppermute | solution.py:312
  15.1 2.2 %collective-permute-done.1 = bf16[136,256]{1,0:T(8,128)(2,1)S(1)} collective-permute-done((bf16[136,256]{1,0:T(8,128)(2,1)}, bf16[136,256]{1,0:T(8,128)(2,1)S(1)}, u32[]{:S(2)}, u32[]{:S(2)}) %collective-permute-start.1) | collective-permute-done | bytes 69664 | tf_op jit(solution)/shard_map/ppermute | solution.py:312
  17.3 1.5 %collective-permute-done.2 = bf16[136,256]{1,0:T(8,128)(2,1)S(1)} collective-permute-done((bf16[136,256]{1,0:T(8,128)(2,1)}, bf16[136,256]{1,0:T(8,128)(2,1)S(1)}, u32[]{:S(2)}, u32[]{:S(2)}) %collective-permute-start.2) | collective-permute-done | bytes 69664 | tf_op jit(solution)/shard_map/ppermute | solution.py:312
  18.7 0.9 pad_maximum_fusion.rest_0_
  19.7 1.7 %collective-permute-start.3 = (bf16[4,136,256]{2,1,0:T(8,128)(2,1)S(1)}, bf16[4,136,256]{2,1,0:T(8,128)(2,1)S(1)}, u32[]{:S(2)}, u32[]{:S(2)}) collective-permute-start(bf16[4,136,256]{2,1,0:T(8,128)(2,1)S(1)} %pad_maximum_fusion.rest_0_), channel_id=1, source_target_pairs={{0,4},{1,5},{2,6},{3,7},{4,8},{5,9},{6,10},{7,11},{8,12},{9,13},{1... | collective-permute-start | bytes 835592 | tf_op jit(solution)/shard_map/ppermute | solution.py:316
  21.4 4.0 %collective-permute-start.4 = (bf16[4,136,256]{2,1,0:T(8,128)(2,1)S(1)}, bf16[4,136,256]{2,1,0:T(8,128)(2,1)S(1)}, u32[]{:S(2)}, u32[]{:S(2)}) collective-permute-start(bf16[4,136,256]{2,1,0:T(8,128)(2,1)S(1)} %pad_maximum_fusion.rest_0_), channel_id=1, source_target_pairs={{0,28},{1,29},{2,30},{3,31},{4,0},{5,1},{6,2},{7,3},{8,4},{9,5},{1... | collective-permute-start | bytes 835592 | tf_op jit(solution)/shard_map/ppermute | solution.py:316
  26.0 4.6 %collective-permute-done.3.rest_1_ = bf16[4,136,256]{2,1,0:T(8,128)(2,1)S(1)} collective-permute-done((bf16[4,136,256]{2,1,0:T(8,128)(2,1)S(1)}, bf16[4,136,256]{2,1,0:T(8,128)(2,1)S(1)}, u32[]{:S(2)}, u32[]{:S(2)}) %collective-permute-start.3) | collective-permute-done | bytes 278560 | tf_op jit(solution)/shard_map/ppermute | solution.py:316
  30.8 3.2 %collective-permute-start.6 = (bf16[4,136,256]{2,1,0:T(8,128)(2,1)S(1)}, bf16[4,136,256]{2,1,0:T(8,128)(2,1)S(1)}, u32[]{:S(2)}, u32[]{:S(2)}) collective-permute-start(bf16[4,136,256]{2,1,0:T(8,128)(2,1)S(1)} %collective-permute-done.4.rest_2_), channel_id=1, source_target_pairs={{0,28},{1,29},{2,30},{3,31},{4,0},{5,1},{6,2},{7,3},{8,4},{9,5},{1... | collective-permute-start | bytes 835592 | tf_op jit(solution)/shard_map/ppermute | solution.py:316
  34.0 1.0 copy.17
  35.7 2.8 %collective-permute-done.5.rest_3_ = bf16[4,136,256]{2,1,0:T(8,128)(2,1)S(1)} collective-permute-done((bf16[4,136,256]{2,1,0:T(8,128)(2,1)S(1)}, bf16[4,136,256]{2,1,0:T(8,128)(2,1)S(1)}, u32[]{:S(2)}, u32[]{:S(2)}) %collective-permute-start.5) | collective-permute-done | bytes 278560 | tf_op jit(solution)/shard_map/ppermute | solution.py:316
  38.5 0.8 broadcast_in_dim.9.taps_ref
  39.4 0.7 broadcast_in_dim.20.gain_ref
  40.1 2.4 %collective-permute-start.7 = (bf16[4,136,256]{2,1,0:T(8,128)(2,1)S(1)}, bf16[4,136,256]{2,1,0:T(8,128)(2,1)S(1)}, u32[]{:S(2)}, u32[]{:S(2)}) collective-permute-start(bf16[4,136,256]{2,1,0:T(8,128)(2,1)S(1)} %collective-permute-done.5.rest_3_), channel_id=1, source_target_pairs={{0,4},{1,5},{2,6},{3,7},{4,8},{5,9},{6,10},{7,11},{8,12},{9,13},{1... | collective-permute-start | bytes 835592 | tf_op jit(solution)/shard_map/ppermute | solution.py:316
  42.5 0.9 collective-permute-start.8
  43.4 6.7 %read_in.2.rest_0_ = bf16[20,128,128]{2,1,0:T(8,128)(2,1)} custom-call(bf16[16,256,128]{2,1,0:T(8,128)(2,1)} %all-gather.5.cloned.1.call-done.weight_hbm, bf16[4,136,256]{2,1,0:T(8,128)(2,1)} %copy-done.1, bf16[4,136,256]{2,1,0:T(8,128)(2,1)} %copy-done.5, bf16[4,136,256]{2,1,0:T(8,128)(2,1)} %copy-done.6, bf16[4,136,256]{2,1,0:T(8,128)(2,1)} %copy-done.7, ...), custom_call_target="tpu_custom_call" | custom-call | flops 536870912 | bytes 4194304 | tf_op jit(solution)/shard_map/read_in/pallas_call | solution.py:378
  50.1 1.2 collective-permute-start.9
  51.3 4.5 %filter_transform.1.filter_hbm = bf16[8,256,256]{2,1,0:T(8,128)(2,1)} custom-call(f32[64,4096]{1,0:T(8,128)} %filter_ref, bf16[512,256]{1,0:T(8,128)(2,1)} %constant.48.clone.first_ref.rest_2_, bf16[256,256]{1,0:T(8,128)(2,1)} %constant.49.clone.second_ref.rest_3_, f32[2,32,128]{2,1,0:T(8,128)} %constant.52.clone.twist_ref), custom_call_target="tpu_custom_call" | custom-call | flops 536870912 | bytes 4194304 | tf_op jit(solution)/shard_map/filter_transform/pallas_call | solution.py:397
  55.8 2.1 %collective-permute-done.9.rest_2_ = bf16[4,136,256]{2,1,0:T(8,128)(2,1)S(1)} collective-permute-done((bf16[4,136,256]{2,1,0:T(8,128)(2,1)S(1)}, bf16[4,136,256]{2,1,0:T(8,128)(2,1)S(1)}, u32[]{:S(2)}, u32[]{:S(2)}) %collective-permute-start.9) | collective-permute-done | bytes 278560 | tf_op jit(solution)/shard_map/ppermute | solution.py:316
  57.9 8.5 %all-to-all-start.2 = ((bf16[32,64,128]{2,1,0:T(8,128)(2,1)}), bf16[32,64,128]{2,1,0:T(8,128)(2,1)S(1)}, u32[]{:S(2)}, u32[]{:S(2)}) async-start(bf16[32,64,128]{2,1,0:T(8,128)(2,1)} %bitcast.10), calls=%async_computation.2 | async-start | bytes 1048576 | tf_op jit(solution)/shard_map/all_to_all | solution.py:409
  66.6 4.8 %read_in.3.rest_1_ = bf16[12,128,128]{2,1,0:T(8,128)(2,1)} custom-call(bf16[16,256,128]{2,1,0:T(8,128)(2,1)} %all-gather.5.cloned.1.call-done.weight_hbm, bf16[4,136,256]{2,1,0:T(8,128)(2,1)} %copy-done.9, bf16[4,136,256]{2,1,0:T(8,128)(2,1)} %copy-done.10, bf16[4,136,256]{2,1,0:T(8,128)(2,1)} %copy-done.11), custom_call_target="tpu_custom_call" | custom-call | flops 536870912 | bytes 4194304 | tf_op jit(solution)/shard_map/read_in/pallas_call | solution.py:378
  71.5 7.1 %long_convolution.1 = (bf16[32,64,128]{2,1,0:T(8,128)(2,1)}, bf16[32,64,128]{2,1,0:T(8,128)(2,1)}, bf16[8,256,256]{2,1,0:T(8,128)(2,1)}) custom-call(s32[2]{0:T(128)} %pad_add_fusion.place_ref, f32[3,64,128]{2,1,0:T(8,128)} %broadcast_in_dim.9.taps_ref, f32[64,128]{1,0:T(8,128)} %broadcast_in_dim.20.gain_ref, f32[2,32,128]{2,1,0:T(8,128)} %constant.52.clone.twist_ref, ...), custom_call_target="tpu_custom_call" | custom-call | flops 2147483648 | bytes 8388608 | tf_op jit(solution)/shard_map/long_convolution/pallas_call | solution.py:413
  78.6 1.5 %all-to-all-done.2.grad_ref = bf16[32,64,128]{2,1,0:T(8,128)(2,1)S(1)} async-done(((bf16[32,64,128]{2,1,0:T(8,128)(2,1)}), bf16[32,64,128]{2,1,0:T(8,128)(2,1)S(1)}, u32[]{:S(2)}, u32[]{:S(2)}) %all-to-all-start.2) | async-done | bytes 524320 | tf_op jit(solution)/shard_map/all_to_all | solution.py:409
  80.1 0.8 copy-done.3
  80.9 4.9 %filter_gradient.1 = bf16[64,4096]{1,0:T(8,128)(2,1)} custom-call(bf16[32,64,128]{2,1,0:T(8,128)(2,1)} %copy-done.3, bf16[32,64,128]{2,1,0:T(8,128)(2,1)} %get-tuple-element.50.gate_ref, bf16[8,256,256]{2,1,0:T(8,128)(2,1)} %get-tuple-element.51.spectrum_ref, bf16[512,256]{1,0:T(8,128)(2,1)} %constant.48.clone.first_ref.rest_2_, ...), custom_call_target="tpu_custom_call" | custom-call | flops 1073741824 | bytes 4194304 | tf_op jit(solution)/shard_map/filter_gradient/pallas_call | solution.py:438
  85.8 19.0 %all_to_all.15.rows_hbm = bf16[8,4,64,128]{3,2,1,0:T(8,128)(2,1)} all-to-all(bf16[8,4,64,128]{3,2,1,0:T(8,128)(2,1)S(1)} %bitcast.20), channel_id=1, replica_groups={{0,4,8,12,16,20,24,28},{1,5,9,13,17,21,25,29},{2,6,10,14,18,22,26,30},{..., dimensions={0} | all-to-all | bytes 1048576 | tf_op jit(solution)/shard_map/all_to_all | solution.py:437
  104.8 6.3 %read_out.1 = bf16[4,128,256]{2,1,0:T(8,128)(2,1)} custom-call(s32[2]{0:T(128)} %pad_add_fusion.place_ref, bf16[8,4,64,128]{3,2,1,0:T(8,128)(2,1)} %all_to_all.15.rows_hbm, bf16[4,8,256]{2,1,0:T(8,128)(2,1)} %slice.4.marks_hbm, bf16[16,512,256]{2,1,0:T(8,128)(2,1)} %all-gather.7.cloned.1.call-done.weight_hbm), custom_call_target="tpu_custom_call" | custom-call | flops 2147483648 | bytes 6291456 | tf_op jit(solution)/shard_map/read_out/pallas_call | solution.py:467
  111.2 10.0 %all_to_all.16 = bf16[4,128,256]{2,1,0:T(8,128)(2,1)S(1)} all-to-all(bf16[4,128,256]{2,1,0:T(8,128)(2,1)} %read_out.1), channel_id=1, replica_groups={{0,1,2,3},{4,5,6,7},{8,9,10,11},{12,13,14,15},{16,17,18,19},{20,21,22,2..., dimensions={0} | all-to-all | bytes 524288 | tf_op jit(solution)/shard_map/all_to_all | solution.py:482
  121.2 0.7 reduce_sum.12
  121.8 3.4 %sum_gradients.1 = f32[64,4096]{1,0:T(8,128)} custom-call(bf16[8,64,4096]{2,1,0:T(8,128)(2,1)} %bitcast.16), custom_call_target="tpu_custom_call" | custom-call | flops 2097152 | bytes 5242880 | tf_op jit(solution)/shard_map/sum_gradients/pallas_call | solution.py:452
  (43 shorter events, 2.2 us)
Async XLA Ops:
  7.2 28.5 %copy-start = (f32[3,2048]{1,0:T(4,128)S(1)}, f32[3,2048]{1,0:T(4,128)}, u32[]{:S(2)}) copy-start(f32[3,2048]{1,0:T(4,128)} %param.18) | copy-start | bytes 73732
  7.2 26.8 %copy-start.2 = (bf16[1,128,2048]{2,1,0:T(8,128)(2,1)S(1)}, bf16[1,128,2048]{2,1,0:T(8,128)(2,1)}, u32[]{:S(2)}) copy-start(bf16[1,128,2048]{2,1,0:T(8,128)(2,1)} %param.22) | copy-start | bytes 1572868
  7.2 36.1 %all-gather.5.cloned.1.call-start = ((), (), s32[]{:S(2)}) async-start(), calls=%async_computation.3 | async-start | bytes 1179648 | tf_op jit(solution)/shard_map/all_gather | solution.py:360
  7.2 32.2 %copy-start.12 = (f32[64]{0:T(128)S(1)}, f32[64]{0:T(128)}, u32[]{:S(2)}) copy-start(f32[64]{0:T(128)} %param.20) | copy-start | bytes 772
  10.3 94.5 %all-gather.7.cloned.1.call-start = ((), (), s32[]{:S(2)}) async-start(), calls=%async_computation.4 | async-start | bytes 4718592 | tf_op jit(solution)/shard_map/all_gather | solution.py:363
  10.4 4.8 %collective-permute-start = (bf16[136,256]{1,0:T(8,128)(2,1)}, bf16[136,256]{1,0:T(8,128)(2,1)S(1)}, u32[]{:S(2)}, u32[]{:S(2)}) collective-permute-start(bf16[136,256]{1,0:T(8,128)(2,1)} %get-tuple-element.27), channel_id=1, source_target_pairs={{0,1},{1,2},{2,3},{3,0},{4,5},{5,6},{6,7},{7,4},{8,9},{9,10},{10,1... | collective-permute-start | bytes 208904 | tf_op jit(solution)/shard_map/ppermute | solution.py:312
  12.0 5.3 %collective-permute-start.1 = (bf16[136,256]{1,0:T(8,128)(2,1)}, bf16[136,256]{1,0:T(8,128)(2,1)S(1)}, u32[]{:S(2)}, u32[]{:S(2)}) collective-permute-start(bf16[136,256]{1,0:T(8,128)(2,1)} %get-tuple-element.27), channel_id=1, source_target_pairs={{0,3},{1,0},{2,1},{3,2},{4,7},{5,4},{6,5},{7,6},{8,11},{9,8},{10,9... | collective-permute-start | bytes 208904 | tf_op jit(solution)/shard_map/ppermute | solution.py:312
  12.7 6.0 %collective-permute-start.2 = (bf16[136,256]{1,0:T(8,128)(2,1)}, bf16[136,256]{1,0:T(8,128)(2,1)S(1)}, u32[]{:S(2)}, u32[]{:S(2)}) collective-permute-start(bf16[136,256]{1,0:T(8,128)(2,1)} %get-tuple-element.27), channel_id=1, source_target_pairs={{0,2},{1,3},{2,0},{3,1},{4,6},{5,7},{6,4},{7,5},{8,10},{9,11},{10,... | collective-permute-start | bytes 208904 | tf_op jit(solution)/shard_map/ppermute | solution.py:312
  19.7 23.7 %copy-start.1 = (bf16[4,136,256]{2,1,0:T(8,128)(2,1)}, bf16[4,136,256]{2,1,0:T(8,128)(2,1)S(1)}, u32[]{:S(2)}) copy-start(bf16[4,136,256]{2,1,0:T(8,128)(2,1)S(1)} %pad_maximum_fusion.rest_0_) | copy-start | bytes 835588
  19.7 11.0 %collective-permute-start.3 = (bf16[4,136,256]{2,1,0:T(8,128)(2,1)S(1)}, bf16[4,136,256]{2,1,0:T(8,128)(2,1)S(1)}, u32[]{:S(2)}, u32[]{:S(2)}) collective-permute-start(bf16[4,136,256]{2,1,0:T(8,128)(2,1)S(1)} %pad_maximum_fusion.rest_0_), channel_id=1, source_target_pairs={{0,4},{1,5},{2,6},{3,7},{4,8},{5,9},{6,10},{7,11},{8,12},{9,13},{1... | collective-permute-start | bytes 835592 | tf_op jit(solution)/shard_map/ppermute | solution.py:316
  21.4 9.3 %collective-permute-start.4 = (bf16[4,136,256]{2,1,0:T(8,128)(2,1)S(1)}, bf16[4,136,256]{2,1,0:T(8,128)(2,1)S(1)}, u32[]{:S(2)}, u32[]{:S(2)}) collective-permute-start(bf16[4,136,256]{2,1,0:T(8,128)(2,1)S(1)} %pad_maximum_fusion.rest_0_), channel_id=1, source_target_pairs={{0,28},{1,29},{2,30},{3,31},{4,0},{5,1},{6,2},{7,3},{8,4},{9,5},{1... | collective-permute-start | bytes 835592 | tf_op jit(solution)/shard_map/ppermute | solution.py:316
  30.7 12.7 %copy-start.5 = (bf16[4,136,256]{2,1,0:T(8,128)(2,1)}, bf16[4,136,256]{2,1,0:T(8,128)(2,1)S(1)}, u32[]{:S(2)}) copy-start(bf16[4,136,256]{2,1,0:T(8,128)(2,1)S(1)} %collective-permute-done.3.rest_1_) | copy-start | bytes 835588
  30.7 12.7 %copy-start.6 = (bf16[4,136,256]{2,1,0:T(8,128)(2,1)}, bf16[4,136,256]{2,1,0:T(8,128)(2,1)S(1)}, u32[]{:S(2)}) copy-start(bf16[4,136,256]{2,1,0:T(8,128)(2,1)S(1)} %collective-permute-done.4.rest_2_) | copy-start | bytes 835588
  30.7 7.8 %collective-permute-start.5 = (bf16[4,136,256]{2,1,0:T(8,128)(2,1)S(1)}, bf16[4,136,256]{2,1,0:T(8,128)(2,1)S(1)}, u32[]{:S(2)}, u32[]{:S(2)}) collective-permute-start(bf16[4,136,256]{2,1,0:T(8,128)(2,1)S(1)} %collective-permute-done.3.rest_1_), channel_id=1, source_target_pairs={{0,4},{1,5},{2,6},{3,7},{4,8},{5,9},{6,10},{7,11},{8,12},{9,13},{1... | collective-permute-start | bytes 835592 | tf_op jit(solution)/shard_map/ppermute | solution.py:316
  30.8 7.8 %collective-permute-start.6 = (bf16[4,136,256]{2,1,0:T(8,128)(2,1)S(1)}, bf16[4,136,256]{2,1,0:T(8,128)(2,1)S(1)}, u32[]{:S(2)}, u32[]{:S(2)}) collective-permute-start(bf16[4,136,256]{2,1,0:T(8,128)(2,1)S(1)} %collective-permute-done.4.rest_2_), channel_id=1, source_target_pairs={{0,28},{1,29},{2,30},{3,31},{4,0},{5,1},{6,2},{7,3},{8,4},{9,5},{1... | collective-permute-start | bytes 835592 | tf_op jit(solution)/shard_map/ppermute | solution.py:316
  38.5 4.8 %copy-start.7 = (bf16[4,136,256]{2,1,0:T(8,128)(2,1)}, bf16[4,136,256]{2,1,0:T(8,128)(2,1)S(1)}, u32[]{:S(2)}) copy-start(bf16[4,136,256]{2,1,0:T(8,128)(2,1)S(1)} %collective-permute-done.5.rest_3_) | copy-start | bytes 835588
  38.5 4.8 %copy-start.8 = (bf16[4,136,256]{2,1,0:T(8,128)(2,1)}, bf16[4,136,256]{2,1,0:T(8,128)(2,1)S(1)}, u32[]{:S(2)}) copy-start(bf16[4,136,256]{2,1,0:T(8,128)(2,1)S(1)} %collective-permute-done.6.rest_4_) | copy-start | bytes 835588
  40.1 9.9 %collective-permute-start.7 = (bf16[4,136,256]{2,1,0:T(8,128)(2,1)S(1)}, bf16[4,136,256]{2,1,0:T(8,128)(2,1)S(1)}, u32[]{:S(2)}, u32[]{:S(2)}) collective-permute-start(bf16[4,136,256]{2,1,0:T(8,128)(2,1)S(1)} %collective-permute-done.5.rest_3_), channel_id=1, source_target_pairs={{0,4},{1,5},{2,6},{3,7},{4,8},{5,9},{6,10},{7,11},{8,12},{9,13},{1... | collective-permute-start | bytes 835592 | tf_op jit(solution)/shard_map/ppermute | solution.py:316
  42.5 7.6 %collective-permute-start.8 = (bf16[4,136,256]{2,1,0:T(8,128)(2,1)S(1)}, bf16[4,136,256]{2,1,0:T(8,128)(2,1)S(1)}, u32[]{:S(2)}, u32[]{:S(2)}) collective-permute-start(bf16[4,136,256]{2,1,0:T(8,128)(2,1)S(1)} %collective-permute-done.6.rest_4_), channel_id=1, source_target_pairs={{0,28},{1,29},{2,30},{3,31},{4,0},{5,1},{6,2},{7,3},{8,4},{9,5},{1... | collective-permute-start | bytes 835592 | tf_op jit(solution)/shard_map/ppermute | solution.py:316
  50.0 16.6 %copy-start.9 = (bf16[4,136,256]{2,1,0:T(8,128)(2,1)}, bf16[4,136,256]{2,1,0:T(8,128)(2,1)S(1)}, u32[]{:S(2)}) copy-start(bf16[4,136,256]{2,1,0:T(8,128)(2,1)S(1)} %collective-permute-done.7.rest_0_) | copy-start | bytes 835588
  50.1 16.6 %copy-start.10 = (bf16[4,136,256]{2,1,0:T(8,128)(2,1)}, bf16[4,136,256]{2,1,0:T(8,128)(2,1)S(1)}, u32[]{:S(2)}) copy-start(bf16[4,136,256]{2,1,0:T(8,128)(2,1)S(1)} %collective-permute-done.8.rest_1_) | copy-start | bytes 835588
  50.1 7.8 %collective-permute-start.9 = (bf16[4,136,256]{2,1,0:T(8,128)(2,1)S(1)}, bf16[4,136,256]{2,1,0:T(8,128)(2,1)S(1)}, u32[]{:S(2)}, u32[]{:S(2)}) collective-permute-start(bf16[4,136,256]{2,1,0:T(8,128)(2,1)S(1)} %collective-permute-done.7.rest_0_), channel_id=1, source_target_pairs={{0,4},{1,5},{2,6},{3,7},{4,8},{5,9},{6,10},{7,11},{8,12},{9,13},{1... | collective-permute-start | bytes 835592 | tf_op jit(solution)/shard_map/ppermute | solution.py:316
  57.9 8.7 %copy-start.11 = (bf16[4,136,256]{2,1,0:T(8,128)(2,1)}, bf16[4,136,256]{2,1,0:T(8,128)(2,1)S(1)}, u32[]{:S(2)}) copy-start(bf16[4,136,256]{2,1,0:T(8,128)(2,1)S(1)} %collective-permute-done.9.rest_2_) | copy-start | bytes 835588
  57.9 22.2 %all-to-all-start.2 = ((bf16[32,64,128]{2,1,0:T(8,128)(2,1)}), bf16[32,64,128]{2,1,0:T(8,128)(2,1)S(1)}, u32[]{:S(2)}, u32[]{:S(2)}) async-start(bf16[32,64,128]{2,1,0:T(8,128)(2,1)} %bitcast.10), calls=%async_computation.2 | async-start | bytes 1048576 | tf_op jit(solution)/shard_map/all_to_all | solution.py:409
  66.4 55.5 %all-gather.9.cloned.1.call-start = ((), (), s32[]{:S(2)}) async-start(), calls=%async_computation.5 | async-start | bytes 4718592 | tf_op jit(solution)/shard_map/all_gather | solution.py:450
  78.6 7.2 %copy-start.4 = (bf16[32,64,128]{2,1,0:T(8,128)(2,1)S(1)}, bf16[32,64,128]{2,1,0:T(8,128)(2,1)}, u32[]{:S(2)}) copy-start(bf16[32,64,128]{2,1,0:T(8,128)(2,1)} %get-tuple-element.46) | copy-start | bytes 1572868
  80.1 0.8 copy-start.3
Sparse Core Ops, SparseCore 0:
  10.4 28.7 all-gather.4
  41.1 34.5 all-gather.6
  85.9 34.1 all-gather.8

commit v12 on v11

--- a/solution.py
+++ b/solution.py
@@ -149,7 +149,7 @@
 
 
 def forward_kernel(place_ref, taps_ref, gain_ref, twist_ref, filter_hbm, *rest):
-    early_hbms, table_hbms, rest = rest[:2], rest[2:6], rest[6:]
+    early_hbms, table_hbms, rest = rest[:3], rest[3:7], rest[7:]
     gated_hbm, gate_hbm, spectrum_hbm, both, spectra, gated_all, spectrum_all, *rest = rest
     tables = rest[:4]
     early_sems, sems, store_sems = rest[4:]
@@ -358,7 +358,18 @@
     chunks = [chunk, right, left]
 
     in_weights = lax.all_gather(own_weights, "grp", axis=0, tiled=True)
-    right, left, own_marks, own_out = lax.optimization_barrier((right, left, own_marks, own_out))
+    filter_spectrum = pl.pallas_call(
+        filter_kernel,
+        out_shape=spectrum_shape,
+        grid=(GROUPS // 2,),
+        in_specs=[pl.BlockSpec((pair, LENGTH), lambda i: (i, 0))] + [same(table) for table in (first, second, twists)],
+        out_specs=pl.BlockSpec((2,) + spectrum_shape.shape[1:], lambda i: (i, 0, 0)),
+        compiler_params=params,
+        cost_estimate=pl.CostEstimate(flops=work, bytes_accessed=4 << 20, transcendentals=0),
+        name="filter_transform",
+    )(long_filter, first, second, twists)
+    ready = (right, left, own_marks, own_out, filter_spectrum)
+    right, left, own_marks, own_out, filter_spectrum = lax.optimization_barrier(ready)
     split = own_out.reshape(2, Z * CHANS, in_chans)
     out_weights = lax.all_gather(split, "grp", axis=0, tiled=True)
     right, left = along_z(right, 1), along_z(left, -1)
@@ -391,21 +402,11 @@
             name="read_in",
         )(in_weights, *pieces)
 
-    early = read_in(chunks)
-    right, left, early, long_filter = lax.optimization_barrier((right, left, early, long_filter))
+    early = read_in(chunks[:3])
+    right, left, early, *chunks = lax.optimization_barrier((right, left, early, *chunks))
     last = along_z(right, 1)
-    filter_spectrum = pl.pallas_call(
-        filter_kernel,
-        out_shape=spectrum_shape,
-        grid=(GROUPS // 2,),
-        in_specs=[pl.BlockSpec((pair, LENGTH), lambda i: (i, 0))] + [same(table) for table in (first, second, twists)],
-        out_specs=pl.BlockSpec((2,) + spectrum_shape.shape[1:], lambda i: (i, 0, 0)),
-        compiler_params=params,
-        cost_estimate=pl.CostEstimate(flops=work, bytes_accessed=4 << 20, transcendentals=0),
-        name="filter_transform",
-    )(long_filter, first, second, twists)
-    ready = (right, left, last, filter_spectrum, turned)
-    right, left, last, filter_spectrum, turned = lax.optimization_barrier(ready)
+    middle = read_in(chunks[3:])
+    right, left, last, middle, turned = lax.optimization_barrier((right, left, last, middle, turned))
     grads = lax.all_to_all(turned, "seq", split_axis=0, concat_axis=0, tiled=True)
     later = read_in([right, left, last])
 
@@ -417,7 +418,7 @@
             jax.ShapeDtypeStruct(plane, bf16),
             spectrum_shape,
         ),
-        in_specs=[scalar] + whole(3) + [hbm] * (3 + 4),
+        in_specs=[scalar] + whole(3) + [hbm] * (4 + 4),
         out_specs=(hbm,) * 3,
         scratch_shapes=[
             pltpu.VMEM((BLOCKS, 2 * CHANS, BLOCK), bf16),
@@ -431,7 +432,7 @@
         compiler_params=params,
         cost_estimate=pl.CostEstimate(flops=4 * work, bytes_accessed=8 << 20, transcendentals=0),
         name="long_convolution",
-    )(coords, taps, gains, twists, filter_spectrum, early, later, *tables)
+    )(coords, taps, gains, twists, filter_spectrum, early, middle, later, *tables)
 
     gated = gated.reshape(Z, Y, CHANS, BLOCK)
     arrived = lax.all_to_all(gated, "seq", split_axis=0, concat_axis=0, tiled=True, axis_index_groups=z_groups)

time: 133 us -> 131 us (0.985)
  waiting for transfers between devices: 15.1 us -> 10.7 us
  Pallas kernels: 40.7 us -> 42.8 us
    ppermute x7, waiting for transfers between devices: 9.54 us -> 5.53 us  [along_z(): lax.ppermute(value, 'seq', [(z * Y + y, (z + step) % Z * Y + y) for z in...]
    pallas_call x2 -> x3, Pallas kernels: 11.5 us -> 13.6 us  [read_in(): pl.pallas_call(read_in_kernel, out_shape=jax.ShapeDtypeStruct((blocks, wi...]
  transfers between devices with their start and end apart: 14 -> 14, of which waited for: 7 -> 8; matrix products, arithmetic and copies ran while one was open for 4% -> 4% of each run, Pallas kernels for 26% -> 28%
where the time goes in v12:
time: 131 us; the launch traced here: 130 us
  Pallas kernels  42.8 us (33%)
  blocking collectives  29 us (22%)
  starting transfers between devices  27.1 us (21%)
  between operations  13.9 us (11%)
  waiting for transfers between devices  10.7 us (8%)
  local copies, waits for them, and re-layouts  4.05 us (3%)
  other arithmetic  2.21 us (2%)
    all_to_all x1, blocking collectives, local(): lax.all_to_all(gated, 'seq', split_axis=0, concat_axis=0, tiled=True, axi...  18.9 us
    ppermute x7, starting transfers between devices, along_z(): lax.ppermute(value, 'seq', [(z * Y + y, (z + step) % Z * Y + y) for z in...  14.3 us
    pallas_call x3, Pallas kernels, read_in(): pl.pallas_call(read_in_kernel, out_shape=jax.ShapeDtypeStruct((blocks, wi...  13.6 us
    all_to_all x1, blocking collectives, local(): lax.all_to_all(partial, 'seq', split_axis=0, concat_axis=0, tiled=True, a...  10 us
    all_to_all x1, starting transfers between devices, local(): lax.all_to_all(turned, 'seq', split_axis=0, concat_axis=0, tiled=True)  8.09 us
    pallas_call x1, Pallas kernels, local(): pl.pallas_call(forward_kernel, out_shape=(jax.ShapeDtypeStruct(plane, bf1...  7.06 us
    pallas_call x1, Pallas kernels, local(): pl.pallas_call(read_out_kernel, out_shape=jax.ShapeDtypeStruct((Y, BLOCK,...  6.34 us
    ppermute x7, waiting for transfers between devices, along_z(): lax.ppermute(value, 'seq', [(z * Y + y, (z + step) % Z * Y + y) for z in...  5.53 us
  transfers between devices with their start and end apart: 14, of which 8 were waited for; matrix products, arithmetic and copies ran while one was open for 4% of the time, Pallas kernels for 28%

profile of v12, /device:TPU:8, one launch (start us, length us, event | category | flops | bytes accessed | tf_op | source)
XLA Modules:
  0.0 129.9 jit_solution(2571109194332913762)
XLA Ops:
  7.3 3.0 %prepare.1 = (bf16[136,256]{1,0:T(8,128)(2,1)}, bf16[2,256,128]{2,1,0:T(8,128)(2,1)}, bf16[2,8,64,256]{3,2,1,0:T(8,128)(2,1)}) custom-call(s32[1]{0:T(128)} %bitcast.place_ref, s32[1,128]{1,0:T(1,128)} %session_ref.1, s32[16]{0:T(128)} %slot_ref.1, bf16[1,128,256]{2,1,0:T(8,128)(2,1)} %spikes_ref.1, bf16[2,256,4096]{2,1,0:T(8,128)(2,1)} %weight_hbm.1, ...), custom_call_target="tpu_custom_call" | custom-call | flops 65536 | bytes 524288 | tf_op jit(solution)/shard_map/prepare/pallas_call | solution.py:341
  10.4 1.7 %collective-permute-start = (bf16[136,256]{1,0:T(8,128)(2,1)}, bf16[136,256]{1,0:T(8,128)(2,1)S(1)}, u32[]{:S(2)}, u32[]{:S(2)}) collective-permute-start(bf16[136,256]{1,0:T(8,128)(2,1)} %get-tuple-element.29), channel_id=1, source_target_pairs={{0,1},{1,2},{2,3},{3,0},{4,5},{5,6},{6,7},{7,4},{8,9},{9,10},{10,1... | collective-permute-start | bytes 208904 | tf_op jit(solution)/shard_map/ppermute | solution.py:312
  12.0 0.7 collective-permute-start.1
  12.7 2.0 %collective-permute-start.2 = (bf16[136,256]{1,0:T(8,128)(2,1)}, bf16[136,256]{1,0:T(8,128)(2,1)S(1)}, u32[]{:S(2)}, u32[]{:S(2)}) collective-permute-start(bf16[136,256]{1,0:T(8,128)(2,1)} %get-tuple-element.29), channel_id=1, source_target_pairs={{0,2},{1,3},{2,0},{3,1},{4,6},{5,7},{6,4},{7,5},{8,10},{9,11},{10,... | collective-permute-start | bytes 208904 | tf_op jit(solution)/shard_map/ppermute | solution.py:312
  15.1 2.2 %collective-permute-done.1 = bf16[136,256]{1,0:T(8,128)(2,1)S(1)} collective-permute-done((bf16[136,256]{1,0:T(8,128)(2,1)}, bf16[136,256]{1,0:T(8,128)(2,1)S(1)}, u32[]{:S(2)}, u32[]{:S(2)}) %collective-permute-start.1) | collective-permute-done | bytes 69664 | tf_op jit(solution)/shard_map/ppermute | solution.py:312
  17.3 1.5 %collective-permute-done.2 = bf16[136,256]{1,0:T(8,128)(2,1)S(1)} collective-permute-done((bf16[136,256]{1,0:T(8,128)(2,1)}, bf16[136,256]{1,0:T(8,128)(2,1)S(1)}, u32[]{:S(2)}, u32[]{:S(2)}) %collective-permute-start.2) | collective-permute-done | bytes 69664 | tf_op jit(solution)/shard_map/ppermute | solution.py:312
  18.7 0.9 pad_maximum_fusion.rest_0_
  19.7 1.7 %collective-permute-start.3 = (bf16[4,136,256]{2,1,0:T(8,128)(2,1)S(1)}, bf16[4,136,256]{2,1,0:T(8,128)(2,1)S(1)}, u32[]{:S(2)}, u32[]{:S(2)}) collective-permute-start(bf16[4,136,256]{2,1,0:T(8,128)(2,1)S(1)} %pad_maximum_fusion.rest_0_), channel_id=1, source_target_pairs={{0,4},{1,5},{2,6},{3,7},{4,8},{5,9},{6,10},{7,11},{8,12},{9,13},{1... | collective-permute-start | bytes 835592 | tf_op jit(solution)/shard_map/ppermute | solution.py:316
  21.4 4.0 %collective-permute-start.4 = (bf16[4,136,256]{2,1,0:T(8,128)(2,1)S(1)}, bf16[4,136,256]{2,1,0:T(8,128)(2,1)S(1)}, u32[]{:S(2)}, u32[]{:S(2)}) collective-permute-start(bf16[4,136,256]{2,1,0:T(8,128)(2,1)S(1)} %pad_maximum_fusion.rest_0_), channel_id=1, source_target_pairs={{0,28},{1,29},{2,30},{3,31},{4,0},{5,1},{6,2},{7,3},{8,4},{9,5},{1... | collective-permute-start | bytes 835592 | tf_op jit(solution)/shard_map/ppermute | solution.py:316
  25.5 4.5 %filter_transform.1.filter_hbm = bf16[8,256,256]{2,1,0:T(8,128)(2,1)} custom-call(f32[64,4096]{1,0:T(8,128)} %filter_ref.1, bf16[512,256]{1,0:T(8,128)(2,1)} %constant.48.clone.first_ref.rest_3_, bf16[256,256]{1,0:T(8,128)(2,1)} %constant.49.clone.second_ref.rest_4_, f32[2,32,128]{2,1,0:T(8,128)} %constant.52.clone.twist_ref), custom_call_target="tpu_custom_call" | custom-call | flops 536870912 | bytes 4194304 | tf_op jit(solution)/shard_map/filter_transform/pallas_call | solution.py:361
  30.8 3.2 %collective-permute-start.6 = (bf16[4,136,256]{2,1,0:T(8,128)(2,1)S(1)}, bf16[4,136,256]{2,1,0:T(8,128)(2,1)S(1)}, u32[]{:S(2)}, u32[]{:S(2)}) collective-permute-start(bf16[4,136,256]{2,1,0:T(8,128)(2,1)S(1)} %collective-permute-done.4.rest_2_), channel_id=1, source_target_pairs={{0,28},{1,29},{2,30},{3,31},{4,0},{5,1},{6,2},{7,3},{8,4},{9,5},{1... | collective-permute-start | bytes 835592 | tf_op jit(solution)/shard_map/ppermute | solution.py:316
  34.0 1.0 copy.17
  35.7 2.9 %collective-permute-done.5.rest_0_ = bf16[4,136,256]{2,1,0:T(8,128)(2,1)S(1)} collective-permute-done((bf16[4,136,256]{2,1,0:T(8,128)(2,1)S(1)}, bf16[4,136,256]{2,1,0:T(8,128)(2,1)S(1)}, u32[]{:S(2)}, u32[]{:S(2)}) %collective-permute-start.5) | collective-permute-done | bytes 278560 | tf_op jit(solution)/shard_map/ppermute | solution.py:316
  38.6 0.8 broadcast_in_dim.9.taps_ref
  39.4 0.7 broadcast_in_dim.20.gain_ref
  40.1 2.3 %collective-permute-start.7 = (bf16[4,136,256]{2,1,0:T(8,128)(2,1)S(1)}, bf16[4,136,256]{2,1,0:T(8,128)(2,1)S(1)}, u32[]{:S(2)}, u32[]{:S(2)}) collective-permute-start(bf16[4,136,256]{2,1,0:T(8,128)(2,1)S(1)} %collective-permute-done.5.rest_0_), channel_id=1, source_target_pairs={{0,4},{1,5},{2,6},{3,7},{4,8},{5,9},{6,10},{7,11},{8,12},{9,13},{1... | collective-permute-start | bytes 835592 | tf_op jit(solution)/shard_map/ppermute | solution.py:316
  42.4 0.9 collective-permute-start.8
  43.4 4.8 %read_in.3.rest_0_ = bf16[12,128,128]{2,1,0:T(8,128)(2,1)} custom-call(bf16[16,256,128]{2,1,0:T(8,128)(2,1)} %all-gather.5.cloned.1.call-done.weight_hbm, bf16[4,136,256]{2,1,0:T(8,128)(2,1)} %copy-done.1, bf16[4,136,256]{2,1,0:T(8,128)(2,1)} %copy-done.5, bf16[4,136,256]{2,1,0:T(8,128)(2,1)} %copy-done.6), custom_call_target="tpu_custom_call" | custom-call | flops 536870912 | bytes 4194304 | tf_op jit(solution)/shard_map/read_in/pallas_call | solution.py:389
  48.2 0.8 collective-permute-done.8.rest_1_
  49.0 2.0 %collective-permute-start.9 = (bf16[4,136,256]{2,1,0:T(8,128)(2,1)S(1)}, bf16[4,136,256]{2,1,0:T(8,128)(2,1)S(1)}, u32[]{:S(2)}, u32[]{:S(2)}) collective-permute-start(bf16[4,136,256]{2,1,0:T(8,128)(2,1)S(1)} %collective-permute-done.7.rest_0_), channel_id=1, source_target_pairs={{0,4},{1,5},{2,6},{3,7},{4,8},{5,9},{6,10},{7,11},{8,12},{9,13},{1... | collective-permute-start | bytes 835592 | tf_op jit(solution)/shard_map/ppermute | solution.py:316
  51.0 3.9 %read_in.4.rest_1_ = bf16[8,128,128]{2,1,0:T(8,128)(2,1)} custom-call(bf16[16,256,128]{2,1,0:T(8,128)(2,1)} %all-gather.5.cloned.1.call-done.weight_hbm, bf16[4,136,256]{2,1,0:T(8,128)(2,1)} %copy-done.11, bf16[4,136,256]{2,1,0:T(8,128)(2,1)} %copy-done.12), custom_call_target="tpu_custom_call" | custom-call | flops 536870912 | bytes 4194304 | tf_op jit(solution)/shard_map/read_in/pallas_call | solution.py:389
  55.0 1.8 %collective-permute-done.9.rest_2_ = bf16[4,136,256]{2,1,0:T(8,128)(2,1)S(1)} collective-permute-done((bf16[4,136,256]{2,1,0:T(8,128)(2,1)S(1)}, bf16[4,136,256]{2,1,0:T(8,128)(2,1)S(1)}, u32[]{:S(2)}, u32[]{:S(2)}) %collective-permute-start.9) | collective-permute-done | bytes 278560 | tf_op jit(solution)/shard_map/ppermute | solution.py:316
  56.8 8.1 %all-to-all-start.2 = ((bf16[32,64,128]{2,1,0:T(8,128)(2,1)}), bf16[32,64,128]{2,1,0:T(8,128)(2,1)S(1)}, u32[]{:S(2)}, u32[]{:S(2)}) async-start(bf16[32,64,128]{2,1,0:T(8,128)(2,1)} %bitcast.10), calls=%async_computation.2 | async-start | bytes 1048576 | tf_op jit(solution)/shard_map/all_to_all | solution.py:410
  65.1 4.9 %read_in.5.rest_2_ = bf16[12,128,128]{2,1,0:T(8,128)(2,1)} custom-call(bf16[16,256,128]{2,1,0:T(8,128)(2,1)} %all-gather.5.cloned.1.call-done.weight_hbm, bf16[4,136,256]{2,1,0:T(8,128)(2,1)} %copy-done.7, bf16[4,136,256]{2,1,0:T(8,128)(2,1)} %copy-done.8, bf16[4,136,256]{2,1,0:T(8,128)(2,1)} %copy-done.9), custom_call_target="tpu_custom_call" | custom-call | flops 536870912 | bytes 4194304 | tf_op jit(solution)/shard_map/read_in/pallas_call | solution.py:389
  70.0 7.1 %long_convolution.1 = (bf16[32,64,128]{2,1,0:T(8,128)(2,1)}, bf16[32,64,128]{2,1,0:T(8,128)(2,1)}, bf16[8,256,256]{2,1,0:T(8,128)(2,1)}) custom-call(s32[2]{0:T(128)} %pad_add_fusion.place_ref, f32[3,64,128]{2,1,0:T(8,128)} %broadcast_in_dim.9.taps_ref, f32[64,128]{1,0:T(8,128)} %broadcast_in_dim.20.gain_ref, f32[2,32,128]{2,1,0:T(8,128)} %constant.52.clone.twist_ref, ...), custom_call_target="tpu_custom_call" | custom-call | flops 2147483648 | bytes 8388608 | tf_op jit(solution)/shard_map/long_convolution/pallas_call | solution.py:414
  77.1 1.2 all-to-all-done.2.grad_ref
  78.2 0.8 copy-done.3
  79.0 4.9 %filter_gradient.1 = bf16[64,4096]{1,0:T(8,128)(2,1)} custom-call(bf16[32,64,128]{2,1,0:T(8,128)(2,1)} %copy-done.3, bf16[32,64,128]{2,1,0:T(8,128)(2,1)} %get-tuple-element.54.gate_ref, bf16[8,256,256]{2,1,0:T(8,128)(2,1)} %get-tuple-element.55.spectrum_ref, bf16[512,256]{1,0:T(8,128)(2,1)} %constant.48.clone.first_ref.rest_3_, ...), custom_call_target="tpu_custom_call" | custom-call | flops 1073741824 | bytes 4194304 | tf_op jit(solution)/shard_map/filter_gradient/pallas_call | solution.py:439
  84.0 18.9 %all_to_all.15.rows_hbm = bf16[8,4,64,128]{3,2,1,0:T(8,128)(2,1)} all-to-all(bf16[8,4,64,128]{3,2,1,0:T(8,128)(2,1)S(1)} %bitcast.20), channel_id=1, replica_groups={{0,4,8,12,16,20,24,28},{1,5,9,13,17,21,25,29},{2,6,10,14,18,22,26,30},{..., dimensions={0} | all-to-all | bytes 1048576 | tf_op jit(solution)/shard_map/all_to_all | solution.py:438
  102.9 6.3 %read_out.1 = bf16[4,128,256]{2,1,0:T(8,128)(2,1)} custom-call(s32[2]{0:T(128)} %pad_add_fusion.place_ref, bf16[8,4,64,128]{3,2,1,0:T(8,128)(2,1)} %all_to_all.15.rows_hbm, bf16[4,8,256]{2,1,0:T(8,128)(2,1)} %slice.4.marks_hbm, bf16[16,512,256]{2,1,0:T(8,128)(2,1)} %all-gather.7.cloned.1.call-done.weight_hbm), custom_call_target="tpu_custom_call" | custom-call | flops 2147483648 | bytes 6291456 | tf_op jit(solution)/shard_map/read_out/pallas_call | solution.py:468
  109.2 10.0 %all_to_all.16 = bf16[4,128,256]{2,1,0:T(8,128)(2,1)S(1)} all-to-all(bf16[4,128,256]{2,1,0:T(8,128)(2,1)} %read_out.1), channel_id=1, replica_groups={{0,1,2,3},{4,5,6,7},{8,9,10,11},{12,13,14,15},{16,17,18,19},{20,21,22,2..., dimensions={0} | all-to-all | bytes 524288 | tf_op jit(solution)/shard_map/all_to_all | solution.py:483
  119.9 3.4 %sum_gradients.1 = f32[64,4096]{1,0:T(8,128)} custom-call(bf16[8,64,4096]{2,1,0:T(8,128)(2,1)} %bitcast.16), custom_call_target="tpu_custom_call" | custom-call | flops 2097152 | bytes 5242880 | tf_op jit(solution)/shard_map/sum_gradients/pallas_call | solution.py:453
  (44 shorter events, 2.9 us)
Async XLA Ops:
  7.2 28.5 %copy-start = (f32[3,2048]{1,0:T(4,128)S(1)}, f32[3,2048]{1,0:T(4,128)}, u32[]{:S(2)}) copy-start(f32[3,2048]{1,0:T(4,128)} %param.18) | copy-start | bytes 73732
  7.2 36.2 %all-gather.5.cloned.1.call-start = ((), (), s32[]{:S(2)}) async-start(), calls=%async_computation.3 | async-start | bytes 1179648 | tf_op jit(solution)/shard_map/all_gather | solution.py:360
  7.2 26.8 %copy-start.2 = (bf16[1,128,2048]{2,1,0:T(8,128)(2,1)S(1)}, bf16[1,128,2048]{2,1,0:T(8,128)(2,1)}, u32[]{:S(2)}) copy-start(bf16[1,128,2048]{2,1,0:T(8,128)(2,1)} %param.22) | copy-start | bytes 1572868
  7.2 32.2 %copy-start.10 = (f32[64]{0:T(128)S(1)}, f32[64]{0:T(128)}, u32[]{:S(2)}) copy-start(f32[64]{0:T(128)} %param.20) | copy-start | bytes 772
  10.3 92.6 %all-gather.7.cloned.1.call-start = ((), (), s32[]{:S(2)}) async-start(), calls=%async_computation.4 | async-start | bytes 4718592 | tf_op jit(solution)/shard_map/all_gather | solution.py:374
  10.4 4.8 %collective-permute-start = (bf16[136,256]{1,0:T(8,128)(2,1)}, bf16[136,256]{1,0:T(8,128)(2,1)S(1)}, u32[]{:S(2)}, u32[]{:S(2)}) collective-permute-start(bf16[136,256]{1,0:T(8,128)(2,1)} %get-tuple-element.29), channel_id=1, source_target_pairs={{0,1},{1,2},{2,3},{3,0},{4,5},{5,6},{6,7},{7,4},{8,9},{9,10},{10,1... | collective-permute-start | bytes 208904 | tf_op jit(solution)/shard_map/ppermute | solution.py:312
  12.0 5.3 %collective-permute-start.1 = (bf16[136,256]{1,0:T(8,128)(2,1)}, bf16[136,256]{1,0:T(8,128)(2,1)S(1)}, u32[]{:S(2)}, u32[]{:S(2)}) collective-permute-start(bf16[136,256]{1,0:T(8,128)(2,1)} %get-tuple-element.29), channel_id=1, source_target_pairs={{0,3},{1,0},{2,1},{3,2},{4,7},{5,4},{6,5},{7,6},{8,11},{9,8},{10,9... | collective-permute-start | bytes 208904 | tf_op jit(solution)/shard_map/ppermute | solution.py:312
  12.7 6.0 %collective-permute-start.2 = (bf16[136,256]{1,0:T(8,128)(2,1)}, bf16[136,256]{1,0:T(8,128)(2,1)S(1)}, u32[]{:S(2)}, u32[]{:S(2)}) collective-permute-start(bf16[136,256]{1,0:T(8,128)(2,1)} %get-tuple-element.29), channel_id=1, source_target_pairs={{0,2},{1,3},{2,0},{3,1},{4,6},{5,7},{6,4},{7,5},{8,10},{9,11},{10,... | collective-permute-start | bytes 208904 | tf_op jit(solution)/shard_map/ppermute | solution.py:312
  19.7 23.7 %copy-start.1 = (bf16[4,136,256]{2,1,0:T(8,128)(2,1)}, bf16[4,136,256]{2,1,0:T(8,128)(2,1)S(1)}, u32[]{:S(2)}) copy-start(bf16[4,136,256]{2,1,0:T(8,128)(2,1)S(1)} %pad_maximum_fusion.rest_0_) | copy-start | bytes 835588
  19.7 11.0 %collective-permute-start.3 = (bf16[4,136,256]{2,1,0:T(8,128)(2,1)S(1)}, bf16[4,136,256]{2,1,0:T(8,128)(2,1)S(1)}, u32[]{:S(2)}, u32[]{:S(2)}) collective-permute-start(bf16[4,136,256]{2,1,0:T(8,128)(2,1)S(1)} %pad_maximum_fusion.rest_0_), channel_id=1, source_target_pairs={{0,4},{1,5},{2,6},{3,7},{4,8},{5,9},{6,10},{7,11},{8,12},{9,13},{1... | collective-permute-start | bytes 835592 | tf_op jit(solution)/shard_map/ppermute | solution.py:316
  21.4 9.3 %collective-permute-start.4 = (bf16[4,136,256]{2,1,0:T(8,128)(2,1)S(1)}, bf16[4,136,256]{2,1,0:T(8,128)(2,1)S(1)}, u32[]{:S(2)}, u32[]{:S(2)}) collective-permute-start(bf16[4,136,256]{2,1,0:T(8,128)(2,1)S(1)} %pad_maximum_fusion.rest_0_), channel_id=1, source_target_pairs={{0,28},{1,29},{2,30},{3,31},{4,0},{5,1},{6,2},{7,3},{8,4},{9,5},{1... | collective-permute-start | bytes 835592 | tf_op jit(solution)/shard_map/ppermute | solution.py:316
  30.7 12.7 %copy-start.5 = (bf16[4,136,256]{2,1,0:T(8,128)(2,1)}, bf16[4,136,256]{2,1,0:T(8,128)(2,1)S(1)}, u32[]{:S(2)}) copy-start(bf16[4,136,256]{2,1,0:T(8,128)(2,1)S(1)} %collective-permute-done.3.rest_1_) | copy-start | bytes 835588
  30.7 12.7 %copy-start.6 = (bf16[4,136,256]{2,1,0:T(8,128)(2,1)}, bf16[4,136,256]{2,1,0:T(8,128)(2,1)S(1)}, u32[]{:S(2)}) copy-start(bf16[4,136,256]{2,1,0:T(8,128)(2,1)S(1)} %collective-permute-done.4.rest_2_) | copy-start | bytes 835588
  30.7 7.9 %collective-permute-start.5 = (bf16[4,136,256]{2,1,0:T(8,128)(2,1)S(1)}, bf16[4,136,256]{2,1,0:T(8,128)(2,1)S(1)}, u32[]{:S(2)}, u32[]{:S(2)}) collective-permute-start(bf16[4,136,256]{2,1,0:T(8,128)(2,1)S(1)} %collective-permute-done.3.rest_1_), channel_id=1, source_target_pairs={{0,4},{1,5},{2,6},{3,7},{4,8},{5,9},{6,10},{7,11},{8,12},{9,13},{1... | collective-permute-start | bytes 835592 | tf_op jit(solution)/shard_map/ppermute | solution.py:316
  30.8 7.8 %collective-permute-start.6 = (bf16[4,136,256]{2,1,0:T(8,128)(2,1)S(1)}, bf16[4,136,256]{2,1,0:T(8,128)(2,1)S(1)}, u32[]{:S(2)}, u32[]{:S(2)}) collective-permute-start(bf16[4,136,256]{2,1,0:T(8,128)(2,1)S(1)} %collective-permute-done.4.rest_2_), channel_id=1, source_target_pairs={{0,28},{1,29},{2,30},{3,31},{4,0},{5,1},{6,2},{7,3},{8,4},{9,5},{1... | collective-permute-start | bytes 835592 | tf_op jit(solution)/shard_map/ppermute | solution.py:316
  38.6 12.4 %copy-start.11 = (bf16[4,136,256]{2,1,0:T(8,128)(2,1)}, bf16[4,136,256]{2,1,0:T(8,128)(2,1)S(1)}, u32[]{:S(2)}) copy-start(bf16[4,136,256]{2,1,0:T(8,128)(2,1)S(1)} %collective-permute-done.5.rest_0_) | copy-start | bytes 835588
  38.6 12.4 %copy-start.12 = (bf16[4,136,256]{2,1,0:T(8,128)(2,1)}, bf16[4,136,256]{2,1,0:T(8,128)(2,1)S(1)}, u32[]{:S(2)}) copy-start(bf16[4,136,256]{2,1,0:T(8,128)(2,1)S(1)} %collective-permute-done.6.rest_1_) | copy-start | bytes 835588
  40.1 8.1 %collective-permute-start.7 = (bf16[4,136,256]{2,1,0:T(8,128)(2,1)S(1)}, bf16[4,136,256]{2,1,0:T(8,128)(2,1)S(1)}, u32[]{:S(2)}, u32[]{:S(2)}) collective-permute-start(bf16[4,136,256]{2,1,0:T(8,128)(2,1)S(1)} %collective-permute-done.5.rest_0_), channel_id=1, source_target_pairs={{0,4},{1,5},{2,6},{3,7},{4,8},{5,9},{6,10},{7,11},{8,12},{9,13},{1... | collective-permute-start | bytes 835592 | tf_op jit(solution)/shard_map/ppermute | solution.py:316
  42.4 6.5 %collective-permute-start.8 = (bf16[4,136,256]{2,1,0:T(8,128)(2,1)S(1)}, bf16[4,136,256]{2,1,0:T(8,128)(2,1)S(1)}, u32[]{:S(2)}, u32[]{:S(2)}) collective-permute-start(bf16[4,136,256]{2,1,0:T(8,128)(2,1)S(1)} %collective-permute-done.6.rest_1_), channel_id=1, source_target_pairs={{0,28},{1,29},{2,30},{3,31},{4,0},{5,1},{6,2},{7,3},{8,4},{9,5},{1... | collective-permute-start | bytes 835592 | tf_op jit(solution)/shard_map/ppermute | solution.py:316
  48.2 16.9 %copy-start.7 = (bf16[4,136,256]{2,1,0:T(8,128)(2,1)}, bf16[4,136,256]{2,1,0:T(8,128)(2,1)S(1)}, u32[]{:S(2)}) copy-start(bf16[4,136,256]{2,1,0:T(8,128)(2,1)S(1)} %collective-permute-done.7.rest_0_) | copy-start | bytes 835588
  49.0 16.1 %copy-start.8 = (bf16[4,136,256]{2,1,0:T(8,128)(2,1)}, bf16[4,136,256]{2,1,0:T(8,128)(2,1)S(1)}, u32[]{:S(2)}) copy-start(bf16[4,136,256]{2,1,0:T(8,128)(2,1)S(1)} %collective-permute-done.8.rest_1_) | copy-start | bytes 835588
  49.0 7.8 %collective-permute-start.9 = (bf16[4,136,256]{2,1,0:T(8,128)(2,1)S(1)}, bf16[4,136,256]{2,1,0:T(8,128)(2,1)S(1)}, u32[]{:S(2)}, u32[]{:S(2)}) collective-permute-start(bf16[4,136,256]{2,1,0:T(8,128)(2,1)S(1)} %collective-permute-done.7.rest_0_), channel_id=1, source_target_pairs={{0,4},{1,5},{2,6},{3,7},{4,8},{5,9},{6,10},{7,11},{8,12},{9,13},{1... | collective-permute-start | bytes 835592 | tf_op jit(solution)/shard_map/ppermute | solution.py:316
  56.8 8.4 %copy-start.9 = (bf16[4,136,256]{2,1,0:T(8,128)(2,1)}, bf16[4,136,256]{2,1,0:T(8,128)(2,1)S(1)}, u32[]{:S(2)}) copy-start(bf16[4,136,256]{2,1,0:T(8,128)(2,1)S(1)} %collective-permute-done.9.rest_2_) | copy-start | bytes 835588
  56.8 21.5 %all-to-all-start.2 = ((bf16[32,64,128]{2,1,0:T(8,128)(2,1)}), bf16[32,64,128]{2,1,0:T(8,128)(2,1)S(1)}, u32[]{:S(2)}, u32[]{:S(2)}) async-start(bf16[32,64,128]{2,1,0:T(8,128)(2,1)} %bitcast.10), calls=%async_computation.2 | async-start | bytes 1048576 | tf_op jit(solution)/shard_map/all_to_all | solution.py:410
  64.9 55.1 %all-gather.9.cloned.1.call-start = ((), (), s32[]{:S(2)}) async-start(), calls=%async_computation.5 | async-start | bytes 4718592 | tf_op jit(solution)/shard_map/all_gather | solution.py:451
  77.0 6.9 %copy-start.4 = (bf16[32,64,128]{2,1,0:T(8,128)(2,1)S(1)}, bf16[32,64,128]{2,1,0:T(8,128)(2,1)}, u32[]{:S(2)}) copy-start(bf16[32,64,128]{2,1,0:T(8,128)(2,1)} %get-tuple-element.50) | copy-start | bytes 1572868
  78.2 0.8 copy-start.3
Sparse Core Ops, SparseCore 0:
  10.4 28.7 all-gather.4
  41.1 34.5 all-gather.6
  84.1 34.4 all-gather.8

commit v13 on v12

--- a/solution.py
+++ b/solution.py
@@ -247,9 +247,11 @@
     rows = jnp.concatenate([rows_all[:, block, :, :].reshape(inner, BLOCK).T for block in places], 0)
     marks = chunk_all[...].astype(f32).reshape(Y * trials, width)
     marks = jnp.broadcast_to(marks[:, None, :], (Y * trials, TRIAL, width)).reshape(Y * BLOCK, width)
-    wait_all(loads)
     total = jnp.zeros((Y * BLOCK, width), f32)
+    half = slots // 2
     for slot in range(slots):
+        if slot % half == 0:
+            wait_all(loads[slot : slot + half])
         product = jnp.dot(rows, weight[slot], preferred_element_type=f32)
         total = jnp.where(marks == slot, product, total)
     for index, block in enumerate(places):

time: 131 us -> 132 us (level)
  no operation moved by 1% of the time
where the time goes in v13:
time: 132 us; the launch traced here: 130 us
  Pallas kernels  43 us (33%)
  blocking collectives  29 us (22%)
  starting transfers between devices  27.1 us (21%)
  between operations  13.9 us (11%)
  waiting for transfers between devices  10.7 us (8%)
  local copies, waits for them, and re-layouts  4.05 us (3%)
  other arithmetic  2.21 us (2%)
    all_to_all x1, blocking collectives, local(): lax.all_to_all(gated, 'seq', split_axis=0, concat_axis=0, tiled=True, axi...  18.9 us
    ppermute x7, starting transfers between devices, along_z(): lax.ppermute(value, 'seq', [(z * Y + y, (z + step) % Z * Y + y) for z in...  14.3 us
    pallas_call x3, Pallas kernels, read_in(): pl.pallas_call(read_in_kernel, out_shape=jax.ShapeDtypeStruct((blocks, wi...  13.6 us
    all_to_all x1, blocking collectives, local(): lax.all_to_all(partial, 'seq', split_axis=0, concat_axis=0, tiled=True, a...  10 us
    all_to_all x1, starting transfers between devices, local(): lax.all_to_all(turned, 'seq', split_axis=0, concat_axis=0, tiled=True)  8.09 us
    pallas_call x1, Pallas kernels, local(): pl.pallas_call(forward_kernel, out_shape=(jax.ShapeDtypeStruct(plane, bf1...  7.06 us
    pallas_call x1, Pallas kernels, local(): pl.pallas_call(read_out_kernel, out_shape=jax.ShapeDtypeStruct((Y, BLOCK,...  6.5 us
    ppermute x7, waiting for transfers between devices, along_z(): lax.ppermute(value, 'seq', [(z * Y + y, (z + step) % Z * Y + y) for z in...  5.53 us
  transfers between devices with their start and end apart: 14, of which 8 were waited for; matrix products, arithmetic and copies ran while one was open for 4% of the time, Pallas kernels for 28%

profile of v13, /device:TPU:8, one launch (start us, length us, event | category | flops | bytes accessed | tf_op | source)
XLA Modules:
  0.0 130.0 jit_solution(6432796891761535650)
XLA Ops:
  7.3 3.0 %prepare.1 = (bf16[136,256]{1,0:T(8,128)(2,1)}, bf16[2,256,128]{2,1,0:T(8,128)(2,1)}, bf16[2,8,64,256]{3,2,1,0:T(8,128)(2,1)}) custom-call(s32[1]{0:T(128)} %bitcast.place_ref, s32[1,128]{1,0:T(1,128)} %session_ref.1, s32[16]{0:T(128)} %slot_ref.1, bf16[1,128,256]{2,1,0:T(8,128)(2,1)} %spikes_ref.1, bf16[2,256,4096]{2,1,0:T(8,128)(2,1)} %weight_hbm.1, ...), custom_call_target="tpu_custom_call" | custom-call | flops 65536 | bytes 524288 | tf_op jit(solution)/shard_map/prepare/pallas_call | solution.py:343
  10.4 1.7 %collective-permute-start = (bf16[136,256]{1,0:T(8,128)(2,1)}, bf16[136,256]{1,0:T(8,128)(2,1)S(1)}, u32[]{:S(2)}, u32[]{:S(2)}) collective-permute-start(bf16[136,256]{1,0:T(8,128)(2,1)} %get-tuple-element.29), channel_id=1, source_target_pairs={{0,1},{1,2},{2,3},{3,0},{4,5},{5,6},{6,7},{7,4},{8,9},{9,10},{10,1... | collective-permute-start | bytes 208904 | tf_op jit(solution)/shard_map/ppermute | solution.py:314
  12.0 0.7 collective-permute-start.1
  12.7 2.0 %collective-permute-start.2 = (bf16[136,256]{1,0:T(8,128)(2,1)}, bf16[136,256]{1,0:T(8,128)(2,1)S(1)}, u32[]{:S(2)}, u32[]{:S(2)}) collective-permute-start(bf16[136,256]{1,0:T(8,128)(2,1)} %get-tuple-element.29), channel_id=1, source_target_pairs={{0,2},{1,3},{2,0},{3,1},{4,6},{5,7},{6,4},{7,5},{8,10},{9,11},{10,... | collective-permute-start | bytes 208904 | tf_op jit(solution)/shard_map/ppermute | solution.py:314
  15.1 2.2 %collective-permute-done.1 = bf16[136,256]{1,0:T(8,128)(2,1)S(1)} collective-permute-done((bf16[136,256]{1,0:T(8,128)(2,1)}, bf16[136,256]{1,0:T(8,128)(2,1)S(1)}, u32[]{:S(2)}, u32[]{:S(2)}) %collective-permute-start.1) | collective-permute-done | bytes 69664 | tf_op jit(solution)/shard_map/ppermute | solution.py:314
  17.3 1.5 %collective-permute-done.2 = bf16[136,256]{1,0:T(8,128)(2,1)S(1)} collective-permute-done((bf16[136,256]{1,0:T(8,128)(2,1)}, bf16[136,256]{1,0:T(8,128)(2,1)S(1)}, u32[]{:S(2)}, u32[]{:S(2)}) %collective-permute-start.2) | collective-permute-done | bytes 69664 | tf_op jit(solution)/shard_map/ppermute | solution.py:314
  18.7 0.9 pad_maximum_fusion.rest_0_
  19.7 1.7 %collective-permute-start.3 = (bf16[4,136,256]{2,1,0:T(8,128)(2,1)S(1)}, bf16[4,136,256]{2,1,0:T(8,128)(2,1)S(1)}, u32[]{:S(2)}, u32[]{:S(2)}) collective-permute-start(bf16[4,136,256]{2,1,0:T(8,128)(2,1)S(1)} %pad_maximum_fusion.rest_0_), channel_id=1, source_target_pairs={{0,4},{1,5},{2,6},{3,7},{4,8},{5,9},{6,10},{7,11},{8,12},{9,13},{1... | collective-permute-start | bytes 835592 | tf_op jit(solution)/shard_map/ppermute | solution.py:318
  21.4 4.0 %collective-permute-start.4 = (bf16[4,136,256]{2,1,0:T(8,128)(2,1)S(1)}, bf16[4,136,256]{2,1,0:T(8,128)(2,1)S(1)}, u32[]{:S(2)}, u32[]{:S(2)}) collective-permute-start(bf16[4,136,256]{2,1,0:T(8,128)(2,1)S(1)} %pad_maximum_fusion.rest_0_), channel_id=1, source_target_pairs={{0,28},{1,29},{2,30},{3,31},{4,0},{5,1},{6,2},{7,3},{8,4},{9,5},{1... | collective-permute-start | bytes 835592 | tf_op jit(solution)/shard_map/ppermute | solution.py:318
  25.5 4.5 %filter_transform.1.filter_hbm = bf16[8,256,256]{2,1,0:T(8,128)(2,1)} custom-call(f32[64,4096]{1,0:T(8,128)} %filter_ref.1, bf16[512,256]{1,0:T(8,128)(2,1)} %constant.48.clone.first_ref.rest_3_, bf16[256,256]{1,0:T(8,128)(2,1)} %constant.49.clone.second_ref.rest_4_, f32[2,32,128]{2,1,0:T(8,128)} %constant.52.clone.twist_ref), custom_call_target="tpu_custom_call" | custom-call | flops 536870912 | bytes 4194304 | tf_op jit(solution)/shard_map/filter_transform/pallas_call | solution.py:363
  30.8 3.2 %collective-permute-start.6 = (bf16[4,136,256]{2,1,0:T(8,128)(2,1)S(1)}, bf16[4,136,256]{2,1,0:T(8,128)(2,1)S(1)}, u32[]{:S(2)}, u32[]{:S(2)}) collective-permute-start(bf16[4,136,256]{2,1,0:T(8,128)(2,1)S(1)} %collective-permute-done.4.rest_2_), channel_id=1, source_target_pairs={{0,28},{1,29},{2,30},{3,31},{4,0},{5,1},{6,2},{7,3},{8,4},{9,5},{1... | collective-permute-start | bytes 835592 | tf_op jit(solution)/shard_map/ppermute | solution.py:318
  34.0 1.0 copy.17
  35.7 2.9 %collective-permute-done.5.rest_0_ = bf16[4,136,256]{2,1,0:T(8,128)(2,1)S(1)} collective-permute-done((bf16[4,136,256]{2,1,0:T(8,128)(2,1)S(1)}, bf16[4,136,256]{2,1,0:T(8,128)(2,1)S(1)}, u32[]{:S(2)}, u32[]{:S(2)}) %collective-permute-start.5) | collective-permute-done | bytes 278560 | tf_op jit(solution)/shard_map/ppermute | solution.py:318
  38.6 0.8 broadcast_in_dim.9.taps_ref
  39.4 0.7 broadcast_in_dim.20.gain_ref
  40.1 2.3 %collective-permute-start.7 = (bf16[4,136,256]{2,1,0:T(8,128)(2,1)S(1)}, bf16[4,136,256]{2,1,0:T(8,128)(2,1)S(1)}, u32[]{:S(2)}, u32[]{:S(2)}) collective-permute-start(bf16[4,136,256]{2,1,0:T(8,128)(2,1)S(1)} %collective-permute-done.5.rest_0_), channel_id=1, source_target_pairs={{0,4},{1,5},{2,6},{3,7},{4,8},{5,9},{6,10},{7,11},{8,12},{9,13},{1... | collective-permute-start | bytes 835592 | tf_op jit(solution)/shard_map/ppermute | solution.py:318
  42.4 0.9 collective-permute-start.8
  43.4 4.8 %read_in.3.rest_0_ = bf16[12,128,128]{2,1,0:T(8,128)(2,1)} custom-call(bf16[16,256,128]{2,1,0:T(8,128)(2,1)} %all-gather.5.cloned.1.call-done.weight_hbm, bf16[4,136,256]{2,1,0:T(8,128)(2,1)} %copy-done.1, bf16[4,136,256]{2,1,0:T(8,128)(2,1)} %copy-done.5, bf16[4,136,256]{2,1,0:T(8,128)(2,1)} %copy-done.6), custom_call_target="tpu_custom_call" | custom-call | flops 536870912 | bytes 4194304 | tf_op jit(solution)/shard_map/read_in/pallas_call | solution.py:391
  48.2 0.8 collective-permute-done.8.rest_1_
  49.0 2.0 %collective-permute-start.9 = (bf16[4,136,256]{2,1,0:T(8,128)(2,1)S(1)}, bf16[4,136,256]{2,1,0:T(8,128)(2,1)S(1)}, u32[]{:S(2)}, u32[]{:S(2)}) collective-permute-start(bf16[4,136,256]{2,1,0:T(8,128)(2,1)S(1)} %collective-permute-done.7.rest_0_), channel_id=1, source_target_pairs={{0,4},{1,5},{2,6},{3,7},{4,8},{5,9},{6,10},{7,11},{8,12},{9,13},{1... | collective-permute-start | bytes 835592 | tf_op jit(solution)/shard_map/ppermute | solution.py:318
  51.0 3.9 %read_in.4.rest_1_ = bf16[8,128,128]{2,1,0:T(8,128)(2,1)} custom-call(bf16[16,256,128]{2,1,0:T(8,128)(2,1)} %all-gather.5.cloned.1.call-done.weight_hbm, bf16[4,136,256]{2,1,0:T(8,128)(2,1)} %copy-done.11, bf16[4,136,256]{2,1,0:T(8,128)(2,1)} %copy-done.12), custom_call_target="tpu_custom_call" | custom-call | flops 536870912 | bytes 4194304 | tf_op jit(solution)/shard_map/read_in/pallas_call | solution.py:391
  55.0 1.8 %collective-permute-done.9.rest_2_ = bf16[4,136,256]{2,1,0:T(8,128)(2,1)S(1)} collective-permute-done((bf16[4,136,256]{2,1,0:T(8,128)(2,1)S(1)}, bf16[4,136,256]{2,1,0:T(8,128)(2,1)S(1)}, u32[]{:S(2)}, u32[]{:S(2)}) %collective-permute-start.9) | collective-permute-done | bytes 278560 | tf_op jit(solution)/shard_map/ppermute | solution.py:318
  56.8 8.1 %all-to-all-start.2 = ((bf16[32,64,128]{2,1,0:T(8,128)(2,1)}), bf16[32,64,128]{2,1,0:T(8,128)(2,1)S(1)}, u32[]{:S(2)}, u32[]{:S(2)}) async-start(bf16[32,64,128]{2,1,0:T(8,128)(2,1)} %bitcast.10), calls=%async_computation.2 | async-start | bytes 1048576 | tf_op jit(solution)/shard_map/all_to_all | solution.py:412
  65.1 4.9 %read_in.5.rest_2_ = bf16[12,128,128]{2,1,0:T(8,128)(2,1)} custom-call(bf16[16,256,128]{2,1,0:T(8,128)(2,1)} %all-gather.5.cloned.1.call-done.weight_hbm, bf16[4,136,256]{2,1,0:T(8,128)(2,1)} %copy-done.7, bf16[4,136,256]{2,1,0:T(8,128)(2,1)} %copy-done.8, bf16[4,136,256]{2,1,0:T(8,128)(2,1)} %copy-done.9), custom_call_target="tpu_custom_call" | custom-call | flops 536870912 | bytes 4194304 | tf_op jit(solution)/shard_map/read_in/pallas_call | solution.py:391
  70.0 7.1 %long_convolution.1 = (bf16[32,64,128]{2,1,0:T(8,128)(2,1)}, bf16[32,64,128]{2,1,0:T(8,128)(2,1)}, bf16[8,256,256]{2,1,0:T(8,128)(2,1)}) custom-call(s32[2]{0:T(128)} %pad_add_fusion.place_ref, f32[3,64,128]{2,1,0:T(8,128)} %broadcast_in_dim.9.taps_ref, f32[64,128]{1,0:T(8,128)} %broadcast_in_dim.20.gain_ref, f32[2,32,128]{2,1,0:T(8,128)} %constant.52.clone.twist_ref, ...), custom_call_target="tpu_custom_call" | custom-call | flops 2147483648 | bytes 8388608 | tf_op jit(solution)/shard_map/long_convolution/pallas_call | solution.py:416
  77.1 1.2 all-to-all-done.2.grad_ref
  78.2 0.8 copy-done.3
  79.0 4.9 %filter_gradient.1 = bf16[64,4096]{1,0:T(8,128)(2,1)} custom-call(bf16[32,64,128]{2,1,0:T(8,128)(2,1)} %copy-done.3, bf16[32,64,128]{2,1,0:T(8,128)(2,1)} %get-tuple-element.54.gate_ref, bf16[8,256,256]{2,1,0:T(8,128)(2,1)} %get-tuple-element.55.spectrum_ref, bf16[512,256]{1,0:T(8,128)(2,1)} %constant.48.clone.first_ref.rest_3_, ...), custom_call_target="tpu_custom_call" | custom-call | flops 1073741824 | bytes 4194304 | tf_op jit(solution)/shard_map/filter_gradient/pallas_call | solution.py:441
  84.0 18.9 %all_to_all.15.rows_hbm = bf16[8,4,64,128]{3,2,1,0:T(8,128)(2,1)} all-to-all(bf16[8,4,64,128]{3,2,1,0:T(8,128)(2,1)S(1)} %bitcast.20), channel_id=1, replica_groups={{0,4,8,12,16,20,24,28},{1,5,9,13,17,21,25,29},{2,6,10,14,18,22,26,30},{..., dimensions={0} | all-to-all | bytes 1048576 | tf_op jit(solution)/shard_map/all_to_all | solution.py:440
  102.9 6.5 %read_out.1 = bf16[4,128,256]{2,1,0:T(8,128)(2,1)} custom-call(s32[2]{0:T(128)} %pad_add_fusion.place_ref, bf16[8,4,64,128]{3,2,1,0:T(8,128)(2,1)} %all_to_all.15.rows_hbm, bf16[4,8,256]{2,1,0:T(8,128)(2,1)} %slice.4.marks_hbm, bf16[16,512,256]{2,1,0:T(8,128)(2,1)} %all-gather.7.cloned.1.call-done.weight_hbm), custom_call_target="tpu_custom_call" | custom-call | flops 2147483648 | bytes 6291456 | tf_op jit(solution)/shard_map/read_out/pallas_call | solution.py:470
  109.4 10.0 %all_to_all.16 = bf16[4,128,256]{2,1,0:T(8,128)(2,1)S(1)} all-to-all(bf16[4,128,256]{2,1,0:T(8,128)(2,1)} %read_out.1), channel_id=1, replica_groups={{0,1,2,3},{4,5,6,7},{8,9,10,11},{12,13,14,15},{16,17,18,19},{20,21,22,2..., dimensions={0} | all-to-all | bytes 524288 | tf_op jit(solution)/shard_map/all_to_all | solution.py:485
  120.1 3.4 %sum_gradients.1 = f32[64,4096]{1,0:T(8,128)} custom-call(bf16[8,64,4096]{2,1,0:T(8,128)(2,1)} %bitcast.16), custom_call_target="tpu_custom_call" | custom-call | flops 2097152 | bytes 5242880 | tf_op jit(solution)/shard_map/sum_gradients/pallas_call | solution.py:455
  (44 shorter events, 2.9 us)
Async XLA Ops:
  7.2 28.5 %copy-start = (f32[3,2048]{1,0:T(4,128)S(1)}, f32[3,2048]{1,0:T(4,128)}, u32[]{:S(2)}) copy-start(f32[3,2048]{1,0:T(4,128)} %param.18) | copy-start | bytes 73732
  7.2 36.2 %all-gather.5.cloned.1.call-start = ((), (), s32[]{:S(2)}) async-start(), calls=%async_computation.3 | async-start | bytes 1179648 | tf_op jit(solution)/shard_map/all_gather | solution.py:362
  7.2 26.8 %copy-start.2 = (bf16[1,128,2048]{2,1,0:T(8,128)(2,1)S(1)}, bf16[1,128,2048]{2,1,0:T(8,128)(2,1)}, u32[]{:S(2)}) copy-start(bf16[1,128,2048]{2,1,0:T(8,128)(2,1)} %param.22) | copy-start | bytes 1572868
  7.2 32.2 %copy-start.10 = (f32[64]{0:T(128)S(1)}, f32[64]{0:T(128)}, u32[]{:S(2)}) copy-start(f32[64]{0:T(128)} %param.20) | copy-start | bytes 772
  10.3 92.6 %all-gather.7.cloned.1.call-start = ((), (), s32[]{:S(2)}) async-start(), calls=%async_computation.4 | async-start | bytes 4718592 | tf_op jit(solution)/shard_map/all_gather | solution.py:376
  10.4 4.8 %collective-permute-start = (bf16[136,256]{1,0:T(8,128)(2,1)}, bf16[136,256]{1,0:T(8,128)(2,1)S(1)}, u32[]{:S(2)}, u32[]{:S(2)}) collective-permute-start(bf16[136,256]{1,0:T(8,128)(2,1)} %get-tuple-element.29), channel_id=1, source_target_pairs={{0,1},{1,2},{2,3},{3,0},{4,5},{5,6},{6,7},{7,4},{8,9},{9,10},{10,1... | collective-permute-start | bytes 208904 | tf_op jit(solution)/shard_map/ppermute | solution.py:314
  12.0 5.3 %collective-permute-start.1 = (bf16[136,256]{1,0:T(8,128)(2,1)}, bf16[136,256]{1,0:T(8,128)(2,1)S(1)}, u32[]{:S(2)}, u32[]{:S(2)}) collective-permute-start(bf16[136,256]{1,0:T(8,128)(2,1)} %get-tuple-element.29), channel_id=1, source_target_pairs={{0,3},{1,0},{2,1},{3,2},{4,7},{5,4},{6,5},{7,6},{8,11},{9,8},{10,9... | collective-permute-start | bytes 208904 | tf_op jit(solution)/shard_map/ppermute | solution.py:314
  12.7 6.0 %collective-permute-start.2 = (bf16[136,256]{1,0:T(8,128)(2,1)}, bf16[136,256]{1,0:T(8,128)(2,1)S(1)}, u32[]{:S(2)}, u32[]{:S(2)}) collective-permute-start(bf16[136,256]{1,0:T(8,128)(2,1)} %get-tuple-element.29), channel_id=1, source_target_pairs={{0,2},{1,3},{2,0},{3,1},{4,6},{5,7},{6,4},{7,5},{8,10},{9,11},{10,... | collective-permute-start | bytes 208904 | tf_op jit(solution)/shard_map/ppermute | solution.py:314
  19.7 23.7 %copy-start.1 = (bf16[4,136,256]{2,1,0:T(8,128)(2,1)}, bf16[4,136,256]{2,1,0:T(8,128)(2,1)S(1)}, u32[]{:S(2)}) copy-start(bf16[4,136,256]{2,1,0:T(8,128)(2,1)S(1)} %pad_maximum_fusion.rest_0_) | copy-start | bytes 835588
  19.7 11.0 %collective-permute-start.3 = (bf16[4,136,256]{2,1,0:T(8,128)(2,1)S(1)}, bf16[4,136,256]{2,1,0:T(8,128)(2,1)S(1)}, u32[]{:S(2)}, u32[]{:S(2)}) collective-permute-start(bf16[4,136,256]{2,1,0:T(8,128)(2,1)S(1)} %pad_maximum_fusion.rest_0_), channel_id=1, source_target_pairs={{0,4},{1,5},{2,6},{3,7},{4,8},{5,9},{6,10},{7,11},{8,12},{9,13},{1... | collective-permute-start | bytes 835592 | tf_op jit(solution)/shard_map/ppermute | solution.py:318
  21.4 9.3 %collective-permute-start.4 = (bf16[4,136,256]{2,1,0:T(8,128)(2,1)S(1)}, bf16[4,136,256]{2,1,0:T(8,128)(2,1)S(1)}, u32[]{:S(2)}, u32[]{:S(2)}) collective-permute-start(bf16[4,136,256]{2,1,0:T(8,128)(2,1)S(1)} %pad_maximum_fusion.rest_0_), channel_id=1, source_target_pairs={{0,28},{1,29},{2,30},{3,31},{4,0},{5,1},{6,2},{7,3},{8,4},{9,5},{1... | collective-permute-start | bytes 835592 | tf_op jit(solution)/shard_map/ppermute | solution.py:318
  30.7 12.7 %copy-start.5 = (bf16[4,136,256]{2,1,0:T(8,128)(2,1)}, bf16[4,136,256]{2,1,0:T(8,128)(2,1)S(1)}, u32[]{:S(2)}) copy-start(bf16[4,136,256]{2,1,0:T(8,128)(2,1)S(1)} %collective-permute-done.3.rest_1_) | copy-start | bytes 835588
  30.7 12.7 %copy-start.6 = (bf16[4,136,256]{2,1,0:T(8,128)(2,1)}, bf16[4,136,256]{2,1,0:T(8,128)(2,1)S(1)}, u32[]{:S(2)}) copy-start(bf16[4,136,256]{2,1,0:T(8,128)(2,1)S(1)} %collective-permute-done.4.rest_2_) | copy-start | bytes 835588
  30.7 7.9 %collective-permute-start.5 = (bf16[4,136,256]{2,1,0:T(8,128)(2,1)S(1)}, bf16[4,136,256]{2,1,0:T(8,128)(2,1)S(1)}, u32[]{:S(2)}, u32[]{:S(2)}) collective-permute-start(bf16[4,136,256]{2,1,0:T(8,128)(2,1)S(1)} %collective-permute-done.3.rest_1_), channel_id=1, source_target_pairs={{0,4},{1,5},{2,6},{3,7},{4,8},{5,9},{6,10},{7,11},{8,12},{9,13},{1... | collective-permute-start | bytes 835592 | tf_op jit(solution)/shard_map/ppermute | solution.py:318
  30.8 7.8 %collective-permute-start.6 = (bf16[4,136,256]{2,1,0:T(8,128)(2,1)S(1)}, bf16[4,136,256]{2,1,0:T(8,128)(2,1)S(1)}, u32[]{:S(2)}, u32[]{:S(2)}) collective-permute-start(bf16[4,136,256]{2,1,0:T(8,128)(2,1)S(1)} %collective-permute-done.4.rest_2_), channel_id=1, source_target_pairs={{0,28},{1,29},{2,30},{3,31},{4,0},{5,1},{6,2},{7,3},{8,4},{9,5},{1... | collective-permute-start | bytes 835592 | tf_op jit(solution)/shard_map/ppermute | solution.py:318
  38.6 12.4 %copy-start.11 = (bf16[4,136,256]{2,1,0:T(8,128)(2,1)}, bf16[4,136,256]{2,1,0:T(8,128)(2,1)S(1)}, u32[]{:S(2)}) copy-start(bf16[4,136,256]{2,1,0:T(8,128)(2,1)S(1)} %collective-permute-done.5.rest_0_) | copy-start | bytes 835588
  38.6 12.4 %copy-start.12 = (bf16[4,136,256]{2,1,0:T(8,128)(2,1)}, bf16[4,136,256]{2,1,0:T(8,128)(2,1)S(1)}, u32[]{:S(2)}) copy-start(bf16[4,136,256]{2,1,0:T(8,128)(2,1)S(1)} %collective-permute-done.6.rest_1_) | copy-start | bytes 835588
  40.1 8.1 %collective-permute-start.7 = (bf16[4,136,256]{2,1,0:T(8,128)(2,1)S(1)}, bf16[4,136,256]{2,1,0:T(8,128)(2,1)S(1)}, u32[]{:S(2)}, u32[]{:S(2)}) collective-permute-start(bf16[4,136,256]{2,1,0:T(8,128)(2,1)S(1)} %collective-permute-done.5.rest_0_), channel_id=1, source_target_pairs={{0,4},{1,5},{2,6},{3,7},{4,8},{5,9},{6,10},{7,11},{8,12},{9,13},{1... | collective-permute-start | bytes 835592 | tf_op jit(solution)/shard_map/ppermute | solution.py:318
  42.4 6.5 %collective-permute-start.8 = (bf16[4,136,256]{2,1,0:T(8,128)(2,1)S(1)}, bf16[4,136,256]{2,1,0:T(8,128)(2,1)S(1)}, u32[]{:S(2)}, u32[]{:S(2)}) collective-permute-start(bf16[4,136,256]{2,1,0:T(8,128)(2,1)S(1)} %collective-permute-done.6.rest_1_), channel_id=1, source_target_pairs={{0,28},{1,29},{2,30},{3,31},{4,0},{5,1},{6,2},{7,3},{8,4},{9,5},{1... | collective-permute-start | bytes 835592 | tf_op jit(solution)/shard_map/ppermute | solution.py:318
  48.2 16.9 %copy-start.7 = (bf16[4,136,256]{2,1,0:T(8,128)(2,1)}, bf16[4,136,256]{2,1,0:T(8,128)(2,1)S(1)}, u32[]{:S(2)}) copy-start(bf16[4,136,256]{2,1,0:T(8,128)(2,1)S(1)} %collective-permute-done.7.rest_0_) | copy-start | bytes 835588
  49.0 16.1 %copy-start.8 = (bf16[4,136,256]{2,1,0:T(8,128)(2,1)}, bf16[4,136,256]{2,1,0:T(8,128)(2,1)S(1)}, u32[]{:S(2)}) copy-start(bf16[4,136,256]{2,1,0:T(8,128)(2,1)S(1)} %collective-permute-done.8.rest_1_) | copy-start | bytes 835588
  49.0 7.8 %collective-permute-start.9 = (bf16[4,136,256]{2,1,0:T(8,128)(2,1)S(1)}, bf16[4,136,256]{2,1,0:T(8,128)(2,1)S(1)}, u32[]{:S(2)}, u32[]{:S(2)}) collective-permute-start(bf16[4,136,256]{2,1,0:T(8,128)(2,1)S(1)} %collective-permute-done.7.rest_0_), channel_id=1, source_target_pairs={{0,4},{1,5},{2,6},{3,7},{4,8},{5,9},{6,10},{7,11},{8,12},{9,13},{1... | collective-permute-start | bytes 835592 | tf_op jit(solution)/shard_map/ppermute | solution.py:318
  56.8 8.4 %copy-start.9 = (bf16[4,136,256]{2,1,0:T(8,128)(2,1)}, bf16[4,136,256]{2,1,0:T(8,128)(2,1)S(1)}, u32[]{:S(2)}) copy-start(bf16[4,136,256]{2,1,0:T(8,128)(2,1)S(1)} %collective-permute-done.9.rest_2_) | copy-start | bytes 835588
  56.8 21.5 %all-to-all-start.2 = ((bf16[32,64,128]{2,1,0:T(8,128)(2,1)}), bf16[32,64,128]{2,1,0:T(8,128)(2,1)S(1)}, u32[]{:S(2)}, u32[]{:S(2)}) async-start(bf16[32,64,128]{2,1,0:T(8,128)(2,1)} %bitcast.10), calls=%async_computation.2 | async-start | bytes 1048576 | tf_op jit(solution)/shard_map/all_to_all | solution.py:412
  64.9 55.2 %all-gather.9.cloned.1.call-start = ((), (), s32[]{:S(2)}) async-start(), calls=%async_computation.5 | async-start | bytes 4718592 | tf_op jit(solution)/shard_map/all_gather | solution.py:453
  77.0 6.9 %copy-start.4 = (bf16[32,64,128]{2,1,0:T(8,128)(2,1)S(1)}, bf16[32,64,128]{2,1,0:T(8,128)(2,1)}, u32[]{:S(2)}) copy-start(bf16[32,64,128]{2,1,0:T(8,128)(2,1)} %get-tuple-element.50) | copy-start | bytes 1572868
  78.2 0.8 copy-start.3
Sparse Core Ops, SparseCore 0:
  10.4 28.7 all-gather.4
  41.1 34.5 all-gather.6
  84.1 34.4 all-gather.8

commit v14 on v12

--- a/solution.py
+++ b/solution.py
@@ -439,11 +439,11 @@
     own_grad = pl.pallas_call(
         gradient_kernel,
         out_shape=jax.ShapeDtypeStruct((CHANS, LENGTH), bf16),
-        grid=(GROUPS // 4,),
-        in_specs=[pl.BlockSpec((BLOCKS, 2 * pair, BLOCK), lambda i: (0, i, 0))] * 2
-        + [pl.BlockSpec((4,) + spectrum_shape.shape[1:], lambda i: (i, 0, 0))]
+        grid=(GROUPS // 8,),
+        in_specs=[pl.BlockSpec((BLOCKS, 4 * pair, BLOCK), lambda i: (0, i, 0))] * 2
+        + [pl.BlockSpec((8,) + spectrum_shape.shape[1:], lambda i: (i, 0, 0))]
         + [same(table) for table in tables + (twists,)],
-        out_specs=pl.BlockSpec((2 * pair, LENGTH), lambda i: (i, 0)),
+        out_specs=pl.BlockSpec((4 * pair, LENGTH), lambda i: (i, 0)),
         compiler_params=params,
         cost_estimate=pl.CostEstimate(flops=2 * work, bytes_accessed=4 << 20, transcendentals=0),
         name="filter_gradient",

time: 131 us -> 131 us (level)
  no operation moved by 1% of the time
where the time goes in v14:
time: 131 us; the launch traced here: 130 us
  Pallas kernels  42.9 us (33%)
  blocking collectives  28.9 us (22%)
  starting transfers between devices  27.1 us (21%)
  between operations  13.9 us (11%)
  waiting for transfers between devices  10.7 us (8%)
  local copies, waits for them, and re-layouts  4.05 us (3%)
  other arithmetic  2.21 us (2%)
    all_to_all x1, blocking collectives, local(): lax.all_to_all(gated, 'seq', split_axis=0, concat_axis=0, tiled=True, axi...  18.9 us
    ppermute x7, starting transfers between devices, along_z(): lax.ppermute(value, 'seq', [(z * Y + y, (z + step) % Z * Y + y) for z in...  14.3 us
    pallas_call x3, Pallas kernels, read_in(): pl.pallas_call(read_in_kernel, out_shape=jax.ShapeDtypeStruct((blocks, wi...  13.6 us
    all_to_all x1, blocking collectives, local(): lax.all_to_all(partial, 'seq', split_axis=0, concat_axis=0, tiled=True, a...  10 us
    all_to_all x1, starting transfers between devices, local(): lax.all_to_all(turned, 'seq', split_axis=0, concat_axis=0, tiled=True)  8.09 us
    pallas_call x1, Pallas kernels, local(): pl.pallas_call(forward_kernel, out_shape=(jax.ShapeDtypeStruct(plane, bf1...  7.06 us
    pallas_call x1, Pallas kernels, local(): pl.pallas_call(read_out_kernel, out_shape=jax.ShapeDtypeStruct((Y, BLOCK,...  6.34 us
    ppermute x7, waiting for transfers between devices, along_z(): lax.ppermute(value, 'seq', [(z * Y + y, (z + step) % Z * Y + y) for z in...  5.53 us
  transfers between devices with their start and end apart: 14, of which 8 were waited for; matrix products, arithmetic and copies ran while one was open for 4% of the time, Pallas kernels for 28%

profile of v14, /device:TPU:8, one launch (start us, length us, event | category | flops | bytes accessed | tf_op | source)
XLA Modules:
  0.0 129.9 jit_solution(18147508600740219224)
XLA Ops:
  7.3 3.0 %prepare.1 = (bf16[136,256]{1,0:T(8,128)(2,1)}, bf16[2,256,128]{2,1,0:T(8,128)(2,1)}, bf16[2,8,64,256]{3,2,1,0:T(8,128)(2,1)}) custom-call(s32[1]{0:T(128)} %bitcast.place_ref, s32[1,128]{1,0:T(1,128)} %session_ref.1, s32[16]{0:T(128)} %slot_ref.1, bf16[1,128,256]{2,1,0:T(8,128)(2,1)} %spikes_ref.1, bf16[2,256,4096]{2,1,0:T(8,128)(2,1)} %weight_hbm.1, ...), custom_call_target="tpu_custom_call" | custom-call | flops 65536 | bytes 524288 | tf_op jit(solution)/shard_map/prepare/pallas_call | solution.py:341
  10.4 1.7 %collective-permute-start = (bf16[136,256]{1,0:T(8,128)(2,1)}, bf16[136,256]{1,0:T(8,128)(2,1)S(1)}, u32[]{:S(2)}, u32[]{:S(2)}) collective-permute-start(bf16[136,256]{1,0:T(8,128)(2,1)} %get-tuple-element.29), channel_id=1, source_target_pairs={{0,1},{1,2},{2,3},{3,0},{4,5},{5,6},{6,7},{7,4},{8,9},{9,10},{10,1... | collective-permute-start | bytes 208904 | tf_op jit(solution)/shard_map/ppermute | solution.py:312
  12.0 0.7 collective-permute-start.1
  12.7 2.0 %collective-permute-start.2 = (bf16[136,256]{1,0:T(8,128)(2,1)}, bf16[136,256]{1,0:T(8,128)(2,1)S(1)}, u32[]{:S(2)}, u32[]{:S(2)}) collective-permute-start(bf16[136,256]{1,0:T(8,128)(2,1)} %get-tuple-element.29), channel_id=1, source_target_pairs={{0,2},{1,3},{2,0},{3,1},{4,6},{5,7},{6,4},{7,5},{8,10},{9,11},{10,... | collective-permute-start | bytes 208904 | tf_op jit(solution)/shard_map/ppermute | solution.py:312
  15.1 2.2 %collective-permute-done.1 = bf16[136,256]{1,0:T(8,128)(2,1)S(1)} collective-permute-done((bf16[136,256]{1,0:T(8,128)(2,1)}, bf16[136,256]{1,0:T(8,128)(2,1)S(1)}, u32[]{:S(2)}, u32[]{:S(2)}) %collective-permute-start.1) | collective-permute-done | bytes 69664 | tf_op jit(solution)/shard_map/ppermute | solution.py:312
  17.3 1.5 %collective-permute-done.2 = bf16[136,256]{1,0:T(8,128)(2,1)S(1)} collective-permute-done((bf16[136,256]{1,0:T(8,128)(2,1)}, bf16[136,256]{1,0:T(8,128)(2,1)S(1)}, u32[]{:S(2)}, u32[]{:S(2)}) %collective-permute-start.2) | collective-permute-done | bytes 69664 | tf_op jit(solution)/shard_map/ppermute | solution.py:312
  18.7 0.9 pad_maximum_fusion.rest_0_
  19.7 1.7 %collective-permute-start.3 = (bf16[4,136,256]{2,1,0:T(8,128)(2,1)S(1)}, bf16[4,136,256]{2,1,0:T(8,128)(2,1)S(1)}, u32[]{:S(2)}, u32[]{:S(2)}) collective-permute-start(bf16[4,136,256]{2,1,0:T(8,128)(2,1)S(1)} %pad_maximum_fusion.rest_0_), channel_id=1, source_target_pairs={{0,4},{1,5},{2,6},{3,7},{4,8},{5,9},{6,10},{7,11},{8,12},{9,13},{1... | collective-permute-start | bytes 835592 | tf_op jit(solution)/shard_map/ppermute | solution.py:316
  21.4 4.0 %collective-permute-start.4 = (bf16[4,136,256]{2,1,0:T(8,128)(2,1)S(1)}, bf16[4,136,256]{2,1,0:T(8,128)(2,1)S(1)}, u32[]{:S(2)}, u32[]{:S(2)}) collective-permute-start(bf16[4,136,256]{2,1,0:T(8,128)(2,1)S(1)} %pad_maximum_fusion.rest_0_), channel_id=1, source_target_pairs={{0,28},{1,29},{2,30},{3,31},{4,0},{5,1},{6,2},{7,3},{8,4},{9,5},{1... | collective-permute-start | bytes 835592 | tf_op jit(solution)/shard_map/ppermute | solution.py:316
  25.5 4.5 %filter_transform.1.filter_hbm = bf16[8,256,256]{2,1,0:T(8,128)(2,1)} custom-call(f32[64,4096]{1,0:T(8,128)} %filter_ref.1, bf16[512,256]{1,0:T(8,128)(2,1)} %constant.48.clone.first_ref.rest_3_, bf16[256,256]{1,0:T(8,128)(2,1)} %constant.49.clone.second_ref.rest_4_, f32[2,32,128]{2,1,0:T(8,128)} %constant.52.clone.twist_ref), custom_call_target="tpu_custom_call" | custom-call | flops 536870912 | bytes 4194304 | tf_op jit(solution)/shard_map/filter_transform/pallas_call | solution.py:361
  30.8 3.2 %collective-permute-start.6 = (bf16[4,136,256]{2,1,0:T(8,128)(2,1)S(1)}, bf16[4,136,256]{2,1,0:T(8,128)(2,1)S(1)}, u32[]{:S(2)}, u32[]{:S(2)}) collective-permute-start(bf16[4,136,256]{2,1,0:T(8,128)(2,1)S(1)} %collective-permute-done.4.rest_2_), channel_id=1, source_target_pairs={{0,28},{1,29},{2,30},{3,31},{4,0},{5,1},{6,2},{7,3},{8,4},{9,5},{1... | collective-permute-start | bytes 835592 | tf_op jit(solution)/shard_map/ppermute | solution.py:316
  34.0 1.0 copy.17
  35.7 2.9 %collective-permute-done.5.rest_0_ = bf16[4,136,256]{2,1,0:T(8,128)(2,1)S(1)} collective-permute-done((bf16[4,136,256]{2,1,0:T(8,128)(2,1)S(1)}, bf16[4,136,256]{2,1,0:T(8,128)(2,1)S(1)}, u32[]{:S(2)}, u32[]{:S(2)}) %collective-permute-start.5) | collective-permute-done | bytes 278560 | tf_op jit(solution)/shard_map/ppermute | solution.py:316
  38.6 0.8 broadcast_in_dim.9.taps_ref
  39.4 0.7 broadcast_in_dim.20.gain_ref
  40.1 2.3 %collective-permute-start.7 = (bf16[4,136,256]{2,1,0:T(8,128)(2,1)S(1)}, bf16[4,136,256]{2,1,0:T(8,128)(2,1)S(1)}, u32[]{:S(2)}, u32[]{:S(2)}) collective-permute-start(bf16[4,136,256]{2,1,0:T(8,128)(2,1)S(1)} %collective-permute-done.5.rest_0_), channel_id=1, source_target_pairs={{0,4},{1,5},{2,6},{3,7},{4,8},{5,9},{6,10},{7,11},{8,12},{9,13},{1... | collective-permute-start | bytes 835592 | tf_op jit(solution)/shard_map/ppermute | solution.py:316
  42.4 0.9 collective-permute-start.8
  43.4 4.8 %read_in.3.rest_0_ = bf16[12,128,128]{2,1,0:T(8,128)(2,1)} custom-call(bf16[16,256,128]{2,1,0:T(8,128)(2,1)} %all-gather.5.cloned.1.call-done.weight_hbm, bf16[4,136,256]{2,1,0:T(8,128)(2,1)} %copy-done.1, bf16[4,136,256]{2,1,0:T(8,128)(2,1)} %copy-done.5, bf16[4,136,256]{2,1,0:T(8,128)(2,1)} %copy-done.6), custom_call_target="tpu_custom_call" | custom-call | flops 536870912 | bytes 4194304 | tf_op jit(solution)/shard_map/read_in/pallas_call | solution.py:389
  48.2 0.8 collective-permute-done.8.rest_1_
  49.0 2.0 %collective-permute-start.9 = (bf16[4,136,256]{2,1,0:T(8,128)(2,1)S(1)}, bf16[4,136,256]{2,1,0:T(8,128)(2,1)S(1)}, u32[]{:S(2)}, u32[]{:S(2)}) collective-permute-start(bf16[4,136,256]{2,1,0:T(8,128)(2,1)S(1)} %collective-permute-done.7.rest_0_), channel_id=1, source_target_pairs={{0,4},{1,5},{2,6},{3,7},{4,8},{5,9},{6,10},{7,11},{8,12},{9,13},{1... | collective-permute-start | bytes 835592 | tf_op jit(solution)/shard_map/ppermute | solution.py:316
  51.0 3.9 %read_in.4.rest_1_ = bf16[8,128,128]{2,1,0:T(8,128)(2,1)} custom-call(bf16[16,256,128]{2,1,0:T(8,128)(2,1)} %all-gather.5.cloned.1.call-done.weight_hbm, bf16[4,136,256]{2,1,0:T(8,128)(2,1)} %copy-done.11, bf16[4,136,256]{2,1,0:T(8,128)(2,1)} %copy-done.12), custom_call_target="tpu_custom_call" | custom-call | flops 536870912 | bytes 4194304 | tf_op jit(solution)/shard_map/read_in/pallas_call | solution.py:389
  55.0 1.8 %collective-permute-done.9.rest_2_ = bf16[4,136,256]{2,1,0:T(8,128)(2,1)S(1)} collective-permute-done((bf16[4,136,256]{2,1,0:T(8,128)(2,1)S(1)}, bf16[4,136,256]{2,1,0:T(8,128)(2,1)S(1)}, u32[]{:S(2)}, u32[]{:S(2)}) %collective-permute-start.9) | collective-permute-done | bytes 278560 | tf_op jit(solution)/shard_map/ppermute | solution.py:316
  56.8 8.1 %all-to-all-start.2 = ((bf16[32,64,128]{2,1,0:T(8,128)(2,1)}), bf16[32,64,128]{2,1,0:T(8,128)(2,1)S(1)}, u32[]{:S(2)}, u32[]{:S(2)}) async-start(bf16[32,64,128]{2,1,0:T(8,128)(2,1)} %bitcast.10), calls=%async_computation.2 | async-start | bytes 1048576 | tf_op jit(solution)/shard_map/all_to_all | solution.py:410
  65.1 4.9 %read_in.5.rest_2_ = bf16[12,128,128]{2,1,0:T(8,128)(2,1)} custom-call(bf16[16,256,128]{2,1,0:T(8,128)(2,1)} %all-gather.5.cloned.1.call-done.weight_hbm, bf16[4,136,256]{2,1,0:T(8,128)(2,1)} %copy-done.7, bf16[4,136,256]{2,1,0:T(8,128)(2,1)} %copy-done.8, bf16[4,136,256]{2,1,0:T(8,128)(2,1)} %copy-done.9), custom_call_target="tpu_custom_call" | custom-call | flops 536870912 | bytes 4194304 | tf_op jit(solution)/shard_map/read_in/pallas_call | solution.py:389
  70.0 7.1 %long_convolution.1 = (bf16[32,64,128]{2,1,0:T(8,128)(2,1)}, bf16[32,64,128]{2,1,0:T(8,128)(2,1)}, bf16[8,256,256]{2,1,0:T(8,128)(2,1)}) custom-call(s32[2]{0:T(128)} %pad_add_fusion.place_ref, f32[3,64,128]{2,1,0:T(8,128)} %broadcast_in_dim.9.taps_ref, f32[64,128]{1,0:T(8,128)} %broadcast_in_dim.20.gain_ref, f32[2,32,128]{2,1,0:T(8,128)} %constant.52.clone.twist_ref, ...), custom_call_target="tpu_custom_call" | custom-call | flops 2147483648 | bytes 8388608 | tf_op jit(solution)/shard_map/long_convolution/pallas_call | solution.py:414
  77.1 1.2 all-to-all-done.2.grad_ref
  78.2 0.8 copy-done.3
  79.0 4.9 %filter_gradient.1 = bf16[64,4096]{1,0:T(8,128)(2,1)} custom-call(bf16[32,64,128]{2,1,0:T(8,128)(2,1)} %copy-done.3, bf16[32,64,128]{2,1,0:T(8,128)(2,1)} %get-tuple-element.54.gate_ref, bf16[8,256,256]{2,1,0:T(8,128)(2,1)} %get-tuple-element.55.spectrum_ref, bf16[512,256]{1,0:T(8,128)(2,1)} %constant.48.clone.first_ref.rest_3_, ...), custom_call_target="tpu_custom_call" | custom-call | flops 1073741824 | bytes 4194304 | tf_op jit(solution)/shard_map/filter_gradient/pallas_call | solution.py:439
  84.0 18.9 %all_to_all.15.rows_hbm = bf16[8,4,64,128]{3,2,1,0:T(8,128)(2,1)} all-to-all(bf16[8,4,64,128]{3,2,1,0:T(8,128)(2,1)S(1)} %bitcast.20), channel_id=1, replica_groups={{0,4,8,12,16,20,24,28},{1,5,9,13,17,21,25,29},{2,6,10,14,18,22,26,30},{..., dimensions={0} | all-to-all | bytes 1048576 | tf_op jit(solution)/shard_map/all_to_all | solution.py:438
  102.9 6.3 %read_out.1 = bf16[4,128,256]{2,1,0:T(8,128)(2,1)} custom-call(s32[2]{0:T(128)} %pad_add_fusion.place_ref, bf16[8,4,64,128]{3,2,1,0:T(8,128)(2,1)} %all_to_all.15.rows_hbm, bf16[4,8,256]{2,1,0:T(8,128)(2,1)} %slice.4.marks_hbm, bf16[16,512,256]{2,1,0:T(8,128)(2,1)} %all-gather.7.cloned.1.call-done.weight_hbm), custom_call_target="tpu_custom_call" | custom-call | flops 2147483648 | bytes 6291456 | tf_op jit(solution)/shard_map/read_out/pallas_call | solution.py:468
  109.3 10.0 %all_to_all.16 = bf16[4,128,256]{2,1,0:T(8,128)(2,1)S(1)} all-to-all(bf16[4,128,256]{2,1,0:T(8,128)(2,1)} %read_out.1), channel_id=1, replica_groups={{0,1,2,3},{4,5,6,7},{8,9,10,11},{12,13,14,15},{16,17,18,19},{20,21,22,2..., dimensions={0} | all-to-all | bytes 524288 | tf_op jit(solution)/shard_map/all_to_all | solution.py:483
  120.0 3.4 %sum_gradients.1 = f32[64,4096]{1,0:T(8,128)} custom-call(bf16[8,64,4096]{2,1,0:T(8,128)(2,1)} %bitcast.16), custom_call_target="tpu_custom_call" | custom-call | flops 2097152 | bytes 5242880 | tf_op jit(solution)/shard_map/sum_gradients/pallas_call | solution.py:453
  (44 shorter events, 2.9 us)
Async XLA Ops:
  7.2 28.5 %copy-start = (f32[3,2048]{1,0:T(4,128)S(1)}, f32[3,2048]{1,0:T(4,128)}, u32[]{:S(2)}) copy-start(f32[3,2048]{1,0:T(4,128)} %param.18) | copy-start | bytes 73732
  7.2 36.2 %all-gather.5.cloned.1.call-start = ((), (), s32[]{:S(2)}) async-start(), calls=%async_computation.3 | async-start | bytes 1179648 | tf_op jit(solution)/shard_map/all_gather | solution.py:360
  7.2 26.8 %copy-start.2 = (bf16[1,128,2048]{2,1,0:T(8,128)(2,1)S(1)}, bf16[1,128,2048]{2,1,0:T(8,128)(2,1)}, u32[]{:S(2)}) copy-start(bf16[1,128,2048]{2,1,0:T(8,128)(2,1)} %param.22) | copy-start | bytes 1572868
  7.2 32.2 %copy-start.10 = (f32[64]{0:T(128)S(1)}, f32[64]{0:T(128)}, u32[]{:S(2)}) copy-start(f32[64]{0:T(128)} %param.20) | copy-start | bytes 772
  10.3 92.6 %all-gather.7.cloned.1.call-start = ((), (), s32[]{:S(2)}) async-start(), calls=%async_computation.4 | async-start | bytes 4718592 | tf_op jit(solution)/shard_map/all_gather | solution.py:374
  10.4 4.8 %collective-permute-start = (bf16[136,256]{1,0:T(8,128)(2,1)}, bf16[136,256]{1,0:T(8,128)(2,1)S(1)}, u32[]{:S(2)}, u32[]{:S(2)}) collective-permute-start(bf16[136,256]{1,0:T(8,128)(2,1)} %get-tuple-element.29), channel_id=1, source_target_pairs={{0,1},{1,2},{2,3},{3,0},{4,5},{5,6},{6,7},{7,4},{8,9},{9,10},{10,1... | collective-permute-start | bytes 208904 | tf_op jit(solution)/shard_map/ppermute | solution.py:312
  12.0 5.3 %collective-permute-start.1 = (bf16[136,256]{1,0:T(8,128)(2,1)}, bf16[136,256]{1,0:T(8,128)(2,1)S(1)}, u32[]{:S(2)}, u32[]{:S(2)}) collective-permute-start(bf16[136,256]{1,0:T(8,128)(2,1)} %get-tuple-element.29), channel_id=1, source_target_pairs={{0,3},{1,0},{2,1},{3,2},{4,7},{5,4},{6,5},{7,6},{8,11},{9,8},{10,9... | collective-permute-start | bytes 208904 | tf_op jit(solution)/shard_map/ppermute | solution.py:312
  12.7 6.0 %collective-permute-start.2 = (bf16[136,256]{1,0:T(8,128)(2,1)}, bf16[136,256]{1,0:T(8,128)(2,1)S(1)}, u32[]{:S(2)}, u32[]{:S(2)}) collective-permute-start(bf16[136,256]{1,0:T(8,128)(2,1)} %get-tuple-element.29), channel_id=1, source_target_pairs={{0,2},{1,3},{2,0},{3,1},{4,6},{5,7},{6,4},{7,5},{8,10},{9,11},{10,... | collective-permute-start | bytes 208904 | tf_op jit(solution)/shard_map/ppermute | solution.py:312
  19.7 23.7 %copy-start.1 = (bf16[4,136,256]{2,1,0:T(8,128)(2,1)}, bf16[4,136,256]{2,1,0:T(8,128)(2,1)S(1)}, u32[]{:S(2)}) copy-start(bf16[4,136,256]{2,1,0:T(8,128)(2,1)S(1)} %pad_maximum_fusion.rest_0_) | copy-start | bytes 835588
  19.7 11.0 %collective-permute-start.3 = (bf16[4,136,256]{2,1,0:T(8,128)(2,1)S(1)}, bf16[4,136,256]{2,1,0:T(8,128)(2,1)S(1)}, u32[]{:S(2)}, u32[]{:S(2)}) collective-permute-start(bf16[4,136,256]{2,1,0:T(8,128)(2,1)S(1)} %pad_maximum_fusion.rest_0_), channel_id=1, source_target_pairs={{0,4},{1,5},{2,6},{3,7},{4,8},{5,9},{6,10},{7,11},{8,12},{9,13},{1... | collective-permute-start | bytes 835592 | tf_op jit(solution)/shard_map/ppermute | solution.py:316
  21.4 9.3 %collective-permute-start.4 = (bf16[4,136,256]{2,1,0:T(8,128)(2,1)S(1)}, bf16[4,136,256]{2,1,0:T(8,128)(2,1)S(1)}, u32[]{:S(2)}, u32[]{:S(2)}) collective-permute-start(bf16[4,136,256]{2,1,0:T(8,128)(2,1)S(1)} %pad_maximum_fusion.rest_0_), channel_id=1, source_target_pairs={{0,28},{1,29},{2,30},{3,31},{4,0},{5,1},{6,2},{7,3},{8,4},{9,5},{1... | collective-permute-start | bytes 835592 | tf_op jit(solution)/shard_map/ppermute | solution.py:316
  30.7 12.7 %copy-start.5 = (bf16[4,136,256]{2,1,0:T(8,128)(2,1)}, bf16[4,136,256]{2,1,0:T(8,128)(2,1)S(1)}, u32[]{:S(2)}) copy-start(bf16[4,136,256]{2,1,0:T(8,128)(2,1)S(1)} %collective-permute-done.3.rest_1_) | copy-start | bytes 835588
  30.7 12.7 %copy-start.6 = (bf16[4,136,256]{2,1,0:T(8,128)(2,1)}, bf16[4,136,256]{2,1,0:T(8,128)(2,1)S(1)}, u32[]{:S(2)}) copy-start(bf16[4,136,256]{2,1,0:T(8,128)(2,1)S(1)} %collective-permute-done.4.rest_2_) | copy-start | bytes 835588
  30.7 7.9 %collective-permute-start.5 = (bf16[4,136,256]{2,1,0:T(8,128)(2,1)S(1)}, bf16[4,136,256]{2,1,0:T(8,128)(2,1)S(1)}, u32[]{:S(2)}, u32[]{:S(2)}) collective-permute-start(bf16[4,136,256]{2,1,0:T(8,128)(2,1)S(1)} %collective-permute-done.3.rest_1_), channel_id=1, source_target_pairs={{0,4},{1,5},{2,6},{3,7},{4,8},{5,9},{6,10},{7,11},{8,12},{9,13},{1... | collective-permute-start | bytes 835592 | tf_op jit(solution)/shard_map/ppermute | solution.py:316
  30.8 7.8 %collective-permute-start.6 = (bf16[4,136,256]{2,1,0:T(8,128)(2,1)S(1)}, bf16[4,136,256]{2,1,0:T(8,128)(2,1)S(1)}, u32[]{:S(2)}, u32[]{:S(2)}) collective-permute-start(bf16[4,136,256]{2,1,0:T(8,128)(2,1)S(1)} %collective-permute-done.4.rest_2_), channel_id=1, source_target_pairs={{0,28},{1,29},{2,30},{3,31},{4,0},{5,1},{6,2},{7,3},{8,4},{9,5},{1... | collective-permute-start | bytes 835592 | tf_op jit(solution)/shard_map/ppermute | solution.py:316
  38.6 12.4 %copy-start.11 = (bf16[4,136,256]{2,1,0:T(8,128)(2,1)}, bf16[4,136,256]{2,1,0:T(8,128)(2,1)S(1)}, u32[]{:S(2)}) copy-start(bf16[4,136,256]{2,1,0:T(8,128)(2,1)S(1)} %collective-permute-done.5.rest_0_) | copy-start | bytes 835588
  38.6 12.4 %copy-start.12 = (bf16[4,136,256]{2,1,0:T(8,128)(2,1)}, bf16[4,136,256]{2,1,0:T(8,128)(2,1)S(1)}, u32[]{:S(2)}) copy-start(bf16[4,136,256]{2,1,0:T(8,128)(2,1)S(1)} %collective-permute-done.6.rest_1_) | copy-start | bytes 835588
  40.1 8.1 %collective-permute-start.7 = (bf16[4,136,256]{2,1,0:T(8,128)(2,1)S(1)}, bf16[4,136,256]{2,1,0:T(8,128)(2,1)S(1)}, u32[]{:S(2)}, u32[]{:S(2)}) collective-permute-start(bf16[4,136,256]{2,1,0:T(8,128)(2,1)S(1)} %collective-permute-done.5.rest_0_), channel_id=1, source_target_pairs={{0,4},{1,5},{2,6},{3,7},{4,8},{5,9},{6,10},{7,11},{8,12},{9,13},{1... | collective-permute-start | bytes 835592 | tf_op jit(solution)/shard_map/ppermute | solution.py:316
  42.4 6.5 %collective-permute-start.8 = (bf16[4,136,256]{2,1,0:T(8,128)(2,1)S(1)}, bf16[4,136,256]{2,1,0:T(8,128)(2,1)S(1)}, u32[]{:S(2)}, u32[]{:S(2)}) collective-permute-start(bf16[4,136,256]{2,1,0:T(8,128)(2,1)S(1)} %collective-permute-done.6.rest_1_), channel_id=1, source_target_pairs={{0,28},{1,29},{2,30},{3,31},{4,0},{5,1},{6,2},{7,3},{8,4},{9,5},{1... | collective-permute-start | bytes 835592 | tf_op jit(solution)/shard_map/ppermute | solution.py:316
  48.2 16.9 %copy-start.7 = (bf16[4,136,256]{2,1,0:T(8,128)(2,1)}, bf16[4,136,256]{2,1,0:T(8,128)(2,1)S(1)}, u32[]{:S(2)}) copy-start(bf16[4,136,256]{2,1,0:T(8,128)(2,1)S(1)} %collective-permute-done.7.rest_0_) | copy-start | bytes 835588
  49.0 16.1 %copy-start.8 = (bf16[4,136,256]{2,1,0:T(8,128)(2,1)}, bf16[4,136,256]{2,1,0:T(8,128)(2,1)S(1)}, u32[]{:S(2)}) copy-start(bf16[4,136,256]{2,1,0:T(8,128)(2,1)S(1)} %collective-permute-done.8.rest_1_) | copy-start | bytes 835588
  49.0 7.8 %collective-permute-start.9 = (bf16[4,136,256]{2,1,0:T(8,128)(2,1)S(1)}, bf16[4,136,256]{2,1,0:T(8,128)(2,1)S(1)}, u32[]{:S(2)}, u32[]{:S(2)}) collective-permute-start(bf16[4,136,256]{2,1,0:T(8,128)(2,1)S(1)} %collective-permute-done.7.rest_0_), channel_id=1, source_target_pairs={{0,4},{1,5},{2,6},{3,7},{4,8},{5,9},{6,10},{7,11},{8,12},{9,13},{1... | collective-permute-start | bytes 835592 | tf_op jit(solution)/shard_map/ppermute | solution.py:316
  56.8 8.4 %copy-start.9 = (bf16[4,136,256]{2,1,0:T(8,128)(2,1)}, bf16[4,136,256]{2,1,0:T(8,128)(2,1)S(1)}, u32[]{:S(2)}) copy-start(bf16[4,136,256]{2,1,0:T(8,128)(2,1)S(1)} %collective-permute-done.9.rest_2_) | copy-start | bytes 835588
  56.8 21.5 %all-to-all-start.2 = ((bf16[32,64,128]{2,1,0:T(8,128)(2,1)}), bf16[32,64,128]{2,1,0:T(8,128)(2,1)S(1)}, u32[]{:S(2)}, u32[]{:S(2)}) async-start(bf16[32,64,128]{2,1,0:T(8,128)(2,1)} %bitcast.10), calls=%async_computation.2 | async-start | bytes 1048576 | tf_op jit(solution)/shard_map/all_to_all | solution.py:410
  64.9 55.1 %all-gather.9.cloned.1.call-start = ((), (), s32[]{:S(2)}) async-start(), calls=%async_computation.5 | async-start | bytes 4718592 | tf_op jit(solution)/shard_map/all_gather | solution.py:451
  77.0 6.9 %copy-start.4 = (bf16[32,64,128]{2,1,0:T(8,128)(2,1)S(1)}, bf16[32,64,128]{2,1,0:T(8,128)(2,1)}, u32[]{:S(2)}) copy-start(bf16[32,64,128]{2,1,0:T(8,128)(2,1)} %get-tuple-element.50) | copy-start | bytes 1572868
  78.2 0.8 copy-start.3
Sparse Core Ops, SparseCore 0:
  10.4 28.7 all-gather.4
  41.1 34.5 all-gather.6
  84.1 34.4 all-gather.8
